TPU v7x, 32 devices: a whole 2x2x4 slice. The times are simulated.
32 devices in a mesh: section: 2 (over core), dp: 4 (over z), heads: 4 (over y, x).
Axes of the slice: x: 2, y: 2, z: 4, core: 2. Of those that a mesh axis runs over, the one named last changes fastest.
Arguments:
- query_embed: bfloat16 [256, 16, 768], P('heads', 'dp'), may hold values from -6 to 6
- key_embed: bfloat16 [256, 16, 768], P('heads', 'dp'), may hold values from -6 to 6
- crop_counts: int32 [16, 2], P('dp'), may hold values from 1 to 256, as said below
- pair_mask: int32 [16], P('dp'), may hold values from 0 to 1, as said below
- negative_queue: bfloat16 [4096, 768], P('dp'), may hold values from -6 to 6
- online_inproj: bfloat16 [2, 768, 3, 768], P('section', None, None, 'heads'), may hold values from -0.21875 to 0.21875
- online_inbias: bfloat16 [2, 2, 12, 64], P('section', None, 'heads'), may hold values from -3 to 3
- online_outproj: bfloat16 [2, 768, 768], P('section', 'heads'), may hold values from -0.625 to 0.625
- online_gains: bfloat16 [2, 2, 768], P('section'), may hold values from 0.5 to 1.5
- online_shifts: bfloat16 [2, 4, 768], P('section'), may hold values from -1.1953125 to 1.1953125
- online_expand: bfloat16 [2, 768, 3072], P('section', None, 'heads'), may hold values from -0.21875 to 0.21875
- online_expbias: bfloat16 [2, 12, 256], P('section', 'heads'), may hold values from -3 to 3
- online_contract: bfloat16 [2, 3072, 768], P('section', 'heads'), may hold values from -0.109375 to 0.109375
- momentum_inproj: bfloat16 [2, 768, 3, 768], P('section', None, None, 'heads'), may hold values from -0.21875 to 0.21875
- momentum_inbias: bfloat16 [2, 2, 12, 64], P('section', None, 'heads'), may hold values from -3 to 3
- momentum_outproj: bfloat16 [2, 768, 768], P('section', 'heads'), may hold values from -0.625 to 0.625
- momentum_gains: bfloat16 [2, 2, 768], P('section'), may hold values from 0.5 to 1.5
- momentum_shifts: bfloat16 [2, 4, 768], P('section'), may hold values from -1.1953125 to 1.1953125
- momentum_expand: bfloat16 [2, 768, 3072], P('section', None, 'heads'), may hold values from -0.21875 to 0.21875
- momentum_expbias: bfloat16 [2, 12, 256], P('section', 'heads'), may hold values from -3 to 3
- momentum_contract: bfloat16 [2, 3072, 768], P('section', 'heads'), may hold values from -0.109375 to 0.109375
Outputs:
- loss_value: float32 [], replicated
- input_grad: bfloat16 [256, 16, 768], P('heads', 'dp', 'section')
- grad_inproj: float32 [2, 768, 3, 768], P('section', 'dp', None, 'heads')
- grad_inbias: float32 [2, 2, 12, 64], P('section', None, 'heads', 'dp')
- grad_outproj: float32 [2, 768, 768], P('section', 'heads', 'dp')
- grad_gains: float32 [2, 2, 768], P('section', None, ('dp', 'heads'))
- grad_shifts: float32 [2, 4, 768], P('section', None, ('dp', 'heads'))
- grad_expand: float32 [2, 768, 3072], P('section', 'dp', 'heads')
- grad_expbias: float32 [2, 12, 256], P('section', 'heads', 'dp')
- grad_contract: float32 [2, 3072, 768], P('section', 'heads', 'dp')
- rms_values: float32 [2, 3], replicated
Inputs may be any that keep to these rules, and one draw needn't show every extreme that they name: `crop_counts`: every crop has at least one valid token; some pair has both crops full. `pair_mask`: at least one pair is live.
All inputs are finite; a program needn't handle non-finite values.
Results may differ from a plain program's by a relative error of at most 0.028.
Values may be sent and summed in bfloat16 or wider, within the bound.
No kernel may reach another device: no remote copies, remote signals or barrier semaphores. Data moves between devices by JAX's collectives and lax.ppermute only.
A program may use at most 128 MiB of HBM per device.

v0:
```python
import jax
import jax.numpy as jnp
from jax import lax
from jax.sharding import PartitionSpec as P

MICRO = 2


TEMPER = 0.05
NORM_EPS = 1e-06
NEG_FILL = -1000000000.0


def shifted(value, axis, steps):
    count = lax.axis_size(axis)
    leading, last = (max(0, -steps), min(count, count - steps))
    return lax.ppermute(value, axis, [(source, source + steps) for source in range(leading, last)])


def from_behind(block, axis, distance):
    devices = range(lax.axis_size(axis))
    route = [((i - distance) % len(devices), i) for i in devices]
    return lax.ppermute(block, axis, route)


def layer_norm(values, gain_row, shift_row):
    center = values - jnp.mean(values, axis=-1, keepdims=True)
    spread = jnp.mean(center * center, axis=-1, keepdims=True)
    return center * lax.rsqrt(spread + NORM_EPS) * gain_row + shift_row


def norm_rows(values, gain_row, shift_row):
    return layer_norm(values, gain_row[None, :, None, :], shift_row[None, :, None, :])


def normalize(values):
    return values * lax.rsqrt(jnp.sum(values * values, axis=-1, keepdims=True) + NORM_EPS)


def exact_gelu(values):
    return jax.nn.gelu(values, approximate=False)


def gather_rows(values):
    return lax.all_gather(values, "heads", axis=0, tiled=True)


def gather_grads(values):
    return lax.all_gather(values, "heads", axis=0, tiled=True)


def scatter_rows(left_side, right_side, formula, row_total):

    def row_term(row_start, row_span):
        return jnp.einsum(formula, left_side, right_side, preferred_element_type=jnp.float32)

    return lax.psum_scatter(
        row_term(jnp.int32(0), lax.axis_size("heads") * row_total).astype(jnp.bfloat16),
        "heads",
        scatter_dimension=0,
        tiled=True,
    ).astype(jnp.float32)


def scatter_grads(left_side, right_side, formula, row_total):

    def row_term(row_start, row_span):
        return jnp.einsum(formula, left_side, right_side, preferred_element_type=jnp.float32)

    return lax.psum_scatter(
        row_term(jnp.int32(0), lax.axis_size("heads") * row_total).astype(jnp.bfloat16),
        "heads",
        scatter_dimension=0,
        tiled=True,
    ).astype(jnp.float32)


def reduce_weights(gradients):
    return (
        lax.psum_scatter(
            gradients[0].astype(jnp.bfloat16), "dp", scatter_dimension=1, tiled=True
        ).astype(jnp.float32),
        lax.psum_scatter(
            gradients[1].astype(jnp.bfloat16), "dp", scatter_dimension=3, tiled=True
        ).astype(jnp.float32),
        lax.psum_scatter(
            gradients[2].astype(jnp.bfloat16), "dp", scatter_dimension=2, tiled=True
        ).astype(jnp.float32),
        lax.psum_scatter(
            gradients[3].astype(jnp.bfloat16), "dp", scatter_dimension=1, tiled=True
        ).astype(jnp.float32),
        lax.psum_scatter(
            gradients[4].astype(jnp.bfloat16), "dp", scatter_dimension=2, tiled=True
        ).astype(jnp.float32),
        lax.psum_scatter(
            gradients[5].astype(jnp.bfloat16), "dp", scatter_dimension=2, tiled=True
        ).astype(jnp.float32),
    )


def reduce_norms(gradients):
    return (
        lax.psum_scatter(gradients[0], ("dp", "heads"), scatter_dimension=2, tiled=True),
        lax.psum_scatter(gradients[1], ("dp", "heads"), scatter_dimension=2, tiled=True),
    )


def key_mask(keep):
    return jnp.moveaxis(keep, 0, -1)[None, :, :, None, :]


def masked_scores(queries, keys_here, keep, scale):
    scores = (
        jnp.einsum("qebhd,kebhd->qebhk", queries, keys_here, preferred_element_type=jnp.float32)
        * scale
    )
    return jnp.where(key_mask(keep), scores, NEG_FILL)


def attend_forward(queries, keys_here, values, keep, scale):
    scores = masked_scores(queries, keys_here, keep, scale)
    highest = jnp.max(scores, axis=-1, keepdims=True)
    raised = jnp.exp(scores - highest)
    totals = jnp.sum(raised, axis=-1, keepdims=True)
    shares_low = (raised / totals).astype(jnp.bfloat16)
    context = jnp.einsum(
        "qebhk,kebhd->qebhd", shares_low, values, preferred_element_type=jnp.float32
    ).astype(jnp.bfloat16)
    return (context, (highest + jnp.log(totals))[..., 0])


def attend_backward(queries, keys_here, values, log_total, d_context, keep, scale):
    scores = masked_scores(queries, keys_here, keep, scale)
    shares = jnp.exp(scores - log_total[..., None])
    d_values = jnp.einsum(
        "qebhk,qebhd->kebhd",
        shares.astype(jnp.bfloat16),
        d_context,
        preferred_element_type=jnp.float32,
    )
    d_shares = jnp.einsum(
        "qebhd,kebhd->qebhk", d_context, values, preferred_element_type=jnp.float32
    )
    d_scores = (shares * (d_shares - jnp.sum(d_shares * shares, axis=-1, keepdims=True))).astype(
        jnp.bfloat16
    )
    d_queries = (
        jnp.einsum("qebhk,kebhd->qebhd", d_scores, keys_here, preferred_element_type=jnp.float32)
        * scale
    )
    d_keys = (
        jnp.einsum("qebhk,qebhd->kebhd", d_scores, queries, preferred_element_type=jnp.float32)
        * scale
    )
    return (d_queries, d_keys, d_values)


def layer_forward(layer_in, keep, weights):
    inproj, inbias, outproj, gains, shifts, expand, expbias, contract = weights
    local_len = layer_in.shape[0]
    gains = gains.astype(jnp.float32)
    shifts = shifts.astype(jnp.float32)
    full_in = gather_rows(layer_in)
    full_len, encoders, micro_rows, feature_width = full_in.shape
    heads_here, head_width = (inbias.shape[2], inbias.shape[3])
    local_width = heads_here * head_width
    scale = head_width ** (-0.5)
    project = jnp.einsum("lebd,edcn->lebcn", full_in, inproj, preferred_element_type=jnp.float32)
    bias = inbias.astype(jnp.float32).reshape(encoders, 2, local_width)
    head_shape = (full_len, encoders, micro_rows, heads_here, head_width)
    queries = (
        (project[:, :, :, 0] + bias[None, :, None, 0]).astype(jnp.bfloat16).reshape(head_shape)
    )
    keys_here = project[:, :, :, 1].astype(jnp.bfloat16).reshape(head_shape)
    values = (project[:, :, :, 2] + bias[None, :, None, 1]).astype(jnp.bfloat16).reshape(head_shape)
    context, log_total = attend_forward(queries, keys_here, values, keep, scale)
    context_flat = context.reshape(full_len, encoders, micro_rows, local_width)
    attention_out = (
        scatter_rows(context_flat, outproj, "lebn,end->lebd", local_len) + shifts[None, :, None, 0]
    )
    mixed = layer_in.astype(jnp.float32) + attention_out
    hidden = norm_rows(mixed, gains[:, 0], shifts[:, 1])
    full_hidden = gather_rows(hidden.astype(jnp.bfloat16))
    inner = jnp.einsum("lebd,edf->lebf", full_hidden, expand, preferred_element_type=jnp.float32)
    inner = inner + expbias.astype(jnp.float32).reshape(encoders, -1)[None, :, None, :]
    active = exact_gelu(inner).astype(jnp.bfloat16)
    feed_out = (
        scatter_rows(active, contract, "lebf,efd->lebd", local_len) + shifts[None, :, None, 2]
    )
    summed = hidden + feed_out
    layer_out = norm_rows(summed, gains[:, 1], shifts[:, 3])
    cached = (
        full_in,
        queries,
        keys_here,
        values,
        log_total,
        context_flat,
        mixed,
        full_hidden,
        inner,
        active,
        summed,
    )
    return (layer_out, attention_out, feed_out, cached)


def layer_backward(d_out, cached, weights, keep):
    inproj, inbias, outproj, gains, shifts, expand, expbias, contract = weights
    (
        full_in,
        queries,
        keys_here,
        values,
        log_total,
        context_flat,
        mixed,
        full_hidden,
        inner,
        active,
        summed,
    ) = cached
    gains = gains.astype(jnp.float32)
    shifts = shifts.astype(jnp.float32)
    local_len = d_out.shape[0]
    full_len, encoders, micro_rows = (queries.shape[0], queries.shape[1], queries.shape[2])
    scale = queries.shape[4] ** (-0.5)
    local_width = context_flat.shape[3]
    _, pull_out = jax.vjp(norm_rows, summed, gains[:, 1], shifts[:, 3])
    d_summed, d_gain_out, d_shift_out = pull_out(d_out)
    full_d_feed = gather_grads(d_summed.astype(jnp.bfloat16))
    g_contract = jnp.einsum(
        "lebf,lebd->efd", active, full_d_feed, preferred_element_type=jnp.float32
    )
    d_active = jnp.einsum(
        "lebd,efd->lebf", full_d_feed, contract, preferred_element_type=jnp.float32
    )
    _, pull_gelu = jax.vjp(exact_gelu, inner)
    d_inner = pull_gelu(d_active)[0]
    g_expbias = jnp.sum(d_inner, axis=(0, 2)).reshape(expbias.shape)
    d_inner_low = d_inner.astype(jnp.bfloat16)
    g_expand = jnp.einsum(
        "lebd,lebf->edf", full_hidden, d_inner_low, preferred_element_type=jnp.float32
    )
    d_hidden = d_summed + scatter_grads(d_inner_low, expand, "lebf,edf->lebd", local_len)
    _, pull_mid = jax.vjp(norm_rows, mixed, gains[:, 0], shifts[:, 1])
    d_mixed, d_gain_mid, d_shift_mid = pull_mid(d_hidden)
    full_d_attn = gather_grads(d_mixed.astype(jnp.bfloat16))
    g_outproj = jnp.einsum(
        "lebn,lebd->end", context_flat, full_d_attn, preferred_element_type=jnp.float32
    )
    d_context = jnp.einsum(
        "lebd,end->lebn", full_d_attn, outproj, preferred_element_type=jnp.float32
    )
    d_context = d_context.astype(jnp.bfloat16).reshape(queries.shape)
    d_queries, d_keys, d_values = attend_backward(
        queries, keys_here, values, log_total, d_context, keep, scale
    )
    g_inbias = jnp.stack([jnp.sum(d_queries, axis=(0, 2)), jnp.sum(d_values, axis=(0, 2))], axis=1)
    d_project = jnp.stack([d_queries, d_keys, d_values], axis=3)
    d_project = d_project.reshape(full_len, encoders, micro_rows, 3, local_width).astype(
        jnp.bfloat16
    )
    g_inproj = jnp.einsum(
        "lebd,lebcn->edcn", full_in, d_project, preferred_element_type=jnp.float32
    )
    d_in = d_mixed + scatter_grads(d_project, inproj, "lebcn,edcn->lebd", local_len)
    g_gains = jnp.stack([d_gain_mid, d_gain_out], axis=1)
    g_shifts = jnp.stack(
        [jnp.sum(d_mixed, axis=(0, 2)), d_shift_mid, jnp.sum(d_summed, axis=(0, 2)), d_shift_out],
        axis=1,
    )
    return (
        d_in,
        (g_inproj, g_inbias, g_outproj, g_expand, g_expbias, g_contract),
        (g_gains, g_shifts),
    )


def per_device(
    query_embed,
    key_embed,
    crop_counts,
    pair_mask,
    negative_queue,
    online_inproj,
    online_inbias,
    online_outproj,
    online_gains,
    online_shifts,
    online_expand,
    online_expbias,
    online_contract,
    momentum_inproj,
    momentum_inbias,
    momentum_outproj,
    momentum_gains,
    momentum_shifts,
    momentum_expand,
    momentum_expbias,
    momentum_contract,
):
    online = (
        online_inproj,
        online_inbias,
        online_outproj,
        online_gains,
        online_shifts,
        online_expand,
        online_expbias,
        online_contract,
    )
    momentum = (
        momentum_inproj,
        momentum_inbias,
        momentum_outproj,
        momentum_gains,
        momentum_shifts,
        momentum_expand,
        momentum_expbias,
        momentum_contract,
    )
    paired = tuple(
        (
            jnp.concatenate([online_part, momentum_part], axis=0)
            for online_part, momentum_part in zip(online, momentum)
        )
    )
    section_index = lax.axis_index("section")
    head_index = lax.axis_index("heads")
    data_index = lax.axis_index("dp")
    local_len, pairs_dev, feature_width = query_embed.shape
    half_width = feature_width // lax.axis_size("section")
    full_len = local_len * lax.axis_size("heads")
    micro_rows = pairs_dev // MICRO
    positions = jnp.arange(full_len)
    query_keep = positions[:, None] < crop_counts[None, :, 0]
    key_keep = positions[:, None] < crop_counts[None, :, 1]
    row_keep = lax.dynamic_slice_in_dim(query_keep, head_index * local_len, local_len, 0)
    key_rows = lax.dynamic_slice_in_dim(key_keep, head_index * local_len, local_len, 0)

    def pick_pairs(table, micro_index):
        first_pair = jnp.clip(micro_index, 0, MICRO - 1) * micro_rows
        return lax.dynamic_slice_in_dim(table, first_pair, micro_rows, 1)

    received = jnp.zeros((local_len, 2, micro_rows, feature_width), jnp.bfloat16)
    caches = []
    pooled = []
    branch_sums = jnp.zeros((3,), jnp.float32)
    for moment in range(MICRO + 1):
        micro_index = moment - section_index
        is_valid = ((micro_index >= 0) & (micro_index < MICRO)).astype(jnp.float32)
        if moment < MICRO:
            arriving = jnp.stack(
                [
                    query_embed[:, moment * micro_rows : (moment + 1) * micro_rows],
                    key_embed[:, moment * micro_rows : (moment + 1) * micro_rows],
                ],
                axis=1,
            )
        else:
            arriving = jnp.zeros_like(received)
        layer_in = jnp.where(section_index == 0, arriving, received)
        keep_full = jnp.stack(
            [pick_pairs(query_keep, micro_index), pick_pairs(key_keep, micro_index)], axis=1
        )
        keep_here = jnp.stack(
            [pick_pairs(row_keep, micro_index), pick_pairs(key_rows, micro_index)], axis=1
        )
        layer_out, attention_out, feed_out, cached = layer_forward(layer_in, keep_full, paired)
        row_weight = keep_here[:, 0, :, None].astype(jnp.float32)
        branch_sums = branch_sums + is_valid * jnp.stack(
            [
                jnp.sum(row_weight * attention_out[:, 0] * attention_out[:, 0]),
                jnp.sum(row_weight * feed_out[:, 0] * feed_out[:, 0]),
                jnp.sum(row_weight * layer_out[:, 0] * layer_out[:, 0]),
            ]
        )
        if moment >= 1:
            partial_pool = jnp.sum(jnp.where(keep_here[..., None], layer_out, 0.0), axis=0)
            pooled.append(lax.psum(partial_pool, "heads"))
        caches.append(jax.tree.map(lambda member: member[:, :1], cached))
        if moment < MICRO:
            received = shifted(layer_out.astype(jnp.bfloat16), "section", 1)
    pooled_all = jnp.concatenate(pooled, axis=1)
    counts = crop_counts.astype(jnp.float32)
    query_vec = pooled_all[0] / counts[:, 0, None]
    key_vec = pooled_all[1] / counts[:, 1, None]
    key_low = normalize(key_vec).astype(jnp.bfloat16)
    queue_low = normalize(negative_queue.astype(jnp.float32)).astype(jnp.bfloat16)
    live_low = pair_mask.astype(jnp.bfloat16)
    all_keys, all_live, all_queue = (
        lax.all_gather(key_low, "dp", axis=0, tiled=True),
        lax.all_gather(live_low, "dp", axis=0, tiled=True),
        lax.all_gather(queue_low, "dp", axis=0, tiled=True),
    )
    query_unit, pull_unit = jax.vjp(normalize, query_vec)
    query_low = query_unit.astype(jnp.bfloat16)
    live_all = all_live.astype(jnp.float32)
    positive = (
        jnp.einsum("pd,kd->pk", query_low, all_keys, preferred_element_type=jnp.float32) / TEMPER
    )
    positive = jnp.where(live_all[None, :] > 0, positive, NEG_FILL)
    negative = (
        jnp.einsum("pd,kd->pk", query_low, all_queue, preferred_element_type=jnp.float32) / TEMPER
    )
    highest = jnp.maximum(jnp.max(positive, axis=1), jnp.max(negative, axis=1))[:, None]
    pos_raised = jnp.exp(positive - highest)
    neg_raised = jnp.exp(negative - highest)
    totals = jnp.sum(pos_raised, axis=1) + jnp.sum(neg_raised, axis=1)
    log_sums = highest[:, 0] + jnp.log(totals)
    targets = data_index * pairs_dev + jnp.arange(pairs_dev)
    own_pair = (jnp.arange(positive.shape[1])[None, :] == targets[:, None]).astype(jnp.float32)
    own_logit = jnp.sum(own_pair * positive, axis=1)
    pair_weight = pair_mask.astype(jnp.float32) / jnp.sum(live_all)
    loss_part = jnp.sum(pair_weight * (log_sums - own_logit))
    d_positive = (pair_weight[:, None] * (pos_raised / totals[:, None] - own_pair) / TEMPER).astype(
        jnp.bfloat16
    )
    d_negative = (pair_weight[:, None] * (neg_raised / totals[:, None]) / TEMPER).astype(
        jnp.bfloat16
    )
    d_unit = jnp.einsum("pk,kd->pd", d_positive, all_keys, preferred_element_type=jnp.float32)
    d_unit = d_unit + jnp.einsum(
        "pk,kd->pd", d_negative, all_queue, preferred_element_type=jnp.float32
    )
    d_pool = pull_unit(d_unit)[0] / counts[:, 0, None]
    received_grad = jnp.zeros((local_len, 1, micro_rows, feature_width), jnp.bfloat16)
    input_pieces = []
    big_total = None
    small_total = None
    for moment in range(MICRO + 1):
        micro_index = jnp.where(section_index == 1, moment, moment - 1)
        if moment < MICRO:
            rows_now = row_keep[:, moment * micro_rows : (moment + 1) * micro_rows].astype(
                jnp.float32
            )
            arriving = (
                rows_now[..., None] * d_pool[moment * micro_rows : (moment + 1) * micro_rows][None]
            )[:, None]
        else:
            arriving = jnp.zeros((local_len, 1, micro_rows, feature_width), jnp.float32)
        d_here = jnp.where(section_index == 1, arriving, received_grad.astype(jnp.float32))
        later = caches[min(moment + 1, MICRO)]
        earlier = caches[max(moment - 1, 0)]
        cached = jax.tree.map(
            lambda late_part, early_part: jnp.where(section_index == 1, late_part, early_part),
            later,
            earlier,
        )
        keep_full = pick_pairs(query_keep, micro_index)[:, None]
        d_in, big_grads, small_grads = layer_backward(d_here, cached, online, keep_full)
        low_in = d_in.astype(jnp.bfloat16)
        received_grad = from_behind(low_in, "section", -1)
        if moment >= 1:
            whole_grad = jnp.where(section_index == 0, low_in, received_grad)[:, 0]
            input_pieces.append(
                lax.dynamic_slice_in_dim(whole_grad, section_index * half_width, half_width, 2)
            )
        big_part = reduce_weights(big_grads)
        small_part = reduce_norms(small_grads)
        if big_total is None:
            big_total = big_part
            small_total = small_part
        else:
            big_total = jax.tree.map(jnp.add, big_total, big_part)
            small_total = jax.tree.map(jnp.add, small_total, small_part)
    layer_pick = (jnp.arange(2) == section_index).astype(jnp.float32)
    rms_terms = layer_pick[:, None] * branch_sums[None, :]
    loss_term = jnp.where((section_index == 1) & (head_index == 0), loss_part, 0.0)
    token_term = jnp.where(section_index == 0, jnp.sum(row_keep.astype(jnp.float32)), 0.0)
    loss_total, rms_total, token_total = lax.psum(
        (loss_term, rms_terms, token_term), ("section", "dp", "heads")
    )
    rms_values = jnp.sqrt(rms_total / (token_total * feature_width))
    input_grad = jnp.concatenate(input_pieces, axis=1)
    return (
        loss_total,
        input_grad,
        big_total[0],
        big_total[1],
        big_total[2],
        small_total[0],
        small_total[1],
        big_total[3],
        big_total[4],
        big_total[5],
        rms_values,
    )


def solution(mesh):
    placed = (
        P("heads", "dp", None),
        P("heads", "dp", None),
        P("dp", None),
        P("dp"),
        P("dp", None),
        P("section", None, None, "heads"),
        P("section", None, "heads", None),
        P("section", "heads", None),
        P("section", None, None),
        P("section", None, None),
        P("section", None, "heads"),
        P("section", "heads", None),
        P("section", "heads", None),
        P("section", None, None, "heads"),
        P("section", None, "heads", None),
        P("section", "heads", None),
        P("section", None, None),
        P("section", None, None),
        P("section", None, "heads"),
        P("section", "heads", None),
        P("section", "heads", None),
    )
    return jax.shard_map(
        per_device,
        mesh=mesh,
        in_specs=placed,
        out_specs=(
            P(),
            P("heads", "dp", "section"),
            P("section", "dp", None, "heads"),
            P("section", None, "heads", "dp"),
            P("section", "heads", "dp"),
            P("section", None, ("dp", "heads")),
            P("section", None, ("dp", "heads")),
            P("section", "dp", "heads"),
            P("section", "heads", "dp"),
            P("section", "heads", "dp"),
            P(),
        ),
        check_vma=False,
    )
```

profile of v0, /device:TPU:1, one launch (start us, length us, event | category | flops | bytes accessed | tf_op | source)
XLA Modules:
  0.0 1555.8 jit_solution(12320386162537323816)
XLA Ops:
  15.1 31.5 %all-gather.9.cloned.1.call-done = bf16[256,2,2,768]{3,0,2,1:T(8,128)(2,1)} async-done(((bf16[64,2,2,768]{3,0,2,1:T(8,128)(2,1)}), bf16[256,2,2,768]{3,0,2,1:T(8,128)(2,1)}) %all-gather.9.cloned.1.call-update) | async-done | bytes 1572880 | tf_op jit(solution)/shard_map/all_gather | solution.py:45
  55.3 30.3 %reduce-scatter.67.cloned.1.call-done = bf16[64,2,2,768]{3,0,2,1:T(8,128)(2,1)} async-done(((bf16[256,2,2,768]{3,0,2,1:T(8,128)(2,1)}), bf16[64,2,2,768]{3,0,2,1:T(8,128)(2,1)}) %reduce-scatter.67.cloned.1.call-update) | async-done | bytes 393232 | tf_op jit(solution)/shard_map/reduce_scatter | solution.py:57
  91.9 28.1 %all-gather.11.cloned.1.call-done = bf16[256,2,2,768]{3,0,2,1:T(8,128)(2,1)} async-done(((bf16[64,2,2,768]{3,0,2,1:T(8,128)(2,1)}), bf16[256,2,2,768]{3,0,2,1:T(8,128)(2,1)}) %all-gather.11.cloned.1.call-update) | async-done | bytes 1572880 | tf_op jit(solution)/shard_map/all_gather | solution.py:45
  120.0 11.0 fusion.4
  135.4 30.4 %reduce-scatter.69.cloned.1.call-done = bf16[64,2,2,768]{3,0,2,1:T(8,128)(2,1)} async-done(((bf16[256,2,2,768]{3,0,2,1:T(8,128)(2,1)}), bf16[64,2,2,768]{3,0,2,1:T(8,128)(2,1)}) %reduce-scatter.69.cloned.1.call-update) | async-done | bytes 393232 | tf_op jit(solution)/shard_map/reduce_scatter | solution.py:57
  175.0 30.4 %all-gather.13.cloned.1.call-done = bf16[256,2,2,768]{3,0,2,1:T(8,128)(2,1)} async-done(((bf16[64,2,2,768]{3,0,2,1:T(8,128)(2,1)}), bf16[256,2,2,768]{3,0,2,1:T(8,128)(2,1)}) %all-gather.13.cloned.1.call-update) | async-done | bytes 1572880 | tf_op jit(solution)/shard_map/all_gather | solution.py:45
  214.1 31.0 %reduce-scatter.71.cloned.1.call-done = bf16[64,2,2,768]{3,0,2,1:T(8,128)(2,1)} async-done(((bf16[256,2,2,768]{3,0,2,1:T(8,128)(2,1)}), bf16[64,2,2,768]{3,0,2,1:T(8,128)(2,1)}) %reduce-scatter.71.cloned.1.call-update) | async-done | bytes 393232 | tf_op jit(solution)/shard_map/reduce_scatter | solution.py:57
  248.5 31.1 %all-gather.15.cloned.1.call-done = bf16[256,2,2,768]{3,0,2,1:T(8,128)(2,1)} async-done(((bf16[64,2,2,768]{3,0,2,1:T(8,128)(2,1)}), bf16[256,2,2,768]{3,0,2,1:T(8,128)(2,1)}) %all-gather.15.cloned.1.call-update) | async-done | bytes 1572880 | tf_op jit(solution)/shard_map/all_gather | solution.py:45
  279.6 11.3 fusion.7
  296.0 29.7 %reduce-scatter.73.cloned.1.call-done = bf16[64,2,2,768]{3,0,2,1:T(8,128)(2,1)} async-done(((bf16[256,2,2,768]{3,0,2,1:T(8,128)(2,1)}), bf16[64,2,2,768]{3,0,2,1:T(8,128)(2,1)}) %reduce-scatter.73.cloned.1.call-update) | async-done | bytes 393232 | tf_op jit(solution)/shard_map/reduce_scatter | solution.py:57
  333.9 30.3 %all-gather.17.cloned.1.call-done = bf16[256,2,2,768]{3,0,2,1:T(8,128)(2,1)} async-done(((bf16[64,2,2,768]{3,0,2,1:T(8,128)(2,1)}), bf16[256,2,2,768]{3,0,2,1:T(8,128)(2,1)}) %all-gather.17.cloned.1.call-update) | async-done | bytes 1572880 | tf_op jit(solution)/shard_map/all_gather | solution.py:45
  364.2 3.1 convolution_bitcast_fusion
  372.7 31.0 %reduce-scatter.75.cloned.1.call-done = bf16[64,2,2,768]{3,0,2,1:T(8,128)(2,1)} async-done(((bf16[256,2,2,768]{3,0,2,1:T(8,128)(2,1)}), bf16[64,2,2,768]{3,0,2,1:T(8,128)(2,1)}) %reduce-scatter.75.cloned.1.call-update) | async-done | bytes 393232 | tf_op jit(solution)/shard_map/reduce_scatter | solution.py:57
  407.2 31.0 %all-gather.19.cloned.1.call-done = bf16[256,2,2,768]{3,0,2,1:T(8,128)(2,1)} async-done(((bf16[64,2,2,768]{3,0,2,1:T(8,128)(2,1)}), bf16[256,2,2,768]{3,0,2,1:T(8,128)(2,1)}) %all-gather.19.cloned.1.call-update) | async-done | bytes 1572880 | tf_op jit(solution)/shard_map/all_gather | solution.py:45
  438.2 11.1 fusion.10
  458.8 9.8 all-reduce
  471.5 12.7 reduce-scatter.77.cloned.1.call-done
  488.5 13.1 all-reduce.2
  501.9 12.9 all-gather
  520.3 52.3 %all-gather.21.cloned.1.call-done = bf16[4096,768]{1,0:T(8,128)(2,1)} async-done(((bf16[1024,768]{1,0:T(8,128)(2,1)}), bf16[4096,768]{1,0:T(8,128)(2,1)}) %all-gather.21.cloned.1.call-update) | async-done | bytes 6291472 | tf_op jit(solution)/shard_map/all_gather | solution.py:395
  572.6 4.8 fusion.393
  581.8 10.4 all_gather.54
  592.2 5.0 fusion.396
  603.8 20.8 %reduce-scatter.79.cloned.1.call-done = bf16[64,1,2,768]{3,0,2,1:T(8,128)(2,1)} async-done(((bf16[256,1,2,768]{3,0,2,1:T(8,128)(2,1)}), bf16[64,1,2,768]{3,0,2,1:T(8,128)(2,1)}) %reduce-scatter.79.cloned.1.call-update) | async-done | bytes 196624 | tf_op jit(solution)/shard_map/reduce_scatter | solution.py:70
  628.5 9.3 all_gather.55
  643.8 27.8 %reduce-scatter.81.cloned.1.call-done = bf16[64,1,2,768]{3,0,2,1:T(8,128)(2,1)} async-done(((bf16[256,1,2,768]{3,0,2,1:T(8,128)(2,1)}), bf16[64,1,2,768]{3,0,2,1:T(8,128)(2,1)}) %reduce-scatter.81.cloned.1.call-update) | async-done | bytes 196624 | tf_op jit(solution)/shard_map/reduce_scatter | solution.py:70
  675.2 10.7 all_gather.56
  685.9 6.8 fusion.395
  694.8 27.1 %reduce-scatter.83.cloned.1.call-done = bf16[64,1,2,768]{3,0,2,1:T(8,128)(2,1)} async-done(((bf16[256,1,2,768]{3,0,2,1:T(8,128)(2,1)}), bf16[64,1,2,768]{3,0,2,1:T(8,128)(2,1)}) %reduce-scatter.83.cloned.1.call-update) | async-done | bytes 196624 | tf_op jit(solution)/shard_map/reduce_scatter | solution.py:70
  724.5 9.4 all_gather.57
  740.5 27.8 %reduce-scatter.85.cloned.1.call-done = bf16[64,1,2,768]{3,0,2,1:T(8,128)(2,1)} async-done(((bf16[256,1,2,768]{3,0,2,1:T(8,128)(2,1)}), bf16[64,1,2,768]{3,0,2,1:T(8,128)(2,1)}) %reduce-scatter.85.cloned.1.call-update) | async-done | bytes 196624 | tf_op jit(solution)/shard_map/reduce_scatter | solution.py:70
  771.8 10.5 all_gather.58
  782.4 6.3 fusion.394
  795.9 3.2 fusion.110
  799.1 5.8 copy.233
  806.2 3.2 fusion.113
  818.4 3.2 fusion.111
  821.7 5.8 copy.235
  838.6 9.3 all_gather.59
  857.7 3.2 fusion.112
  860.9 5.8 copy.237
  868.0 3.6 fusion.107
  871.7 3.0 fusion.108
  874.8 3.5 fusion.109
  886.4 5.8 fusion.324
  892.6 2.9 fusion.118
  895.7 43.0 %all-reduce.1 = (f32[]{:T(128)}, f32[2,3]{1,0:T(2,128)S(1)}, f32[]{:T(128)}) all-reduce(f32[]{:T(128)S(6)} %select_n.338, f32[2,3]{1,0:T(2,128)S(1)} %broadcast_multiply_fusion.6, f32[]{:T(128)S(6)} %select_n.397), channel_id=1, replica_groups=mesh['section'=2,'dp'=4,'heads'=4] {'section','dp','heads'}, use_global_device_ids=true, to_apply=%region_38.39 | all-reduce | flops 8 | bytes 64 | tf_op jit(solution)/shard_map/psum | solution.py:472
  946.7 8.9 reduce-scatter.117.cloned.1.call-done
  957.1 17.7 %reduce-scatter.105.cloned.1.call-done = bf16[16,6]{1,0:T(8,128)(2,1)} async-done(((bf16[64,6]{1,0:T(8,128)(2,1)}), bf16[16,6]{1,0:T(8,128)(2,1)}) %reduce-scatter.105.cloned.1.call-update) | async-done | bytes 208
  975.7 21.8 %reduce-scatter.111.cloned.1.call-done = bf16[192,192]{1,0:T(8,128)(2,1)} async-done(((bf16[768,192]{1,0:T(8,128)(2,1)}), bf16[192,192]{1,0:T(8,128)(2,1)}) %reduce-scatter.111.cloned.1.call-update) | async-done | bytes 73744
  999.2 29.0 %reduce-scatter.123.cloned.1.call-done = bf16[192,768]{1,0:T(8,128)(2,1)} async-done(((bf16[768,768]{1,0:T(8,128)(2,1)}), bf16[192,768]{1,0:T(8,128)(2,1)}) %reduce-scatter.123.cloned.1.call-update) | async-done | bytes 294928
  1030.1 25.4 %reduce-scatter.99.cloned.1.call-done = bf16[192,576]{1,0:T(8,128)(2,1)} async-done(((bf16[768,576]{1,0:T(8,128)(2,1)}), bf16[192,576]{1,0:T(8,128)(2,1)}) %reduce-scatter.99.cloned.1.call-update) | async-done | bytes 221200
  1057.5 3.0 fusion.115
  1065.3 7.9 reduce-scatter.119.cloned.1.call-done
  1074.8 17.9 %reduce-scatter.107.cloned.1.call-done = bf16[16,6]{1,0:T(8,128)(2,1)} async-done(((bf16[64,6]{1,0:T(8,128)(2,1)}), bf16[16,6]{1,0:T(8,128)(2,1)}) %reduce-scatter.107.cloned.1.call-update) | async-done | bytes 208
  1094.1 123.7 %reduce-scatter.127.cloned.1.call-done = f32[48,2]{1,0:T(8,128)} async-done(((f32[768,2]{1,0:T(8,128)}), f32[48,2]{1,0:T(8,128)}) %reduce-scatter.127.cloned.1.call-update) | async-done | bytes 400
  1219.2 124.7 %reduce-scatter.129.cloned.1.call-done = f32[48,4]{1,0:T(8,128)} async-done(((f32[768,4]{1,0:T(8,128)}), f32[48,4]{1,0:T(8,128)}) %reduce-scatter.129.cloned.1.call-update) | async-done | bytes 784
  1345.2 21.5 %reduce-scatter.113.cloned.1.call-done = bf16[192,192]{1,0:T(8,128)(2,1)} async-done(((bf16[768,192]{1,0:T(8,128)(2,1)}), bf16[192,192]{1,0:T(8,128)(2,1)}) %reduce-scatter.113.cloned.1.call-update) | async-done | bytes 73744
  1368.6 29.0 %reduce-scatter.125.cloned.1.call-done = bf16[192,768]{1,0:T(8,128)(2,1)} async-done(((bf16[768,768]{1,0:T(8,128)(2,1)}), bf16[192,768]{1,0:T(8,128)(2,1)}) %reduce-scatter.125.cloned.1.call-update) | async-done | bytes 294928
  1400.7 27.4 %reduce-scatter.91.cloned.1.call-done = bf16[1,192,768]{2,1,0:T(8,128)(2,1)} async-done(((bf16[1,768,768]{2,1,0:T(8,128)(2,1)}), bf16[1,192,768]{2,1,0:T(8,128)(2,1)}) %reduce-scatter.91.cloned.1.call-update) | async-done | bytes 294928 | tf_op jit(solution)/shard_map/reduce_scatter | solution.py:89
  1428.0 30.3 %reduce-scatter.93.cloned.1.call-done = bf16[1,192,768]{2,1,0:T(8,128)(2,1)} async-done(((bf16[1,768,768]{2,1,0:T(8,128)(2,1)}), bf16[1,192,768]{2,1,0:T(8,128)(2,1)}) %reduce-scatter.93.cloned.1.call-update) | async-done | bytes 294928 | tf_op jit(solution)/shard_map/reduce_scatter | solution.py:89
  1458.4 30.2 %reduce-scatter.95.cloned.1.call-done = bf16[1,192,768]{2,1,0:T(8,128)(2,1)} async-done(((bf16[1,768,768]{2,1,0:T(8,128)(2,1)}), bf16[1,192,768]{2,1,0:T(8,128)(2,1)}) %reduce-scatter.95.cloned.1.call-update) | async-done | bytes 294928 | tf_op jit(solution)/shard_map/reduce_scatter | solution.py:89
  1490.6 25.9 %reduce-scatter.89.cloned.1.call-done = bf16[64,1,2,768]{3,0,2,1:T(8,128)(2,1)} async-done(((bf16[256,1,2,768]{3,0,2,1:T(8,128)(2,1)}), bf16[64,1,2,768]{3,0,2,1:T(8,128)(2,1)}) %reduce-scatter.89.cloned.1.call-update) | async-done | bytes 196624 | tf_op jit(solution)/shard_map/reduce_scatter | solution.py:70
  1518.3 26.6 %reduce-scatter.101.cloned.1.call-done = bf16[192,576]{1,0:T(8,128)(2,1)} async-done(((bf16[768,576]{1,0:T(8,128)(2,1)}), bf16[192,576]{1,0:T(8,128)(2,1)}) %reduce-scatter.101.cloned.1.call-update) | async-done | bytes 221200
  (780 shorter events, 213.5 us)
Async XLA Ops:
  8.0 38.6 %all-gather.9.cloned.1.call-start = ((), (), s32[]{:S(2)}) async-start(), calls=%async_computation.32 | async-start | bytes 1966080 | tf_op jit(solution)/shard_map/all_gather | solution.py:45
  10.2 36.4 %copy-start.162 = (bf16[1,768,3,192]{1,3,2,0:T(8,128)(2,1)S(1)}, bf16[1,768,3,192]{1,3,2,0:T(8,128)(2,1)}, u32[]{:S(2)}) copy-start(bf16[1,768,3,192]{1,3,2,0:T(8,128)(2,1)} %param.34) | copy-start | bytes 2654212
  10.2 36.4 %copy-start.164 = (bf16[1,768,3,192]{1,3,2,0:T(8,128)(2,1)S(1)}, bf16[1,768,3,192]{1,3,2,0:T(8,128)(2,1)}, u32[]{:S(2)}) copy-start(bf16[1,768,3,192]{1,3,2,0:T(8,128)(2,1)} %param.26) | copy-start | bytes 2654212
  13.4 72.2 %reduce-scatter.67.cloned.1.call-start = ((), (), s32[]{:S(2)}) async-start(), calls=%async_computation.33 | async-start | bytes 1966080 | tf_op jit(solution)/shard_map/reduce_scatter | solution.py:57
  54.5 65.5 %all-gather.11.cloned.1.call-start = ((), (), s32[]{:S(2)}) async-start(), calls=%async_computation.34 | async-start | bytes 1966080 | tf_op jit(solution)/shard_map/all_gather | solution.py:45
  88.9 77.0 %reduce-scatter.69.cloned.1.call-start = ((), (), s32[]{:S(2)}) async-start(), calls=%async_computation.35 | async-start | bytes 1966080 | tf_op jit(solution)/shard_map/reduce_scatter | solution.py:57
  91.9 39.1 %copy-start.120 = (f32[2,768]{1,0:T(2,128)}, f32[2,768]{1,0:T(2,128)S(1)}, u32[]{:S(2)}) copy-start(f32[2,768]{1,0:T(2,128)S(1)} %maximum_convert_fusion.2) | copy-start | bytes 18436
  91.9 40.2 %copy-start.72 = (bf16[1,768,768]{1,2,0:T(8,128)(2,1)S(1)}, bf16[1,768,768]{1,2,0:T(8,128)(2,1)}, u32[]{:S(2)}) copy-start(bf16[1,768,768]{1,2,0:T(8,128)(2,1)} %copy.133) | copy-start | bytes 3538948
  91.9 40.2 %copy-start.75 = (bf16[1,768,768]{1,2,0:T(8,128)(2,1)S(1)}, bf16[1,768,768]{1,2,0:T(8,128)(2,1)}, u32[]{:S(2)}) copy-start(bf16[1,768,768]{1,2,0:T(8,128)(2,1)} %copy.132) | copy-start | bytes 3538948
  134.7 70.6 %all-gather.13.cloned.1.call-start = ((), (), s32[]{:S(2)}) async-start(), calls=%async_computation.36 | async-start | bytes 1966080 | tf_op jit(solution)/shard_map/all_gather | solution.py:45
  169.4 36.0 %copy-start.163 = (bf16[1,768,3,192]{1,3,2,0:T(8,128)(2,1)S(1)}, bf16[1,768,3,192]{1,3,2,0:T(8,128)(2,1)}, u32[]{:S(2)}) copy-start(bf16[1,768,3,192]{1,3,2,0:T(8,128)(2,1)} %param.34) | copy-start | bytes 2654212
  169.4 36.0 %copy-start.165 = (bf16[1,768,3,192]{1,3,2,0:T(8,128)(2,1)S(1)}, bf16[1,768,3,192]{1,3,2,0:T(8,128)(2,1)}, u32[]{:S(2)}) copy-start(bf16[1,768,3,192]{1,3,2,0:T(8,128)(2,1)} %param.26) | copy-start | bytes 2654212
  169.4 3.7 collective-permute-start
  174.8 70.4 %reduce-scatter.71.cloned.1.call-start = ((), (), s32[]{:S(2)}) async-start(), calls=%async_computation.37 | async-start | bytes 1966080 | tf_op jit(solution)/shard_map/reduce_scatter | solution.py:57
  175.0 33.4 %copy-start.110 = (pred[2,2,256]{2,1,0:T(4,128)(4,1)}, pred[2,2,256]{2,1,0:T(4,128)(4,1)S(1)}, u32[]{:S(2)}) copy-start(pred[2,2,256]{2,1,0:T(4,128)(4,1)S(1)} %add_bitcast_fusion.4) | copy-start | bytes 3076
  208.3 432.1 %copy-start.5 = (bf16[256,2,2,3,64]{0,4,3,2,1:T(8,128)(2,1)}, bf16[256,2,2,3,64]{0,4,3,2,1:T(8,128)(2,1)S(1)}, u32[]{:S(2)}) copy-start(bf16[256,2,2,3,64]{0,4,3,2,1:T(8,128)(2,1)S(1)} %add_convert_fusion.2) | copy-start | bytes 1179652
  212.2 33.0 %copy-start.41 = (bf16[64,1,2,768]{3,0,2,1:T(8,128)(2,1)S(1)}, bf16[64,1,2,768]{3,0,2,1:T(8,128)(2,1)}, u32[]{:S(2)}) copy-start(bf16[64,1,2,768]{3,0,2,1:T(8,128)(2,1)} %copy-done.40) | copy-start | bytes 589828
  212.2 33.0 %copy-start.43 = (bf16[64,1,2,768]{3,0,2,1:T(8,128)(2,1)S(1)}, bf16[64,1,2,768]{3,0,2,1:T(8,128)(2,1)}, u32[]{:S(2)}) copy-start(bf16[64,1,2,768]{3,0,2,1:T(8,128)(2,1)} %copy-done.42) | copy-start | bytes 589828
  214.1 65.5 %all-gather.15.cloned.1.call-start = ((), (), s32[]{:S(2)}) async-start(), calls=%async_computation.38 | async-start | bytes 1966080 | tf_op jit(solution)/shard_map/all_gather | solution.py:45
  248.5 43.6 %copy-start.73 = (bf16[1,768,768]{1,2,0:T(8,128)(2,1)S(1)}, bf16[1,768,768]{1,2,0:T(8,128)(2,1)}, u32[]{:S(2)}) copy-start(bf16[1,768,768]{1,2,0:T(8,128)(2,1)} %copy.133) | copy-start | bytes 3538948
  248.5 77.3 %reduce-scatter.73.cloned.1.call-start = ((), (), s32[]{:S(2)}) async-start(), calls=%async_computation.39 | async-start | bytes 1966080 | tf_op jit(solution)/shard_map/reduce_scatter | solution.py:57
  294.7 69.5 %all-gather.17.cloned.1.call-start = ((), (), s32[]{:S(2)}) async-start(), calls=%async_computation.40 | async-start | bytes 1966080 | tf_op jit(solution)/shard_map/all_gather | solution.py:45
  329.1 38.2 %copy-start.20 = (f32[64,2,2,768]{3,0,2,1:T(8,128)}, f32[64,2,2,768]{3,0,2,1:T(8,128)S(1)}, u32[]{:S(2)}) copy-start(f32[64,2,2,768]{3,0,2,1:T(8,128)S(1)} %get-tuple-element.118) | copy-start | bytes 2359300
  329.1 3.6 collective-permute-start.1
  333.6 70.2 %reduce-scatter.75.cloned.1.call-start = ((), (), s32[]{:S(2)}) async-start(), calls=%async_computation.41 | async-start | bytes 1966080 | tf_op jit(solution)/shard_map/reduce_scatter | solution.py:57
  372.7 65.5 %all-gather.19.cloned.1.call-start = ((), (), s32[]{:S(2)}) async-start(), calls=%async_computation.42 | async-start | bytes 1966080 | tf_op jit(solution)/shard_map/all_gather | solution.py:45
  407.2 77.1 %reduce-scatter.77.cloned.1.call-start = ((), (), s32[]{:S(2)}) async-start(), calls=%async_computation.43 | async-start | bytes 1966080 | tf_op jit(solution)/shard_map/reduce_scatter | solution.py:57
  453.1 119.4 %all-gather.21.cloned.1.call-start = ((), (), s32[]{:S(2)}) async-start(), calls=%async_computation.44 | async-start | bytes 7864320 | tf_op jit(solution)/shard_map/all_gather | solution.py:395
  456.7 168.0 %reduce-scatter.79.cloned.1.call-start = ((), (), s32[]{:S(2)}) async-start(), calls=%async_computation.45 | async-start | bytes 983040 | tf_op jit(solution)/shard_map/reduce_scatter | solution.py:70
  599.9 71.6 %reduce-scatter.81.cloned.1.call-start = ((), (), s32[]{:S(2)}) async-start(), calls=%async_computation.46 | async-start | bytes 983040 | tf_op jit(solution)/shard_map/reduce_scatter | solution.py:70
  643.5 78.4 %reduce-scatter.83.cloned.1.call-start = ((), (), s32[]{:S(2)}) async-start(), calls=%async_computation.47 | async-start | bytes 983040 | tf_op jit(solution)/shard_map/reduce_scatter | solution.py:70
  672.6 1.8 collective-permute-start.2
  694.5 73.8 %reduce-scatter.85.cloned.1.call-start = ((), (), s32[]{:S(2)}) async-start(), calls=%async_computation.48 | async-start | bytes 983040 | tf_op jit(solution)/shard_map/reduce_scatter | solution.py:70
  740.2 95.8 %reduce-scatter.87.cloned.1.call-start = ((), (), s32[]{:S(2)}) async-start(), calls=%async_computation.49 | async-start | bytes 983040 | tf_op jit(solution)/shard_map/reduce_scatter | solution.py:70
  769.4 1.8 collective-permute-start.3
  791.3 148.6 %reduce-scatter.115.cloned.1.call-start = ((), (), s32[]{:S(2)}) async-start(), calls=%async_computation.63 | async-start | bytes 81920
  792.6 148.2 %reduce-scatter.103.cloned.1.call-start = ((), (), s32[]{:S(2)}) async-start(), calls=%async_computation.57 | async-start | bytes 20480
  793.6 148.1 %reduce-scatter.109.cloned.1.call-start = ((), (), s32[]{:S(2)}) async-start(), calls=%async_computation.60 | async-start | bytes 491520
  795.5 148.0 %reduce-scatter.121.cloned.1.call-start = ((), (), s32[]{:S(2)}) async-start(), calls=%async_computation.66 | async-start | bytes 1474560
  806.1 139.2 %reduce-scatter.97.cloned.1.call-start = ((), (), s32[]{:S(2)}) async-start(), calls=%async_computation.54 | async-start | bytes 1228800
  814.2 141.3 %reduce-scatter.117.cloned.1.call-start = ((), (), s32[]{:S(2)}) async-start(), calls=%async_computation.64 | async-start | bytes 81920
  815.6 159.2 %reduce-scatter.105.cloned.1.call-start = ((), (), s32[]{:S(2)}) async-start(), calls=%async_computation.58 | async-start | bytes 20480
  816.5 180.9 %reduce-scatter.111.cloned.1.call-start = ((), (), s32[]{:S(2)}) async-start(), calls=%async_computation.61 | async-start | bytes 491520
  818.4 209.9 %reduce-scatter.123.cloned.1.call-start = ((), (), s32[]{:S(2)}) async-start(), calls=%async_computation.67 | async-start | bytes 1474560
  828.7 226.7 %reduce-scatter.99.cloned.1.call-start = ((), (), s32[]{:S(2)}) async-start(), calls=%async_computation.55 | async-start | bytes 1228800
  834.2 239.1 %reduce-scatter.119.cloned.1.call-start = ((), (), s32[]{:S(2)}) async-start(), calls=%async_computation.65 | async-start | bytes 81920
  835.9 256.7 %reduce-scatter.107.cloned.1.call-start = ((), (), s32[]{:S(2)}) async-start(), calls=%async_computation.59 | async-start | bytes 20480
  853.1 364.6 %reduce-scatter.127.cloned.1.call-start = ((), (), s32[]{:S(2)}) async-start(), calls=%async_computation.69 | async-start | bytes 417792
  854.3 489.6 %reduce-scatter.129.cloned.1.call-start = ((), (), s32[]{:S(2)}) async-start(), calls=%async_computation.70 | async-start | bytes 417792
  855.4 511.4 %reduce-scatter.113.cloned.1.call-start = ((), (), s32[]{:S(2)}) async-start(), calls=%async_computation.62 | async-start | bytes 491520
  857.3 540.4 %reduce-scatter.125.cloned.1.call-start = ((), (), s32[]{:S(2)}) async-start(), calls=%async_computation.68 | async-start | bytes 1474560
  868.0 560.0 %reduce-scatter.91.cloned.1.call-start = ((), (), s32[]{:S(2)}) async-start(), calls=%async_computation.51 | async-start | bytes 1474560 | tf_op jit(solution)/shard_map/reduce_scatter | solution.py:89
  871.7 586.7 %reduce-scatter.93.cloned.1.call-start = ((), (), s32[]{:S(2)}) async-start(), calls=%async_computation.52 | async-start | bytes 1474560 | tf_op jit(solution)/shard_map/reduce_scatter | solution.py:89
  874.8 613.8 %reduce-scatter.95.cloned.1.call-start = ((), (), s32[]{:S(2)}) async-start(), calls=%async_computation.53 | async-start | bytes 1474560 | tf_op jit(solution)/shard_map/reduce_scatter | solution.py:89
  878.4 638.2 %reduce-scatter.89.cloned.1.call-start = ((), (), s32[]{:S(2)}) async-start(), calls=%async_computation.50 | async-start | bytes 983040 | tf_op jit(solution)/shard_map/reduce_scatter | solution.py:70
  895.5 649.4 %reduce-scatter.101.cloned.1.call-start = ((), (), s32[]{:S(2)}) async-start(), calls=%async_computation.56 | async-start | bytes 1228800
  999.2 57.6 %copy-start.66 = (bf16[64,1,2,768]{3,0,2,1:T(8,128)(2,1)S(1)}, bf16[64,1,2,768]{3,0,2,1:T(8,128)(2,1)}, u32[]{:S(2)}) copy-start(bf16[64,1,2,768]{3,0,2,1:T(8,128)(2,1)} %copy-done.65) | copy-start | bytes 589828
  999.2 57.6 %copy-start.87 = (bf16[64,1,2,768]{3,0,2,1:T(8,128)(2,1)S(1)}, bf16[64,1,2,768]{3,0,2,1:T(8,128)(2,1)}, u32[]{:S(2)}) copy-start(bf16[64,1,2,768]{3,0,2,1:T(8,128)(2,1)} %copy-done.86) | copy-start | bytes 589828
  999.2 58.3 %copy-start.92 = (bf16[256,1,2,3,64]{0,4,3,2,1:T(8,128)(2,1)S(1)}, bf16[256,1,2,3,64]{0,4,3,2,1:T(8,128)(2,1)}, u32[]{:S(2)}) copy-start(bf16[256,1,2,3,64]{0,4,3,2,1:T(8,128)(2,1)} %get-tuple-element.172) | copy-start | bytes 589828
  999.2 58.3 %copy-start.100 = (bf16[2,3,64,256]{3,2,1,0:T(8,128)(2,1)S(1)}, bf16[2,3,64,256]{3,2,1,0:T(8,128)(2,1)}, u32[]{:S(2)}) copy-start(bf16[2,3,64,256]{3,2,1,0:T(8,128)(2,1)} %copy-done.99) | copy-start | bytes 589828
  999.2 58.3 %copy-start.169 = (bf16[256,1,2,3,64]{0,4,3,2,1:T(8,128)(2,1)S(1)}, bf16[256,1,2,3,64]{0,4,3,2,1:T(8,128)(2,1)}, u32[]{:S(2)}) copy-start(bf16[256,1,2,3,64]{0,4,3,2,1:T(8,128)(2,1)} %get-tuple-element.170) | copy-start | bytes 589828
  1065.3 302.6 %copy-start.89 = (bf16[1,192,192]{2,1,0:T(8,128)(2,1)S(1)}, bf16[1,192,192]{2,1,0:T(8,128)(2,1)}, u32[]{:S(2)}) copy-start(bf16[1,192,192]{2,1,0:T(8,128)(2,1)} %copy.222) | copy-start | bytes 221188
  1065.3 302.6 %copy-start.90 = (bf16[1,192,192]{2,1,0:T(8,128)(2,1)S(1)}, bf16[1,192,192]{2,1,0:T(8,128)(2,1)}, u32[]{:S(2)}) copy-start(bf16[1,192,192]{2,1,0:T(8,128)(2,1)} %copy.224) | copy-start | bytes 221188
  1517.6 29.9 %collective-permute-start.4 = (bf16[64,1,2,768]{3,0,2,1:T(8,128)(2,1)S(1)}, bf16[64,1,2,768]{3,0,2,1:T(8,128)(2,1)S(1)}, u32[]{:S(2)}, u32[]{:S(2)}) collective-permute-start(bf16[64,1,2,768]{3,0,2,1:T(8,128)(2,1)S(1)} %add_convert_fusion.6), channel_id=1, source_target_pairs={{16,0},{0,16},{17,1},{1,17},{18,2},{2,18},{19,3},{3,19},{20,4},{4,... | collective-permute-start | bytes 589832 | tf_op jit(solution)/shard_map/ppermute | solution.py:23
  (164 other events, 875.5 us)
Sparse Core Ops, SparseCore 0:
  13.5 33.0 all-gather.8
  54.6 30.8 reduce-scatter.66
  89.0 30.9 all-gather.10
  134.9 30.9 reduce-scatter.68
  174.9 30.4 all-gather.12
  214.2 30.9 reduce-scatter.70
  248.6 30.9 all-gather.14
  294.8 30.8 reduce-scatter.72
  333.7 30.4 all-gather.16
  372.8 30.9 reduce-scatter.74
  407.3 30.8 all-gather.18
  453.3 30.9 reduce-scatter.76
  600.1 24.5 reduce-scatter.78
  643.6 27.9 reduce-scatter.80
  694.6 27.2 reduce-scatter.82
  740.4 27.9 reduce-scatter.84
  791.4 27.1 reduce-scatter.86
  820.7 16.7 reduce-scatter.114
  839.9 17.0 reduce-scatter.102
  859.1 19.7 reduce-scatter.108
  881.3 28.4 reduce-scatter.120
  912.3 25.4 reduce-scatter.96
  940.0 15.5 reduce-scatter.116
  957.7 17.0 reduce-scatter.104
  977.7 19.7 reduce-scatter.110
  999.7 28.5 reduce-scatter.122
  1030.6 24.8 reduce-scatter.98
  1057.7 15.5 reduce-scatter.118
  1075.6 17.0 reduce-scatter.106
  1097.7 119.9 reduce-scatter.126
  1223.1 120.6 reduce-scatter.128
  1346.7 20.0 reduce-scatter.112
  1369.0 28.5 reduce-scatter.124
  1400.1 27.8 reduce-scatter.90
  1430.4 27.8 reduce-scatter.92
  1460.6 27.8 reduce-scatter.94
  1491.6 24.9 reduce-scatter.88
  1519.0 25.9 reduce-scatter.100
Sparse Core Ops, SparseCore 1:
  456.8 115.8 all-gather.20
where the time goes:
time: 1570 us; the launch traced here: 1560 us
  waiting for transfers between devices  1080 us (69%)
  blocking collectives  138 us (9%)
  matrix products  137 us (9%)
  local copies, waits for them, and re-layouts  97.9 us (6%)
  other arithmetic  74.7 us (5%)
  between operations  21.5 us (1%)
    unnamed x56, waiting for transfers between devices  455 us
    all_gather x6, waiting for transfers between devices, gather_rows(): return lax.all_gather(values, 'heads', axis=0, tiled=True)  182 us
    reduce_scatter x6, waiting for transfers between devices, scatter_rows(): lax.psum_scatter(row_term(jnp.int32(0), lax.axis_size('heads') * row_tota...  165 us
    reduce_scatter x6, waiting for transfers between devices, scatter_grads(): lax.psum_scatter(row_term(jnp.int32(0), lax.axis_size('heads') * row_tota...  129 us
    unnamed x450, local copies, waits for them, and re-layouts  89.8 us
    reduce_scatter x3, waiting for transfers between devices, reduce_weights(): lax.psum_scatter(gradients[3].astype(jnp.bfloat16), 'dp', scatter_dimensi...  87.9 us
    all_gather x6, blocking collectives, gather_grads(): return lax.all_gather(values, 'heads', axis=0, tiled=True)  59.6 us
    all_gather x1, waiting for transfers between devices, per_device(): lax.all_gather(queue_low, 'dp', axis=0, tiled=True)  52.3 us
  transfers between devices with their start and end apart: 44, of which 37 were waited for; matrix products, arithmetic and copies ran while one was open for 10% of the time, Pallas kernels for 0%

commit v1 on v0

v1 whole, which is shorter than its diff:
```python
import functools

import jax
import jax.numpy as jnp
from jax import lax
from jax.experimental import pallas as pl
from jax.experimental.pallas import tpu as pltpu
from jax.sharding import PartitionSpec as P

TEMPER = 0.05
NORM_EPS = 1e-06
NEG_FILL = -1000000000.0
F32 = jnp.float32
LOW = jnp.bfloat16
VMEM_LIMIT = 40 * 1024 * 1024

ROW_GAIN = 0
ROW_SHIFT = 2
ROW_EXP = 6
ROW_IN = 7


def dot_nn(a, b):
    return lax.dot_general(a, b, (((1,), (0,)), ((), ())), preferred_element_type=F32)


def dot_nt(a, b):
    return lax.dot_general(a, b, (((1,), (1,)), ((), ())), preferred_element_type=F32)


def dot_tn(a, b):
    return lax.dot_general(a, b, (((0,), (0,)), ((), ())), preferred_element_type=F32)


def kernel_call(body, outs, scalars, arrays, flops, name):
    in_specs = [pl.BlockSpec(memory_space=pltpu.SMEM)] + [
        pl.BlockSpec(memory_space=pltpu.VMEM) for _ in arrays
    ]
    moved = sum(a.size * a.dtype.itemsize for a in arrays) + sum(
        functools.reduce(lambda x, y: x * y, s, 1) * jnp.dtype(d).itemsize for s, d in outs
    )
    return pl.pallas_call(
        body,
        out_shape=[jax.ShapeDtypeStruct(s, d) for s, d in outs],
        in_specs=in_specs,
        out_specs=[pl.BlockSpec(memory_space=pltpu.VMEM) for _ in outs],
        compiler_params=pltpu.CompilerParams(vmem_limit_bytes=VMEM_LIMIT),
        cost_estimate=pl.CostEstimate(flops=flops, bytes_accessed=moved, transcendentals=0),
        name=name,
    )(scalars, *arrays)


def swap(value, axis, distance):
    count = lax.axis_size(axis)
    return lax.ppermute(value, axis, [(i, i ^ distance) for i in range(count)])


def over_x(value):
    return swap(value, "heads", 1)


def over_y(value):
    return swap(value, "heads", 2)


def over_core(value):
    return swap(value, "section", 1)


def bf(value):
    return value.astype(LOW)


def norm_parts(values):
    mean = jnp.mean(values, axis=-1, keepdims=True)
    center = values - mean
    spread = jnp.mean(center * center, axis=-1, keepdims=True)
    rstd = lax.rsqrt(spread + NORM_EPS)
    return center * rstd, rstd


def row_keep(scal, pair, rows):
    position = scal[0] * rows + lax.broadcasted_iota(jnp.int32, (rows, 1), 0)
    return position < scal[3 + pair]


def key_keep(scal, pair, rows, order):
    lane = lax.broadcasted_iota(jnp.int32, (1, 4 * rows), 1)
    slot = lane // rows
    inner = lane - slot * rows
    if order == (0, 2, 1, 3):
        slot = (slot & 1) * 2 + slot // 2
    block = jnp.bitwise_xor(slot, scal[0])
    return block * rows + inner < scal[3 + pair]


def attn_forward(scal, own, first, second, wqkv, wout, small, order, save):
    pairs, rows, width = own.shape
    local = wout.shape[0]
    heads = local // 64
    full = 4 * rows

    def body(s, own_r, g1_r, g2_r, wq_r, wo_r, sm_r, p0_r, p1_r, p2_r, *kept):
        def one(pair, _):
            rows_in = jnp.concatenate([own_r[pair], g1_r[pair], g2_r[0, pair], g2_r[1, pair]], axis=0)
            project = dot_nt(rows_in, wq_r[...])
            q = bf(project[:, :local] + sm_r[ROW_IN : ROW_IN + 1, :local])
            k = bf(project[:, local : 2 * local])
            v = bf(project[:, 2 * local :] + sm_r[ROW_IN : ROW_IN + 1, local : 2 * local])
            if save:
                kept[0][pair, :, :local] = q
                kept[0][pair, :, local : 2 * local] = k
                kept[0][pair, :, 2 * local :] = v
            keep = key_keep(s, pair, rows, order)
            pieces = []
            for h in range(heads):
                cut = slice(64 * h, 64 * h + 64)
                scores = jnp.where(keep, dot_nt(q[:, cut] * 0.125, k[:, cut]), NEG_FILL)
                raised = jnp.exp(scores - jnp.max(scores, axis=-1, keepdims=True))
                shares = bf(raised / jnp.sum(raised, axis=-1, keepdims=True))
                if save:
                    kept[1][pair, h] = shares
                pieces.append(bf(dot_nn(shares, v[:, cut])))
            context = jnp.concatenate(pieces, axis=1)
            if save:
                kept[2][pair] = context
            out = dot_nn(context, wo_r[...])
            p0_r[pair] = out[:rows]
            p1_r[pair] = bf(out[rows : 2 * rows])
            p2_r[0, pair] = bf(out[2 * rows : 3 * rows])
            p2_r[1, pair] = bf(out[3 * rows :])
            return 0

        lax.fori_loop(0, pairs, one, 0)

    outs = [
        ((pairs, rows, width), F32),
        ((pairs, rows, width), LOW),
        ((2, pairs, rows, width), LOW),
    ]
    if save:
        outs += [
            ((pairs, full, 3 * local), LOW),
            ((pairs, heads, full, full), LOW),
            ((pairs, full, local), LOW),
        ]
    flops = 2 * pairs * full * (4 * local * width + 2 * local * full)
    return kernel_call(body, outs, scal, [own, first, second, wqkv, wout, small], flops, "attn_forward")


def feed_forward(scal, own, first, second, wexp, wcon, small, order, save):
    pairs, rows, width = own.shape
    hidden_units = wexp.shape[1]
    full = 4 * rows

    def body(s, own_r, g1_r, g2_r, we_r, wc_r, sm_r, p0_r, p1_r, p2_r, *kept):
        def one(pair, _):
            rows_in = jnp.concatenate([own_r[pair], g1_r[pair], g2_r[0, pair], g2_r[1, pair]], axis=0)
            inner = dot_nn(rows_in, we_r[...]) + sm_r[ROW_EXP : ROW_EXP + 1, :]
            phi = 0.5 * (1.0 + lax.erf(inner * (0.5**0.5)))
            active = bf(inner * phi)
            if save:
                density = jnp.exp(-0.5 * inner * inner) * 0.3989422804014327
                kept[0][pair] = active
                kept[1][pair] = bf(phi + inner * density)
            out = dot_nn(active, wc_r[...])
            p0_r[pair] = out[:rows]
            p1_r[pair] = bf(out[rows : 2 * rows])
            p2_r[0, pair] = bf(out[2 * rows : 3 * rows])
            p2_r[1, pair] = bf(out[3 * rows :])
            return 0

        lax.fori_loop(0, pairs, one, 0)

    outs = [
        ((pairs, rows, width), F32),
        ((pairs, rows, width), LOW),
        ((2, pairs, rows, width), LOW),
    ]
    if save:
        outs += [((pairs, full, hidden_units), LOW), ((pairs, full, hidden_units), LOW)]
    flops = 4 * pairs * full * width * hidden_units
    return kernel_call(body, outs, scal, [own, first, second, wexp, wcon, small], flops, "feed_forward")


def norm_middle(scal, part, second, first, layer_in, small, save):
    pairs, rows, width = part.shape

    def body(s, p_r, g_r, f_r, x_r, sm_r, hid_r, low_r, *kept):
        total = jnp.zeros((1, width), F32)
        for pair in range(pairs):
            attn = p_r[pair] + g_r[0, pair].astype(F32) + f_r[pair].astype(F32)
            attn = attn + sm_r[ROW_SHIFT : ROW_SHIFT + 1, :]
            mixed = x_r[pair].astype(F32) + attn
            xhat, _ = norm_parts(mixed)
            hidden = xhat * sm_r[ROW_GAIN : ROW_GAIN + 1, :] + sm_r[ROW_SHIFT + 1 : ROW_SHIFT + 2, :]
            hid_r[pair] = hidden
            low_r[pair] = bf(hidden)
            if save:
                kept[0][pair] = mixed
                square = jnp.where(row_keep(s, pair, rows), attn * attn, 0.0)
                total = total + jnp.sum(square, axis=0, keepdims=True)
        if save:
            kept[1][...] = total

    outs = [((pairs, rows, width), F32), ((pairs, rows, width), LOW)]
    if save:
        outs += [((pairs, rows, width), F32), ((1, width), F32)]
    return kernel_call(
        body, outs, scal, [part, second, first, layer_in, small], 20 * part.size, "norm_middle"
    )


def norm_last(scal, part, second, first, hidden, small, save, pool):
    pairs, rows, width = part.shape

    def body(s, p_r, g_r, f_r, h_r, sm_r, out_r, *kept):
        feed_total = jnp.zeros((1, width), F32)
        out_total = jnp.zeros((1, width), F32)
        for pair in range(pairs):
            feed = p_r[pair] + g_r[0, pair].astype(F32) + f_r[pair].astype(F32)
            feed = feed + sm_r[ROW_SHIFT + 2 : ROW_SHIFT + 3, :]
            summed = h_r[pair] + feed
            xhat, _ = norm_parts(summed)
            out = xhat * sm_r[ROW_GAIN + 1 : ROW_GAIN + 2, :] + sm_r[ROW_SHIFT + 3 : ROW_SHIFT + 4, :]
            keep = row_keep(s, pair, rows)
            if pool:
                out_r[pair : pair + 1, :] = jnp.sum(jnp.where(keep, out, 0.0), axis=0, keepdims=True)
            else:
                out_r[pair] = bf(out)
            if save:
                kept[0][pair] = summed
                feed_total += jnp.sum(jnp.where(keep, feed * feed, 0.0), axis=0, keepdims=True)
                out_total += jnp.sum(jnp.where(keep, out * out, 0.0), axis=0, keepdims=True)
        if save:
            kept[1][0:1, :] = feed_total
            kept[1][1:2, :] = out_total

    outs = [((pairs, width), F32) if pool else ((pairs, rows, width), LOW)]
    if save:
        outs += [((pairs, rows, width), F32), ((2, width), F32)]
    return kernel_call(
        body, outs, scal, [part, second, first, hidden, small], 20 * part.size, "norm_last"
    )


def scatter_mid(first, received):
    return bf(first.astype(F32) + received[1].astype(F32))


def gather_stream(own, hop_one, hop_two):
    first = hop_one(own)
    second = hop_two(jnp.stack([own, first]))
    return first, second


def scatter_stream(p1, p2, hop_one, hop_two):
    second = hop_two(p2)
    first = hop_one(scatter_mid(p1, second))
    return second, first


def joined(low_half, high_half, pair, half):
    return low_half[pair] if pair < half else high_half[pair - half]


def whole_rows(half, pair, own_a, own_b, g1a, g1b, g2a, g2b):
    if pair < half:
        return jnp.concatenate([own_a[pair], g1a[pair], g2a[0, pair], g2a[1, pair]], axis=0)
    at = pair - half
    return jnp.concatenate([own_b[at], g2b[0, at], g1b[at], g2b[1, at]], axis=0)


def store_parts(half, pair, rows, out, p0, pfa, pfb, pga, pgb):
    p0[pair] = out[:rows]
    if pair < half:
        pfa[pair] = bf(out[rows : 2 * rows])
        pga[0, pair] = bf(out[2 * rows : 3 * rows])
        pga[1, pair] = bf(out[3 * rows :])
    else:
        at = pair - half
        pfb[at] = bf(out[2 * rows : 3 * rows])
        pgb[0, at] = bf(out[rows : 2 * rows])
        pgb[1, at] = bf(out[3 * rows :])


def parts_shapes(pairs, rows, width):
    half = pairs // 2
    rest = pairs - half
    return [
        ((pairs, rows, width), F32),
        ((half, rows, width), LOW),
        ((rest, rows, width), LOW),
        ((2, half, rows, width), LOW),
        ((2, rest, rows, width), LOW),
    ]


def gather_halves(own_a, own_b):
    g1a, g1b = over_x(own_a), over_y(own_b)
    g2a, g2b = over_y(jnp.stack([own_a, g1a])), over_x(jnp.stack([own_b, g1b]))
    return [own_a, own_b, g1a, g1b, g2a, g2b]


def scatter_halves(pfa, pfb, pga, pgb):
    rga, rgb = over_y(pga), over_x(pgb)
    rfa, rfb = over_x(scatter_mid(pfa, rga)), over_y(scatter_mid(pfb, rgb))
    return [rga, rgb, rfa, rfb]


def scattered(half, pair, p0, rga, rgb, rfa, rfb):
    if pair < half:
        return p0[pair] + rga[0, pair].astype(F32) + rfa[pair].astype(F32)
    at = pair - half
    return p0[pair] + rgb[0, at].astype(F32) + rfb[at].astype(F32)


def norm_backward(values, grad, gain_row):
    xhat, rstd = norm_parts(values)
    scaled = grad * gain_row
    d_values = rstd * (
        scaled
        - jnp.mean(scaled, axis=-1, keepdims=True)
        - xhat * jnp.mean(scaled * xhat, axis=-1, keepdims=True)
    )
    return d_values, jnp.sum(grad * xhat, axis=0, keepdims=True)


def column_sum(values):
    return jnp.sum(values, axis=0, keepdims=True)


def last_backward(scal, summed, small, pooled=None, residual=None, pieces=None):
    pairs, rows, width = summed.shape
    half = pairs // 2

    def body(s, y_r, sm_r, *rest):
        if pooled is not None:
            source, outs = rest[:1], rest[1:]
        else:
            source, outs = rest[:6], rest[6:]
        d_r, la_r, lb_r, rows_r = outs
        totals = [jnp.zeros((1, width), F32) for _ in range(3)]
        for pair in range(pairs):
            if pooled is not None:
                grad = jnp.where(row_keep(s, pair, rows), source[0][pair : pair + 1, :], 0.0)
            else:
                grad = source[0][pair] + scattered(half, pair, *source[1:])
                grad = bf(grad).astype(F32)
            d_summed, d_gain = norm_backward(y_r[pair], grad, sm_r[ROW_GAIN + 1 : ROW_GAIN + 2, :])
            d_r[pair] = d_summed
            if pair < half:
                la_r[pair] = bf(d_summed)
            else:
                lb_r[pair - half] = bf(d_summed)
            for i, v in enumerate((d_gain, column_sum(grad), column_sum(d_summed))):
                totals[i] = totals[i] + v
        for i in range(3):
            rows_r[i : i + 1, :] = totals[i]

    source = [pooled] if pooled is not None else [residual] + pieces
    outs = [
        ((pairs, rows, width), F32),
        ((half, rows, width), LOW),
        ((pairs - half, rows, width), LOW),
        ((3, width), F32),
    ]
    return kernel_call(body, outs, scal, [summed, small] + source, 30 * summed.size, "last_backward")


def middle_backward(scal, mixed, small, residual, pieces):
    pairs, rows, width = mixed.shape
    half = pairs // 2

    def body(s, y_r, sm_r, *rest):
        source, outs = rest[:6], rest[6:]
        d_r, la_r, lb_r, rows_r = outs
        totals = [jnp.zeros((1, width), F32) for _ in range(3)]
        for pair in range(pairs):
            grad = source[0][pair] + scattered(half, pair, *source[1:])
            d_mixed, d_gain = norm_backward(y_r[pair], grad, sm_r[ROW_GAIN : ROW_GAIN + 1, :])
            d_r[pair] = d_mixed
            if pair < half:
                la_r[pair] = bf(d_mixed)
            else:
                lb_r[pair - half] = bf(d_mixed)
            for i, v in enumerate((d_gain, column_sum(grad), column_sum(d_mixed))):
                totals[i] = totals[i] + v
        for i in range(3):
            rows_r[i : i + 1, :] = totals[i]

    outs = [
        ((pairs, rows, width), F32),
        ((half, rows, width), LOW),
        ((pairs - half, rows, width), LOW),
        ((3, width), F32),
    ]
    return kernel_call(
        body, outs, scal, [mixed, small, residual] + pieces, 30 * mixed.size, "middle_backward"
    )


def feed_backward(scal, grads, slope, wexp, wcon):
    pairs, full, units = slope.shape
    rows, width = full // 4, wexp.shape[0]
    half = pairs // 2

    def body(s, *refs):
        grad_r, (sl_r, we_r, wc_r), outs = refs[:6], refs[6:9], refs[9:]
        dinner_r, bias_r = outs[5:]
        total = jnp.zeros((1, units), F32)
        for pair in range(pairs):
            d_feed = whole_rows(half, pair, *grad_r)
            d_inner = dot_nt(d_feed, wc_r[...]) * sl_r[pair].astype(F32)
            total = total + column_sum(d_inner)
            low = bf(d_inner)
            dinner_r[pair] = low
            store_parts(half, pair, rows, dot_nt(low, we_r[...]), *outs[:5])
        bias_r[...] = total

    outs = parts_shapes(pairs, rows, width) + [((pairs, full, units), LOW), ((1, units), F32)]
    flops = 4 * pairs * full * width * units
    return kernel_call(body, outs, scal, grads + [slope, wexp, wcon], flops, "feed_backward")


def attn_backward(scal, grads, qkv, shares, context, wqkv, wout):
    pairs, full, triple = qkv.shape
    local = triple // 3
    heads = local // 64
    rows, width = full // 4, wout.shape[1]
    half = pairs // 2

    def body(s, *refs):
        grad_r, (qkv_r, sh_r, cx_r, wq_r, wo_r), outs = refs[:6], refs[6:11], refs[11:]
        dproj_r, bias_r = outs[5:]
        q_total = jnp.zeros((1, local), F32)
        v_total = jnp.zeros((1, local), F32)
        for pair in range(pairs):
            d_attn = whole_rows(half, pair, *grad_r)
            d_context = bf(dot_nt(d_attn, wo_r[...]))
            q = qkv_r[pair, :, :local]
            k = qkv_r[pair, :, local : 2 * local]
            v = qkv_r[pair, :, 2 * local :]
            weighted = d_context.astype(F32) * cx_r[pair].astype(F32)
            dqs, dks, dvs = [], [], []
            for h in range(heads):
                cut = slice(64 * h, 64 * h + 64)
                share = sh_r[pair, h]
                dc = d_context[:, cut]
                dvs.append(dot_tn(share, dc))
                drop = jnp.sum(weighted[:, cut], axis=-1, keepdims=True)
                d_scores = bf(share.astype(F32) * (dot_nt(dc, v[:, cut]) - drop))
                dqs.append(dot_nn(d_scores, k[:, cut]) * 0.125)
                dks.append(dot_tn(d_scores, q[:, cut]) * 0.125)
            dq = jnp.concatenate(dqs, axis=1)
            dk = jnp.concatenate(dks, axis=1)
            dv = jnp.concatenate(dvs, axis=1)
            q_total = q_total + column_sum(dq)
            v_total = v_total + column_sum(dv)
            d_project = bf(jnp.concatenate([dq, dk, dv], axis=1))
            dproj_r[pair] = d_project
            store_parts(half, pair, rows, dot_nn(d_project, wq_r[...]), *outs[:5])
        bias_r[...] = jnp.zeros((1, width), F32)
        bias_r[:, :local] = q_total
        bias_r[:, local : 2 * local] = v_total

    outs = parts_shapes(pairs, rows, width) + [((pairs, full, triple), LOW), ((1, width), F32)]
    flops = 2 * pairs * full * (4 * local * width + 4 * local * full)
    return kernel_call(
        body, outs, scal, grads + [qkv, shares, context, wqkv, wout], flops, "attn_backward"
    )


def put_blocks(s, out_ref, at, value, blocks):
    span = value.shape[0] // blocks
    half = span // 2
    for block in range(blocks):
        for side in range(2):
            piece = value[block * span + side * half : block * span + (side + 1) * half]
            core = jnp.bitwise_xor(s[1], side)
            place = jnp.bitwise_xor(s[2], block)
            if at is None:
                out_ref[core, place] = piece
            else:
                out_ref[core, place, at] = piece


def feed_weights(scal, grads, hidden, active, d_inner, blocks):
    pairs, full, units = active.shape
    own, first, second = hidden
    rows, width = full // 4, own.shape[2]
    half = pairs // 2
    split = blocks > 1

    def body(s, *refs):
        grad_r, (o_r, f_r, g_r, a_r, d_r, out_r) = refs[:6], refs[6:]
        contract = jnp.zeros((width, units), F32)
        expand = jnp.zeros((width, units), F32)
        for pair in range(pairs):
            d_feed = whole_rows(half, pair, *grad_r)
            contract = contract + dot_tn(d_feed, a_r[pair])
            rows_in = jnp.concatenate([o_r[pair], f_r[pair], g_r[0, pair], g_r[1, pair]], axis=0)
            expand = expand + dot_tn(rows_in, d_r[pair])
        if split:
            put_blocks(s, out_r, 0, bf(contract), blocks)
            put_blocks(s, out_r, 1, bf(expand), blocks)
        else:
            out_r[0] = bf(contract)
            out_r[1] = bf(expand)

    shape = (2, blocks, 2, width // blocks // 2, units) if split else (2, width, units)
    flops = 4 * pairs * full * width * units
    return kernel_call(
        body, [(shape, LOW)], scal, grads + [own, first, second, active, d_inner], flops, "feed_weights"
    )[0]


def attn_weights(scal, grads, layer_in, context, d_project, blocks):
    pairs, full, local = context.shape
    own, first, second = layer_in
    width = own.shape[2]
    half = pairs // 2
    split = blocks > 1

    def body(s, *refs):
        grad_r, (o_r, f_r, g_r, c_r, d_r, out_r) = refs[:6], refs[6:]
        outproj = jnp.zeros((width, local), F32)
        inproj = jnp.zeros((width, 3 * local), F32)
        for pair in range(pairs):
            d_attn = whole_rows(half, pair, *grad_r)
            outproj = outproj + dot_tn(d_attn, c_r[pair])
            rows_in = jnp.concatenate([o_r[pair], f_r[pair], g_r[0, pair], g_r[1, pair]], axis=0)
            inproj = inproj + dot_tn(rows_in, d_r[pair])
        both = bf(jnp.concatenate([inproj, outproj], axis=1))
        if split:
            put_blocks(s, out_r, None, both, blocks)
        else:
            out_r[...] = both

    shape = (2, blocks, width // blocks // 2, 4 * local) if split else (width, 4 * local)
    flops = 8 * pairs * full * width * local
    return kernel_call(
        body, [(shape, LOW)], scal, grads + [own, first, second, context, d_project], flops, "attn_weights"
    )[0]


def reduce_blocks(grads):
    count = lax.axis_size("dp")
    mine = grads[0].astype(F32) + over_core(grads[1]).astype(F32)
    low = bf(mine)
    total = mine[0]
    for distance in range(1, count):
        total = total + swap(low[distance], "dp", distance).astype(F32)
    return total


def both_halves(section, layer_zero, layer_one):
    first = section == 0
    kept = jnp.where(first, layer_zero, layer_one)
    arrived = over_core(bf(jnp.where(first, layer_one, layer_zero))).astype(F32)
    return jnp.where(first, kept, arrived), jnp.where(first, arrived, kept)


def summed_over(value, axis):
    count = lax.axis_size(axis)
    distance = 1
    while distance < count:
        value = value + swap(value, axis, distance)
        distance *= 2
    return value


def by_distance(entries, axis):
    count = entries.shape[0]
    order = jnp.bitwise_xor(jnp.arange(count), lax.axis_index(axis))
    chosen = (order[:, None] == jnp.arange(count)[None, :]).astype(entries.dtype)
    flat = jnp.dot(chosen, entries.reshape(count, -1), precision=lax.Precision.HIGHEST)
    return flat.astype(entries.dtype).reshape(entries.shape)


def loss_section(pooled, counts, live, queue_unit, section):
    pairs = pooled.shape[1]
    count = lax.axis_size("dp")
    with jax.named_scope("pool"):
        pooled = summed_over(pooled, "heads")
    vectors = pooled / counts.T[:, :, None]
    inverse = lax.rsqrt(jnp.sum(vectors * vectors, axis=-1, keepdims=True) + NORM_EPS)
    units = vectors * inverse
    low = bf(units)
    width = low.shape[-1]
    flags = jnp.zeros((1, width), LOW).at[0, :pairs].set(bf(live))
    packet = jnp.concatenate([low[0], low[1], flags], axis=0)
    with jax.named_scope("keys"):
        if count <= 8:
            lanes = jnp.stack([packet] + [swap(packet, "dp", r) for r in range(1, count)])
        else:
            lanes = lax.all_gather(packet, "dp", axis=0)
            lanes = by_distance(lanes, "dp")
        every = jnp.stack([lanes, over_core(lanes)])
    keys = every[:, :, pairs : 2 * pairs].reshape(2 * count * pairs, width)
    alive = every[:, :, 2 * pairs, :pairs].reshape(2 * count * pairs).astype(F32)
    queries = lanes[:, :pairs].reshape(count * pairs, width)
    negative = dot_nt(queries, queue_unit) / TEMPER
    raised = jnp.exp(negative)
    mass = jnp.sum(raised, axis=1)
    pull = dot_nn(bf(raised), queue_unit)
    spread = jnp.concatenate([pull, jnp.broadcast_to(mass[:, None], (count * pairs, 128))], axis=1)
    spread = spread.reshape(count, pairs, width + 128)
    with jax.named_scope("pulls"):
        if count <= 8:
            total = spread[0]
            for r in range(1, count):
                total = total + swap(spread[r], "dp", r)
        else:
            placed = by_distance(spread, "dp")
            total = lax.psum_scatter(placed, "dp", scatter_dimension=0, tiled=True)[0]
    positive = dot_nt(low[0], keys) / TEMPER
    positive = jnp.where(alive[None, :] > 0, positive, NEG_FILL)
    pos_raised = jnp.exp(positive)
    mass = total[:, width] + jnp.sum(pos_raised, axis=1)
    own_pair = (jnp.arange(keys.shape[0])[None, :] == jnp.arange(pairs)[:, None]).astype(F32)
    weight = live / jnp.sum(alive)
    loss_part = jnp.sum(weight * (jnp.log(mass) - jnp.sum(own_pair * positive, axis=1)))
    d_positive = bf(weight[:, None] * (pos_raised / mass[:, None] - own_pair) / TEMPER)
    d_unit = dot_nn(d_positive, keys) + (weight / mass / TEMPER)[:, None] * total[:, :width]
    d_vector = inverse[0] * (d_unit - units[0] * jnp.sum(units[0] * d_unit, axis=-1, keepdims=True))
    return loss_part, d_vector / counts[:, 0:1]


def small_rows(gains, shifts, expbias, inbias):
    width = gains.shape[-1]
    inrow = inbias.reshape(1, -1)
    inrow = jnp.concatenate([inrow, jnp.zeros((1, width - inrow.shape[1]), LOW)], axis=1)
    return jnp.concatenate([gains[0], shifts[0], expbias.reshape(1, width), inrow], axis=0)


def per_device(
    query_embed,
    key_embed,
    crop_counts,
    pair_mask,
    negative_queue,
    online_inproj,
    online_inbias,
    online_outproj,
    online_gains,
    online_shifts,
    online_expand,
    online_expbias,
    online_contract,
    momentum_inproj,
    momentum_inbias,
    momentum_outproj,
    momentum_gains,
    momentum_shifts,
    momentum_expand,
    momentum_expbias,
    momentum_contract,
):
    section = lax.axis_index("section")
    head = lax.axis_index("heads")
    data = lax.axis_index("dp")
    dp_count = lax.axis_size("dp")
    rows, pairs_dev, width = query_embed.shape
    pairs = pairs_dev // lax.axis_size("section")
    local = online_outproj.shape[1]
    blocks = dp_count if width % (dp_count * 32) == 0 and dp_count <= 8 else 1

    def own_pairs(table, axis):
        return lax.dynamic_slice_in_dim(table, section * pairs, pairs, axis)

    own_counts = own_pairs(crop_counts, 0)
    scal_q = jnp.concatenate([jnp.stack([head, section, data]), own_counts[:, 0]]).astype(jnp.int32)
    scal_k = jnp.concatenate([jnp.stack([head, section, data]), own_counts[:, 1]]).astype(jnp.int32)

    def weight_set(inproj, inbias, outproj, gains, shifts, expand, expbias, contract):
        return [
            jnp.transpose(inproj[0], (1, 2, 0)).reshape(3 * local, width),
            outproj[0],
            small_rows(gains, shifts, expbias, inbias),
            expand[0],
            contract[0],
        ]

    held_q = weight_set(
        online_inproj,
        online_inbias,
        online_outproj,
        online_gains,
        online_shifts,
        online_expand,
        online_expbias,
        online_contract,
    )
    held_k = weight_set(
        momentum_inproj,
        momentum_inbias,
        momentum_outproj,
        momentum_gains,
        momentum_shifts,
        momentum_expand,
        momentum_expbias,
        momentum_contract,
    )

    def two_layers(held):
        arrived = [over_core(w) for w in held]
        zero = [jnp.where(section == 0, a, b) for a, b in zip(held, arrived)]
        one = [jnp.where(section == 0, b, a) for a, b in zip(held, arrived)]
        for layer in (zero, one):
            layer[2] = layer[2].astype(F32)
        return zero, one

    with jax.named_scope("weights"):
        weights_q = two_layers(held_q)
        weights_k = two_layers(held_k)

    embed_q = jnp.transpose(own_pairs(query_embed, 1), (1, 0, 2))
    embed_k = jnp.transpose(own_pairs(key_embed, 1), (1, 0, 2))
    streams = {
        "q": dict(x=embed_q, scal=scal_q, w=weights_q, one=over_x, two=over_y, order=(0, 1, 2, 3)),
        "k": dict(x=embed_k, scal=scal_k, w=weights_k, one=over_y, two=over_x, order=(0, 2, 1, 3)),
    }
    saved = [{}, {}]
    rms_rows = []
    pooled = {}
    for layer in range(2):
        for name in ("q", "k"):
            st = streams[name]
            save = name == "q"
            wqkv, wout, small, wexp, wcon = st["w"][layer]
            with jax.named_scope("gather_in"):
                first, second = gather_stream(st["x"], st["one"], st["two"])
            p0, p1, p2, *kept = attn_forward(
                st["scal"], st["x"], first, second, wqkv, wout, small, st["order"], save
            )
            with jax.named_scope("scatter_attn"):
                got2, got1 = scatter_stream(p1, p2, st["one"], st["two"])
            hidden, low, *kept_mid = norm_middle(st["scal"], p0, got2, got1, st["x"], small, save)
            if save:
                saved[layer].update(
                    x=[st["x"], first, second],
                    qkv=kept[0],
                    shares=kept[1],
                    context=kept[2],
                    mixed=kept_mid[0],
                )
            with jax.named_scope("gather_hidden"):
                first, second = gather_stream(low, st["one"], st["two"])
            p0, p1, p2, *kept = feed_forward(
                st["scal"], low, first, second, wexp, wcon, small, st["order"], save
            )
            with jax.named_scope("scatter_feed"):
                got2, got1 = scatter_stream(p1, p2, st["one"], st["two"])
            out, *kept_last = norm_last(st["scal"], p0, got2, got1, hidden, small, save, layer == 1)
            if save:
                saved[layer].update(
                    hidden=[low, first, second],
                    active=kept[0],
                    slope=kept[1],
                    summed=kept_last[0],
                )
                rms_rows += [kept_mid[1], kept_last[1]]
            if layer == 0:
                st["x"] = out
            else:
                pooled[name] = out

    queue = negative_queue.astype(F32)
    queue_unit = bf(queue * lax.rsqrt(jnp.sum(queue * queue, axis=-1, keepdims=True) + NORM_EPS))
    live = own_pairs(pair_mask, 0).astype(F32)
    with jax.named_scope("loss"):
        loss_part, d_pool = loss_section(
            jnp.stack([pooled["q"], pooled["k"]]), own_counts.astype(F32), live, queue_unit, section
        )

    feed_grads, attn_grads, norm_rows, bias_rows = [None] * 2, [None] * 2, [None] * 2, [None] * 2
    residual, pieces = None, None
    for layer in (1, 0):
        wqkv, wout, small, wexp, wcon = weights_q[layer]
        kept = saved[layer]
        if layer == 1:
            d_summed, low_a, low_b, rows_last = last_backward(
                scal_q, kept["summed"], small, pooled=d_pool
            )
        else:
            d_summed, low_a, low_b, rows_last = last_backward(
                scal_q, kept["summed"], small, residual=residual, pieces=pieces
            )
        with jax.named_scope("gather_dfeed"):
            grads = gather_halves(low_a, low_b)
        *parts, d_inner, exp_row = feed_backward(scal_q, grads, kept["slope"], wexp, wcon)
        with jax.named_scope("scatter_dhidden"):
            pieces = [parts[0]] + scatter_halves(*parts[1:])
        feed_grads[layer] = feed_weights(
            scal_q, grads, kept["hidden"], kept["active"], d_inner, blocks
        )
        d_mixed, low_a, low_b, rows_mid = middle_backward(
            scal_q, kept["mixed"], small, d_summed, pieces
        )
        with jax.named_scope("gather_dattn"):
            grads = gather_halves(low_a, low_b)
        *parts, d_project, in_row = attn_backward(
            scal_q, grads, kept["qkv"], kept["shares"], kept["context"], wqkv, wout
        )
        with jax.named_scope("scatter_dx"):
            pieces = [parts[0]] + scatter_halves(*parts[1:])
        residual = d_mixed
        attn_grads[layer] = attn_weights(scal_q, grads, kept["x"], kept["context"], d_project, blocks)
        norm_rows[layer] = jnp.concatenate(
            [rows_mid[0:1], rows_last[0:1], rows_mid[2:3], rows_mid[1:2], rows_last[2:3], rows_last[1:2]]
        )
        bias_rows[layer] = jnp.concatenate([exp_row, in_row])

    half = pairs // 2
    p0, rga, rgb, rfa, rfb = pieces
    arrived = jnp.concatenate([rga[0], rgb[0]]).astype(F32) + jnp.concatenate([rfa, rfb]).astype(F32)
    d_in = bf(residual + p0 + arrived)
    with jax.named_scope("input_grad"):
        half_width = width // 2
        mine = lax.dynamic_slice_in_dim(d_in, section * half_width, half_width, 2)
        other = lax.dynamic_slice_in_dim(d_in, (1 - section) * half_width, half_width, 2)
        other = over_core(other)
        ordered = jnp.where(
            section == 0, jnp.concatenate([mine, other]), jnp.concatenate([other, mine])
        )
        input_grad = jnp.transpose(ordered, (1, 0, 2))

    with jax.named_scope("weight_grads"):
        if blocks > 1:
            feed_a, feed_b = both_halves(section, *[reduce_blocks(g) for g in feed_grads])
            attn_a, attn_b = both_halves(section, *[reduce_blocks(g) for g in attn_grads])
            feed_sum = jnp.concatenate([feed_a, feed_b], axis=1)
            attn_sum = jnp.concatenate([attn_a, attn_b], axis=0)
        else:
            def owned(layers):
                return layers[0].astype(F32), layers[1].astype(F32)

            def reduce_plain(layers):
                zero, one = owned(layers)
                mine = jnp.where(section == 0, zero, one)
                other = over_core(bf(jnp.where(section == 0, one, zero)))
                return bf(mine + other.astype(F32))

            feed_sum = lax.psum_scatter(
                reduce_plain(feed_grads), "dp", scatter_dimension=1, tiled=True
            ).astype(F32)
            attn_sum = lax.psum_scatter(
                reduce_plain(attn_grads), "dp", scatter_dimension=0, tiled=True
            ).astype(F32)
    grad_contract = jnp.transpose(feed_sum[0])[None]
    grad_expand = feed_sum[1][None]
    grad_inproj = attn_sum[:, : 3 * local].reshape(1, -1, 3, local)
    grad_outproj = jnp.transpose(attn_sum[:, 3 * local :])[None]

    with jax.named_scope("small_grads"):
        across = jnp.concatenate(norm_rows + rms_rows)
        across = summed_over(across, "heads")
        tokens = jnp.sum(own_counts[:, 0]).astype(F32)
        scalar_row = jnp.zeros((1, width), F32).at[0, 0].set(loss_part).at[0, 1].set(tokens)
        table = jnp.concatenate([across] + bias_rows + [scalar_row])
        table = summed_over(table, "section")
        table = summed_over(table, "dp")
    scalars = table[-1]
    loss_total = scalars[0]
    rms_total = jnp.sum(table[12:18], axis=1).reshape(2, 3)
    rms_values = jnp.sqrt(rms_total / (scalars[1] * width))
    norms = jnp.where(section == 0, table[0:6], table[6:12])
    biases = jnp.where(section == 0, table[18:20], table[20:22])
    cut = width // (dp_count * lax.axis_size("heads"))
    norms = lax.dynamic_slice_in_dim(norms, (data * lax.axis_size("heads") + head) * cut, cut, 1)
    exp_shape, in_shape = online_expbias.shape, online_inbias.shape
    grad_expbias = lax.dynamic_slice_in_dim(
        biases[0].reshape(exp_shape), data * (exp_shape[2] // dp_count), exp_shape[2] // dp_count, 2
    )
    grad_inbias = lax.dynamic_slice_in_dim(
        biases[1, : 2 * local].reshape(in_shape),
        data * (in_shape[3] // dp_count),
        in_shape[3] // dp_count,
        3,
    )
    return (
        loss_total,
        input_grad,
        grad_inproj,
        grad_inbias,
        grad_outproj,
        norms[None, 0:2],
        norms[None, 2:6],
        grad_expand,
        grad_expbias,
        grad_contract,
        rms_values,
    )


def solution(mesh):
    placed = (
        P("heads", "dp", None),
        P("heads", "dp", None),
        P("dp", None),
        P("dp"),
        P("dp", None),
        P("section", None, None, "heads"),
        P("section", None, "heads", None),
        P("section", "heads", None),
        P("section", None, None),
        P("section", None, None),
        P("section", None, "heads"),
        P("section", "heads", None),
        P("section", "heads", None),
        P("section", None, None, "heads"),
        P("section", None, "heads", None),
        P("section", "heads", None),
        P("section", None, None),
        P("section", None, None),
        P("section", None, "heads"),
        P("section", "heads", None),
        P("section", "heads", None),
    )
    return jax.shard_map(
        per_device,
        mesh=mesh,
        in_specs=placed,
        out_specs=(
            P(),
            P("heads", "dp", "section"),
            P("section", "dp", None, "heads"),
            P("section", None, "heads", "dp"),
            P("section", "heads", "dp"),
            P("section", None, ("dp", "heads")),
            P("section", None, ("dp", "heads")),
            P("section", "dp", "heads"),
            P("section", "heads", "dp"),
            P("section", "heads", "dp"),
            P(),
        ),
        check_vma=False,
    )
```

time: 1570 us -> 477 us (0.30)
  waiting for transfers between devices: 1080 us -> 165 us
  blocking collectives: 138 us -> 0 us
  matrix products: 137 us -> 3.31 us
  starting transfers between devices: 7.6 us -> 140 us
  Pallas kernels: 0 us -> 56.3 us
  other arithmetic: 74.7 us -> 34.7 us
  local copies, waits for them, and re-layouts: 97.9 us -> 68 us
  between operations: 21.5 us -> 5.35 us
    unnamed x56 -> x0, waiting for transfers between devices: 455 us -> none
    reduce_scatter x15 -> x0, waiting for transfers between devices: 383 us -> none  [the longest x6 165 us: scatter_rows(): lax.psum_scatter(row_term(jnp.int32(0), lax.axis_size('heads') * row_tota...]
    all_gather x7 -> x0, waiting for transfers between devices: 235 us -> none  [the longest x6 182 us: gather_rows(): return lax.all_gather(values, 'heads', axis=0, tiled=True)]
    ppermute x5 -> x107, waiting for transfers between devices: 6.66 us -> 165 us  [swap(): return lax.ppermute(value, axis, [(i, i ^ distance) for i in range(count)])]
    ppermute x5 -> x107, starting transfers between devices: 5.01 us -> 140 us  [swap(): return lax.ppermute(value, axis, [(i, i ^ distance) for i in range(count)])]
    dot_general x61 -> x4, matrix products: 137 us -> 3.31 us  [the longest x2 2.52 us: dot_nt(): lax.dot_general(a, b, (((1,), (1,)), ((), ())), preferred_element_type=F32)]
    all_gather x7 -> x0, blocking collectives: 72.5 us -> none  [the longest x6 59.6 us: gather_grads(): return lax.all_gather(values, 'heads', axis=0, tiled=True)]
    pallas_call x0 -> x28, Pallas kernels: none -> 56.3 us  [kernel_call(): pl.pallas_call(body, out_shape=[jax.ShapeDtypeStruct(s, d) for s, d in ou...]
  transfers between devices with their start and end apart: 44 -> 107, of which waited for: 37 -> 51; matrix products, arithmetic and copies ran while one was open for 10% -> 11% of each run, Pallas kernels for 0% -> 11%
where the time goes in v1:
time: 477 us; the launch traced here: 473 us
  waiting for transfers between devices  165 us (35%)
  starting transfers between devices  140 us (29%)
  local copies, waits for them, and re-layouts  68 us (14%)
  Pallas kernels  56.3 us (12%)
  other arithmetic  34.7 us (7%)
  between operations  5.35 us (1%)
    ppermute x107, waiting for transfers between devices, swap(): return lax.ppermute(value, axis, [(i, i ^ distance) for i in range(count)])  165 us
    ppermute x107, starting transfers between devices, swap(): return lax.ppermute(value, axis, [(i, i ^ distance) for i in range(count)])  140 us
    pallas_call x28, Pallas kernels, kernel_call(): pl.pallas_call(body, out_shape=[jax.ShapeDtypeStruct(s, d) for s, d in ou...  56.3 us
    unnamed x299, local copies, waits for them, and re-layouts  49.1 us
  transfers between devices with their start and end apart: 107, of which 51 were waited for; matrix products, arithmetic and copies ran while one was open for 11% of the time, Pallas kernels for 11%

profile of v1, /device:TPU:1, one launch (start us, length us, event | category | flops | bytes accessed | tf_op | source)
XLA Modules:
  0.0 472.9 jit_solution(18394172360346937385)
XLA Ops:
  7.8 2.3 collective-permute-start
  13.5 3.4 collective-permute-done.21.g1_r
  21.2 8.9 %collective-permute-done.22.g2_r = bf16[2,2,64,768]{3,2,1,0:T(8,128)(2,1)S(1)} collective-permute-done((bf16[2,2,64,768]{3,2,1,0:T(8,128)(2,1)S(1)}, bf16[2,2,64,768]{3,2,1,0:T(8,128)(2,1)S(1)}, u32[]{:S(2)}, u32[]{:S(2)}) %collective-permute-start.22) | collective-permute-done | bytes 393248 | tf_op jit(solution)/shard_map/gather_in/ppermute | solution.py:55
  30.9 3.8 attn_forward.6
  35.2 3.3 attn_forward.4
  41.6 3.8 collective-permute-done.26.g_r
  50.1 2.6 collective-permute-done.27.f_r
  60.0 2.0 collective-permute-done.7.g1_r.refs_7_
  62.2 8.2 %collective-permute-done.29.g2_r = bf16[2,2,64,768]{3,2,1,0:T(8,128)(2,1)S(1)} collective-permute-done((bf16[2,2,64,768]{3,2,1,0:T(8,128)(2,1)S(1)}, bf16[2,2,64,768]{3,2,1,0:T(8,128)(2,1)S(1)}, u32[]{:S(2)}, u32[]{:S(2)}) %collective-permute-start.29) | collective-permute-done | bytes 393248 | tf_op jit(solution)/shard_map/gather_hidden/ppermute | solution.py:55
  70.4 2.4 feed_forward.6
  74.3 2.6 feed_forward.4
  78.1 2.5 collective-permute-done.32.g_r
  80.9 4.4 collective-permute-done.11.g_r
  85.7 3.9 collective-permute-done.33.f_r
  92.5 2.8 collective-permute-done.34.g1_r
  95.6 3.3 collective-permute-done.13.g1_r.refs_7_
  99.3 3.6 collective-permute-done.35.g2_r
  102.9 3.3 attn_forward.7
  106.5 3.3 attn_forward.5
  111.5 2.8 collective-permute-done.36.g_r
  114.4 3.4 collective-permute-done.15.g_r
  121.4 3.3 collective-permute-done.16.f_r
  126.0 2.0 collective-permute-done.38.g1_r
  130.6 6.2 %collective-permute-done.39.g2_r = bf16[2,2,64,768]{3,2,1,0:T(8,128)(2,1)S(1)} collective-permute-done((bf16[2,2,64,768]{3,2,1,0:T(8,128)(2,1)S(1)}, bf16[2,2,64,768]{3,2,1,0:T(8,128)(2,1)S(1)}, u32[]{:S(2)}, u32[]{:S(2)}) %collective-permute-start.39) | collective-permute-done | bytes 393248 | tf_op jit(solution)/shard_map/gather_hidden/ppermute | solution.py:55
  136.8 2.6 feed_forward.7
  140.0 2.6 feed_forward.5
  144.2 6.3 %collective-permute-done.40.g_r = bf16[2,2,64,768]{3,2,1,0:T(8,128)(2,1)S(1)} collective-permute-done((bf16[2,2,64,768]{3,2,1,0:T(8,128)(2,1)S(1)}, bf16[2,2,64,768]{3,2,1,0:T(8,128)(2,1)S(1)}, u32[]{:S(2)}, u32[]{:S(2)}) %collective-permute-start.40) | collective-permute-done | bytes 393248 | tf_op jit(solution)/shard_map/scatter_feed/ppermute | solution.py:55
  152.4 3.2 collective-permute-done.41.f_r
  163.9 2.2 collective-permute-start.45
  168.7 3.1 collective-permute-done.46
  171.9 2.3 fusion.77
  175.0 2.4 collective-permute-start.49
  177.5 20.3 %collective-permute-start.47 = (bf16[4,5,768]{2,1,0:T(8,128)(2,1)S(1)}, bf16[4,5,768]{2,1,0:T(8,128)(2,1)S(1)}, u32[]{:S(2)}, u32[]{:S(2)}) collective-permute-start(bf16[4,5,768]{2,1,0:T(8,128)(2,1)S(1)} %get-tuple-element.337), channel_id=1, source_target_pairs={{0,16},{16,0},{1,17},{17,1},{2,18},{18,2},{3,19},{19,3},{4,20},{20... | collective-permute-start | bytes 92168 | tf_op jit(solution)/shard_map/loss/keys/ppermute | solution.py:55
  203.4 2.7 collective-permute-done.51.refs_2_
  208.0 2.8 collective-permute-done.53.refs_4_
  214.7 2.8 feed_backward.2
  232.2 1.9 fusion.78
  246.8 2.0 feed_weights.3
  250.5 1.9 collective-permute-done.60.refs_3_
  253.2 7.0 %collective-permute-start.102 = (bf16[4,2,96,768]{3,2,1,0:T(8,128)(2,1)S(1)}, bf16[4,2,96,768]{3,2,1,0:T(8,128)(2,1)S(1)}, u32[]{:S(2)}, u32[]{:S(2)}) collective-permute-start(bf16[4,2,96,768]{3,2,1,0:T(8,128)(2,1)S(1)} %slice_bitcast_fusion), channel_id=1, source_target_pairs={{0,16},{16,0},{1,17},{17,1},{2,18},{18,2},{3,19},{19,3},{4,20},{20... | collective-permute-start | bytes 3538952 | tf_op jit(solution)/shard_map/weight_grads/ppermute | solution.py:55
  260.2 4.0 attn_backward.2
  270.7 7.2 %collective-permute-start.93 = (bf16[4,96,768]{2,1,0:T(8,128)(2,1)S(1)}, bf16[4,96,768]{2,1,0:T(8,128)(2,1)S(1)}, u32[]{:S(2)}, u32[]{:S(2)}) collective-permute-start(bf16[4,96,768]{2,1,0:T(8,128)(2,1)S(1)} %slice_bitcast_fusion.6), channel_id=1, source_target_pairs={{0,16},{16,0},{1,17},{17,1},{2,18},{18,2},{3,19},{19,3},{4,20},{20... | collective-permute-start | bytes 1769480 | tf_op jit(solution)/shard_map/weight_grads/ppermute | solution.py:55
  280.4 2.1 collective-permute-done.67.refs_2_
  286.0 2.2 collective-permute-done.69.refs_4_
  288.5 2.1 feed_backward.3
  300.0 2.8 collective-permute-done.74.rest_5_
  305.8 1.9 concatenate.62
  319.7 2.0 feed_weights.2
  330.9 4.4 attn_backward.3
  340.1 2.9 concatenate.63
  343.0 10.2 %collective-permute-start.81 = (f32[23,768]{1,0:T(8,128)}, f32[23,768]{1,0:T(8,128)S(1)}, u32[]{:S(2)}, u32[]{:S(2)}) collective-permute-start(f32[23,768]{1,0:T(8,128)} %concatenate.63), channel_id=1, source_target_pairs={{0,16},{16,0},{1,17},{17,1},{2,18},{18,2},{3,19},{19,3},{4,20},{20... | collective-permute-start | bytes 211976 | tf_op jit(solution)/shard_map/small_grads/ppermute | solution.py:55
  364.7 1.9 attn_weights.2
  370.9 2.2 collective-permute-start.89
  373.0 2.8 collective-permute-start.83
  386.9 2.8 collective-permute-start.96
  396.6 2.5 collective-permute-start.92
  399.1 4.4 collective-permute-done.95
  403.7 6.3 %collective-permute-start.105 = (bf16[2,96,768]{2,1,0:T(8,128)(2,1)S(1)}, bf16[2,96,768]{2,1,0:T(8,128)(2,1)S(1)}, u32[]{:S(2)}, u32[]{:S(2)}) collective-permute-start(bf16[2,96,768]{2,1,0:T(8,128)(2,1)S(1)} %copy-done.135), channel_id=1, source_target_pairs={{0,12},{4,8},{8,4},{12,0},{1,13},{5,9},{9,5},{13,1},{2,14},{6,10},... | collective-permute-start | bytes 884744 | tf_op jit(solution)/shard_map/weight_grads/ppermute | solution.py:55
  411.4 2.1 collective-permute-start.101
  413.5 12.3 %collective-permute-done.91 = bf16[96,768]{1,0:T(8,128)(2,1)S(1)} collective-permute-done((bf16[96,768]{1,0:T(8,128)(2,1)S(1)}, bf16[96,768]{1,0:T(8,128)(2,1)S(1)}, u32[]{:S(2)}, u32[]{:S(2)}) %collective-permute-start.91) | collective-permute-done | bytes 147488 | tf_op jit(solution)/shard_map/weight_grads/ppermute | solution.py:55
  427.8 5.8 %collective-permute-start.97 = (bf16[96,768]{1,0:T(8,128)(2,1)S(1)}, bf16[96,768]{1,0:T(8,128)(2,1)S(1)}, u32[]{:S(2)}, u32[]{:S(2)}) collective-permute-start(bf16[96,768]{1,0:T(8,128)(2,1)S(1)} %get-tuple-element.268), channel_id=1, source_target_pairs={{0,16},{16,0},{1,17},{17,1},{2,18},{18,2},{3,19},{19,3},{4,20},{20... | collective-permute-start | bytes 442376 | tf_op jit(solution)/shard_map/weight_grads/ppermute | solution.py:55
  433.7 19.5 %collective-permute-done.104 = bf16[2,96,768]{2,1,0:T(8,128)(2,1)S(1)} collective-permute-done((bf16[2,96,768]{2,1,0:T(8,128)(2,1)S(1)}, bf16[2,96,768]{2,1,0:T(8,128)(2,1)S(1)}, u32[]{:S(2)}, u32[]{:S(2)}) %collective-permute-start.104) | collective-permute-done | bytes 294944 | tf_op jit(solution)/shard_map/weight_grads/ppermute | solution.py:55
  453.2 12.6 %collective-permute-done.100 = bf16[2,96,768]{2,1,0:T(8,128)(2,1)S(1)} collective-permute-done((bf16[2,96,768]{2,1,0:T(8,128)(2,1)S(1)}, bf16[2,96,768]{2,1,0:T(8,128)(2,1)S(1)}, u32[]{:S(2)}, u32[]{:S(2)}) %collective-permute-start.100) | collective-permute-done | bytes 294944 | tf_op jit(solution)/shard_map/weight_grads/ppermute | solution.py:55
  467.3 1.8 collective-permute-start.106
  (617 shorter events, 194.1 us)
Async XLA Ops:
  2.9 9.5 %collective-permute-start.4 = (bf16[8,768]{1,0:T(8,128)(2,1)S(1)}, bf16[8,768]{1,0:T(8,128)(2,1)S(1)}, u32[]{:S(2)}, u32[]{:S(2)}) collective-permute-start(bf16[8,768]{1,0:T(8,128)(2,1)S(1)} %fusion.45), channel_id=1, source_target_pairs={{0,16},{16,0},{1,17},{17,1},{2,18},{18,2},{3,19},{19,3},{4,20},{20... | collective-permute-start | bytes 36872 | tf_op jit(solution)/shard_map/weights/ppermute | solution.py:55
  5.8 12.9 %collective-permute-start.24 = (bf16[192,768]{1,0:T(8,128)(2,1)}, bf16[192,768]{1,0:T(8,128)(2,1)S(1)}, u32[]{:S(2)}, u32[]{:S(2)}) collective-permute-start(bf16[192,768]{1,0:T(8,128)(2,1)} %bitcast.377), channel_id=1, source_target_pairs={{0,16},{16,0},{1,17},{17,1},{2,18},{18,2},{3,19},{19,3},{4,20},{20... | collective-permute-start | bytes 884744 | tf_op jit(solution)/shard_map/weights/ppermute | solution.py:55
  5.8 13.5 %collective-permute-start.3 = (bf16[192,768]{1,0:T(8,128)(2,1)}, bf16[192,768]{1,0:T(8,128)(2,1)S(1)}, u32[]{:S(2)}, u32[]{:S(2)}) collective-permute-start(bf16[192,768]{1,0:T(8,128)(2,1)} %bitcast.378), channel_id=1, source_target_pairs={{0,16},{16,0},{1,17},{17,1},{2,18},{18,2},{3,19},{19,3},{4,20},{20... | collective-permute-start | bytes 884744 | tf_op jit(solution)/shard_map/weights/ppermute | solution.py:55
  7.8 10.7 %collective-permute-start = (bf16[2,64,768]{2,1,0:T(8,128)(2,1)S(1)}, bf16[2,64,768]{2,1,0:T(8,128)(2,1)S(1)}, u32[]{:S(2)}, u32[]{:S(2)}) collective-permute-start(bf16[2,64,768]{2,1,0:T(8,128)(2,1)S(1)} %bitcast.328), channel_id=1, source_target_pairs={{0,1},{1,0},{2,3},{3,2},{4,5},{5,4},{6,7},{7,6},{8,9},{9,8},{10,11... | collective-permute-start | bytes 589832 | tf_op jit(solution)/shard_map/gather_in/ppermute | solution.py:55
  12.4 7.2 %collective-permute-start.23 = (bf16[576,768]{1,0:T(8,128)(2,1)S(1)}, bf16[576,768]{1,0:T(8,128)(2,1)S(1)}, u32[]{:S(2)}, u32[]{:S(2)}) collective-permute-start(bf16[576,768]{1,0:T(8,128)(2,1)S(1)} %bitcast.375), channel_id=1, source_target_pairs={{0,16},{16,0},{1,17},{17,1},{2,18},{18,2},{3,19},{19,3},{4,20},{20... | collective-permute-start | bytes 2654216 | tf_op jit(solution)/shard_map/weights/ppermute | solution.py:55
  16.9 17.9 %collective-permute-start.2 = (bf16[576,768]{1,0:T(8,128)(2,1)}, bf16[576,768]{1,0:T(8,128)(2,1)S(1)}, u32[]{:S(2)}, u32[]{:S(2)}) collective-permute-start(bf16[576,768]{1,0:T(8,128)(2,1)} %bitcast.376), channel_id=1, source_target_pairs={{0,16},{16,0},{1,17},{17,1},{2,18},{18,2},{3,19},{19,3},{4,20},{20... | collective-permute-start | bytes 2654216 | tf_op jit(solution)/shard_map/weights/ppermute | solution.py:55
  18.5 20.0 %collective-permute-start.31 = (bf16[768,768]{1,0:T(8,128)(2,1)}, bf16[768,768]{1,0:T(8,128)(2,1)S(1)}, u32[]{:S(2)}, u32[]{:S(2)}) collective-permute-start(bf16[768,768]{1,0:T(8,128)(2,1)} %bitcast.44), channel_id=1, source_target_pairs={{0,16},{16,0},{1,17},{17,1},{2,18},{18,2},{3,19},{19,3},{4,20},{20... | collective-permute-start | bytes 3538952 | tf_op jit(solution)/shard_map/weights/ppermute | solution.py:55
  18.7 36.4 %collective-permute-start.30 = (bf16[768,768]{1,0:T(8,128)(2,1)}, bf16[768,768]{1,0:T(8,128)(2,1)S(1)}, u32[]{:S(2)}, u32[]{:S(2)}) collective-permute-start(bf16[768,768]{1,0:T(8,128)(2,1)} %bitcast.43), channel_id=1, source_target_pairs={{0,16},{16,0},{1,17},{17,1},{2,18},{18,2},{3,19},{19,3},{4,20},{20... | collective-permute-start | bytes 3538952 | tf_op jit(solution)/shard_map/weights/ppermute | solution.py:55
  19.3 10.8 %collective-permute-start.22 = (bf16[2,2,64,768]{3,2,1,0:T(8,128)(2,1)S(1)}, bf16[2,2,64,768]{3,2,1,0:T(8,128)(2,1)S(1)}, u32[]{:S(2)}, u32[]{:S(2)}) collective-permute-start(bf16[2,2,64,768]{3,2,1,0:T(8,128)(2,1)S(1)} %pad_maximum_fusion.5), channel_id=1, source_target_pairs={{0,1},{1,0},{2,3},{3,2},{4,5},{5,4},{6,7},{7,6},{8,9},{9,8},{10,11... | collective-permute-start | bytes 1179656 | tf_op jit(solution)/shard_map/gather_in/ppermute | solution.py:55
  19.6 15.5 %collective-permute-start.1 = (bf16[2,2,64,768]{3,2,1,0:T(8,128)(2,1)S(1)}, bf16[2,2,64,768]{3,2,1,0:T(8,128)(2,1)S(1)}, u32[]{:S(2)}, u32[]{:S(2)}) collective-permute-start(bf16[2,2,64,768]{3,2,1,0:T(8,128)(2,1)S(1)} %pad_maximum_fusion.1), channel_id=1, source_target_pairs={{0,2},{1,3},{2,0},{3,1},{4,6},{5,7},{6,4},{7,5},{8,10},{9,11},{10,... | collective-permute-start | bytes 1179656 | tf_op jit(solution)/shard_map/gather_in/ppermute | solution.py:55
  30.1 29.6 %collective-permute-start.10 = (bf16[768,768]{1,0:T(8,128)(2,1)S(1)}, bf16[768,768]{1,0:T(8,128)(2,1)S(1)}, u32[]{:S(2)}, u32[]{:S(2)}) collective-permute-start(bf16[768,768]{1,0:T(8,128)(2,1)S(1)} %bitcast.373), channel_id=1, source_target_pairs={{0,16},{16,0},{1,17},{17,1},{2,18},{18,2},{3,19},{19,3},{4,20},{20... | collective-permute-start | bytes 3538952 | tf_op jit(solution)/shard_map/weights/ppermute | solution.py:55
  34.8 39.3 %collective-permute-start.9 = (bf16[768,768]{1,0:T(8,128)(2,1)S(1)}, bf16[768,768]{1,0:T(8,128)(2,1)S(1)}, u32[]{:S(2)}, u32[]{:S(2)}) collective-permute-start(bf16[768,768]{1,0:T(8,128)(2,1)S(1)} %bitcast.374), channel_id=1, source_target_pairs={{0,16},{16,0},{1,17},{17,1},{2,18},{18,2},{3,19},{19,3},{4,20},{20... | collective-permute-start | bytes 3538952 | tf_op jit(solution)/shard_map/weights/ppermute | solution.py:55
  35.1 10.3 %collective-permute-start.26 = (bf16[2,2,64,768]{3,2,1,0:T(8,128)(2,1)S(1)}, bf16[2,2,64,768]{3,2,1,0:T(8,128)(2,1)S(1)}, u32[]{:S(2)}, u32[]{:S(2)}) collective-permute-start(bf16[2,2,64,768]{3,2,1,0:T(8,128)(2,1)S(1)} %get-tuple-element.166), channel_id=1, source_target_pairs={{0,1},{1,0},{2,3},{3,2},{4,5},{5,4},{6,7},{7,6},{8,9},{9,8},{10,11... | collective-permute-start | bytes 1179656 | tf_op jit(solution)/shard_map/scatter_attn/ppermute | solution.py:55
  38.6 9.9 %collective-permute-start.5 = (bf16[2,2,64,768]{3,2,1,0:T(8,128)(2,1)S(1)}, bf16[2,2,64,768]{3,2,1,0:T(8,128)(2,1)S(1)}, u32[]{:S(2)}, u32[]{:S(2)}) collective-permute-start(bf16[2,2,64,768]{3,2,1,0:T(8,128)(2,1)S(1)} %get-tuple-element.144), channel_id=1, source_target_pairs={{0,2},{1,3},{2,0},{3,1},{4,6},{5,7},{6,4},{7,5},{8,10},{9,11},{10,... | collective-permute-start | bytes 1179656 | tf_op jit(solution)/shard_map/scatter_attn/ppermute | solution.py:55
  45.4 7.3 %collective-permute-start.27 = (bf16[2,64,768]{2,1,0:T(8,128)(2,1)S(1)}, bf16[2,64,768]{2,1,0:T(8,128)(2,1)S(1)}, u32[]{:S(2)}, u32[]{:S(2)}) collective-permute-start(bf16[2,64,768]{2,1,0:T(8,128)(2,1)S(1)} %fusion.19), channel_id=1, source_target_pairs={{0,2},{1,3},{2,0},{3,1},{4,6},{5,7},{6,4},{7,5},{8,10},{9,11},{10,... | collective-permute-start | bytes 589832 | tf_op jit(solution)/shard_map/scatter_attn/ppermute | solution.py:55
  48.6 8.0 %collective-permute-start.6 = (bf16[2,64,768]{2,1,0:T(8,128)(2,1)S(1)}, bf16[2,64,768]{2,1,0:T(8,128)(2,1)S(1)}, u32[]{:S(2)}, u32[]{:S(2)}) collective-permute-start(bf16[2,64,768]{2,1,0:T(8,128)(2,1)S(1)} %fusion.23), channel_id=1, source_target_pairs={{0,1},{1,0},{2,3},{3,2},{4,5},{5,4},{6,7},{7,6},{8,9},{9,8},{10,11... | collective-permute-start | bytes 589832 | tf_op jit(solution)/shard_map/scatter_attn/ppermute | solution.py:55
  58.8 11.6 %collective-permute-start.29 = (bf16[2,2,64,768]{3,2,1,0:T(8,128)(2,1)S(1)}, bf16[2,2,64,768]{3,2,1,0:T(8,128)(2,1)S(1)}, u32[]{:S(2)}, u32[]{:S(2)}) collective-permute-start(bf16[2,2,64,768]{3,2,1,0:T(8,128)(2,1)S(1)} %pad_maximum_fusion.6), channel_id=1, source_target_pairs={{0,1},{1,0},{2,3},{3,2},{4,5},{5,4},{6,7},{7,6},{8,9},{9,8},{10,11... | collective-permute-start | bytes 1179656 | tf_op jit(solution)/shard_map/gather_hidden/ppermute | solution.py:55
  62.1 12.2 %collective-permute-start.8 = (bf16[2,2,64,768]{3,2,1,0:T(8,128)(2,1)S(1)}, bf16[2,2,64,768]{3,2,1,0:T(8,128)(2,1)S(1)}, u32[]{:S(2)}, u32[]{:S(2)}) collective-permute-start(bf16[2,2,64,768]{3,2,1,0:T(8,128)(2,1)S(1)} %pad_maximum_fusion.2), channel_id=1, source_target_pairs={{0,2},{1,3},{2,0},{3,1},{4,6},{5,7},{6,4},{7,5},{8,10},{9,11},{10,... | collective-permute-start | bytes 1179656 | tf_op jit(solution)/shard_map/gather_hidden/ppermute | solution.py:55
  72.8 7.8 %collective-permute-start.32 = (bf16[2,2,64,768]{3,2,1,0:T(8,128)(2,1)S(1)}, bf16[2,2,64,768]{3,2,1,0:T(8,128)(2,1)S(1)}, u32[]{:S(2)}, u32[]{:S(2)}) collective-permute-start(bf16[2,2,64,768]{3,2,1,0:T(8,128)(2,1)S(1)} %get-tuple-element.170), channel_id=1, source_target_pairs={{0,1},{1,0},{2,3},{3,2},{4,5},{5,4},{6,7},{7,6},{8,9},{9,8},{10,11... | collective-permute-start | bytes 1179656 | tf_op jit(solution)/shard_map/scatter_feed/ppermute | solution.py:55
  77.8 7.5 %collective-permute-start.11 = (bf16[2,2,64,768]{3,2,1,0:T(8,128)(2,1)S(1)}, bf16[2,2,64,768]{3,2,1,0:T(8,128)(2,1)S(1)}, u32[]{:S(2)}, u32[]{:S(2)}) collective-permute-start(bf16[2,2,64,768]{3,2,1,0:T(8,128)(2,1)S(1)} %get-tuple-element.149), channel_id=1, source_target_pairs={{0,2},{1,3},{2,0},{3,1},{4,6},{5,7},{6,4},{7,5},{8,10},{9,11},{10,... | collective-permute-start | bytes 1179656 | tf_op jit(solution)/shard_map/scatter_feed/ppermute | solution.py:55
  80.7 8.9 %collective-permute-start.33 = (bf16[2,64,768]{2,1,0:T(8,128)(2,1)S(1)}, bf16[2,64,768]{2,1,0:T(8,128)(2,1)S(1)}, u32[]{:S(2)}, u32[]{:S(2)}) collective-permute-start(bf16[2,64,768]{2,1,0:T(8,128)(2,1)S(1)} %fusion.18), channel_id=1, source_target_pairs={{0,2},{1,3},{2,0},{3,1},{4,6},{5,7},{6,4},{7,5},{8,10},{9,11},{10,... | collective-permute-start | bytes 589832 | tf_op jit(solution)/shard_map/scatter_feed/ppermute | solution.py:55
  95.3 7.6 %collective-permute-start.35 = (bf16[2,2,64,768]{3,2,1,0:T(8,128)(2,1)S(1)}, bf16[2,2,64,768]{3,2,1,0:T(8,128)(2,1)S(1)}, u32[]{:S(2)}, u32[]{:S(2)}) collective-permute-start(bf16[2,2,64,768]{3,2,1,0:T(8,128)(2,1)S(1)} %pad_maximum_fusion.7), channel_id=1, source_target_pairs={{0,1},{1,0},{2,3},{3,2},{4,5},{5,4},{6,7},{7,6},{8,9},{9,8},{10,11... | collective-permute-start | bytes 1179656 | tf_op jit(solution)/shard_map/gather_in/ppermute | solution.py:55
  99.0 7.5 %collective-permute-start.14 = (bf16[2,2,64,768]{3,2,1,0:T(8,128)(2,1)S(1)}, bf16[2,2,64,768]{3,2,1,0:T(8,128)(2,1)S(1)}, u32[]{:S(2)}, u32[]{:S(2)}) collective-permute-start(bf16[2,2,64,768]{3,2,1,0:T(8,128)(2,1)S(1)} %pad_maximum_fusion.3), channel_id=1, source_target_pairs={{0,2},{1,3},{2,0},{3,1},{4,6},{5,7},{6,4},{7,5},{8,10},{9,11},{10,... | collective-permute-start | bytes 1179656 | tf_op jit(solution)/shard_map/gather_in/ppermute | solution.py:55
  106.2 8.1 %collective-permute-start.36 = (bf16[2,2,64,768]{3,2,1,0:T(8,128)(2,1)S(1)}, bf16[2,2,64,768]{3,2,1,0:T(8,128)(2,1)S(1)}, u32[]{:S(2)}, u32[]{:S(2)}) collective-permute-start(bf16[2,2,64,768]{3,2,1,0:T(8,128)(2,1)S(1)} %get-tuple-element.174), channel_id=1, source_target_pairs={{0,1},{1,0},{2,3},{3,2},{4,5},{5,4},{6,7},{7,6},{8,9},{9,8},{10,11... | collective-permute-start | bytes 1179656 | tf_op jit(solution)/shard_map/scatter_attn/ppermute | solution.py:55
  110.7 7.1 %collective-permute-start.15 = (bf16[2,2,64,768]{3,2,1,0:T(8,128)(2,1)S(1)}, bf16[2,2,64,768]{3,2,1,0:T(8,128)(2,1)S(1)}, u32[]{:S(2)}, u32[]{:S(2)}) collective-permute-start(bf16[2,2,64,768]{3,2,1,0:T(8,128)(2,1)S(1)} %get-tuple-element.155), channel_id=1, source_target_pairs={{0,2},{1,3},{2,0},{3,1},{4,6},{5,7},{6,4},{7,5},{8,10},{9,11},{10,... | collective-permute-start | bytes 1179656 | tf_op jit(solution)/shard_map/scatter_attn/ppermute | solution.py:55
  128.0 8.8 %collective-permute-start.39 = (bf16[2,2,64,768]{3,2,1,0:T(8,128)(2,1)S(1)}, bf16[2,2,64,768]{3,2,1,0:T(8,128)(2,1)S(1)}, u32[]{:S(2)}, u32[]{:S(2)}) collective-permute-start(bf16[2,2,64,768]{3,2,1,0:T(8,128)(2,1)S(1)} %pad_maximum_fusion.8), channel_id=1, source_target_pairs={{0,1},{1,0},{2,3},{3,2},{4,5},{5,4},{6,7},{7,6},{8,9},{9,8},{10,11... | collective-permute-start | bytes 1179656 | tf_op jit(solution)/shard_map/gather_hidden/ppermute | solution.py:55
  130.5 9.4 %collective-permute-start.18 = (bf16[2,2,64,768]{3,2,1,0:T(8,128)(2,1)S(1)}, bf16[2,2,64,768]{3,2,1,0:T(8,128)(2,1)S(1)}, u32[]{:S(2)}, u32[]{:S(2)}) collective-permute-start(bf16[2,2,64,768]{3,2,1,0:T(8,128)(2,1)S(1)} %pad_maximum_fusion.4), channel_id=1, source_target_pairs={{0,2},{1,3},{2,0},{3,1},{4,6},{5,7},{6,4},{7,5},{8,10},{9,11},{10,... | collective-permute-start | bytes 1179656 | tf_op jit(solution)/shard_map/gather_hidden/ppermute | solution.py:55
  139.4 11.1 %collective-permute-start.40 = (bf16[2,2,64,768]{3,2,1,0:T(8,128)(2,1)S(1)}, bf16[2,2,64,768]{3,2,1,0:T(8,128)(2,1)S(1)}, u32[]{:S(2)}, u32[]{:S(2)}) collective-permute-start(bf16[2,2,64,768]{3,2,1,0:T(8,128)(2,1)S(1)} %get-tuple-element.178), channel_id=1, source_target_pairs={{0,1},{1,0},{2,3},{3,2},{4,5},{5,4},{6,7},{7,6},{8,9},{9,8},{10,11... | collective-permute-start | bytes 1179656 | tf_op jit(solution)/shard_map/scatter_feed/ppermute | solution.py:55
  142.6 8.8 %collective-permute-start.19 = (bf16[2,2,64,768]{3,2,1,0:T(8,128)(2,1)S(1)}, bf16[2,2,64,768]{3,2,1,0:T(8,128)(2,1)S(1)}, u32[]{:S(2)}, u32[]{:S(2)}) collective-permute-start(bf16[2,2,64,768]{3,2,1,0:T(8,128)(2,1)S(1)} %get-tuple-element.160), channel_id=1, source_target_pairs={{0,2},{1,3},{2,0},{3,1},{4,6},{5,7},{6,4},{7,5},{8,10},{9,11},{10,... | collective-permute-start | bytes 1179656 | tf_op jit(solution)/shard_map/scatter_feed/ppermute | solution.py:55
  174.8 23.0 %collective-permute-start.48 = (f32[2,896]{1,0:T(2,128)S(1)}, f32[2,896]{1,0:T(2,128)S(1)}, u32[]{:S(2)}, u32[]{:S(2)}) collective-permute-start(f32[2,896]{1,0:T(2,128)S(1)} %get-tuple-element.338), channel_id=1, source_target_pairs={{0,4},{4,0},{8,12},{12,8},{1,5},{5,1},{9,13},{13,9},{2,6},{6,2},{1... | collective-permute-start | bytes 21512 | tf_op jit(solution)/shard_map/loss/pulls/ppermute | solution.py:55
  174.8 22.9 %collective-permute-start.50 = (f32[2,896]{1,0:T(2,128)S(1)}, f32[2,896]{1,0:T(2,128)S(1)}, u32[]{:S(2)}, u32[]{:S(2)}) collective-permute-start(f32[2,896]{1,0:T(2,128)S(1)} %get-tuple-element.339), channel_id=1, source_target_pairs={{0,12},{4,8},{8,4},{12,0},{1,13},{5,9},{9,5},{13,1},{2,14},{6,10},... | collective-permute-start | bytes 21512 | tf_op jit(solution)/shard_map/loss/pulls/ppermute | solution.py:55
  175.0 22.7 %collective-permute-start.49 = (f32[2,896]{1,0:T(2,128)S(1)}, f32[2,896]{1,0:T(2,128)S(1)}, u32[]{:S(2)}, u32[]{:S(2)}) collective-permute-start(f32[2,896]{1,0:T(2,128)S(1)} %get-tuple-element.340), channel_id=1, source_target_pairs={{0,8},{4,12},{8,0},{12,4},{1,9},{5,13},{9,1},{13,5},{2,10},{6,14},... | collective-permute-start | bytes 21512 | tf_op jit(solution)/shard_map/loss/pulls/ppermute | solution.py:55
  177.5 21.2 %collective-permute-start.47 = (bf16[4,5,768]{2,1,0:T(8,128)(2,1)S(1)}, bf16[4,5,768]{2,1,0:T(8,128)(2,1)S(1)}, u32[]{:S(2)}, u32[]{:S(2)}) collective-permute-start(bf16[4,5,768]{2,1,0:T(8,128)(2,1)S(1)} %get-tuple-element.337), channel_id=1, source_target_pairs={{0,16},{16,0},{1,17},{17,1},{2,18},{18,2},{3,19},{19,3},{4,20},{20... | collective-permute-start | bytes 92168 | tf_op jit(solution)/shard_map/loss/keys/ppermute | solution.py:55
  226.0 9.7 %collective-permute-start.57 = (bf16[1,64,768]{2,1,0:T(8,128)(2,1)}, bf16[1,64,768]{2,1,0:T(8,128)(2,1)}, u32[]{:S(2)}, u32[]{:S(2)}) collective-permute-start(bf16[1,64,768]{2,1,0:T(8,128)(2,1)} %fusion.39), channel_id=1, source_target_pairs={{0,1},{1,0},{2,3},{3,2},{4,5},{5,4},{6,7},{7,6},{8,9},{9,8},{10,11... | collective-permute-start | bytes 294920 | tf_op jit(solution)/shard_map/scatter_dhidden/ppermute | solution.py:55
  242.1 7.2 %collective-permute-start.59 = (bf16[1,64,768]{2,1,0:T(8,128)(2,1)S(1)}, bf16[1,64,768]{2,1,0:T(8,128)(2,1)S(1)}, u32[]{:S(2)}, u32[]{:S(2)}) collective-permute-start(bf16[1,64,768]{2,1,0:T(8,128)(2,1)S(1)} %get-tuple-element.191.refs_0_), channel_id=1, source_target_pairs={{0,1},{1,0},{2,3},{3,2},{4,5},{5,4},{6,7},{7,6},{8,9},{9,8},{10,11... | collective-permute-start | bytes 294920 | tf_op jit(solution)/shard_map/gather_dattn/ppermute | solution.py:55
  249.4 10.8 %collective-permute-start.61 = (bf16[2,1,64,768]{3,2,1,0:T(8,128)(2,1)S(1)}, bf16[2,1,64,768]{3,2,1,0:T(8,128)(2,1)S(1)}, u32[]{:S(2)}, u32[]{:S(2)}) collective-permute-start(bf16[2,1,64,768]{3,2,1,0:T(8,128)(2,1)S(1)} %pad_maximum_fusion.12), channel_id=1, source_target_pairs={{0,2},{1,3},{2,0},{3,1},{4,6},{5,7},{6,4},{7,5},{8,10},{9,11},{10,... | collective-permute-start | bytes 589832 | tf_op jit(solution)/shard_map/gather_dattn/ppermute | solution.py:55
  252.4 7.8 %collective-permute-start.62 = (bf16[2,1,64,768]{3,2,1,0:T(8,128)(2,1)S(1)}, bf16[2,1,64,768]{3,2,1,0:T(8,128)(2,1)S(1)}, u32[]{:S(2)}, u32[]{:S(2)}) collective-permute-start(bf16[2,1,64,768]{3,2,1,0:T(8,128)(2,1)S(1)} %pad_maximum_fusion.13), channel_id=1, source_target_pairs={{0,1},{1,0},{2,3},{3,2},{4,5},{5,4},{6,7},{7,6},{8,9},{9,8},{10,11... | collective-permute-start | bytes 589832 | tf_op jit(solution)/shard_map/gather_dattn/ppermute | solution.py:55
  253.2 30.9 %collective-permute-start.102 = (bf16[4,2,96,768]{3,2,1,0:T(8,128)(2,1)S(1)}, bf16[4,2,96,768]{3,2,1,0:T(8,128)(2,1)S(1)}, u32[]{:S(2)}, u32[]{:S(2)}) collective-permute-start(bf16[4,2,96,768]{3,2,1,0:T(8,128)(2,1)S(1)} %slice_bitcast_fusion), channel_id=1, source_target_pairs={{0,16},{16,0},{1,17},{17,1},{2,18},{18,2},{3,19},{19,3},{4,20},{20... | collective-permute-start | bytes 3538952 | tf_op jit(solution)/shard_map/weight_grads/ppermute | solution.py:55
  268.8 9.1 %collective-permute-start.65 = (bf16[1,64,768]{2,1,0:T(8,128)(2,1)S(1)}, bf16[1,64,768]{2,1,0:T(8,128)(2,1)S(1)}, u32[]{:S(2)}, u32[]{:S(2)}) collective-permute-start(bf16[1,64,768]{2,1,0:T(8,128)(2,1)S(1)} %fusion.37), channel_id=1, source_target_pairs={{0,1},{1,0},{2,3},{3,2},{4,5},{5,4},{6,7},{7,6},{8,9},{9,8},{10,11... | collective-permute-start | bytes 294920 | tf_op jit(solution)/shard_map/scatter_dx/ppermute | solution.py:55
  269.8 8.2 %collective-permute-start.66 = (bf16[1,64,768]{2,1,0:T(8,128)(2,1)S(1)}, bf16[1,64,768]{2,1,0:T(8,128)(2,1)S(1)}, u32[]{:S(2)}, u32[]{:S(2)}) collective-permute-start(bf16[1,64,768]{2,1,0:T(8,128)(2,1)S(1)} %fusion.36), channel_id=1, source_target_pairs={{0,2},{1,3},{2,0},{3,1},{4,6},{5,7},{6,4},{7,5},{8,10},{9,11},{10,... | collective-permute-start | bytes 294920 | tf_op jit(solution)/shard_map/scatter_dx/ppermute | solution.py:55
  270.7 27.8 %collective-permute-start.93 = (bf16[4,96,768]{2,1,0:T(8,128)(2,1)S(1)}, bf16[4,96,768]{2,1,0:T(8,128)(2,1)S(1)}, u32[]{:S(2)}, u32[]{:S(2)}) collective-permute-start(bf16[4,96,768]{2,1,0:T(8,128)(2,1)S(1)} %slice_bitcast_fusion.6), channel_id=1, source_target_pairs={{0,16},{16,0},{1,17},{17,1},{2,18},{18,2},{3,19},{19,3},{4,20},{20... | collective-permute-start | bytes 1769480 | tf_op jit(solution)/shard_map/weight_grads/ppermute | solution.py:55
  292.5 111.1 %collective-permute-start.103 = (bf16[2,96,768]{2,1,0:T(8,128)(2,1)}, bf16[2,96,768]{2,1,0:T(8,128)(2,1)}, u32[]{:S(2)}, u32[]{:S(2)}) collective-permute-start(bf16[2,96,768]{2,1,0:T(8,128)(2,1)} %get-tuple-element.307), channel_id=1, source_target_pairs={{0,4},{4,0},{8,12},{12,8},{1,5},{5,1},{9,13},{13,9},{2,6},{6,2},{1... | collective-permute-start | bytes 884744 | tf_op jit(solution)/shard_map/weight_grads/ppermute | solution.py:55
  307.7 15.0 %collective-permute-start.75 = (f32[18,768]{1,0:T(8,128)}, f32[18,768]{1,0:T(8,128)S(1)}, u32[]{:S(2)}, u32[]{:S(2)}) collective-permute-start(f32[18,768]{1,0:T(8,128)} %concatenate.62), channel_id=1, source_target_pairs={{0,1},{1,0},{2,3},{3,2},{4,5},{5,4},{6,7},{7,6},{8,9},{9,8},{10,11... | collective-permute-start | bytes 165896 | tf_op jit(solution)/shard_map/small_grads/ppermute | solution.py:55
  308.5 16.0 %collective-permute-start.77 = (bf16[1,64,768]{2,1,0:T(8,128)(2,1)}, bf16[1,64,768]{2,1,0:T(8,128)(2,1)S(1)}, u32[]{:S(2)}, u32[]{:S(2)}) collective-permute-start(bf16[1,64,768]{2,1,0:T(8,128)(2,1)} %get-tuple-element.219.refs_0_), channel_id=1, source_target_pairs={{0,1},{1,0},{2,3},{3,2},{4,5},{5,4},{6,7},{7,6},{8,9},{9,8},{10,11... | collective-permute-start | bytes 294920 | tf_op jit(solution)/shard_map/gather_dattn/ppermute | solution.py:55
  343.0 23.6 %collective-permute-start.81 = (f32[23,768]{1,0:T(8,128)}, f32[23,768]{1,0:T(8,128)S(1)}, u32[]{:S(2)}, u32[]{:S(2)}) collective-permute-start(f32[23,768]{1,0:T(8,128)} %concatenate.63), channel_id=1, source_target_pairs={{0,16},{16,0},{1,17},{17,1},{2,18},{18,2},{3,19},{19,3},{4,20},{20... | collective-permute-start | bytes 211976 | tf_op jit(solution)/shard_map/small_grads/ppermute | solution.py:55
  355.1 37.5 %collective-permute-start.98 = (bf16[4,2,96,768]{3,2,1,0:T(8,128)(2,1)}, bf16[4,2,96,768]{3,2,1,0:T(8,128)(2,1)}, u32[]{:S(2)}, u32[]{:S(2)}) collective-permute-start(bf16[4,2,96,768]{3,2,1,0:T(8,128)(2,1)} %slice_bitcast_fusion.2), channel_id=1, source_target_pairs={{0,16},{16,0},{1,17},{17,1},{2,18},{18,2},{3,19},{19,3},{4,20},{20... | collective-permute-start | bytes 3538952 | tf_op jit(solution)/shard_map/weight_grads/ppermute | solution.py:55
  355.1 17.9 %collective-permute-start.84 = (bf16[2,1,64,768]{3,2,1,0:T(8,128)(2,1)}, bf16[2,1,64,768]{3,2,1,0:T(8,128)(2,1)S(1)}, u32[]{:S(2)}, u32[]{:S(2)}) collective-permute-start(bf16[2,1,64,768]{3,2,1,0:T(8,128)(2,1)} %copy-done.122), channel_id=1, source_target_pairs={{0,2},{1,3},{2,0},{3,1},{4,6},{5,7},{6,4},{7,5},{8,10},{9,11},{10,... | collective-permute-start | bytes 589832 | tf_op jit(solution)/shard_map/scatter_dx/ppermute | solution.py:55
  355.7 21.5 %collective-permute-start.85 = (bf16[2,1,64,768]{3,2,1,0:T(8,128)(2,1)}, bf16[2,1,64,768]{3,2,1,0:T(8,128)(2,1)S(1)}, u32[]{:S(2)}, u32[]{:S(2)}) collective-permute-start(bf16[2,1,64,768]{3,2,1,0:T(8,128)(2,1)} %copy-done.121), channel_id=1, source_target_pairs={{0,1},{1,0},{2,3},{3,2},{4,5},{5,4},{6,7},{7,6},{8,9},{9,8},{10,11... | collective-permute-start | bytes 589832 | tf_op jit(solution)/shard_map/scatter_dx/ppermute | solution.py:55
  370.9 20.2 %collective-permute-start.89 = (bf16[4,96,768]{2,1,0:T(8,128)(2,1)}, bf16[4,96,768]{2,1,0:T(8,128)(2,1)}, u32[]{:S(2)}, u32[]{:S(2)}) collective-permute-start(bf16[4,96,768]{2,1,0:T(8,128)(2,1)} %slice_bitcast_fusion.8), channel_id=1, source_target_pairs={{0,16},{16,0},{1,17},{17,1},{2,18},{18,2},{3,19},{19,3},{4,20},{20... | collective-permute-start | bytes 1769480 | tf_op jit(solution)/shard_map/weight_grads/ppermute | solution.py:55
  373.0 7.0 %collective-permute-start.83 = (f32[23,768]{1,0:T(8,128)S(1)}, f32[23,768]{1,0:T(8,128)S(1)}, u32[]{:S(2)}, u32[]{:S(2)}) collective-permute-start(f32[23,768]{1,0:T(8,128)S(1)} %add.235), channel_id=1, source_target_pairs={{0,8},{4,12},{8,0},{12,4},{1,9},{5,13},{9,1},{13,5},{2,10},{6,14},... | collective-permute-start | bytes 211976 | tf_op jit(solution)/shard_map/small_grads/ppermute | solution.py:55
  377.1 9.4 %collective-permute-start.86 = (bf16[1,64,768]{2,1,0:T(8,128)(2,1)}, bf16[1,64,768]{2,1,0:T(8,128)(2,1)}, u32[]{:S(2)}, u32[]{:S(2)}) collective-permute-start(bf16[1,64,768]{2,1,0:T(8,128)(2,1)} %fusion.33), channel_id=1, source_target_pairs={{0,1},{1,0},{2,3},{3,2},{4,5},{5,4},{6,7},{7,6},{8,9},{9,8},{10,11... | collective-permute-start | bytes 294920 | tf_op jit(solution)/shard_map/scatter_dx/ppermute | solution.py:55
  386.6 9.2 %collective-permute-start.94 = (bf16[96,768]{1,0:T(8,128)(2,1)}, bf16[96,768]{1,0:T(8,128)(2,1)S(1)}, u32[]{:S(2)}, u32[]{:S(2)}) collective-permute-start(bf16[96,768]{1,0:T(8,128)(2,1)} %get-tuple-element.315), channel_id=1, source_target_pairs={{0,4},{4,0},{8,12},{12,8},{1,5},{5,1},{9,13},{13,9},{2,6},{6,2},{1... | collective-permute-start | bytes 442376 | tf_op jit(solution)/shard_map/weight_grads/ppermute | solution.py:55
  386.9 9.7 %collective-permute-start.96 = (bf16[96,768]{1,0:T(8,128)(2,1)}, bf16[96,768]{1,0:T(8,128)(2,1)S(1)}, u32[]{:S(2)}, u32[]{:S(2)}) collective-permute-start(bf16[96,768]{1,0:T(8,128)(2,1)} %get-tuple-element.316), channel_id=1, source_target_pairs={{0,12},{4,8},{8,4},{12,0},{1,13},{5,9},{9,5},{13,1},{2,14},{6,10},... | collective-permute-start | bytes 442376 | tf_op jit(solution)/shard_map/weight_grads/ppermute | solution.py:55
  391.0 12.5 %collective-permute-start.95 = (bf16[96,768]{1,0:T(8,128)(2,1)S(1)}, bf16[96,768]{1,0:T(8,128)(2,1)S(1)}, u32[]{:S(2)}, u32[]{:S(2)}) collective-permute-start(bf16[96,768]{1,0:T(8,128)(2,1)S(1)} %copy-done.138), channel_id=1, source_target_pairs={{0,8},{4,12},{8,0},{12,4},{1,9},{5,13},{9,1},{13,5},{2,10},{6,14},... | collective-permute-start | bytes 442376 | tf_op jit(solution)/shard_map/weight_grads/ppermute | solution.py:55
  392.5 17.4 %collective-permute-start.88 = (bf16[2,64,384]{2,1,0:T(8,128)(2,1)S(1)}, bf16[2,64,384]{2,1,0:T(8,128)(2,1)S(1)}, u32[]{:S(2)}, u32[]{:S(2)}) collective-permute-start(bf16[2,64,384]{2,1,0:T(8,128)(2,1)S(1)} %get-tuple-element.326), channel_id=1, source_target_pairs={{0,16},{16,0},{1,17},{17,1},{2,18},{18,2},{3,19},{19,3},{4,20},{20... | collective-permute-start | bytes 294920 | tf_op jit(solution)/shard_map/input_grad/ppermute | solution.py:55
  395.7 15.7 %collective-permute-start.90 = (bf16[96,768]{1,0:T(8,128)(2,1)S(1)}, bf16[96,768]{1,0:T(8,128)(2,1)S(1)}, u32[]{:S(2)}, u32[]{:S(2)}) collective-permute-start(bf16[96,768]{1,0:T(8,128)(2,1)S(1)} %get-tuple-element.318), channel_id=1, source_target_pairs={{0,4},{4,0},{8,12},{12,8},{1,5},{5,1},{9,13},{13,9},{2,6},{6,2},{1... | collective-permute-start | bytes 442376 | tf_op jit(solution)/shard_map/weight_grads/ppermute | solution.py:55
  396.6 14.8 %collective-permute-start.92 = (bf16[96,768]{1,0:T(8,128)(2,1)S(1)}, bf16[96,768]{1,0:T(8,128)(2,1)S(1)}, u32[]{:S(2)}, u32[]{:S(2)}) collective-permute-start(bf16[96,768]{1,0:T(8,128)(2,1)S(1)} %get-tuple-element.319), channel_id=1, source_target_pairs={{0,12},{4,8},{8,4},{12,0},{1,13},{5,9},{9,5},{13,1},{2,14},{6,10},... | collective-permute-start | bytes 442376 | tf_op jit(solution)/shard_map/weight_grads/ppermute | solution.py:55
  403.6 22.2 %collective-permute-start.91 = (bf16[96,768]{1,0:T(8,128)(2,1)S(1)}, bf16[96,768]{1,0:T(8,128)(2,1)S(1)}, u32[]{:S(2)}, u32[]{:S(2)}) collective-permute-start(bf16[96,768]{1,0:T(8,128)(2,1)S(1)} %get-tuple-element.320), channel_id=1, source_target_pairs={{0,8},{4,12},{8,0},{12,4},{1,9},{5,13},{9,1},{13,5},{2,10},{6,14},... | collective-permute-start | bytes 442376 | tf_op jit(solution)/shard_map/weight_grads/ppermute | solution.py:55
  403.7 24.2 %collective-permute-start.105 = (bf16[2,96,768]{2,1,0:T(8,128)(2,1)S(1)}, bf16[2,96,768]{2,1,0:T(8,128)(2,1)S(1)}, u32[]{:S(2)}, u32[]{:S(2)}) collective-permute-start(bf16[2,96,768]{2,1,0:T(8,128)(2,1)S(1)} %copy-done.135), channel_id=1, source_target_pairs={{0,12},{4,8},{8,4},{12,0},{1,13},{5,9},{9,5},{13,1},{2,14},{6,10},... | collective-permute-start | bytes 884744 | tf_op jit(solution)/shard_map/weight_grads/ppermute | solution.py:55
  410.0 43.2 %collective-permute-start.104 = (bf16[2,96,768]{2,1,0:T(8,128)(2,1)S(1)}, bf16[2,96,768]{2,1,0:T(8,128)(2,1)S(1)}, u32[]{:S(2)}, u32[]{:S(2)}) collective-permute-start(bf16[2,96,768]{2,1,0:T(8,128)(2,1)S(1)} %copy-done.134), channel_id=1, source_target_pairs={{0,8},{4,12},{8,0},{12,4},{1,9},{5,13},{9,1},{13,5},{2,10},{6,14},... | collective-permute-start | bytes 884744 | tf_op jit(solution)/shard_map/weight_grads/ppermute | solution.py:55
  411.4 41.7 %collective-permute-start.99 = (bf16[2,96,768]{2,1,0:T(8,128)(2,1)S(1)}, bf16[2,96,768]{2,1,0:T(8,128)(2,1)S(1)}, u32[]{:S(2)}, u32[]{:S(2)}) collective-permute-start(bf16[2,96,768]{2,1,0:T(8,128)(2,1)S(1)} %get-tuple-element.310), channel_id=1, source_target_pairs={{0,4},{4,0},{8,12},{12,8},{1,5},{5,1},{9,13},{13,9},{2,6},{6,2},{1... | collective-permute-start | bytes 884744 | tf_op jit(solution)/shard_map/weight_grads/ppermute | solution.py:55
  411.4 41.7 %collective-permute-start.101 = (bf16[2,96,768]{2,1,0:T(8,128)(2,1)S(1)}, bf16[2,96,768]{2,1,0:T(8,128)(2,1)S(1)}, u32[]{:S(2)}, u32[]{:S(2)}) collective-permute-start(bf16[2,96,768]{2,1,0:T(8,128)(2,1)S(1)} %get-tuple-element.311), channel_id=1, source_target_pairs={{0,12},{4,8},{8,4},{12,0},{1,13},{5,9},{9,5},{13,1},{2,14},{6,10},... | collective-permute-start | bytes 884744 | tf_op jit(solution)/shard_map/weight_grads/ppermute | solution.py:55
  425.8 40.0 %collective-permute-start.100 = (bf16[2,96,768]{2,1,0:T(8,128)(2,1)S(1)}, bf16[2,96,768]{2,1,0:T(8,128)(2,1)S(1)}, u32[]{:S(2)}, u32[]{:S(2)}) collective-permute-start(bf16[2,96,768]{2,1,0:T(8,128)(2,1)S(1)} %get-tuple-element.312), channel_id=1, source_target_pairs={{0,8},{4,12},{8,0},{12,4},{1,9},{5,13},{9,1},{13,5},{2,10},{6,14},... | collective-permute-start | bytes 884744 | tf_op jit(solution)/shard_map/weight_grads/ppermute | solution.py:55
  427.8 41.3 %collective-permute-start.97 = (bf16[96,768]{1,0:T(8,128)(2,1)S(1)}, bf16[96,768]{1,0:T(8,128)(2,1)S(1)}, u32[]{:S(2)}, u32[]{:S(2)}) collective-permute-start(bf16[96,768]{1,0:T(8,128)(2,1)S(1)} %get-tuple-element.268), channel_id=1, source_target_pairs={{0,16},{16,0},{1,17},{17,1},{2,18},{18,2},{3,19},{19,3},{4,20},{20... | collective-permute-start | bytes 442376 | tf_op jit(solution)/shard_map/weight_grads/ppermute | solution.py:55
  (187 other events, 1391.7 us)

commit v2 on v0

v2 whole, which is shorter than its diff:
```python
import functools
import types

import jax
import jax.numpy as jnp
from jax import lax
from jax.experimental import pallas as pl
from jax.experimental.pallas import tpu as pltpu
from jax.sharding import PartitionSpec as P

TEMPER = 0.05
NORM_EPS = 1e-06
NEG_FILL = -1000000000.0
F32 = jnp.float32
LOW = jnp.bfloat16
HEADS, SECTION, DP = "heads", "section", "dp"
VMEM_SPARE = 6 * 1024 * 1024
EXTRA = 16

ROW_GAIN = 0
ROW_SHIFT = 2
ROW_EXP = 6
ROW_IN = 7


def dot_nn(a, b):
    return lax.dot_general(a, b, (((1,), (0,)), ((), ())), preferred_element_type=F32)


def dot_nt(a, b):
    return lax.dot_general(a, b, (((1,), (1,)), ((), ())), preferred_element_type=F32)


def dot_tn(a, b):
    return lax.dot_general(a, b, (((0,), (0,)), ((), ())), preferred_element_type=F32)


def bytes_of(shape, dtype):
    return functools.reduce(lambda x, y: x * y, shape, 1) * jnp.dtype(dtype).itemsize


class Loaded:
    def __init__(self, source, buffer, sem):
        self.copy = pltpu.make_async_copy(source, buffer, sem)
        self.copy.start()
        self.buffer = buffer
        self.shape = buffer.shape
        self.waiting = True

    def ready(self):
        if self.waiting:
            self.copy.wait()
            self.waiting = False
        return self.buffer

    def __getitem__(self, index):
        return self.ready()[index]

    @property
    def at(self):
        return self.ready().at


class Stored:
    def __init__(self, target, buffer, sems):
        self.target, self.buffer, self.sems = target, buffer, sems
        self.shape, self.dtype = buffer.shape, buffer.dtype
        self.copies = []

    def __setitem__(self, index, value):
        self.buffer[index] = value

    def send(self, start=0, size=None):
        run = pl.ds(start, self.shape[0] if size is None else size)
        copy = pltpu.make_async_copy(
            self.buffer.at[run], self.target.at[run], self.sems.at[len(self.copies)]
        )
        copy.start()
        self.copies.append(copy)

    def finish(self):
        for copy in self.copies:
            copy.wait()


def kernel_call(
    body, outs, scalars, arrays, flops, name, loads=(), stores=(), distant=(), weights=0
):
    side = distant[-1].shape[-1] if weights else 0
    buffers = [(a.shape, a.dtype) for a in loads] + list(stores)
    if weights:
        buffers.append(((weights, side, side), LOW))
    held = sum(bytes_of(*x) for x in [(a.shape, a.dtype) for a in arrays] + list(outs) + buffers)
    sems = [pltpu.SemaphoreType.DMA((max(1, len(loads) + 2 * len(stores)),))]
    if weights:
        sems.append(pltpu.SemaphoreType.DMA((2 * weights,)))
    counts = [len(scalars), len(arrays), len(loads), len(distant), len(outs), len(stores)]

    def whole(*refs):
        groups = []
        for count in counts + [len(loads), len(stores)]:
            groups.append(list(refs[:count]))
            refs = refs[count:]
        scal, near, load_r, far, out_r, store_r, load_b, store_b = groups
        extra = list(refs[:1]) if weights else []
        sem = refs[1] if weights else refs[0]
        loaded = [Loaded(a, b, sem.at[i]) for i, (a, b) in enumerate(zip(load_r, load_b))]
        base = len(loaded)
        stored = [
            Stored(a, b, sem.at[pl.ds(base + 2 * i, 2)]) for i, (a, b) in enumerate(zip(store_r, store_b))
        ]
        if weights:
            extra.append(refs[2])
        body(*scal, *near, *loaded, *far, *out_r, *stored, *extra)
        for item in loaded:
            item.ready()
        for item in stored:
            if not item.copies:
                item.send()
        for item in stored:
            item.finish()

    hbm = pl.BlockSpec(memory_space=pltpu.HBM)
    vmem = pl.BlockSpec(memory_space=pltpu.VMEM)
    in_specs = [pl.BlockSpec(memory_space=pltpu.SMEM)] * len(scalars)
    in_specs += [vmem] * len(arrays) + [hbm] * (len(loads) + len(distant))
    apart = [pltpu.with_memory_space_constraint(d, pltpu.HBM) for d in [*loads, *distant]]
    return pl.pallas_call(
        whole,
        out_shape=[jax.ShapeDtypeStruct(s, d) for s, d in outs]
        + [pltpu.HBM(s, d) for s, d in stores],
        in_specs=in_specs,
        out_specs=[vmem] * len(outs) + [hbm] * len(stores),
        scratch_shapes=[pltpu.VMEM(s, d) for s, d in buffers] + sems,
        compiler_params=pltpu.CompilerParams(vmem_limit_bytes=held + VMEM_SPARE),
        cost_estimate=pl.CostEstimate(flops=flops, bytes_accessed=held, transcendentals=0),
        name=name,
    )(*scalars, *arrays, *apart)


def here():
    head, core, data = [lax.axis_index(a) for a in (HEADS, SECTION, DP)]
    near = jnp.where(core == 0, 1, 2)
    chosen = jnp.where(core == 0, head // 2, head % 2)
    return types.SimpleNamespace(head=head, core=core, data=data, near=near, chosen=chosen)


def count_of(at, counts, encoder, other=0):
    return counts[2 * at.core + jnp.bitwise_xor(at.chosen, other), encoder]


def table_row(at, tables, layer, encoder, row):
    held, came = [t[encoder, row : row + 1, :] for t in tables]
    return jnp.where(at.core == layer, held, came)


def start_fetch(at, layer, held, arrived, target, sem):
    @pl.when(at.core == layer)
    def _():
        pltpu.make_async_copy(held, target, sem).start()

    @pl.when(at.core != layer)
    def _():
        pltpu.make_async_copy(arrived, target, sem).start()

    return pltpu.make_async_copy(held, target, sem)


def start_copy(source, target, sem):
    copy = pltpu.make_async_copy(source, target, sem)
    copy.start()
    return copy


def fetch_attn(at, layer, encoder, refs, scratch, sems):
    cols, outp, cols_too, outp_too = refs[:4]
    cut = cols.shape[0]
    waits = [
        start_fetch(at, layer, cols, cols_too, scratch.at[0, pl.ds(0, cut)], sems.at[0]),
        start_fetch(at, layer, outp, outp_too, scratch.at[0, pl.ds(cut, outp.shape[0])], sems.at[1]),
    ]
    if len(refs) > 4:
        waits.append(start_copy(refs[4], scratch.at[1], sems.at[2]))
    return waits


def fetch_feed(at, layer, refs, scratch, sems):
    exp, con, exp_too, con_too = refs
    return [
        start_fetch(at, layer, exp, exp_too, scratch.at[0], sems.at[0]),
        start_fetch(at, layer, con, con_too, scratch.at[1], sems.at[1]),
    ]


def swap(value, axis, distance):
    count = lax.axis_size(axis)
    return lax.ppermute(value, axis, [(i, i ^ distance) for i in range(count)])


def hop(value, first_core, second_core):
    count = lax.axis_size(HEADS)
    route = [(i, i ^ first_core) for i in range(count)]
    route += [(count + i, count + (i ^ second_core)) for i in range(count)]
    return lax.ppermute(value, (SECTION, HEADS), route)


def hop_one(value):
    return hop(value, 1, 2)


def hop_two(value):
    return hop(value, 2, 1)


def hop_both(value):
    return hop(value, 3, 3)


def over_core(value):
    return swap(value, SECTION, 1)


def behind(value, mark):
    return lax.optimization_barrier((value, mark))[0]


class Order:
    def __init__(self):
        self.last = None

    def tie(self, value):
        return value if self.last is None else behind(value, self.last)

    def mark(self, value):
        self.last = value


def bf(value):
    return value.astype(LOW)


def norm_parts(values):
    mean = jnp.mean(values, axis=-1, keepdims=True)
    center = values - mean
    spread = jnp.mean(center * center, axis=-1, keepdims=True)
    rstd = lax.rsqrt(spread + NORM_EPS)
    return center * rstd, rstd


def row_position(at, rows, shape, other):
    block_rows = rows // 2
    lane = lax.broadcasted_iota(jnp.int32, shape, 0 if shape[1] == 1 else 1)
    slot = lane // block_rows
    far = 3 - at.near
    block = jnp.bitwise_xor(jnp.bitwise_xor(at.head, other * far), (slot & 1) * far)
    block = jnp.bitwise_xor(block, (slot // 2) * at.near)
    return block * block_rows + lane - slot * block_rows


def row_keep(at, counts, encoder, rows):
    return row_position(at, rows, (rows, 1), 0) < count_of(at, counts, encoder)


def key_keep(at, counts, encoder, rows, other):
    return row_position(at, rows, (1, 2 * rows), other) < count_of(at, counts, encoder, other)


def row_groups(sources):
    if len(sources) == 2:
        return [list(sources)] * 2
    if len(sources[0].shape) == 2:
        own, one, two, far = sources
        return [[own, one], [two, far]]
    own, one, two, far = sources
    return [
        [own.at[0], two.at[1], one.at[0], far.at[1]],
        [two.at[0], own.at[1], far.at[0], one.at[1]],
    ]


def stack_rows(group):
    return jnp.concatenate([piece[...] for piece in group], axis=0)


def put_rows(targets, outs):
    if len(targets) == 4:
        half = outs[0].shape[0] // 2
        values = [outs[0][:half], outs[0][half:], outs[1][:half], outs[1][half:]]
    else:
        total = outs[0] + outs[1]
        half = total.shape[0] // 2
        values = [total[:half], total[half:]]
    for target, value in zip(targets, values):
        target[...] = value.astype(target.dtype)


def parts_shapes(rows, width, count):
    return [((rows, width), F32)] + [((rows, width), LOW)] * (count - 1)


def rows_of(sources):
    shape = sources[0].shape
    return (2 * shape[1], shape[2]) if len(shape) == 3 else shape


def attn_forward(counts, sources, tables, theirs, weights, layer, encoder, save):
    wide = len(sources) == 4
    rows, width = rows_of(sources)
    local = width // 4
    heads = local // 64
    full = 2 * rows
    count = len(sources)

    def body(s, *refs):
        at = here()
        tb, th_r, source, refs = refs[:2], refs[2], refs[3 : 3 + count], refs[3 + count :]
        w_refs, refs = refs[: len(weights)], refs[len(weights) :]
        targets, kept, (w_r, sems) = refs[:count], refs[count:-2], refs[-2:]
        waits = fetch_attn(at, layer, encoder, w_refs, w_r, sems)
        groups = row_groups(source)
        outs = []
        for unit in range(2):
            side = 0 if wide else unit
            rows_in = stack_rows(groups[unit])
            keep = key_keep(at, s, encoder, rows, unit if wide else 0)
            bias = th_r[...] if side else table_row(at, tb, layer, encoder, ROW_IN)
            if unit == 0:
                waits[0].wait()
            elif not wide:
                waits[2].wait()
            project = dot_nt(rows_in, w_r[side, : 3 * local, :])
            q = bf(project[:, :local] + bias[:, :local])
            k = bf(project[:, local : 2 * local])
            v = bf(project[:, 2 * local :] + bias[:, local : 2 * local])
            if save:
                kept[0][unit, :, :local] = q
                kept[0][unit, :, local : 2 * local] = k
                kept[0][unit, :, 2 * local :] = v
                kept[0].send(unit, 1)
            pieces = []
            for h in range(heads):
                cut = slice(64 * h, 64 * h + 64)
                scores = jnp.where(keep, dot_nt(q[:, cut] * 0.125, k[:, cut]), NEG_FILL)
                raised = jnp.exp(scores - jnp.max(scores, axis=-1, keepdims=True))
                shares = bf(raised / jnp.sum(raised, axis=-1, keepdims=True))
                if save:
                    kept[1][unit * heads + h] = shares
                pieces.append(bf(dot_nn(shares, v[:, cut])))
            context = jnp.concatenate(pieces, axis=1)
            if save:
                kept[2][unit] = context
                kept[1].send(unit * heads, heads)
                kept[2].send(unit, 1)
            if unit == 0:
                waits[1].wait()
            outs.append(dot_nn(context, w_r[side, 3 * local :, :]))
        put_rows(targets, outs)

    outs, stores = parts_shapes(rows, width, count), []
    if save:
        stores = [
            ((2, full, 3 * local), LOW),
            ((2 * heads, full, full), LOW),
            ((2, full, local), LOW),
        ]
    flops = 4 * full * (4 * local * width + 2 * local * full)
    got = kernel_call(
        body,
        outs,
        [counts],
        tables + [theirs] + sources,
        flops,
        "attn_forward",
        [],
        stores,
        weights,
        1 if wide else 2,
    )
    return got[:count], got[count:]


def feed_forward(counts, sources, tables, weights, layer, encoder, save):
    rows, width = rows_of(sources)
    units = weights[0].shape[1]
    full = 2 * rows
    count = len(sources)

    def body(s, *refs):
        at = here()
        tb, source, refs = refs[:2], refs[2 : 2 + count], refs[2 + count :]
        w_refs, refs = refs[: len(weights)], refs[len(weights) :]
        targets, kept, (w_r, sems) = refs[:count], refs[count:-2], refs[-2:]
        waits = fetch_feed(at, layer, w_refs, w_r, sems)
        groups = row_groups(source)
        bias = table_row(at, tb, layer, encoder, ROW_EXP)
        outs = []
        for unit in range(2):
            rows_in = stack_rows(groups[unit])
            if unit == 0:
                waits[0].wait()
            inner = dot_nn(rows_in, w_r[0]) + bias
            phi = 0.5 * (1.0 + lax.erf(inner * (0.5**0.5)))
            active = bf(inner * phi)
            if save:
                density = jnp.exp(-0.5 * inner * inner) * 0.3989422804014327
                kept[0][unit] = active
                kept[1][unit] = bf(phi + inner * density)
                kept[0].send(unit, 1)
                kept[1].send(unit, 1)
            if unit == 0:
                waits[1].wait()
            outs.append(dot_nn(active, w_r[1]))
        put_rows(targets, outs)

    outs, stores = parts_shapes(rows, width, count), []
    if save:
        stores = [((2, full, units), LOW), ((2, full, units), LOW)]
    flops = 8 * full * width * units
    near = tables + sources
    got = kernel_call(body, outs, [counts], near, flops, "feed_forward", [], stores, weights, 2)
    return got[:count], got[count:]


def masked_squares(at, counts, encoder, values, rows):
    return column_sum(jnp.where(row_keep(at, counts, encoder, rows), values * values, 0.0))


def norm_middle(counts, pieces, layer_in, tables, layer, encoder, save):
    rows, width = pieces[0].shape
    count, inputs = len(pieces), len(layer_in)

    def body(s, *refs):
        at = here()
        tb, added, refs = refs[:2], refs[2 : 2 + count], refs[2 + count :]
        x_refs, refs = refs[:inputs], refs[inputs:]
        (square_r, low_r, mixed_r) = refs if save else (None, refs[0], None)
        if inputs == 1:
            rows_in = x_refs[0][...]
        else:
            rows_in = jnp.concatenate([x_refs[0][0], x_refs[1][1]], axis=0)
        attn = scattered(*added) + table_row(at, tb, layer, encoder, ROW_SHIFT)
        mixed = rows_in.astype(F32) + attn
        if save:
            mixed_r[...] = mixed
            mixed_r.send()
        xhat, _ = norm_parts(mixed)
        gain = table_row(at, tb, layer, encoder, ROW_GAIN)
        low_r[...] = bf(xhat * gain + table_row(at, tb, layer, encoder, ROW_SHIFT + 1))
        if save:
            square_r[...] = masked_squares(at, s, encoder, attn, rows)

    outs, stores = [((rows, width), LOW)], []
    if save:
        outs, stores = [((1, width), F32)] + outs, [((rows, width), F32)]
    near = tables + pieces + layer_in
    return kernel_call(body, outs, [counts], near, 20 * rows * width, "norm_middle", [], stores)


def norm_last(counts, pieces, hidden, tables, layer, encoder, save):
    rows, width = hidden.shape
    count = len(pieces)
    pool = layer == 1

    def body(s, *refs):
        at = here()
        tb, added, h_r, refs = refs[:2], refs[2 : 2 + count], refs[2 + count], list(refs[3 + count :])
        out_r = refs.pop(0)
        square_r = refs.pop(0) if save else None
        feed = scattered(*added) + table_row(at, tb, layer, encoder, ROW_SHIFT + 2)
        summed = h_r[...].astype(F32) + feed
        if save:
            refs[0][...] = summed
            refs[0].send()
        xhat, _ = norm_parts(summed)
        gain = table_row(at, tb, layer, encoder, ROW_GAIN + 1)
        out = xhat * gain + table_row(at, tb, layer, encoder, ROW_SHIFT + 3)
        if pool:
            out_r[...] = column_sum(jnp.where(row_keep(at, s, encoder, rows), out, 0.0))
        else:
            out_r[...] = bf(out)
        if save:
            square_r[0:1, :] = masked_squares(at, s, encoder, feed, rows)
            square_r[1:2, :] = masked_squares(at, s, encoder, out, rows)

    outs, stores = [((1, width), F32) if pool else ((rows, width), LOW)], []
    if save:
        outs, stores = outs + [((2, width), F32)], [((rows, width), F32)]
    near = tables + pieces + [hidden]
    return kernel_call(body, outs, [counts], near, 20 * rows * width, "norm_last", [], stores)


def gather(own, wide):
    hops = (hop_one, hop_two, hop_both) if wide else (hop_one,)
    return [own] + [move(own) for move in hops]


def scatter(part, *others):
    hops = (hop_one, hop_two, hop_both)
    return [part] + [move(value) for move, value in zip(hops, others)]


def scattered(part, *others):
    total = part[...]
    for value in others:
        total = total + value[: part.shape[0], :].astype(F32)
    return total


def norm_backward(values, grad, gain_row):
    xhat, rstd = norm_parts(values)
    scaled = grad * gain_row
    d_values = rstd * (
        scaled
        - jnp.mean(scaled, axis=-1, keepdims=True)
        - xhat * jnp.mean(scaled * xhat, axis=-1, keepdims=True)
    )
    return d_values, jnp.sum(grad * xhat, axis=0, keepdims=True)


def column_sum(values):
    return jnp.sum(values, axis=0, keepdims=True)


def norm_gradient(y_r, grad, gain, low_r):
    d_values, d_gain = norm_backward(y_r[...], grad, gain)
    low_r[...] = bf(d_values)
    return d_gain, column_sum(grad), column_sum(d_values)


def last_backward(counts, summed, tables, layer, pooled=None, residual=None, pieces=None):
    rows, width = summed.shape
    near = [pooled] if pooled is not None else [residual] + pieces[1:]
    loads = [summed] if pooled is not None else [summed, pieces[0]]
    inputs = len(near)

    def body(s, held_r, came_r, *rest):
        at = here()
        near_r, (y_r, *part_r), (rows_r, low_r) = rest[:inputs], rest[inputs:-2], rest[-2:]
        if pooled is not None:
            grad = jnp.where(row_keep(at, s, 0, rows), near_r[0][...], 0.0)
        else:
            grad = bf(scattered(part_r[0], *near_r)).astype(F32)
        gain = table_row(at, (held_r, came_r), layer, 0, ROW_GAIN + 1)
        for i, row in enumerate(norm_gradient(y_r, grad, gain, low_r)):
            rows_r[i : i + 1, :] = row

    outs = [((3, width), F32), ((rows, width), LOW)]
    got = kernel_call(
        body, outs, [counts], tables + near, 30 * summed.size, "last_backward", loads
    )
    return got[1], got[0]


def middle_backward(counts, mixed, tables, layer, residual, pieces, last_rows, above):
    rows, width = mixed.shape
    known = [last_rows] + above

    def body(s, held_r, came_r, *rest):
        at = here()
        last_r, above_r, rest = rest[0], rest[1 : len(known)], rest[len(known) :]
        near_r, (y_r, part_r, rows_r, low_r) = rest[:-4], rest[-4:]
        grad = scattered(part_r, *near_r)
        gain = table_row(at, (held_r, came_r), layer, 0, ROW_GAIN)
        d_gain, in_sum, out_sum = norm_gradient(y_r, grad, gain, low_r)
        last = [last_r[i : i + 1, :] for i in range(3)]
        for i, row in enumerate((d_gain, last[0], out_sum, in_sum, last[2], last[1])):
            rows_r[i : i + 1, :] = row
        if above_r:
            rows_r[6:, :] = above_r[0][...]

    outs = [((6 + 6 * len(above), width), F32), ((rows, width), LOW)]
    near = tables + known + [residual] + pieces[1:]
    loads = [mixed, pieces[0]]
    got = kernel_call(body, outs, [counts], near, 30 * mixed.size, "middle_backward", loads)
    return got[1], got[0]


def feed_backward(counts, grads, slope, weights, layer):
    full, units = slope.shape[1:]
    rows, width = grads[0].shape
    count = len(grads)

    def body(s, *refs):
        source, sl_r, refs = refs[:count], refs[count], refs[count + 1 :]
        w_refs, refs = refs[: len(weights)], refs[len(weights) :]
        others, (bias_r, part, dinner_r, w_r, sems) = refs[: count - 1], refs[count - 1 :]
        targets = [part, *others]
        waits = fetch_feed(here(), layer, w_refs, w_r, sems)
        groups = row_groups(source)
        outs = []
        total = jnp.zeros((1, units), F32)
        for unit in range(2):
            if unit == 0:
                waits[1].wait()
            d_inner = dot_nt(stack_rows(groups[unit]), w_r[1]) * sl_r[unit].astype(F32)
            total = total + column_sum(d_inner)
            low = bf(d_inner)
            dinner_r[unit] = low
            dinner_r.send(unit, 1)
            if unit == 0:
                waits[0].wait()
            outs.append(dot_nt(low, w_r[0]))
        bias_r[...] = total
        put_rows(targets, outs)

    part, *outs = parts_shapes(rows, width, count)
    outs, stores = outs + [((1, units), F32)], [part, ((2, full, units), LOW)]
    flops = 8 * full * width * units
    got = kernel_call(
        body, outs, [counts], grads, flops, "feed_backward", [slope], stores, weights, 2
    )
    return [got[count], *got[: count - 1], got[count + 1], got[count - 1]]


def attn_backward(counts, grads, qkv, shares, context, weights, layer, known):
    wide = len(grads) == 4
    full, triple = qkv.shape[1:]
    local = triple // 3
    heads = local // 64
    rows, width = grads[0].shape
    count, extra = len(grads), len(known)

    def body(s, *refs):
        source, known_r, refs = refs[:count], refs[count : count + extra], refs[count + extra :]
        (qkv_r, sh_r, cx_r), refs = refs[:3], refs[3:]
        w_refs, refs = refs[: len(weights)], refs[len(weights) :]
        others, (bias_r, part, dproj_r, w_r, sems) = refs[: count - 1], refs[count - 1 :]
        targets = [part, *[other.at[:rows] for other in others]]
        for other in others[: extra * count]:
            spare = jnp.zeros((EXTRA - known_r[0].shape[0], width), F32)
            other[rows:, :] = bf(jnp.concatenate([known_r[0][...], spare], axis=0))
        waits = fetch_attn(here(), layer, 0, w_refs, w_r, sems)
        groups = row_groups(source)
        bias_r[...] = jnp.zeros((2, width), F32)
        outs = []
        for unit in range(2):
            side = 0 if wide else unit
            if unit == 0:
                waits[1].wait()
            elif not wide:
                waits[2].wait()
            d_context = bf(dot_nt(stack_rows(groups[unit]), w_r[side, triple:, :]))
            q = qkv_r[unit, :, :local]
            k = qkv_r[unit, :, local : 2 * local]
            v = qkv_r[unit, :, 2 * local :]
            weighted = d_context.astype(F32) * cx_r[unit].astype(F32)
            dqs, dks, dvs = [], [], []
            for h in range(heads):
                cut = slice(64 * h, 64 * h + 64)
                share = sh_r[unit * heads + h]
                dc = d_context[:, cut]
                dvs.append(dot_tn(share, dc))
                drop = jnp.sum(weighted[:, cut], axis=-1, keepdims=True)
                d_scores = bf(share.astype(F32) * (dot_nt(dc, v[:, cut]) - drop))
                dqs.append(dot_nn(d_scores, k[:, cut]) * 0.125)
                dks.append(dot_tn(d_scores, q[:, cut]) * 0.125)
            dq = jnp.concatenate(dqs, axis=1)
            dk = jnp.concatenate(dks, axis=1)
            dv = jnp.concatenate(dvs, axis=1)
            bias_r[unit : unit + 1, :local] = column_sum(dq)
            bias_r[unit : unit + 1, local : 2 * local] = column_sum(dv)
            d_project = bf(jnp.concatenate([dq, dk, dv], axis=1))
            dproj_r[unit] = d_project
            dproj_r.send(unit, 1)
            if unit == 0:
                waits[0].wait()
            outs.append(dot_nn(d_project, w_r[side, :triple, :]))
        put_rows(targets, outs)

    part = ((rows, width), F32)
    outs = [((rows + EXTRA * extra, width), LOW)] * (count - 1)
    outs, stores = outs + [((2, width), F32)], [part, ((2, full, triple), LOW)]
    flops = 4 * full * (4 * local * width + 4 * local * full)
    loads = [qkv, shares, context]
    side = 1 if wide else 2
    got = kernel_call(
        body, outs, [counts], grads + known, flops, "attn_backward", loads, stores, weights, side
    )
    return [got[count], *got[: count - 1], got[count + 1], got[count - 1]]


def put_blocks(at, out_ref, parts, extra, blocks, other):
    if extra.shape[0] < EXTRA:
        extra = jnp.concatenate([extra, jnp.zeros((EXTRA - extra.shape[0], extra.shape[1]), F32)], axis=0)
    extra = bf(extra)
    span = parts[0].shape[0] // blocks
    half = span // 2
    wanted = jnp.bitwise_xor(at.core, other)
    for block in range(blocks):
        for i, value in enumerate(parts):
            halves = [bf(value[block * span + j * half : block * span + (j + 1) * half]) for j in range(2)]
            out_ref[block, i * half : (i + 1) * half, :] = jnp.where(wanted == 0, *halves)
        out_ref[block, len(parts) * half :, :] = extra


def weight_grads(counts, grads, inputs, pairs, bias, blocks, name):
    count = len(grads)
    width = grads[0].shape[-1]
    attention = name == "attn_weights"
    columns = sum(p.shape[2] for p in pairs) if attention else pairs[0].shape[2]
    parts_count = 1 if attention else 2

    def body(s, *refs):
        at = here()
        bias_r, g_refs, refs = refs[0], refs[1 : 1 + count], refs[1 + count :]
        x_refs, (o_r, d_r), targets = refs[:count], refs[count : count + 2], refs[count + 2 :]
        g_rows = [stack_rows(g) for g in row_groups(g_refs)]
        back = dot_tn(g_rows[0], o_r[0]) + dot_tn(g_rows[1], o_r[1])
        x_rows = [stack_rows(x) for x in row_groups(x_refs)]
        ahead = dot_tn(x_rows[0], d_r[0]) + dot_tn(x_rows[1], d_r[1])
        row = bias_r[0:1, :] + bias_r[1:2, :] if bias_r.shape[0] == 2 else bias_r[...]
        parts = [jnp.concatenate([ahead, back], axis=1)] if attention else [back, ahead]
        if blocks > 1:
            put_blocks(at, targets[0], parts, row, blocks, 1)
            put_blocks(at, targets[1], parts, row, blocks, 0)
        else:
            for i, part in enumerate(parts):
                targets[0][i] = bf(part)

    if blocks > 1:
        shape = (blocks, parts_count * (width // blocks // 2) + EXTRA, columns)
        outs, stores = [(shape, LOW)], [(shape, LOW)]
    else:
        outs, stores = [((parts_count, width, columns), LOW)], []
    flops = sum(4 * p.shape[1] * width * p.shape[2] for p in pairs)
    loads = grads + inputs + pairs
    got = kernel_call(body, outs, [counts], [bias], flops, name, loads, stores)
    return [got[1], got[0]] if blocks > 1 else got


def add_cores(counts, mine, came, norms=()):
    blocks, rows = mine.shape[:2]
    start = rows - EXTRA

    def body(s, *refs):
        norm_r, (c_r, m_r, out_r) = refs[: len(norms)], refs[len(norms) :]
        for block in range(blocks):
            total = m_r[block].astype(F32) + c_r[block].astype(F32)
            if norms:
                summed = norm_r[0][...]
                for piece in norm_r[1:]:
                    arrived = piece[piece.shape[0] - EXTRA :, :].astype(F32)
                    summed = summed + arrived[: summed.shape[0]]
                spare = jnp.zeros((EXTRA - 1 - summed.shape[0], summed.shape[1]), F32)
                total = jnp.concatenate([total[: start + 1], summed, spare], axis=0)
            out_r[block] = bf(total)
            if block % 2:
                out_r.send(block - 1, 2)

    stores = [(mine.shape, LOW)]
    near = [*norms, came]
    return kernel_call(body, [], [counts], near, mine.size, "add_cores", [mine], stores)[0]


def trade_layers(counts, zero, one, rows_cut):
    rows, width = zero[0].shape

    def body(s, *refs):
        at = here()
        z_refs, refs = refs[: len(zero)], refs[len(zero) :]
        o_refs, refs = refs[: len(one)], refs[len(one) :]
        outs = [refs[-1], *refs[:-1]]
        sums = []
        for group in (z_refs, o_refs):
            total = group[0][...].astype(F32)
            for piece in group[1:]:
                total = total + piece[...].astype(F32)
            sums.append(total)
        own = at.core == 0
        outs[0][...] = jnp.where(own, sums[0], sums[1])
        outs[1][...] = bf(jnp.where(own, sums[1], sums[0]))
        if rows_cut:
            start = rows - EXTRA + 1
            norms = [sums[0][start + 6 * i : start + 6 * (i + 1), :] for i in range(2)]
            outs[2][...] = jnp.where(own, norms[0], norms[1])
            outs[1][start : start + 6, :] = bf(jnp.where(own, norms[1], norms[0]))

    outs, stores = [((rows, width), LOW)], [((rows, width), F32)]
    if rows_cut:
        outs.append(((6, width), F32))
    got = kernel_call(
        body, outs, [counts], [], 4 * rows * width, "trade_layers", zero + one, stores
    )
    return [got[-1], *got[:-1]]


def in_core_order(at, kept, came, start, size):
    mine = kept[start : start + size, :]
    other = came[start : start + size, :].astype(F32)
    own = at.core == 0
    return jnp.concatenate([jnp.where(own, mine, other), jnp.where(own, other, mine)], axis=0)


def place_feed(counts, kept, came):
    rows, width = kept.shape
    part = (rows - EXTRA) // 2

    def body(s, k_r, c_r, con_r, exp_r):
        at = here()
        con_r[...] = in_core_order(at, k_r, c_r, 0, part)
        exp_r[...] = in_core_order(at, k_r, c_r, part, part)

    stores = [((2 * part, width), F32)] * 2
    return kernel_call(
        body, [], [counts], [], 4 * rows * width, "place_feed", [kept, came], stores
    )


def place_attn(counts, kept, came, norms):
    rows, width = kept.shape
    part = rows - EXTRA
    local = width // 4

    def body(s, n_r, k_r, c_r, norm_r, in_r, out_r):
        norm_r[...] = n_r[...] + c_r[part + 1 : part + 7, :].astype(F32)
        both = in_core_order(here(), k_r, c_r, 0, part)
        for i in range(3):
            in_r[i] = both[:, i * local : (i + 1) * local]
        out_r[...] = both[:, 3 * local :].T

    stores = [((3, 2 * part, local), F32), ((local, 2 * part), F32)]
    outs = [((6, width), F32)]
    return kernel_call(
        body, outs, [counts], [norms], 4 * rows * width, "place_attn", [kept, came], stores
    )


def reduce_plain(layers, section, axis):
    mine = jnp.where(section == 0, layers[0], layers[1]).astype(F32)
    other = over_core(jnp.where(section == 0, layers[1], layers[0]))
    low = bf(mine + other.astype(F32))
    return lax.psum_scatter(low, DP, scatter_dimension=axis, tiled=True).astype(F32)


def summed_over(value, axis):
    count = lax.axis_size(axis)
    distance = 1
    while distance < count:
        value = value + swap(value, axis, distance)
        distance *= 2
    return value


def by_distance(entries, axis):
    count = entries.shape[0]
    order = jnp.bitwise_xor(jnp.arange(count), lax.axis_index(axis))
    chosen = (order[:, None] == jnp.arange(count)[None, :]).astype(entries.dtype)
    flat = jnp.dot(chosen, entries.reshape(count, -1), precision=lax.Precision.HIGHEST)
    return flat.astype(entries.dtype).reshape(entries.shape)


def loss_section(pooled, counts, live, queue_unit):
    count = lax.axis_size(DP)
    width = pooled.shape[-1]
    with jax.named_scope("pool"):
        pooled = pooled + hop_one(pooled)
    vectors = pooled / counts[:, None]
    inverse = lax.rsqrt(jnp.sum(vectors * vectors, axis=-1, keepdims=True) + NORM_EPS)
    units = vectors * inverse
    low = bf(units)
    flags = jnp.broadcast_to(bf(live), (1, width))
    packet = jnp.concatenate([low, flags], axis=0)
    with jax.named_scope("keys"):
        if count <= 8:
            lanes = jnp.stack([packet] + [swap(packet, DP, r) for r in range(1, count)])
        else:
            lanes = by_distance(lax.all_gather(packet, DP, axis=0), DP)
    queries = lanes[:, 0]
    with jax.named_scope("keys"):
        every = jnp.stack([lanes[:, 1:], hop_two(lanes[:, 1:])])
        every = jnp.stack([every, over_core(every)]).reshape(4 * count, 2, width)
    keys, alive = every[:, 0], every[:, 1, 0].astype(F32)
    raised = jnp.exp(dot_nt(queries, queue_unit) / TEMPER)
    mass = jnp.sum(raised, axis=1, keepdims=True)
    pull = dot_nn(bf(raised), queue_unit)
    spread = jnp.concatenate([pull, jnp.broadcast_to(mass, (count, 128))], axis=1)
    with jax.named_scope("pull"):
        if count <= 8:
            total = spread[0:1]
            for r in range(1, count):
                total = total + swap(spread[r : r + 1], DP, r)
        else:
            placed = by_distance(spread, DP)
            total = lax.psum_scatter(placed, DP, scatter_dimension=0, tiled=True)
    positive = dot_nt(low[0:1], keys) / TEMPER
    positive = jnp.where(alive[None, :] > 0, positive, NEG_FILL)
    pos_raised = jnp.exp(positive)
    mass = total[0, width] + jnp.sum(pos_raised)
    own_pair = (jnp.arange(keys.shape[0])[None, :] == 0).astype(F32)
    weight = live / jnp.sum(alive)
    loss_part = weight * (jnp.log(mass) - positive[0, 0])
    d_positive = bf(weight * (pos_raised / mass - own_pair) / TEMPER)
    d_unit = dot_nn(d_positive, keys) + (weight / mass / TEMPER) * total[:, :width]
    unit = units[0:1]
    d_vector = inverse[0:1] * (d_unit - unit * jnp.sum(unit * d_unit, axis=-1, keepdims=True))
    return loss_part, d_vector / counts[0]


def unit_row(total, count):
    vector = total / count.astype(F32)
    inverse = lax.rsqrt(jnp.sum(vector * vector, axis=-1, keepdims=True) + NORM_EPS)
    return vector * inverse, inverse


def queue_units(counts, queue):
    def body(s, x_r, out_r):
        values = x_r[...].astype(F32)
        out_r[...] = bf(values * lax.rsqrt(jnp.sum(values * values, axis=-1, keepdims=True) + NORM_EPS))

    stores = [(queue.shape, LOW)]
    return kernel_call(body, [], [counts], [], 4 * queue.size, "queue_units", [queue], stores)[0]


def live_flag(at, live):
    return live[2 * at.core + at.chosen].astype(F32)


def unit_packet(counts, live, sums):
    width = sums[0].shape[1]

    def body(s, lv, q_r, qc_r, k_r, kc_r, out_r):
        at = here()
        query, _ = unit_row(q_r[...] + qc_r[...], count_of(at, s, 0))
        key, _ = unit_row(k_r[...] + kc_r[...], count_of(at, s, 1))
        flag = jnp.zeros((1, width), F32) + live_flag(at, lv)
        out_r[...] = bf(jnp.concatenate([query, key, flag], axis=0))

    return kernel_call(body, [((3, width), LOW)], [counts, live], sums, 8 * width, "unit_packet")[0]


def queue_scores(counts, lanes, queue):
    count = len(lanes)
    width = queue.shape[1]

    def body(s, *refs):
        lane_r, q_r, outs, key_r = refs[:count], refs[count], refs[count + 1 : -1], refs[-1]
        packets = [lane[...] for lane in lane_r]
        queries = jnp.concatenate([p[0:1] for p in packets], axis=0)
        raised = jnp.exp(dot_nt(queries, q_r[...]) / TEMPER)
        mass = jnp.sum(raised, axis=1, keepdims=True)
        pull = dot_nn(bf(raised), q_r[...])
        for i in range(count):
            outs[i][:, :width] = pull[i : i + 1]
            outs[i][:, width:] = jnp.zeros((1, 128), F32) + mass[i : i + 1]
        key_r[...] = jnp.concatenate([p[1:2] for p in packets] + [p[2:3] for p in packets], axis=0)

    outs = [((1, width + 128), F32)] * count + [((2 * count, width), LOW)]
    return kernel_call(
        body, outs, [counts], lanes, 4 * count * queue.size, "queue_scores", [queue]
    )


def loss_end(counts, live, sums, keys, pulls, squares):
    width = sums[0].shape[1]
    rows = keys[0].shape[0] // 2
    n_keys, n_pulls = len(keys), len(pulls)

    def body(s, lv, q_r, qc_r, *refs):
        at = here()
        key_r, refs = refs[:n_keys], refs[n_keys:]
        pull_r, square_r, (grad_r, row_r) = refs[:n_pulls], refs[n_pulls:-2], refs[-2:]
        unit, inverse = unit_row(q_r[...] + qc_r[...], count_of(at, s, 0))
        low = bf(unit)
        total = pull_r[0][...]
        for piece in pull_r[1:]:
            total = total + piece[...]
        every = jnp.concatenate([k[0:rows] for k in key_r], axis=0)
        alive = jnp.concatenate([k[rows:] for k in key_r], axis=0).astype(F32)
        flags = dot_nt(jnp.ones((1, 128), F32), alive[:, :128]) * (1.0 / 128)
        positive = dot_nt(low, every) / TEMPER
        positive = jnp.where(flags > 0.5, positive, NEG_FILL)
        raised = jnp.exp(positive)
        mass = total[:, width : width + 1] + jnp.sum(raised, axis=-1, keepdims=True)
        weight = live_flag(at, lv) / jnp.sum(flags, axis=-1, keepdims=True)
        own = lax.broadcasted_iota(jnp.int32, positive.shape, 1) == 0
        self_logit = jnp.sum(jnp.where(own, positive, 0.0), axis=-1, keepdims=True)
        loss = weight * (jnp.log(mass) - self_logit)
        d_positive = bf(weight * (raised / mass - own.astype(F32)) / TEMPER)
        d_unit = dot_nn(d_positive, every) + (weight / mass / TEMPER) * total[:, :width]
        d_vector = inverse * (d_unit - unit * jnp.sum(unit * d_unit, axis=-1, keepdims=True))
        grad_r[...] = d_vector / count_of(at, s, 0).astype(F32)
        lane = lax.broadcasted_iota(jnp.int32, (1, 128), 1)
        tokens = 0.5 * count_of(at, s, 0).astype(F32)
        row = jnp.where(lane == 0, 0.5 * loss, jnp.where(lane == 1, tokens, 0.0))
        at_lane = 2
        for piece in square_r:
            values = jnp.sum(piece[...], axis=-1, keepdims=True)
            for i in range(piece.shape[0]):
                row = jnp.where(lane == at_lane, values[i : i + 1], row)
                at_lane += 1
        row_r[...] = row

    outs = [((1, width), F32), ((1, 128), F32)]
    arrays = sums + keys + pulls + squares
    return kernel_call(
        body, outs, [counts, live], arrays, 4 * n_keys * rows * width, "loss_end"
    )


def small_table(counts, encoders):
    width = encoders[0][0].shape[1]
    arrays = [a for e in encoders for a in e]

    def body(s, *refs):
        out_r = refs[-1]
        for e in range(2):
            gain_r, shift_r, exp_r, in_r = refs[4 * e : 4 * e + 4]
            out_r[e, ROW_GAIN : ROW_GAIN + 2, :] = gain_r[...].astype(F32)
            out_r[e, ROW_SHIFT : ROW_SHIFT + 4, :] = shift_r[...].astype(F32)
            groups, heads = exp_r.shape[0], in_r.shape[0]
            pieces = [exp_r[i : i + 1, :].astype(F32) for i in range(groups)]
            out_r[e, ROW_EXP : ROW_EXP + 1, :] = jnp.concatenate(pieces, axis=1)
            pieces = [in_r[h, i : i + 1, :].astype(F32) for i in range(2) for h in range(heads)]
            used = sum(p.shape[1] for p in pieces)
            pieces.append(jnp.zeros((1, width - used), F32))
            out_r[e, ROW_IN : ROW_IN + 1, :] = jnp.concatenate(pieces, axis=1)

    return kernel_call(body, [((2, 8, width), F32)], [counts], arrays, 64 * width, "small_table")[0]


def per_device(
    query_embed,
    key_embed,
    crop_counts,
    pair_mask,
    negative_queue,
    online_inproj,
    online_inbias,
    online_outproj,
    online_gains,
    online_shifts,
    online_expand,
    online_expbias,
    online_contract,
    momentum_inproj,
    momentum_inbias,
    momentum_outproj,
    momentum_gains,
    momentum_shifts,
    momentum_expand,
    momentum_expbias,
    momentum_contract,
):
    section = lax.axis_index(SECTION)
    head = lax.axis_index(HEADS)
    data = lax.axis_index(DP)
    dp_count = lax.axis_size(DP)
    rows, pairs_dev, width = query_embed.shape
    pairs = pairs_dev // lax.axis_size(SECTION)
    local = online_outproj.shape[1]
    blocks = dp_count if width % (dp_count * 32) == 0 and dp_count <= 8 else 1
    few = blocks > 1
    first = section == 0
    counts = crop_counts
    chosen = jnp.where(first, head // 2, head % 2)

    def pair_of(table, axis, pair):
        return lax.dynamic_index_in_dim(table, section * pairs + pair, axis, keepdims=False)

    order = Order()
    with jax.named_scope("in"):
        raw = []
        for table in (query_embed, key_embed):
            raw.append(jnp.stack([pair_of(table, 1, chosen), pair_of(table, 1, 1 - chosen)]))
    with jax.named_scope("ag0"):
        rows_first = [gather(r, True) for r in raw]
    order.mark(raw[1])

    held = [
        [
            jnp.transpose(inproj[0], (1, 2, 0)).reshape(3 * local, width),
            outproj[0],
            expand[0],
            contract[0],
        ]
        for inproj, outproj, expand, contract in (
            (online_inproj, online_outproj, online_expand, online_contract),
            (momentum_inproj, momentum_outproj, momentum_expand, momentum_contract),
        )
    ]
    with jax.named_scope("tab"):
        small = [
            [gains[0], shifts[0], expbias[0], jnp.transpose(inbias[0], (1, 0, 2))]
            for gains, shifts, expbias, inbias in (
                (online_gains, online_shifts, online_expbias, online_inbias),
                (momentum_gains, momentum_shifts, momentum_expbias, momentum_inbias),
            )
        ]
        table = small_table(order.tie(counts), small)
        order.mark(table)
        tables = [table, over_core(table)]
        neighbour_bias = jnp.where(first, tables[1], tables[0])[1, ROW_IN : ROW_IN + 1]
    with jax.named_scope("w"):
        came_weights = [[over_core(w) for w in held[e]] for e in range(2)]
        attn_sets = [held[e][:2] + came_weights[e][:2] for e in range(2)]
        feed_sets = [held[e][2:] + came_weights[e][2:] for e in range(2)]
    span = width // dp_count
    at_row = data * span
    cut = 3 * local

    def share_of(cols, outp):
        low_part = lax.dynamic_slice_in_dim(cols, jnp.minimum(at_row, cut - span), span, 0)
        high = lax.dynamic_slice_in_dim(outp, jnp.clip(at_row - cut, 0, local - span), span, 0)
        return jnp.where(at_row < cut, low_part, high)

    def layer_share(e):
        mine = share_of(held[e][0], held[e][1])
        other = share_of(came_weights[e][0], came_weights[e][1])
        return jnp.where(first, other, mine)

    with jax.named_scope("nb"):
        shares = layer_share(1)
    neighbour = types.SimpleNamespace()
    pooled_bias = jnp.zeros((1, width), F32)
    saved = [types.SimpleNamespace(), types.SimpleNamespace()]
    squares = []
    pooled = [None, None]

    def forward(e):
        save = e == 0
        layer_in = None
        for layer in range(2):
            if layer == 0:
                rows_in = rows_first[e]
                residual = [rows_in[0], rows_in[2]]
                attn_w, theirs = attn_sets[e], pooled_bias
            else:
                with jax.named_scope("ag1"):
                    rows_in = gather(layer_in, save)
                residual = [layer_in]
                attn_w, theirs = attn_sets[e], pooled_bias
                if not save:
                    attn_w, theirs = attn_w + [neighbour.attn], neighbour.bias
            yield
            parts, kept = attn_forward(
                order.tie(counts), rows_in, tables, theirs, attn_w, layer, e, save
            )
            order.mark(parts[0])
            with jax.named_scope("rs1"):
                pieces = scatter(*parts)
            if layer == 0 and e == 1:
                with jax.named_scope("nb"):
                    neighbour.bias = hop_two(behind(neighbour_bias, order.last))
                    neighbour.share = hop_two(behind(shares, order.last))
            yield
            *square, low = norm_middle(order.tie(counts), pieces, residual, tables, layer, e, save)
            if save:
                square, low, mixed = square[0], square[1], low
            order.mark(low)
            if layer == 0 and e == 1:
                with jax.named_scope("nb"):
                    share = behind(neighbour.share, order.last)
                    neighbour.attn = lax.all_gather(share, DP, axis=0, tiled=True)
            if save:
                vars(saved[layer]).update(
                    x=rows_in, qkv=kept[0], shares=kept[1], context=kept[2], mixed=mixed
                )
                squares.append(square)
            with jax.named_scope("ag2"):
                rows_in = gather(low, True)
            yield
            parts, kept = feed_forward(
                order.tie(counts), rows_in, tables, feed_sets[e], layer, e, save
            )
            order.mark(parts[0])
            with jax.named_scope("rs2"):
                pieces = scatter(*parts)
            yield
            outs = list(norm_last(order.tie(counts), pieces, low, tables, layer, e, save))
            out = outs.pop(0)
            order.mark(out)
            if save:
                vars(saved[layer]).update(hidden=rows_in, active=kept[0], slope=kept[1], summed=outs[1])
                squares.append(outs[0])
            layer_in = out
        pooled[e] = out

    threads = [forward(0), forward(1)]
    step = 0
    queue_unit = None
    while threads:
        for thread in list(threads):
            if next(thread, 0) == 0:
                threads.remove(thread)
        step += 1
        if step == 5 and few:
            queue_unit = queue_units(order.tie(counts), negative_queue)
            order.mark(queue_unit)

    with jax.named_scope("loss"):
        if few:
            sums = [pooled[0], hop_one(pooled[0]), pooled[1], hop_one(pooled[1])]
            packet = unit_packet(order.tie(counts), pair_mask, sums)
            lanes = [packet] + [swap(packet, DP, r) for r in range(1, dp_count)]
            *spread, keys = queue_scores(counts, lanes, queue_unit)
            pulls = [spread[0]] + [swap(spread[r], DP, r) for r in range(1, dp_count)]
            keys_two = [keys, hop_two(behind(keys, pulls[1]))]
            keys_all = keys_two + [over_core(k) for k in keys_two]
            d_pool, scalar_row = loss_end(counts, pair_mask, sums[:2], keys_all, pulls, squares)
        else:
            queue = negative_queue.astype(F32)
            norm = lax.rsqrt(jnp.sum(queue * queue, axis=-1, keepdims=True) + NORM_EPS)
            live = pair_of(pair_mask, 0, chosen).astype(F32)
            own_counts = pair_of(crop_counts, 0, chosen).astype(F32)
            both = jnp.concatenate(pooled)
            loss_part, d_pool = loss_section(both, own_counts, live, bf(queue * norm))
            branch = jnp.sum(jnp.concatenate(squares), axis=1)
            scalars = jnp.concatenate([jnp.stack([0.5 * loss_part, 0.5 * own_counts[0]]), branch])
            scalar_row = jnp.zeros((1, 128), F32).at[0, : scalars.shape[0]].set(scalars)

    scalar_hops = [(HEADS, 1), (HEADS, 2), (SECTION, 1)]
    distance = 1
    while distance < dp_count:
        scalar_hops.append((DP, distance))
        distance *= 2

    def scalar_steps(mark, count):
        nonlocal scalar_row
        with jax.named_scope("sc"):
            for _ in range(min(count, len(scalar_hops))):
                axis, far = scalar_hops.pop(0)
                tied = behind(scalar_row, mark)
                scalar_row = tied + swap(tied, axis, far)
        order.mark((order.last, scalar_row))

    order = Order()
    order.mark(d_pool)
    got = {}
    waiting, summed = [], {}

    def share_grads(name, mine, other):
        waiting.append((name, mine, other))

    def add_waiting():
        for name, mine, other in waiting:
            came = over_core(order.tie(other))
            both = add_cores(order.tie(counts), mine, came)
            order.mark(both)
            summed[name] = both
        waiting.clear()

    def reduce_summed(mark):
        for name, both in summed.items():
            with jax.named_scope("rg"):
                both = behind(both, (mark, list(got.values())[-1:]))
                got[name] = lax.psum_scatter(both, DP, scatter_dimension=0, tiled=False)
        summed.clear()

    residual, pieces, rows_above = None, None, []
    plain = types.SimpleNamespace(feed=[None, None], attn=[None, None], bias=[None, None])
    attn_w, feed_w = attn_sets[0], feed_sets[0]
    for layer in (1, 0):
        kept = saved[layer]
        source = dict(pooled=d_pool) if layer == 1 else dict(residual=residual, pieces=pieces)
        low, rows_last = last_backward(
            order.tie(counts), kept.summed, tables, layer, **source
        )
        order.mark(low)
        with jax.named_scope("ag3"):
            grads = gather(low, True)
        add_waiting()
        reduce_summed(grads[1:])
        *parts, d_inner, exp_row = feed_backward(
            order.tie(counts), grads, kept.slope, feed_w, layer
        )
        order.mark(exp_row)
        with jax.named_scope("rs3"):
            pieces = scatter(*parts)
        feed_got = weight_grads(
            order.tie(counts),
            grads,
            kept.hidden,
            [kept.active, d_inner],
            exp_row,
            blocks,
            "feed_weights",
        )
        order.mark(feed_got[0])
        if few:
            share_grads(("feed", layer), *feed_got)
            scalar_steps(exp_row, 1)
        low, norm_rows = middle_backward(
            order.tie(counts), kept.mixed, tables, layer, low, pieces, rows_last, rows_above
        )
        residual = low
        order.mark(low)
        rows_above = [norm_rows]
        with jax.named_scope("ag4"):
            grads = gather(low, True)
        add_waiting()
        reduce_summed(grads[1:])
        *parts, d_project, in_rows = attn_backward(
            order.tie(counts),
            grads,
            kept.qkv,
            kept.shares,
            kept.context,
            attn_w,
            layer,
            [norm_rows] if few and layer == 0 else [],
        )
        order.mark(in_rows)
        with jax.named_scope("rs4"):
            pieces = scatter(*parts)
        attn_got = weight_grads(
            order.tie(counts),
            grads,
            kept.x,
            [kept.context, d_project],
            in_rows,
            blocks,
            "attn_weights",
        )
        order.mark(attn_got[0])
        if few:
            scalar_steps(in_rows, 1)
            if layer == 1:
                share_grads(("attn", layer), *attn_got)
        else:
            plain.feed[layer] = feed_got[0]
            plain.attn[layer] = attn_got[0]
            plain.bias[layer] = jnp.concatenate([exp_row, in_rows[0:1] + in_rows[1:2]])

    if not few:
        scalar_steps(in_rows, len(scalar_hops))

    if few:
        with jax.named_scope("lg"):
            both = add_cores(
                order.tie(counts), attn_got[0], over_core(attn_got[1]), [norm_rows] + pieces[1:]
            )
            order.mark(both)
            scalar_steps(both, len(scalar_hops))
            got["attn", 0] = lax.psum_scatter(both, DP, scatter_dimension=0, tiled=False)
        first_block = both
        d_in = bf(behind(residual, first_block).astype(F32) + scattered(*pieces))
        with jax.named_scope("dx"):
            came = hop_two(d_in[rows:])
            in_order = chosen == 0
            both = jnp.stack([jnp.where(in_order, d_in[:rows], came), jnp.where(in_order, came, d_in[:rows])])
            half_width = width // 2
            mine = lax.dynamic_slice_in_dim(both, section * half_width, half_width, 2)
            other = lax.dynamic_slice_in_dim(both, (1 - section) * half_width, half_width, 2)
            other = over_core(other)
            ordered = jnp.where(first, jnp.concatenate([mine, other]), jnp.concatenate([other, mine]))
            input_grad = jnp.transpose(ordered, (1, 0, 2))
        with jax.named_scope("fg"):
            kept_feed, sent_feed = trade_layers(
                order.tie(counts), [got["feed", 0]], [got["feed", 1]], False
            )
            contract, expand = place_feed(counts, kept_feed, over_core(sent_feed))
            order.mark(contract)
        with jax.named_scope("tg"):
            kept_attn, sent_attn, norms = trade_layers(
                order.tie(counts), [got["attn", 0]], [got["attn", 1]], True
            )
            norms, inproj, outproj = place_attn(counts, kept_attn, over_core(sent_attn), norms)
        exp_row, in_row = kept_feed[kept_feed.shape[0] - EXTRA], kept_attn[kept_attn.shape[0] - EXTRA]
    else:
        first_block = in_rows
        d_in = bf(behind(residual, first_block).astype(F32) + scattered(*pieces))
        with jax.named_scope("dx"):
            came = hop_two(d_in[rows:])
            in_order = chosen == 0
            both = jnp.stack([jnp.where(in_order, d_in[:rows], came), jnp.where(in_order, came, d_in[:rows])])
            half_width = width // 2
            mine = lax.dynamic_slice_in_dim(both, section * half_width, half_width, 2)
            other = lax.dynamic_slice_in_dim(both, (1 - section) * half_width, half_width, 2)
            other = over_core(other)
            ordered = jnp.where(first, jnp.concatenate([mine, other]), jnp.concatenate([other, mine]))
            input_grad = jnp.transpose(ordered, (1, 0, 2))
        contract, expand = reduce_plain(plain.feed, section, 1)
        attn_sum = reduce_plain(plain.attn, section, 1)[0]
        inproj = jnp.transpose(attn_sum[:, :cut].reshape(-1, 3, local), (1, 0, 2))
        outproj = jnp.transpose(attn_sum[:, cut:])
        biases = lax.psum(jnp.stack(plain.bias), (SECTION, DP))
        exp_row, in_row = jnp.where(first, biases[0], biases[1])
        norms = lax.psum(norm_rows, (HEADS, SECTION, DP))
        norms = jnp.where(first, norms[:6], norms[6:])
    loss_total = scalar_row[0, 0]
    rms_values = jnp.sqrt(scalar_row[0, 2:8].reshape(2, 3) / (scalar_row[0, 1] * width))
    piece = width // (dp_count * lax.axis_size(HEADS))
    norms = lax.dynamic_slice_in_dim(norms, (data * lax.axis_size(HEADS) + head) * piece, piece, 1)
    exp_shape, in_shape = online_expbias.shape, online_inbias.shape
    grad_expbias = lax.dynamic_slice_in_dim(
        exp_row.reshape(exp_shape), data * (exp_shape[2] // dp_count), exp_shape[2] // dp_count, 2
    )
    grad_inbias = lax.dynamic_slice_in_dim(
        in_row[: 2 * local].reshape(in_shape),
        data * (in_shape[3] // dp_count),
        in_shape[3] // dp_count,
        3,
    )
    return (
        loss_total,
        input_grad,
        jnp.transpose(inproj, (1, 0, 2))[None],
        grad_inbias,
        outproj[None],
        norms[None, 0:2],
        norms[None, 2:6],
        expand[None],
        grad_expbias,
        jnp.transpose(contract)[None],
        rms_values,
    )


def solution(mesh):
    placed = (
        P(HEADS, DP, None),
        P(HEADS, DP, None),
        P(DP, None),
        P(DP),
        P(DP, None),
        P(SECTION, None, None, HEADS),
        P(SECTION, None, HEADS, None),
        P(SECTION, HEADS, None),
        P(SECTION, None, None),
        P(SECTION, None, None),
        P(SECTION, None, HEADS),
        P(SECTION, HEADS, None),
        P(SECTION, HEADS, None),
        P(SECTION, None, None, HEADS),
        P(SECTION, None, HEADS, None),
        P(SECTION, HEADS, None),
        P(SECTION, None, None),
        P(SECTION, None, None),
        P(SECTION, None, HEADS),
        P(SECTION, HEADS, None),
        P(SECTION, HEADS, None),
    )
    return jax.shard_map(
        per_device,
        mesh=mesh,
        in_specs=placed,
        out_specs=(
            P(),
            P(HEADS, DP, SECTION),
            P(SECTION, DP, None, HEADS),
            P(SECTION, None, HEADS, DP),
            P(SECTION, HEADS, DP),
            P(SECTION, None, (DP, HEADS)),
            P(SECTION, None, (DP, HEADS)),
            P(SECTION, DP, HEADS),
            P(SECTION, HEADS, DP),
            P(SECTION, HEADS, DP),
            P(),
        ),
        check_vma=False,
    )
```

time: 1570 us -> 388 us (0.25)
  waiting for transfers between devices: 1080 us -> 104 us
  blocking collectives: 138 us -> 0 us
  matrix products: 137 us -> 0 us
  Pallas kernels: 0 us -> 132 us
  starting transfers between devices: 7.6 us -> 112 us
  local copies, waits for them, and re-layouts: 97.9 us -> 13.6 us
  other arithmetic: 74.7 us -> 2.38 us
    unnamed x56 -> x5, waiting for transfers between devices: 455 us -> 0.08 us
    reduce_scatter x15 -> x4, waiting for transfers between devices: 383 us -> 6.72 us  [the longest x1 6.72 us: per_device(): lax.psum_scatter(both, DP, scatter_dimension=0, tiled=False)]
    all_gather x7 -> x1, waiting for transfers between devices: 235 us -> 0.01 us  [forward(): neighbour.attn = lax.all_gather(share, DP, axis=0, tiled=True)]
    dot_general x61 -> x0, matrix products: 137 us -> none  [the longest x3 33.4 us: layer_forward(): jnp.einsum('lebd,edf->lebf', full_hidden, expand, preferred_element_type=...]
    pallas_call x0 -> x41, Pallas kernels: none -> 132 us  [kernel_call(): pl.pallas_call(whole, out_shape=[jax.ShapeDtypeStruct(s, d) for s, d in o...]
    ppermute x5 -> x103, starting transfers between devices: 5.01 us -> 111 us  [the longest x74 78.4 us: hop(): return lax.ppermute(value, (SECTION, HEADS), route)]
    ppermute x5 -> x103, waiting for transfers between devices: 6.66 us -> 97.4 us  [the longest x74 81.6 us: hop(): return lax.ppermute(value, (SECTION, HEADS), route)]
    unnamed x450 -> x126, local copies, waits for them, and re-layouts: 89.8 us -> 3.77 us
  transfers between devices with their start and end apart: 44 -> 108, of which waited for: 37 -> 40; matrix products, arithmetic and copies ran while one was open for 10% -> 3% of each run, Pallas kernels for 0% -> 30%
where the time goes in v2:
time: 388 us; the launch traced here: 381 us
  Pallas kernels  132 us (34%)
  starting transfers between devices  112 us (29%)
  waiting for transfers between devices  104 us (27%)
  between operations  16.1 us (4%)
  local copies, waits for them, and re-layouts  13.6 us (4%)
    pallas_call x41, Pallas kernels, kernel_call(): pl.pallas_call(whole, out_shape=[jax.ShapeDtypeStruct(s, d) for s, d in o...  132 us
    ppermute x74, waiting for transfers between devices, hop(): return lax.ppermute(value, (SECTION, HEADS), route)  81.6 us
    ppermute x74, starting transfers between devices, hop(): return lax.ppermute(value, (SECTION, HEADS), route)  78.4 us
    ppermute x29, starting transfers between devices, swap(): return lax.ppermute(value, axis, [(i, i ^ distance) for i in range(count)])  32.8 us
    ppermute x29, waiting for transfers between devices, swap(): return lax.ppermute(value, axis, [(i, i ^ distance) for i in range(count)])  15.8 us
  transfers between devices with their start and end apart: 108, of which 40 were waited for; matrix products, arithmetic and copies ran while one was open for 3% of the time, Pallas kernels for 30%

profile of v2, /device:TPU:1, one launch (start us, length us, event | category | flops | bytes accessed | tf_op | source)
XLA Modules:
  0.0 380.8 jit_solution(2586276859480358009)
XLA Ops:
  7.8 2.2 constant_dynamic-slice_fusion.4
  10.2 2.4 collective-permute-start.1
  16.2 2.2 collective-permute-start.3
  21.5 3.9 %collective-permute-done.3.refs_7_.refs_9_ = bf16[2,64,768]{2,1,0:T(8,128)(2,1)S(1)} collective-permute-done((bf16[2,64,768]{2,1,0:T(8,128)(2,1)S(1)}, bf16[2,64,768]{2,1,0:T(8,128)(2,1)S(1)}, u32[]{:S(2)}, u32[]{:S(2)}) %collective-permute-start.3) | collective-permute-done | bytes 196640 | tf_op jit(solution)/shard_map/ag0/ppermute | solution.py:204
  25.6 3.5 collective-permute-start.10
  29.2 5.6 %attn_forward.4 = (f32[128,768]{1,0:T(8,128)S(1)}, bf16[128,768]{1,0:T(8,128)(2,1)}, bf16[128,768]{1,0:T(8,128)(2,1)S(1)}, bf16[128,768]{1,0:T(8,128)(2,1)S(1)},...) custom-call(s32[4,2]{1,0:T(4,128)S(1)} %copy.81.refs_0_, ...), custom_call_target="tpu_custom_call" | custom-call | flops 704643072 | bytes 4623360 | tf_op jit(solution)/shard_map/attn_forward/pallas_call | solution.py:128
  40.1 4.4 %attn_forward.5 = (f32[128,768]{1,0:T(8,128)S(1)}, bf16[128,768]{1,0:T(8,128)(2,1)S(1)}, bf16[128,768]{1,0:T(8,128)(2,1)S(1)}, bf16[128,768]{1,0:T(8,128)(2,1)S(1)}) custom-call(s32[4,2]{1,0:T(4,128)S(1)} %copy.82.refs_0_, f32[2,8,768]{2,1,0:T(8,128)S(1)} %small_table.1.refs_1_, f32[2,8,768]{2,1,0:T(8,128)S(1)} %collective-permute-done.refs_2_, ...), custom_call_target="tpu_custom_call" | custom-call | flops 704643072 | bytes 3050496 | tf_op jit(solution)/shard_map/attn_forward/pallas_call | solution.py:128
  47.8 2.0 select_select_fusion
  51.9 2.3 collective-permute-start.25
  54.3 2.7 collective-permute-done.16.refs_6_
  61.8 2.1 collective-permute-start.19
  63.8 3.0 collective-permute-done.17.refs_4_.refs_7_
  68.4 5.1 %collective-permute-done.19.refs_6_.refs_9_ = bf16[128,768]{1,0:T(8,128)(2,1)S(1)} collective-permute-done((bf16[128,768]{1,0:T(8,128)(2,1)S(1)}, bf16[128,768]{1,0:T(8,128)(2,1)S(1)}, u32[]{:S(2)}, u32[]{:S(2)}) %collective-permute-start.19) | collective-permute-done | bytes 196640 | tf_op jit(solution)/shard_map/ag2/ppermute | solution.py:204
  73.7 5.2 %feed_forward.4 = (f32[128,768]{1,0:T(8,128)S(1)}, bf16[128,768]{1,0:T(8,128)(2,1)}, bf16[128,768]{1,0:T(8,128)(2,1)}, bf16[128,768]{1,0:T(8,128)(2,1)S(1)}, bf1...) custom-call(s32[4,2]{1,0:T(4,128)S(1)} %copy.85.refs_0_, f32[2,8,768]{2,1,0:T(8,128)S(1)} %small_table.1.refs_1_, ...), custom_call_target="tpu_custom_call" | custom-call | flops 1207959552 | bytes 5799936 | tf_op jit(solution)/shard_map/feed_forward/pallas_call | solution.py:128
  81.7 4.5 %feed_forward.5 = (f32[128,768]{1,0:T(8,128)S(1)}, bf16[128,768]{1,0:T(8,128)(2,1)S(1)}, bf16[128,768]{1,0:T(8,128)(2,1)}, bf16[128,768]{1,0:T(8,128)(2,1)}) custom-call(s32[4,2]{1,0:T(4,128)S(1)} %copy.86.refs_0_, f32[2,8,768]{2,1,0:T(8,128)S(1)} %small_table.1.refs_1_, f32[2,8,768]{2,1,0:T(8,128)S(1)} %collective-permute-done.refs_2_, ...), custom_call_target="tpu_custom_call" | custom-call | flops 1207959552 | bytes 4227072 | tf_op jit(solution)/shard_map/feed_forward/pallas_call | solution.py:128
  95.6 2.3 collective-permute-start.35
  101.8 3.6 queue_units.1.refs_5_
  107.5 4.9 %attn_forward.6 = (f32[128,768]{1,0:T(8,128)S(1)}, bf16[128,768]{1,0:T(8,128)(2,1)S(1)}, bf16[128,768]{1,0:T(8,128)(2,1)S(1)}, bf16[128,768]{1,0:T(8,128)(2,1)S(...) custom-call(s32[4,2]{1,0:T(4,128)S(1)} %copy.90.refs_0_, ...), custom_call_target="tpu_custom_call" | custom-call | flops 704643072 | bytes 4623360 | tf_op jit(solution)/shard_map/attn_forward/pallas_call | solution.py:128
  117.4 7.7 %collective-permute-done.36.refs_3_ = f32[1,768]{1,0:T(1,128)S(1)} collective-permute-done((f32[1,768]{1,0:T(1,128)S(1)}, f32[1,768]{1,0:T(1,128)S(1)}, u32[]{:S(2)}, u32[]{:S(2)}) %collective-permute-start.36) | collective-permute-done | bytes 3104 | tf_op jit(solution)/shard_map/nb/ppermute | solution.py:204
  125.1 4.5 %attn_forward.7 = (f32[128,768]{1,0:T(8,128)S(1)}, bf16[128,768]{1,0:T(8,128)(2,1)S(1)}) custom-call(s32[4,2]{1,0:T(4,128)S(1)} %copy.91.refs_0_, f32[2,8,768]{2,1,0:T(8,128)S(1)} %small_table.1.refs_1_, f32[2,8,768]{2,1,0:T(8,128)S(1)} %collective-permute-done.refs_2_, f32[1,768]{1,0:T(1,128)S(1)} %collective-permute-done.36.refs_3_, ...), custom_call_target="tpu_custom_call" | custom-call | flops 704643072 | bytes 3443712 | tf_op jit(solution)/shard_map/attn_forward/pallas_call | solution.py:128
  136.8 4.7 %collective-permute-start.47 = (bf16[128,768]{1,0:T(8,128)(2,1)S(1)}, bf16[128,768]{1,0:T(8,128)(2,1)S(1)}, u32[]{:S(2)}, u32[]{:S(2)}) collective-permute-start(bf16[128,768]{1,0:T(8,128)(2,1)S(1)} %norm_middle.7.refs_3_.refs_7_), channel_id=1, source_target_pairs={{0,2},{1,3},{2,0},{3,1},{16,17},{17,16},{18,19},{19,18},{4,6},{5,7... | collective-permute-start | bytes 589832 | tf_op jit(solution)/shard_map/ag2/ppermute | solution.py:204
  141.6 2.7 collective-permute-done.43.refs_4_.refs_7_
  144.3 3.4 collective-permute-start.48
  147.8 5.4 %feed_forward.6 = (f32[128,768]{1,0:T(8,128)S(1)}, bf16[128,768]{1,0:T(8,128)(2,1)}, bf16[128,768]{1,0:T(8,128)(2,1)S(1)}, bf16[128,768]{1,0:T(8,128)(2,1)S(1)},...) custom-call(s32[4,2]{1,0:T(4,128)S(1)} %copy.94.refs_0_, f32[2,8,768]{2,1,0:T(8,128)S(1)} %small_table.1.refs_1_, ...), custom_call_target="tpu_custom_call" | custom-call | flops 1207959552 | bytes 5799936 | tf_op jit(solution)/shard_map/feed_forward/pallas_call | solution.py:128
  153.2 2.1 collective-permute-start.49
  156.6 3.7 feed_forward.7
  161.9 3.3 collective-permute-done.49.refs_4_
  168.5 2.2 collective-permute-done.55.refs_6_
  174.8 3.7 collective-permute-start.58
  179.6 3.3 collective-permute-done.59.refs_4_
  182.8 2.8 queue_scores.1
  185.7 2.4 collective-permute-done.60.refs_9_
  188.3 2.2 collective-permute-start.62
  190.7 2.5 collective-permute-start.63
  207.9 5.5 %collective-permute-done.68.refs_4_.refs_5_ = bf16[128,768]{1,0:T(8,128)(2,1)S(1)} collective-permute-done((bf16[128,768]{1,0:T(8,128)(2,1)S(1)}, bf16[128,768]{1,0:T(8,128)(2,1)S(1)}, u32[]{:S(2)}, u32[]{:S(2)}) %collective-permute-start.68) | collective-permute-done | bytes 196640 | tf_op jit(solution)/shard_map/ag3/ppermute | solution.py:204
  213.4 4.9 %feed_backward.2 = (bf16[128,768]{1,0:T(8,128)(2,1)S(1)}, bf16[128,768]{1,0:T(8,128)(2,1)S(1)}, bf16[128,768]{1,0:T(8,128)(2,1)S(1)}, f32[1,768]{1,0:T(1,128)S(1...) custom-call(s32[4,2]{1,0:T(4,128)S(1)} %copy.102.refs_0_, ...), custom_call_target="tpu_custom_call" | custom-call | flops 1207959552 | bytes 5704704 | tf_op jit(solution)/shard_map/feed_backward/pallas_call | solution.py:128
  222.8 5.7 %feed_weights.2 = (bf16[4,208,768]{2,1,0:T(8,128)(2,1)S(1)}, bf16[4,208,768]{2,1,0:T(8,128)(2,1)}) custom-call(s32[4,2]{1,0:T(4,128)S(1)} %copy.103.refs_0_, f32[1,768]{1,0:T(1,128)S(1)} %get-tuple-element.246.refs_1_, bf16[128,768]{1,0:T(8,128)(2,1)} %copy-done.9, bf16[128,768]{1,0:T(8,128)(2,1)} %copy-done.33, bf16[128,768]{1,0:T(8,128)(2,1)} %copy-done.34, ...), custom_call_target="tpu_custom_call" | custom-call | flops 1207959552 | bytes 5704704 | tf_op jit(solution)/shard_map/feed_weights/pallas_call | solution.py:128
  230.2 2.2 middle_backward.2
  236.3 3.1 add_cores.4
  240.7 4.3 %collective-permute-done.76.refs_4_.refs_5_ = bf16[128,768]{1,0:T(8,128)(2,1)S(1)} collective-permute-done((bf16[128,768]{1,0:T(8,128)(2,1)S(1)}, bf16[128,768]{1,0:T(8,128)(2,1)S(1)}, u32[]{:S(2)}, u32[]{:S(2)}) %collective-permute-start.76) | collective-permute-done | bytes 196640 | tf_op jit(solution)/shard_map/ag4/ppermute | solution.py:204
  245.4 6.5 %attn_backward.2 = (bf16[128,768]{1,0:T(8,128)(2,1)S(1)}, bf16[128,768]{1,0:T(8,128)(2,1)S(1)}, bf16[128,768]{1,0:T(8,128)(2,1)S(1)}, f32[2,768]{1,0:T(2,128)S(1...) custom-call(s32[4,2]{1,0:T(4,128)S(1)} %copy.106.refs_0_, ...), custom_call_target="tpu_custom_call" | custom-call | flops 805306368 | bytes 5117952 | tf_op jit(solution)/shard_map/attn_backward/pallas_call | solution.py:128
  255.9 4.8 %attn_weights.2 = (bf16[4,112,768]{2,1,0:T(8,128)(2,1)S(1)}, bf16[4,112,768]{2,1,0:T(8,128)(2,1)}) custom-call(s32[4,2]{1,0:T(4,128)S(1)} %copy.107.refs_0_, f32[2,768]{1,0:T(2,128)S(1)} %get-tuple-element.267.refs_1_, bf16[128,768]{1,0:T(8,128)(2,1)} %copy-done.1, bf16[128,768]{1,0:T(8,128)(2,1)} %copy-done.11, bf16[128,768]{1,0:T(8,128)(2,1)} %copy-done.12, ...), custom_call_target="tpu_custom_call" | custom-call | flops 603979776 | bytes 3741696 | tf_op jit(solution)/shard_map/attn_weights/pallas_call | solution.py:128
  260.8 3.1 collective-permute-done.80.refs_6_
  263.9 2.3 last_backward.3
  269.9 2.7 add_cores.5
  274.5 4.7 %collective-permute-done.84.refs_4_.refs_5_ = bf16[128,768]{1,0:T(8,128)(2,1)S(1)} collective-permute-done((bf16[128,768]{1,0:T(8,128)(2,1)S(1)}, bf16[128,768]{1,0:T(8,128)(2,1)S(1)}, u32[]{:S(2)}, u32[]{:S(2)}) %collective-permute-start.84) | collective-permute-done | bytes 196640 | tf_op jit(solution)/shard_map/ag3/ppermute | solution.py:204
  279.2 4.9 %feed_backward.3 = (bf16[128,768]{1,0:T(8,128)(2,1)S(1)}, bf16[128,768]{1,0:T(8,128)(2,1)S(1)}, bf16[128,768]{1,0:T(8,128)(2,1)S(1)}, f32[1,768]{1,0:T(1,128)S(1...) custom-call(s32[4,2]{1,0:T(4,128)S(1)} %copy.110.refs_0_, ...), custom_call_target="tpu_custom_call" | custom-call | flops 1207959552 | bytes 5704704 | tf_op jit(solution)/shard_map/feed_backward/pallas_call | solution.py:128
  288.3 5.7 %feed_weights.3 = (bf16[4,208,768]{2,1,0:T(8,128)(2,1)S(1)}, bf16[4,208,768]{2,1,0:T(8,128)(2,1)}) custom-call(s32[4,2]{1,0:T(4,128)S(1)} %copy.111.refs_0_, f32[1,768]{1,0:T(1,128)S(1)} %get-tuple-element.284.refs_1_, bf16[128,768]{1,0:T(8,128)(2,1)} %copy-done.17, bf16[128,768]{1,0:T(8,128)(2,1)} %copy-done.30, bf16[128,768]{1,0:T(8,128)(2,1)} %copy-done.31, ...), custom_call_target="tpu_custom_call" | custom-call | flops 1207959552 | bytes 5704704 | tf_op jit(solution)/shard_map/feed_weights/pallas_call | solution.py:128
  294.2 2.3 collective-permute-done.88.refs_8_
  296.5 2.2 middle_backward.3
  302.0 3.1 add_cores.6
  306.9 4.1 %collective-permute-done.92.refs_4_.refs_5_ = bf16[128,768]{1,0:T(8,128)(2,1)S(1)} collective-permute-done((bf16[128,768]{1,0:T(8,128)(2,1)S(1)}, bf16[128,768]{1,0:T(8,128)(2,1)S(1)}, u32[]{:S(2)}, u32[]{:S(2)}) %collective-permute-start.92) | collective-permute-done | bytes 196640 | tf_op jit(solution)/shard_map/ag4/ppermute | solution.py:204
  311.4 7.2 %attn_backward.3 = (bf16[144,768]{1,0:T(8,128)(2,1)}, bf16[144,768]{1,0:T(8,128)(2,1)S(1)}, bf16[144,768]{1,0:T(8,128)(2,1)S(1)}, f32[2,768]{1,0:T(2,128)S(1)}, ...) custom-call(s32[4,2]{1,0:T(4,128)S(1)} %copy.114.refs_0_, bf16[128,768]{1,0:T(8,128)(2,1)S(1)} %get-tuple-element.318.refs_1_.refs_2_, ...), custom_call_target="tpu_custom_call" | custom-call | flops 805306368 | bytes 5228544 | tf_op jit(solution)/shard_map/attn_backward/pallas_call | solution.py:128
  318.8 4.7 %attn_weights.3 = (bf16[4,112,768]{2,1,0:T(8,128)(2,1)S(1)}, bf16[4,112,768]{2,1,0:T(8,128)(2,1)}) custom-call(s32[4,2]{1,0:T(4,128)S(1)} %copy.115.refs_0_, f32[2,768]{1,0:T(2,128)S(1)} %get-tuple-element.307.refs_1_, bf16[128,768]{1,0:T(8,128)(2,1)} %copy-done.3, bf16[128,768]{1,0:T(8,128)(2,1)} %copy-done.14, bf16[128,768]{1,0:T(8,128)(2,1)} %copy-done.15, ...), custom_call_target="tpu_custom_call" | custom-call | flops 603979776 | bytes 3741696 | tf_op jit(solution)/shard_map/attn_weights/pallas_call | solution.py:128
  326.6 3.4 collective-permute-done.93
  330.1 2.5 collective-permute-done.95.refs_3_
  332.6 4.5 %collective-permute-done.96.refs_4_ = bf16[144,768]{1,0:T(8,128)(2,1)S(1)} collective-permute-done((bf16[144,768]{1,0:T(8,128)(2,1)S(1)}, bf16[144,768]{1,0:T(8,128)(2,1)S(1)}, u32[]{:S(2)}, u32[]{:S(2)}) %collective-permute-start.96) | collective-permute-done | bytes 221216 | tf_op jit(solution)/shard_map/rs4/ppermute | solution.py:204
  337.1 2.7 add_cores.7
  347.1 2.6 trade_layers.2
  352.8 2.9 place_feed.1
  355.8 6.7 %reduce-scatter.11.cloned.1.call-done = bf16[1,112,768]{2,1,0:T(8,128)(2,1)} async-done(((bf16[4,112,768]{2,1,0:T(8,128)(2,1)}), bf16[1,112,768]{2,1,0:T(8,128)(2,1)}) %reduce-scatter.11.cloned.1.call-update) | async-done | bytes 172048 | tf_op jit(solution)/shard_map/lg/reduce_scatter | solution.py:1334
  362.5 2.4 trade_layers.3
  364.9 3.0 collective-permute-start.102
  370.0 2.6 place_attn.1
  (389 shorter events, 128.9 us)
Async XLA Ops:
  7.2 117.9 %all-gather.2.cloned.1.call-start = ((), (), s32[]{:S(2)}) async-start(), calls=%async_computation.4 | async-start | bytes 1474560 | tf_op jit(solution)/shard_map/nb/all_gather | solution.py:1153
  7.2 18.4 %collective-permute-start.4 = (bf16[576,768]{1,0:T(8,128)(2,1)}, bf16[576,768]{1,0:T(8,128)(2,1)S(1)}, u32[]{:S(2)}, u32[]{:S(2)}) collective-permute-start(bf16[576,768]{1,0:T(8,128)(2,1)} %bitcast.85), channel_id=1, source_target_pairs={{0,16},{16,0},{1,17},{17,1},{2,18},{18,2},{3,19},{19,3},{4,20},{20... | collective-permute-start | bytes 2654216 | tf_op jit(solution)/shard_map/w/ppermute | solution.py:197
  7.3 32.1 %collective-permute-start.9 = (bf16[576,768]{1,0:T(8,128)(2,1)}, bf16[576,768]{1,0:T(8,128)(2,1)}, u32[]{:S(2)}, u32[]{:S(2)}) collective-permute-start(bf16[576,768]{1,0:T(8,128)(2,1)} %bitcast.90), channel_id=1, source_target_pairs={{0,16},{16,0},{1,17},{17,1},{2,18},{18,2},{3,19},{19,3},{4,20},{20... | collective-permute-start | bytes 2654216 | tf_op jit(solution)/shard_map/w/ppermute | solution.py:197
  12.6 12.9 %collective-permute-start.5 = (bf16[192,768]{1,0:T(8,128)(2,1)S(1)}, bf16[192,768]{1,0:T(8,128)(2,1)S(1)}, u32[]{:S(2)}, u32[]{:S(2)}) collective-permute-start(bf16[192,768]{1,0:T(8,128)(2,1)S(1)} %bitcast.98), channel_id=1, source_target_pairs={{0,16},{16,0},{1,17},{17,1},{2,18},{18,2},{3,19},{19,3},{4,20},{20... | collective-permute-start | bytes 884744 | tf_op jit(solution)/shard_map/w/ppermute | solution.py:197
  16.2 9.3 %collective-permute-start.3 = (bf16[2,64,768]{2,1,0:T(8,128)(2,1)S(1)}, bf16[2,64,768]{2,1,0:T(8,128)(2,1)S(1)}, u32[]{:S(2)}, u32[]{:S(2)}) collective-permute-start(bf16[2,64,768]{2,1,0:T(8,128)(2,1)S(1)} %pad_maximum_fusion.1.refs_4_.refs_7_.refs_6_), channel_id=1, source_target_pairs={{0,3},{1,2},{2,1},{3,0},{16,19},{17,18},{18,17},{19,16},{4,7},{5,6... | collective-permute-start | bytes 589832 | tf_op jit(solution)/shard_map/ag0/ppermute | solution.py:204
  20.3 14.6 %collective-permute-start.6 = (bf16[2,64,768]{2,1,0:T(8,128)(2,1)S(1)}, bf16[2,64,768]{2,1,0:T(8,128)(2,1)S(1)}, u32[]{:S(2)}, u32[]{:S(2)}) collective-permute-start(bf16[2,64,768]{2,1,0:T(8,128)(2,1)S(1)} %pad_maximum_fusion.refs_4_.refs_7_), channel_id=1, source_target_pairs={{0,1},{1,0},{2,3},{3,2},{16,18},{17,19},{18,16},{19,17},{4,5},{5,4... | collective-permute-start | bytes 589832 | tf_op jit(solution)/shard_map/ag0/ppermute | solution.py:204
  25.4 11.1 %collective-permute-start.7 = (bf16[2,64,768]{2,1,0:T(8,128)(2,1)S(1)}, bf16[2,64,768]{2,1,0:T(8,128)(2,1)S(1)}, u32[]{:S(2)}, u32[]{:S(2)}) collective-permute-start(bf16[2,64,768]{2,1,0:T(8,128)(2,1)S(1)} %pad_maximum_fusion.refs_4_.refs_7_), channel_id=1, source_target_pairs={{0,2},{1,3},{2,0},{3,1},{16,17},{17,16},{18,19},{19,18},{4,6},{5,7... | collective-permute-start | bytes 589832 | tf_op jit(solution)/shard_map/ag0/ppermute | solution.py:204
  25.5 11.1 %collective-permute-start.8 = (bf16[2,64,768]{2,1,0:T(8,128)(2,1)S(1)}, bf16[2,64,768]{2,1,0:T(8,128)(2,1)S(1)}, u32[]{:S(2)}, u32[]{:S(2)}) collective-permute-start(bf16[2,64,768]{2,1,0:T(8,128)(2,1)S(1)} %pad_maximum_fusion.refs_4_.refs_7_), channel_id=1, source_target_pairs={{0,3},{1,2},{2,1},{3,0},{16,19},{17,18},{18,17},{19,16},{4,7},{5,6... | collective-permute-start | bytes 589832 | tf_op jit(solution)/shard_map/ag0/ppermute | solution.py:204
  25.6 12.4 %collective-permute-start.10 = (bf16[192,768]{1,0:T(8,128)(2,1)}, bf16[192,768]{1,0:T(8,128)(2,1)S(1)}, u32[]{:S(2)}, u32[]{:S(2)}) collective-permute-start(bf16[192,768]{1,0:T(8,128)(2,1)} %bitcast.99), channel_id=1, source_target_pairs={{0,16},{16,0},{1,17},{17,1},{2,18},{18,2},{3,19},{19,3},{4,20},{20... | collective-permute-start | bytes 884744 | tf_op jit(solution)/shard_map/w/ppermute | solution.py:197
  34.9 9.7 %collective-permute-start.11 = (bf16[128,768]{1,0:T(8,128)(2,1)}, bf16[128,768]{1,0:T(8,128)(2,1)S(1)}, u32[]{:S(2)}, u32[]{:S(2)}) collective-permute-start(bf16[128,768]{1,0:T(8,128)(2,1)} %get-tuple-element.179), channel_id=1, source_target_pairs={{0,1},{1,0},{2,3},{3,2},{16,18},{17,19},{18,16},{19,17},{4,5},{5,4... | collective-permute-start | bytes 589832 | tf_op jit(solution)/shard_map/rs1/ppermute | solution.py:204
  36.6 9.7 %collective-permute-start.12 = (bf16[128,768]{1,0:T(8,128)(2,1)S(1)}, bf16[128,768]{1,0:T(8,128)(2,1)S(1)}, u32[]{:S(2)}, u32[]{:S(2)}) collective-permute-start(bf16[128,768]{1,0:T(8,128)(2,1)S(1)} %get-tuple-element.180), channel_id=1, source_target_pairs={{0,2},{1,3},{2,0},{3,1},{16,17},{17,16},{18,19},{19,18},{4,6},{5,7... | collective-permute-start | bytes 589832 | tf_op jit(solution)/shard_map/rs1/ppermute | solution.py:204
  36.6 9.7 %collective-permute-start.13 = (bf16[128,768]{1,0:T(8,128)(2,1)S(1)}, bf16[128,768]{1,0:T(8,128)(2,1)S(1)}, u32[]{:S(2)}, u32[]{:S(2)}) collective-permute-start(bf16[128,768]{1,0:T(8,128)(2,1)S(1)} %get-tuple-element.181), channel_id=1, source_target_pairs={{0,3},{1,2},{2,1},{3,0},{16,19},{17,18},{18,17},{19,16},{4,7},{5,6... | collective-permute-start | bytes 589832 | tf_op jit(solution)/shard_map/rs1/ppermute | solution.py:204
  38.0 23.4 %collective-permute-start.20 = (bf16[768,768]{1,0:T(8,128)(2,1)}, bf16[768,768]{1,0:T(8,128)(2,1)}, u32[]{:S(2)}, u32[]{:S(2)}) collective-permute-start(bf16[768,768]{1,0:T(8,128)(2,1)} %bitcast.75), channel_id=1, source_target_pairs={{0,16},{16,0},{1,17},{17,1},{2,18},{18,2},{3,19},{19,3},{4,20},{20... | collective-permute-start | bytes 3538952 | tf_op jit(solution)/shard_map/w/ppermute | solution.py:197
  39.5 22.3 %collective-permute-start.21 = (bf16[768,768]{1,0:T(8,128)(2,1)}, bf16[768,768]{1,0:T(8,128)(2,1)}, u32[]{:S(2)}, u32[]{:S(2)}) collective-permute-start(bf16[768,768]{1,0:T(8,128)(2,1)} %bitcast.80), channel_id=1, source_target_pairs={{0,16},{16,0},{1,17},{17,1},{2,18},{18,2},{3,19},{19,3},{4,20},{20... | collective-permute-start | bytes 3538952 | tf_op jit(solution)/shard_map/w/ppermute | solution.py:197
  46.3 10.6 %collective-permute-start.16 = (bf16[128,768]{1,0:T(8,128)(2,1)S(1)}, bf16[128,768]{1,0:T(8,128)(2,1)S(1)}, u32[]{:S(2)}, u32[]{:S(2)}) collective-permute-start(bf16[128,768]{1,0:T(8,128)(2,1)S(1)} %get-tuple-element.186), channel_id=1, source_target_pairs={{0,3},{1,2},{2,1},{3,0},{16,19},{17,18},{18,17},{19,16},{4,7},{5,6... | collective-permute-start | bytes 589832 | tf_op jit(solution)/shard_map/rs1/ppermute | solution.py:204
  50.5 10.0 %collective-permute-start.38 = (bf16[192,768]{1,0:T(8,128)(2,1)}, bf16[192,768]{1,0:T(8,128)(2,1)}, u32[]{:S(2)}, u32[]{:S(2)}) collective-permute-start(bf16[192,768]{1,0:T(8,128)(2,1)} %select_select_fusion), channel_id=1, source_target_pairs={{0,2},{1,3},{2,0},{3,1},{16,17},{17,16},{18,19},{19,18},{4,6},{5,7... | collective-permute-start | bytes 884744 | tf_op jit(solution)/shard_map/nb/ppermute | solution.py:204
  51.9 27.1 %collective-permute-start.25 = (bf16[768,768]{1,0:T(8,128)(2,1)}, bf16[768,768]{1,0:T(8,128)(2,1)}, u32[]{:S(2)}, u32[]{:S(2)}) collective-permute-start(bf16[768,768]{1,0:T(8,128)(2,1)} %bitcast.28.refs_7_), channel_id=1, source_target_pairs={{0,16},{16,0},{1,17},{17,1},{2,18},{18,2},{3,19},{19,3},{4,20},{20... | collective-permute-start | bytes 3538952 | tf_op jit(solution)/shard_map/w/ppermute | solution.py:197
  56.9 22.9 %collective-permute-start.26 = (bf16[768,768]{1,0:T(8,128)(2,1)}, bf16[768,768]{1,0:T(8,128)(2,1)}, u32[]{:S(2)}, u32[]{:S(2)}) collective-permute-start(bf16[768,768]{1,0:T(8,128)(2,1)} %bitcast.29.refs_8_), channel_id=1, source_target_pairs={{0,16},{16,0},{1,17},{17,1},{2,18},{18,2},{3,19},{19,3},{4,20},{20... | collective-permute-start | bytes 3538952 | tf_op jit(solution)/shard_map/w/ppermute | solution.py:197
  60.6 227.6 %reduce-scatter.5.cloned.1.call-start = ((), (), s32[]{:S(2)}) async-start(), calls=%async_computation.5 | async-start | bytes 1597440 | tf_op jit(solution)/shard_map/rg/reduce_scatter | solution.py:1246
  61.8 11.8 %collective-permute-start.19 = (bf16[128,768]{1,0:T(8,128)(2,1)S(1)}, bf16[128,768]{1,0:T(8,128)(2,1)S(1)}, u32[]{:S(2)}, u32[]{:S(2)}) collective-permute-start(bf16[128,768]{1,0:T(8,128)(2,1)S(1)} %get-tuple-element.182.refs_3_.refs_7_.refs_6_), channel_id=1, source_target_pairs={{0,3},{1,2},{2,1},{3,0},{16,19},{17,18},{18,17},{19,16},{4,7},{5,6... | collective-permute-start | bytes 589832 | tf_op jit(solution)/shard_map/ag2/ppermute | solution.py:204
  66.8 14.8 %collective-permute-start.22 = (bf16[128,768]{1,0:T(8,128)(2,1)S(1)}, bf16[128,768]{1,0:T(8,128)(2,1)S(1)}, u32[]{:S(2)}, u32[]{:S(2)}) collective-permute-start(bf16[128,768]{1,0:T(8,128)(2,1)S(1)} %norm_middle.5.refs_3_.refs_7_), channel_id=1, source_target_pairs={{0,1},{1,0},{2,3},{3,2},{16,18},{17,19},{18,16},{19,17},{4,5},{5,4... | collective-permute-start | bytes 589832 | tf_op jit(solution)/shard_map/ag2/ppermute | solution.py:204
  67.6 14.0 %collective-permute-start.23 = (bf16[128,768]{1,0:T(8,128)(2,1)S(1)}, bf16[128,768]{1,0:T(8,128)(2,1)S(1)}, u32[]{:S(2)}, u32[]{:S(2)}) collective-permute-start(bf16[128,768]{1,0:T(8,128)(2,1)S(1)} %norm_middle.5.refs_3_.refs_7_), channel_id=1, source_target_pairs={{0,2},{1,3},{2,0},{3,1},{16,17},{17,16},{18,19},{19,18},{4,6},{5,7... | collective-permute-start | bytes 589832 | tf_op jit(solution)/shard_map/ag2/ppermute | solution.py:204
  79.0 9.9 %collective-permute-start.27 = (bf16[128,768]{1,0:T(8,128)(2,1)}, bf16[128,768]{1,0:T(8,128)(2,1)S(1)}, u32[]{:S(2)}, u32[]{:S(2)}) collective-permute-start(bf16[128,768]{1,0:T(8,128)(2,1)} %get-tuple-element.192), channel_id=1, source_target_pairs={{0,1},{1,0},{2,3},{3,2},{16,18},{17,19},{18,16},{19,17},{4,5},{5,4... | collective-permute-start | bytes 589832 | tf_op jit(solution)/shard_map/rs2/ppermute | solution.py:204
  79.8 9.1 %collective-permute-start.28 = (bf16[128,768]{1,0:T(8,128)(2,1)}, bf16[128,768]{1,0:T(8,128)(2,1)S(1)}, u32[]{:S(2)}, u32[]{:S(2)}) collective-permute-start(bf16[128,768]{1,0:T(8,128)(2,1)} %get-tuple-element.193), channel_id=1, source_target_pairs={{0,2},{1,3},{2,0},{3,1},{16,17},{17,16},{18,19},{19,18},{4,6},{5,7... | collective-permute-start | bytes 589832 | tf_op jit(solution)/shard_map/rs2/ppermute | solution.py:204
  81.6 8.9 %collective-permute-start.29 = (bf16[128,768]{1,0:T(8,128)(2,1)S(1)}, bf16[128,768]{1,0:T(8,128)(2,1)S(1)}, u32[]{:S(2)}, u32[]{:S(2)}) collective-permute-start(bf16[128,768]{1,0:T(8,128)(2,1)S(1)} %get-tuple-element.194), channel_id=1, source_target_pairs={{0,3},{1,2},{2,1},{3,0},{16,19},{17,18},{18,17},{19,16},{4,7},{5,6... | collective-permute-start | bytes 589832 | tf_op jit(solution)/shard_map/rs2/ppermute | solution.py:204
  86.1 9.4 %collective-permute-start.30 = (bf16[128,768]{1,0:T(8,128)(2,1)S(1)}, bf16[128,768]{1,0:T(8,128)(2,1)S(1)}, u32[]{:S(2)}, u32[]{:S(2)}) collective-permute-start(bf16[128,768]{1,0:T(8,128)(2,1)S(1)} %get-tuple-element.197), channel_id=1, source_target_pairs={{0,1},{1,0},{2,3},{3,2},{16,18},{17,19},{18,16},{19,17},{4,5},{5,4... | collective-permute-start | bytes 589832 | tf_op jit(solution)/shard_map/rs2/ppermute | solution.py:204
  87.4 10.5 %collective-permute-start.31 = (bf16[128,768]{1,0:T(8,128)(2,1)}, bf16[128,768]{1,0:T(8,128)(2,1)S(1)}, u32[]{:S(2)}, u32[]{:S(2)}) collective-permute-start(bf16[128,768]{1,0:T(8,128)(2,1)} %get-tuple-element.198), channel_id=1, source_target_pairs={{0,2},{1,3},{2,0},{3,1},{16,17},{17,16},{18,19},{19,18},{4,6},{5,7... | collective-permute-start | bytes 589832 | tf_op jit(solution)/shard_map/rs2/ppermute | solution.py:204
  88.8 10.3 %collective-permute-start.32 = (bf16[128,768]{1,0:T(8,128)(2,1)}, bf16[128,768]{1,0:T(8,128)(2,1)S(1)}, u32[]{:S(2)}, u32[]{:S(2)}) collective-permute-start(bf16[128,768]{1,0:T(8,128)(2,1)} %get-tuple-element.199), channel_id=1, source_target_pairs={{0,3},{1,2},{2,1},{3,0},{16,19},{17,18},{18,17},{19,16},{4,7},{5,6... | collective-permute-start | bytes 589832 | tf_op jit(solution)/shard_map/rs2/ppermute | solution.py:204
  92.1 13.5 %collective-permute-start.33 = (bf16[128,768]{1,0:T(8,128)(2,1)S(1)}, bf16[128,768]{1,0:T(8,128)(2,1)S(1)}, u32[]{:S(2)}, u32[]{:S(2)}) collective-permute-start(bf16[128,768]{1,0:T(8,128)(2,1)S(1)} %get-tuple-element.195.refs_4_.refs_7_.refs_6_), channel_id=1, source_target_pairs={{0,1},{1,0},{2,3},{3,2},{16,18},{17,19},{18,16},{19,17},{4,5},{5,4... | collective-permute-start | bytes 589832 | tf_op jit(solution)/shard_map/ag1/ppermute | solution.py:204
  93.9 11.6 %collective-permute-start.34 = (bf16[128,768]{1,0:T(8,128)(2,1)S(1)}, bf16[128,768]{1,0:T(8,128)(2,1)S(1)}, u32[]{:S(2)}, u32[]{:S(2)}) collective-permute-start(bf16[128,768]{1,0:T(8,128)(2,1)S(1)} %get-tuple-element.195.refs_4_.refs_7_.refs_6_), channel_id=1, source_target_pairs={{0,2},{1,3},{2,0},{3,1},{16,17},{17,16},{18,19},{19,18},{4,6},{5,7... | collective-permute-start | bytes 589832 | tf_op jit(solution)/shard_map/ag1/ppermute | solution.py:204
  95.6 11.9 %collective-permute-start.35 = (bf16[128,768]{1,0:T(8,128)(2,1)S(1)}, bf16[128,768]{1,0:T(8,128)(2,1)S(1)}, u32[]{:S(2)}, u32[]{:S(2)}) collective-permute-start(bf16[128,768]{1,0:T(8,128)(2,1)S(1)} %get-tuple-element.195.refs_4_.refs_7_.refs_6_), channel_id=1, source_target_pairs={{0,3},{1,2},{2,1},{3,0},{16,19},{17,18},{18,17},{19,16},{4,7},{5,6... | collective-permute-start | bytes 589832 | tf_op jit(solution)/shard_map/ag1/ppermute | solution.py:204
  100.0 25.1 %collective-permute-start.37 = (bf16[128,768]{1,0:T(8,128)(2,1)S(1)}, bf16[128,768]{1,0:T(8,128)(2,1)S(1)}, u32[]{:S(2)}, u32[]{:S(2)}) collective-permute-start(bf16[128,768]{1,0:T(8,128)(2,1)S(1)} %norm_last.5.refs_4_.refs_5_), channel_id=1, source_target_pairs={{0,1},{1,0},{2,3},{3,2},{16,18},{17,19},{18,16},{19,17},{4,5},{5,4... | collective-permute-start | bytes 589832 | tf_op jit(solution)/shard_map/ag1/ppermute | solution.py:204
  112.5 17.3 %collective-permute-start.39 = (bf16[128,768]{1,0:T(8,128)(2,1)S(1)}, bf16[128,768]{1,0:T(8,128)(2,1)S(1)}, u32[]{:S(2)}, u32[]{:S(2)}) collective-permute-start(bf16[128,768]{1,0:T(8,128)(2,1)S(1)} %get-tuple-element.209), channel_id=1, source_target_pairs={{0,1},{1,0},{2,3},{3,2},{16,18},{17,19},{18,16},{19,17},{4,5},{5,4... | collective-permute-start | bytes 589832 | tf_op jit(solution)/shard_map/rs1/ppermute | solution.py:204
  114.3 15.5 %collective-permute-start.40 = (bf16[128,768]{1,0:T(8,128)(2,1)S(1)}, bf16[128,768]{1,0:T(8,128)(2,1)S(1)}, u32[]{:S(2)}, u32[]{:S(2)}) collective-permute-start(bf16[128,768]{1,0:T(8,128)(2,1)S(1)} %get-tuple-element.210), channel_id=1, source_target_pairs={{0,2},{1,3},{2,0},{3,1},{16,17},{17,16},{18,19},{19,18},{4,6},{5,7... | collective-permute-start | bytes 589832 | tf_op jit(solution)/shard_map/rs1/ppermute | solution.py:204
  115.9 13.8 %collective-permute-start.41 = (bf16[128,768]{1,0:T(8,128)(2,1)S(1)}, bf16[128,768]{1,0:T(8,128)(2,1)S(1)}, u32[]{:S(2)}, u32[]{:S(2)}) collective-permute-start(bf16[128,768]{1,0:T(8,128)(2,1)S(1)} %get-tuple-element.211), channel_id=1, source_target_pairs={{0,3},{1,2},{2,1},{3,0},{16,19},{17,18},{18,17},{19,16},{4,7},{5,6... | collective-permute-start | bytes 589832 | tf_op jit(solution)/shard_map/rs1/ppermute | solution.py:204
  115.9 9.2 %collective-permute-start.36 = (f32[1,768]{1,0:T(1,128)S(1)}, f32[1,768]{1,0:T(1,128)S(1)}, u32[]{:S(2)}, u32[]{:S(2)}) collective-permute-start(f32[1,768]{1,0:T(1,128)S(1)} %fusion.3), channel_id=1, source_target_pairs={{0,2},{1,3},{2,0},{3,1},{16,17},{17,16},{18,19},{19,18},{4,6},{5,7... | collective-permute-start | bytes 9224 | tf_op jit(solution)/shard_map/nb/ppermute | solution.py:204
  131.4 12.9 %collective-permute-start.43 = (bf16[128,768]{1,0:T(8,128)(2,1)S(1)}, bf16[128,768]{1,0:T(8,128)(2,1)S(1)}, u32[]{:S(2)}, u32[]{:S(2)}) collective-permute-start(bf16[128,768]{1,0:T(8,128)(2,1)S(1)} %get-tuple-element.212.refs_3_.refs_7_.refs_6_), channel_id=1, source_target_pairs={{0,1},{1,0},{2,3},{3,2},{16,18},{17,19},{18,16},{19,17},{4,5},{5,4... | collective-permute-start | bytes 589832 | tf_op jit(solution)/shard_map/ag2/ppermute | solution.py:204
  132.9 14.9 %collective-permute-start.44 = (bf16[128,768]{1,0:T(8,128)(2,1)S(1)}, bf16[128,768]{1,0:T(8,128)(2,1)S(1)}, u32[]{:S(2)}, u32[]{:S(2)}) collective-permute-start(bf16[128,768]{1,0:T(8,128)(2,1)S(1)} %get-tuple-element.212.refs_3_.refs_7_.refs_6_), channel_id=1, source_target_pairs={{0,2},{1,3},{2,0},{3,1},{16,17},{17,16},{18,19},{19,18},{4,6},{5,7... | collective-permute-start | bytes 589832 | tf_op jit(solution)/shard_map/ag2/ppermute | solution.py:204
  134.7 13.1 %collective-permute-start.45 = (bf16[128,768]{1,0:T(8,128)(2,1)S(1)}, bf16[128,768]{1,0:T(8,128)(2,1)S(1)}, u32[]{:S(2)}, u32[]{:S(2)}) collective-permute-start(bf16[128,768]{1,0:T(8,128)(2,1)S(1)} %get-tuple-element.212.refs_3_.refs_7_.refs_6_), channel_id=1, source_target_pairs={{0,3},{1,2},{2,1},{3,0},{16,19},{17,18},{18,17},{19,16},{4,7},{5,6... | collective-permute-start | bytes 589832 | tf_op jit(solution)/shard_map/ag2/ppermute | solution.py:204
  136.5 18.9 %collective-permute-start.46 = (bf16[128,768]{1,0:T(8,128)(2,1)S(1)}, bf16[128,768]{1,0:T(8,128)(2,1)S(1)}, u32[]{:S(2)}, u32[]{:S(2)}) collective-permute-start(bf16[128,768]{1,0:T(8,128)(2,1)S(1)} %norm_middle.7.refs_3_.refs_7_), channel_id=1, source_target_pairs={{0,1},{1,0},{2,3},{3,2},{16,18},{17,19},{18,16},{19,17},{4,5},{5,4... | collective-permute-start | bytes 589832 | tf_op jit(solution)/shard_map/ag2/ppermute | solution.py:204
  136.8 19.8 %collective-permute-start.47 = (bf16[128,768]{1,0:T(8,128)(2,1)S(1)}, bf16[128,768]{1,0:T(8,128)(2,1)S(1)}, u32[]{:S(2)}, u32[]{:S(2)}) collective-permute-start(bf16[128,768]{1,0:T(8,128)(2,1)S(1)} %norm_middle.7.refs_3_.refs_7_), channel_id=1, source_target_pairs={{0,2},{1,3},{2,0},{3,1},{16,17},{17,16},{18,19},{19,18},{4,6},{5,7... | collective-permute-start | bytes 589832 | tf_op jit(solution)/shard_map/ag2/ppermute | solution.py:204
  144.3 12.3 %collective-permute-start.48 = (bf16[128,768]{1,0:T(8,128)(2,1)S(1)}, bf16[128,768]{1,0:T(8,128)(2,1)S(1)}, u32[]{:S(2)}, u32[]{:S(2)}) collective-permute-start(bf16[128,768]{1,0:T(8,128)(2,1)S(1)} %norm_middle.7.refs_3_.refs_7_), channel_id=1, source_target_pairs={{0,3},{1,2},{2,1},{3,0},{16,19},{17,18},{18,17},{19,16},{4,7},{5,6... | collective-permute-start | bytes 589832 | tf_op jit(solution)/shard_map/ag2/ppermute | solution.py:204
  153.2 12.0 %collective-permute-start.49 = (bf16[128,768]{1,0:T(8,128)(2,1)}, bf16[128,768]{1,0:T(8,128)(2,1)S(1)}, u32[]{:S(2)}, u32[]{:S(2)}) collective-permute-start(bf16[128,768]{1,0:T(8,128)(2,1)} %get-tuple-element.220), channel_id=1, source_target_pairs={{0,1},{1,0},{2,3},{3,2},{16,18},{17,19},{18,16},{19,17},{4,5},{5,4... | collective-permute-start | bytes 589832 | tf_op jit(solution)/shard_map/rs2/ppermute | solution.py:204
  155.4 9.9 %collective-permute-start.50 = (bf16[128,768]{1,0:T(8,128)(2,1)S(1)}, bf16[128,768]{1,0:T(8,128)(2,1)S(1)}, u32[]{:S(2)}, u32[]{:S(2)}) collective-permute-start(bf16[128,768]{1,0:T(8,128)(2,1)S(1)} %get-tuple-element.221), channel_id=1, source_target_pairs={{0,2},{1,3},{2,0},{3,1},{16,17},{17,16},{18,19},{19,18},{4,6},{5,7... | collective-permute-start | bytes 589832 | tf_op jit(solution)/shard_map/rs2/ppermute | solution.py:204
  155.4 9.9 %collective-permute-start.51 = (bf16[128,768]{1,0:T(8,128)(2,1)S(1)}, bf16[128,768]{1,0:T(8,128)(2,1)S(1)}, u32[]{:S(2)}, u32[]{:S(2)}) collective-permute-start(bf16[128,768]{1,0:T(8,128)(2,1)S(1)} %get-tuple-element.222), channel_id=1, source_target_pairs={{0,3},{1,2},{2,1},{3,0},{16,19},{17,18},{18,17},{19,16},{4,7},{5,6... | collective-permute-start | bytes 589832 | tf_op jit(solution)/shard_map/rs2/ppermute | solution.py:204
  160.3 8.1 %collective-permute-start.53 = (bf16[128,768]{1,0:T(8,128)(2,1)S(1)}, bf16[128,768]{1,0:T(8,128)(2,1)S(1)}, u32[]{:S(2)}, u32[]{:S(2)}) collective-permute-start(bf16[128,768]{1,0:T(8,128)(2,1)S(1)} %get-tuple-element.225), channel_id=1, source_target_pairs={{0,1},{1,0},{2,3},{3,2},{16,18},{17,19},{18,16},{19,17},{4,5},{5,4... | collective-permute-start | bytes 589832 | tf_op jit(solution)/shard_map/rs2/ppermute | solution.py:204
  188.3 10.1 %collective-permute-start.62 = (bf16[8,768]{1,0:T(8,128)(2,1)S(1)}, bf16[8,768]{1,0:T(8,128)(2,1)S(1)}, u32[]{:S(2)}, u32[]{:S(2)}) collective-permute-start(bf16[8,768]{1,0:T(8,128)(2,1)S(1)} %get-tuple-element.231.refs_4_), channel_id=1, source_target_pairs={{0,16},{16,0},{1,17},{17,1},{2,18},{18,2},{3,19},{19,3},{4,20},{20... | collective-permute-start | bytes 36872 | tf_op jit(solution)/shard_map/loss/ppermute | solution.py:197
  203.6 9.8 %collective-permute-start.68 = (bf16[128,768]{1,0:T(8,128)(2,1)S(1)}, bf16[128,768]{1,0:T(8,128)(2,1)S(1)}, u32[]{:S(2)}, u32[]{:S(2)}) collective-permute-start(bf16[128,768]{1,0:T(8,128)(2,1)S(1)} %get-tuple-element.243.refs_1_.refs_2_.refs_4_), channel_id=1, source_target_pairs={{0,3},{1,2},{2,1},{3,0},{16,19},{17,18},{18,17},{19,16},{4,7},{5,6... | collective-permute-start | bytes 589832 | tf_op jit(solution)/shard_map/ag3/ppermute | solution.py:204
  218.4 10.3 %collective-permute-start.70 = (bf16[128,768]{1,0:T(8,128)(2,1)S(1)}, bf16[128,768]{1,0:T(8,128)(2,1)S(1)}, u32[]{:S(2)}, u32[]{:S(2)}) collective-permute-start(bf16[128,768]{1,0:T(8,128)(2,1)S(1)} %get-tuple-element.254), channel_id=1, source_target_pairs={{0,1},{1,0},{2,3},{3,2},{16,18},{17,19},{18,16},{19,17},{4,5},{5,4... | collective-permute-start | bytes 589832 | tf_op jit(solution)/shard_map/rs3/ppermute | solution.py:204
  218.4 10.2 %collective-permute-start.71 = (bf16[128,768]{1,0:T(8,128)(2,1)S(1)}, bf16[128,768]{1,0:T(8,128)(2,1)S(1)}, u32[]{:S(2)}, u32[]{:S(2)}) collective-permute-start(bf16[128,768]{1,0:T(8,128)(2,1)S(1)} %get-tuple-element.255), channel_id=1, source_target_pairs={{0,2},{1,3},{2,0},{3,1},{16,17},{17,16},{18,19},{19,18},{4,6},{5,7... | collective-permute-start | bytes 589832 | tf_op jit(solution)/shard_map/rs3/ppermute | solution.py:204
  220.1 10.1 %collective-permute-start.72 = (bf16[128,768]{1,0:T(8,128)(2,1)S(1)}, bf16[128,768]{1,0:T(8,128)(2,1)S(1)}, u32[]{:S(2)}, u32[]{:S(2)}) collective-permute-start(bf16[128,768]{1,0:T(8,128)(2,1)S(1)} %get-tuple-element.256), channel_id=1, source_target_pairs={{0,3},{1,2},{2,1},{3,0},{16,19},{17,18},{18,17},{19,16},{4,7},{5,6... | collective-permute-start | bytes 589832 | tf_op jit(solution)/shard_map/rs3/ppermute | solution.py:204
  235.4 9.6 %collective-permute-start.76 = (bf16[128,768]{1,0:T(8,128)(2,1)S(1)}, bf16[128,768]{1,0:T(8,128)(2,1)S(1)}, u32[]{:S(2)}, u32[]{:S(2)}) collective-permute-start(bf16[128,768]{1,0:T(8,128)(2,1)S(1)} %get-tuple-element.259.refs_1_.refs_2_.refs_3_), channel_id=1, source_target_pairs={{0,3},{1,2},{2,1},{3,0},{16,19},{17,18},{18,17},{19,16},{4,7},{5,6... | collective-permute-start | bytes 589832 | tf_op jit(solution)/shard_map/ag4/ppermute | solution.py:204
  245.1 65.9 %reduce-scatter.7.cloned.1.call-start = ((), (), s32[]{:S(2)}) async-start(), calls=%async_computation.6 | async-start | bytes 860160 | tf_op jit(solution)/shard_map/rg/reduce_scatter | solution.py:1246
  252.0 8.8 %collective-permute-start.78 = (bf16[128,768]{1,0:T(8,128)(2,1)S(1)}, bf16[128,768]{1,0:T(8,128)(2,1)S(1)}, u32[]{:S(2)}, u32[]{:S(2)}) collective-permute-start(bf16[128,768]{1,0:T(8,128)(2,1)S(1)} %get-tuple-element.273), channel_id=1, source_target_pairs={{0,1},{1,0},{2,3},{3,2},{16,18},{17,19},{18,16},{19,17},{4,5},{5,4... | collective-permute-start | bytes 589832 | tf_op jit(solution)/shard_map/rs4/ppermute | solution.py:204
  254.6 9.3 %collective-permute-start.80 = (bf16[128,768]{1,0:T(8,128)(2,1)S(1)}, bf16[128,768]{1,0:T(8,128)(2,1)S(1)}, u32[]{:S(2)}, u32[]{:S(2)}) collective-permute-start(bf16[128,768]{1,0:T(8,128)(2,1)S(1)} %get-tuple-element.275), channel_id=1, source_target_pairs={{0,3},{1,2},{2,1},{3,0},{16,19},{17,18},{18,17},{19,16},{4,7},{5,6... | collective-permute-start | bytes 589832 | tf_op jit(solution)/shard_map/rs4/ppermute | solution.py:204
  269.1 10.2 %collective-permute-start.84 = (bf16[128,768]{1,0:T(8,128)(2,1)S(1)}, bf16[128,768]{1,0:T(8,128)(2,1)S(1)}, u32[]{:S(2)}, u32[]{:S(2)}) collective-permute-start(bf16[128,768]{1,0:T(8,128)(2,1)S(1)} %get-tuple-element.278.refs_1_.refs_2_.refs_5_), channel_id=1, source_target_pairs={{0,3},{1,2},{2,1},{3,0},{16,19},{17,18},{18,17},{19,16},{4,7},{5,6... | collective-permute-start | bytes 589832 | tf_op jit(solution)/shard_map/ag3/ppermute | solution.py:204
  284.2 10.0 %collective-permute-start.86 = (bf16[128,768]{1,0:T(8,128)(2,1)S(1)}, bf16[128,768]{1,0:T(8,128)(2,1)S(1)}, u32[]{:S(2)}, u32[]{:S(2)}) collective-permute-start(bf16[128,768]{1,0:T(8,128)(2,1)S(1)} %get-tuple-element.293), channel_id=1, source_target_pairs={{0,1},{1,0},{2,3},{3,2},{16,18},{17,19},{18,16},{19,17},{4,5},{5,4... | collective-permute-start | bytes 589832 | tf_op jit(solution)/shard_map/rs3/ppermute | solution.py:204
  284.9 9.3 %collective-permute-start.87 = (bf16[128,768]{1,0:T(8,128)(2,1)S(1)}, bf16[128,768]{1,0:T(8,128)(2,1)S(1)}, u32[]{:S(2)}, u32[]{:S(2)}) collective-permute-start(bf16[128,768]{1,0:T(8,128)(2,1)S(1)} %get-tuple-element.294), channel_id=1, source_target_pairs={{0,2},{1,3},{2,0},{3,1},{16,17},{17,16},{18,19},{19,18},{4,6},{5,7... | collective-permute-start | bytes 589832 | tf_op jit(solution)/shard_map/rs3/ppermute | solution.py:204
  286.3 10.2 %collective-permute-start.88 = (bf16[128,768]{1,0:T(8,128)(2,1)S(1)}, bf16[128,768]{1,0:T(8,128)(2,1)S(1)}, u32[]{:S(2)}, u32[]{:S(2)}) collective-permute-start(bf16[128,768]{1,0:T(8,128)(2,1)S(1)} %get-tuple-element.295), channel_id=1, source_target_pairs={{0,3},{1,2},{2,1},{3,0},{16,19},{17,18},{18,17},{19,16},{4,7},{5,6... | collective-permute-start | bytes 589832 | tf_op jit(solution)/shard_map/rs3/ppermute | solution.py:204
  288.3 58.9 %reduce-scatter.9.cloned.1.call-start = ((), (), s32[]{:S(2)}) async-start(), calls=%async_computation.7 | async-start | bytes 1597440 | tf_op jit(solution)/shard_map/rg/reduce_scatter | solution.py:1246
  301.4 9.6 %collective-permute-start.92 = (bf16[128,768]{1,0:T(8,128)(2,1)S(1)}, bf16[128,768]{1,0:T(8,128)(2,1)S(1)}, u32[]{:S(2)}, u32[]{:S(2)}) collective-permute-start(bf16[128,768]{1,0:T(8,128)(2,1)S(1)} %get-tuple-element.318.refs_1_.refs_2_), channel_id=1, source_target_pairs={{0,3},{1,2},{2,1},{3,0},{16,19},{17,18},{18,17},{19,16},{4,7},{5,6... | collective-permute-start | bytes 589832 | tf_op jit(solution)/shard_map/ag4/ppermute | solution.py:204
  311.0 51.5 %reduce-scatter.11.cloned.1.call-start = ((), (), s32[]{:S(2)}) async-start(), calls=%async_computation.8 | async-start | bytes 860160 | tf_op jit(solution)/shard_map/lg/reduce_scatter | solution.py:1334
  323.5 13.6 %collective-permute-start.97 = (bf16[4,112,768]{2,1,0:T(8,128)(2,1)S(1)}, bf16[4,112,768]{2,1,0:T(8,128)(2,1)S(1)}, u32[]{:S(2)}, u32[]{:S(2)}) collective-permute-start(bf16[4,112,768]{2,1,0:T(8,128)(2,1)S(1)} %get-tuple-element.316), channel_id=1, source_target_pairs={{0,16},{16,0},{1,17},{17,1},{2,18},{18,2},{3,19},{19,3},{4,20},{20... | collective-permute-start | bytes 2064392 | tf_op jit(solution)/shard_map/lg/ppermute | solution.py:197
  326.5 10.6 %collective-permute-start.96 = (bf16[144,768]{1,0:T(8,128)(2,1)S(1)}, bf16[144,768]{1,0:T(8,128)(2,1)S(1)}, u32[]{:S(2)}, u32[]{:S(2)}) collective-permute-start(bf16[144,768]{1,0:T(8,128)(2,1)S(1)} %get-tuple-element.315), channel_id=1, source_target_pairs={{0,3},{1,2},{2,1},{3,0},{16,19},{17,18},{18,17},{19,16},{4,7},{5,6... | collective-permute-start | bytes 663560 | tf_op jit(solution)/shard_map/rs4/ppermute | solution.py:204
  (103 other events, 838.2 us)
Sparse Core Ops, SparseCore 0:
  60.7 29.4 all-gather.1
  245.2 30.0 reduce-scatter.4
  288.4 18.8 reduce-scatter.6
  311.1 30.0 reduce-scatter.8
  343.5 18.9 reduce-scatter.10

commit v3 on v2

--- a/solution.py
+++ b/solution.py
@@ -551,9 +551,10 @@
     return got[1], got[0]
 
 
-def middle_backward(counts, mixed, tables, layer, residual, pieces, last_rows, above):
+def middle_backward(counts, mixed, tables, layer, residual, pieces, last_rows, above, ride):
     rows, width = mixed.shape
     known = [last_rows] + above
+    total = 6 + 6 * len(above)
 
     def body(s, held_r, came_r, *rest):
         at = here()
@@ -561,14 +562,17 @@
         near_r, (y_r, part_r, rows_r, low_r) = rest[:-4], rest[-4:]
         grad = scattered(part_r, *near_r)
         gain = table_row(at, (held_r, came_r), layer, 0, ROW_GAIN)
-        d_gain, in_sum, out_sum = norm_gradient(y_r, grad, gain, low_r)
+        d_gain, in_sum, out_sum = norm_gradient(y_r, grad, gain, low_r.at[pl.ds(0, rows)])
         last = [last_r[i : i + 1, :] for i in range(3)]
         for i, row in enumerate((d_gain, last[0], out_sum, in_sum, last[2], last[1])):
             rows_r[i : i + 1, :] = row
         if above_r:
             rows_r[6:, :] = above_r[0][...]
-
-    outs = [((6 + 6 * len(above), width), F32), ((rows, width), LOW)]
+        if ride:
+            spare = jnp.zeros((EXTRA - total, width), F32)
+            low_r[rows:, :] = bf(jnp.concatenate([rows_r[...], spare], axis=0))
+
+    outs = [((total, width), F32), ((rows + EXTRA * ride, width), LOW)]
     near = tables + known + [residual] + pieces[1:]
     loads = [mixed, pieces[0]]
     got = kernel_call(body, outs, [counts], near, 30 * mixed.size, "middle_backward", loads)
@@ -612,23 +616,20 @@
     return [got[count], *got[: count - 1], got[count + 1], got[count - 1]]
 
 
-def attn_backward(counts, grads, qkv, shares, context, weights, layer, known):
+def attn_backward(counts, grads, qkv, shares, context, weights, layer):
     wide = len(grads) == 4
     full, triple = qkv.shape[1:]
     local = triple // 3
     heads = local // 64
-    rows, width = grads[0].shape
-    count, extra = len(grads), len(known)
+    rows, width = full // 2, grads[0].shape[1]
+    count = len(grads)
 
     def body(s, *refs):
-        source, known_r, refs = refs[:count], refs[count : count + extra], refs[count + extra :]
+        source, refs = [g.at[pl.ds(0, rows)] for g in refs[:count]], refs[count:]
         (qkv_r, sh_r, cx_r), refs = refs[:3], refs[3:]
         w_refs, refs = refs[: len(weights)], refs[len(weights) :]
         others, (bias_r, part, dproj_r, w_r, sems) = refs[: count - 1], refs[count - 1 :]
-        targets = [part, *[other.at[:rows] for other in others]]
-        for other in others[: extra * count]:
-            spare = jnp.zeros((EXTRA - known_r[0].shape[0], width), F32)
-            other[rows:, :] = bf(jnp.concatenate([known_r[0][...], spare], axis=0))
+        targets = [part, *others]
         waits = fetch_attn(here(), layer, 0, w_refs, w_r, sems)
         groups = row_groups(source)
         bias_r[...] = jnp.zeros((2, width), F32)
@@ -668,13 +669,13 @@
         put_rows(targets, outs)
 
     part = ((rows, width), F32)
-    outs = [((rows + EXTRA * extra, width), LOW)] * (count - 1)
+    outs = [((rows, width), LOW)] * (count - 1)
     outs, stores = outs + [((2, width), F32)], [part, ((2, full, triple), LOW)]
     flops = 4 * full * (4 * local * width + 4 * local * full)
     loads = [qkv, shares, context]
     side = 1 if wide else 2
     got = kernel_call(
-        body, outs, [counts], grads + known, flops, "attn_backward", loads, stores, weights, side
+        body, outs, [counts], grads, flops, "attn_backward", loads, stores, weights, side
     )
     return [got[count], *got[: count - 1], got[count + 1], got[count - 1]]
 
@@ -704,7 +705,8 @@
         at = here()
         bias_r, g_refs, refs = refs[0], refs[1 : 1 + count], refs[1 + count :]
         x_refs, (o_r, d_r), targets = refs[:count], refs[count : count + 2], refs[count + 2 :]
-        g_rows = [stack_rows(g) for g in row_groups(g_refs)]
+        half = pairs[0].shape[1] // 2
+        g_rows = [stack_rows(g) for g in row_groups([g.at[pl.ds(0, half)] for g in g_refs])]
         back = dot_tn(g_rows[0], o_r[0]) + dot_tn(g_rows[1], o_r[1])
         x_rows = [stack_rows(x) for x in row_groups(x_refs)]
         ahead = dot_tn(x_rows[0], d_r[0]) + dot_tn(x_rows[1], d_r[1])
@@ -728,19 +730,19 @@
     return [got[1], got[0]] if blocks > 1 else got
 
 
-def add_cores(counts, mine, came, norms=()):
+def add_cores(counts, mine, came, norms=(), arrived=()):
     blocks, rows = mine.shape[:2]
     start = rows - EXTRA
 
     def body(s, *refs):
-        norm_r, (c_r, m_r, out_r) = refs[: len(norms)], refs[len(norms) :]
+        norm_r, (c_r, m_r, *arrived_r, out_r) = refs[: len(norms)], refs[len(norms) :]
         for block in range(blocks):
             total = m_r[block].astype(F32) + c_r[block].astype(F32)
             if norms:
                 summed = norm_r[0][...]
-                for piece in norm_r[1:]:
-                    arrived = piece[piece.shape[0] - EXTRA :, :].astype(F32)
-                    summed = summed + arrived[: summed.shape[0]]
+                for piece in arrived_r:
+                    rows_there = piece[piece.shape[0] - EXTRA :, :].astype(F32)
+                    summed = summed + rows_there[: summed.shape[0]]
                 spare = jnp.zeros((EXTRA - 1 - summed.shape[0], summed.shape[1]), F32)
                 total = jnp.concatenate([total[: start + 1], summed, spare], axis=0)
             out_r[block] = bf(total)
@@ -748,80 +750,61 @@
                 out_r.send(block - 1, 2)
 
     stores = [(mine.shape, LOW)]
-    near = [*norms, came]
-    return kernel_call(body, [], [counts], near, mine.size, "add_cores", [mine], stores)[0]
-
-
-def trade_layers(counts, zero, one, rows_cut):
-    rows, width = zero[0].shape
+    near, loads = [*norms, came], [mine, *arrived]
+    return kernel_call(body, [], [counts], near, mine.size, "add_cores", loads, stores)[0]
+
+
+def in_core_order(at, refs, start, size):
+    run = slice(start, start + size)
+    mine = jnp.where(at.core == 0, refs[0][run, :], refs[2][run, :]).astype(F32)
+    other = jnp.where(at.core == 0, refs[1][run, :], refs[3][run, :]).astype(F32)
+    own = at.core == 0
+    return jnp.concatenate([jnp.where(own, mine, other), jnp.where(own, other, mine)], axis=0)
+
+
+def own_row(at, refs, row):
+    return jnp.where(at.core == 0, refs[0][row : row + 1, :], refs[2][row : row + 1, :]).astype(F32)
+
+
+def place_feed(counts, shares):
+    rows, width = shares[0].shape
+    part = (rows - EXTRA) // 2
 
     def body(s, *refs):
         at = here()
-        z_refs, refs = refs[: len(zero)], refs[len(zero) :]
-        o_refs, refs = refs[: len(one)], refs[len(one) :]
-        outs = [refs[-1], *refs[:-1]]
-        sums = []
-        for group in (z_refs, o_refs):
-            total = group[0][...].astype(F32)
-            for piece in group[1:]:
-                total = total + piece[...].astype(F32)
-            sums.append(total)
-        own = at.core == 0
-        outs[0][...] = jnp.where(own, sums[0], sums[1])
-        outs[1][...] = bf(jnp.where(own, sums[1], sums[0]))
-        if rows_cut:
-            start = rows - EXTRA + 1
-            norms = [sums[0][start + 6 * i : start + 6 * (i + 1), :] for i in range(2)]
-            outs[2][...] = jnp.where(own, norms[0], norms[1])
-            outs[1][start : start + 6, :] = bf(jnp.where(own, norms[1], norms[0]))
-
-    outs, stores = [((rows, width), LOW)], [((rows, width), F32)]
-    if rows_cut:
-        outs.append(((6, width), F32))
-    got = kernel_call(
-        body, outs, [counts], [], 4 * rows * width, "trade_layers", zero + one, stores
+        refs, (row_r, con_r, exp_r) = refs[:4], refs[4:]
+        con_r[...] = in_core_order(at, refs, 0, part)
+        con_r.send()
+        exp_r[...] = in_core_order(at, refs, part, part)
+        row_r[...] = own_row(at, refs, 2 * part)
+
+    outs, stores = [((1, width), F32)], [((2 * part, width), F32)] * 2
+    return kernel_call(
+        body, outs, [counts], [], 4 * rows * width, "place_feed", shares, stores
     )
-    return [got[-1], *got[:-1]]
-
-
-def in_core_order(at, kept, came, start, size):
-    mine = kept[start : start + size, :]
-    other = came[start : start + size, :].astype(F32)
-    own = at.core == 0
-    return jnp.concatenate([jnp.where(own, mine, other), jnp.where(own, other, mine)], axis=0)
-
-
-def place_feed(counts, kept, came):
-    rows, width = kept.shape
-    part = (rows - EXTRA) // 2
-
-    def body(s, k_r, c_r, con_r, exp_r):
-        at = here()
-        con_r[...] = in_core_order(at, k_r, c_r, 0, part)
-        exp_r[...] = in_core_order(at, k_r, c_r, part, part)
-
-    stores = [((2 * part, width), F32)] * 2
-    return kernel_call(
-        body, [], [counts], [], 4 * rows * width, "place_feed", [kept, came], stores
-    )
-
-
-def place_attn(counts, kept, came, norms):
-    rows, width = kept.shape
+
+
+def place_attn(counts, shares):
+    rows, width = shares[0].shape
     part = rows - EXTRA
     local = width // 4
 
-    def body(s, n_r, k_r, c_r, norm_r, in_r, out_r):
-        norm_r[...] = n_r[...] + c_r[part + 1 : part + 7, :].astype(F32)
-        both = in_core_order(here(), k_r, c_r, 0, part)
+    def body(s, *refs):
+        at = here()
+        refs, (row_r, norm_r, in_r, out_r) = refs[:4], refs[4:]
+        both = in_core_order(at, refs, 0, part)
         for i in range(3):
             in_r[i] = both[:, i * local : (i + 1) * local]
+        in_r.send()
         out_r[...] = both[:, 3 * local :].T
-
+        row_r[...] = own_row(at, refs, part)
+        norms = refs[0][part + 1 : part + 13, :].astype(F32) + refs[1][part + 1 : part + 13, :].astype(F32)
+        norm_r[...] = jnp.where(at.core == 0, norms[:6], norms[6:])
+
+    outs = [((1, width), F32), ((6, width), F32)]
     stores = [((3, 2 * part, local), F32), ((local, 2 * part), F32)]
-    outs = [((6, width), F32)]
     return kernel_call(
-        body, outs, [counts], [norms], 4 * rows * width, "place_attn", [kept, came], stores
+        body, outs, [counts], [], 4 * rows * width, "place_attn", shares, stores
     )
 
 
@@ -1110,6 +1093,7 @@
 
     with jax.named_scope("nb"):
         shares = layer_share(1)
+    order.mark((order.last, shares))
     neighbour = types.SimpleNamespace()
     pooled_bias = jnp.zeros((1, width), F32)
     saved = [types.SimpleNamespace(), types.SimpleNamespace()]
@@ -1280,7 +1264,15 @@
             share_grads(("feed", layer), *feed_got)
             scalar_steps(exp_row, 1)
         low, norm_rows = middle_backward(
-            order.tie(counts), kept.mixed, tables, layer, low, pieces, rows_last, rows_above
+            order.tie(counts),
+            kept.mixed,
+            tables,
+            layer,
+            low,
+            pieces,
+            rows_last,
+            rows_above,
+            int(few and layer == 0),
         )
         residual = low
         order.mark(low)
@@ -1288,7 +1280,7 @@
         with jax.named_scope("ag4"):
             grads = gather(low, True)
         add_waiting()
-        reduce_summed(grads[1:])
+        reduce_summed(grads[1] if layer == 0 else grads[1:])
         *parts, d_project, in_rows = attn_backward(
             order.tie(counts),
             grads,
@@ -1297,7 +1289,6 @@
             kept.context,
             attn_w,
             layer,
-            [norm_rows] if few and layer == 0 else [],
         )
         order.mark(in_rows)
         with jax.named_scope("rs4"):
@@ -1327,13 +1318,13 @@
     if few:
         with jax.named_scope("lg"):
             both = add_cores(
-                order.tie(counts), attn_got[0], over_core(attn_got[1]), [norm_rows] + pieces[1:]
+                order.tie(counts), attn_got[0], over_core(attn_got[1]), [norm_rows], grads[1:]
             )
             order.mark(both)
             scalar_steps(both, len(scalar_hops))
             got["attn", 0] = lax.psum_scatter(both, DP, scatter_dimension=0, tiled=False)
         first_block = both
-        d_in = bf(behind(residual, first_block).astype(F32) + scattered(*pieces))
+        d_in = bf(behind(residual[: 2 * rows], first_block).astype(F32) + scattered(*pieces))
         with jax.named_scope("dx"):
             came = hop_two(d_in[rows:])
             in_order = chosen == 0
@@ -1344,21 +1335,20 @@
             other = over_core(other)
             ordered = jnp.where(first, jnp.concatenate([mine, other]), jnp.concatenate([other, mine]))
             input_grad = jnp.transpose(ordered, (1, 0, 2))
+        def shares_of(name):
+            mine = [got[name, layer] for layer in range(2)]
+            return [mine[0], over_core(mine[0]), mine[1], over_core(mine[1])]
+
         with jax.named_scope("fg"):
-            kept_feed, sent_feed = trade_layers(
-                order.tie(counts), [got["feed", 0]], [got["feed", 1]], False
-            )
-            contract, expand = place_feed(counts, kept_feed, over_core(sent_feed))
+            exp_row, contract, expand = place_feed(order.tie(counts), shares_of("feed"))
             order.mark(contract)
         with jax.named_scope("tg"):
-            kept_attn, sent_attn, norms = trade_layers(
-                order.tie(counts), [got["attn", 0]], [got["attn", 1]], True
-            )
-            norms, inproj, outproj = place_attn(counts, kept_attn, over_core(sent_attn), norms)
-        exp_row, in_row = kept_feed[kept_feed.shape[0] - EXTRA], kept_attn[kept_attn.shape[0] - EXTRA]
+            got["attn", 0] = behind(got["attn", 0], contract)
+            in_row, norms, inproj, outproj = place_attn(order.tie(counts), shares_of("attn"))
+        exp_row, in_row = exp_row[0], in_row[0]
     else:
         first_block = in_rows
-        d_in = bf(behind(residual, first_block).astype(F32) + scattered(*pieces))
+        d_in = bf(behind(residual[: 2 * rows], first_block).astype(F32) + scattered(*pieces))
         with jax.named_scope("dx"):
             came = hop_two(d_in[rows:])
             in_order = chosen == 0

time: 388 us -> 386 us (level)
  starting transfers between devices: 112 us -> 118 us
  Pallas kernels: 132 us -> 127 us
    reduce_scatter x1, waiting for transfers between devices: 6.72 us -> 0.93 us  [per_device(): lax.psum_scatter(both, DP, scatter_dimension=0, tiled=False)]
    pallas_call x41 -> x39, Pallas kernels: 132 us -> 127 us  [kernel_call(): pl.pallas_call(whole, out_shape=[jax.ShapeDtypeStruct(s, d) for s, d in o...]
    ppermute x29 -> x31, starting transfers between devices: 32.8 us -> 34.9 us  [swap(): return lax.ppermute(value, axis, [(i, i ^ distance) for i in range(count)])]
    ppermute x29 -> x31, waiting for transfers between devices: 15.8 us -> 15.4 us  [swap(): return lax.ppermute(value, axis, [(i, i ^ distance) for i in range(count)])]
  transfers between devices with their start and end apart: 108 -> 110, of which waited for: 40 -> 44; matrix products, arithmetic and copies ran while one was open for 3% -> 3% of each run, Pallas kernels for 30% -> 29%
where the time goes in v3:
time: 386 us; the launch traced here: 379 us
  Pallas kernels  127 us (33%)
  starting transfers between devices  118 us (31%)
  waiting for transfers between devices  101 us (26%)
  between operations  16 us (4%)
  local copies, waits for them, and re-layouts  14.2 us (4%)
    pallas_call x39, Pallas kernels, kernel_call(): pl.pallas_call(whole, out_shape=[jax.ShapeDtypeStruct(s, d) for s, d in o...  127 us
    ppermute x74, waiting for transfers between devices, hop(): return lax.ppermute(value, (SECTION, HEADS), route)  83.1 us
    ppermute x74, starting transfers between devices, hop(): return lax.ppermute(value, (SECTION, HEADS), route)  82.3 us
    ppermute x31, starting transfers between devices, swap(): return lax.ppermute(value, axis, [(i, i ^ distance) for i in range(count)])  34.9 us
    ppermute x31, waiting for transfers between devices, swap(): return lax.ppermute(value, axis, [(i, i ^ distance) for i in range(count)])  15.4 us
  transfers between devices with their start and end apart: 110, of which 44 were waited for; matrix products, arithmetic and copies ran while one was open for 3% of the time, Pallas kernels for 29%

profile of v3, /device:TPU:1, one launch (start us, length us, event | category | flops | bytes accessed | tf_op | source)
XLA Modules:
  0.0 379.4 jit_solution(14039187266839380686)
XLA Ops:
  7.9 2.2 constant_dynamic-slice_fusion.4
  10.3 2.7 collective-permute-start.3
  16.4 2.3 collective-permute-start.5
  20.0 4.5 %collective-permute-start.7 = (bf16[192,768]{1,0:T(8,128)(2,1)S(1)}, bf16[192,768]{1,0:T(8,128)(2,1)S(1)}, u32[]{:S(2)}, u32[]{:S(2)}) collective-permute-start(bf16[192,768]{1,0:T(8,128)(2,1)S(1)} %bitcast.88), channel_id=1, source_target_pairs={{0,16},{16,0},{1,17},{17,1},{2,18},{18,2},{3,19},{19,3},{4,20},{20... | collective-permute-start | bytes 884744 | tf_op jit(solution)/shard_map/w/ppermute | solution.py:197
  25.5 2.2 collective-permute-start.8
  27.9 2.0 select_select_fusion
  30.8 5.6 %attn_forward.4 = (f32[128,768]{1,0:T(8,128)S(1)}, bf16[128,768]{1,0:T(8,128)(2,1)}, bf16[128,768]{1,0:T(8,128)(2,1)S(1)}, bf16[128,768]{1,0:T(8,128)(2,1)S(1)},...) custom-call(s32[4,2]{1,0:T(4,128)S(1)} %copy.79.refs_0_, ...), custom_call_target="tpu_custom_call" | custom-call | flops 704643072 | bytes 4623360 | tf_op jit(solution)/shard_map/attn_forward/pallas_call | solution.py:128
  41.2 4.4 %attn_forward.5 = (f32[128,768]{1,0:T(8,128)S(1)}, bf16[128,768]{1,0:T(8,128)(2,1)S(1)}, bf16[128,768]{1,0:T(8,128)(2,1)S(1)}, bf16[128,768]{1,0:T(8,128)(2,1)S(1)}) custom-call(s32[4,2]{1,0:T(4,128)S(1)} %copy.80.refs_0_, f32[2,8,768]{2,1,0:T(8,128)S(1)} %small_table.1.refs_1_, f32[2,8,768]{2,1,0:T(8,128)S(1)} %collective-permute-done.2.refs_2_, ...), custom_call_target="tpu_custom_call" | custom-call | flops 704643072 | bytes 3050496 | tf_op jit(solution)/shard_map/attn_forward/pallas_call | solution.py:128
  49.2 2.0 collective-permute-done.14.refs_4_
  53.3 2.1 collective-permute-start.25
  55.4 2.1 collective-permute-done.16.refs_6_
  64.9 2.4 collective-permute-done.17.refs_4_.refs_7_
  70.4 4.4 %collective-permute-done.19.refs_6_.refs_9_ = bf16[128,768]{1,0:T(8,128)(2,1)S(1)} collective-permute-done((bf16[128,768]{1,0:T(8,128)(2,1)S(1)}, bf16[128,768]{1,0:T(8,128)(2,1)S(1)}, u32[]{:S(2)}, u32[]{:S(2)}) %collective-permute-start.19) | collective-permute-done | bytes 196640 | tf_op jit(solution)/shard_map/ag2/ppermute | solution.py:204
  75.6 5.3 %feed_forward.4 = (f32[128,768]{1,0:T(8,128)S(1)}, bf16[128,768]{1,0:T(8,128)(2,1)}, bf16[128,768]{1,0:T(8,128)(2,1)}, bf16[128,768]{1,0:T(8,128)(2,1)S(1)}, bf1...) custom-call(s32[4,2]{1,0:T(4,128)S(1)} %copy.83.refs_0_, f32[2,8,768]{2,1,0:T(8,128)S(1)} %small_table.1.refs_1_, ...), custom_call_target="tpu_custom_call" | custom-call | flops 1207959552 | bytes 5799936 | tf_op jit(solution)/shard_map/feed_forward/pallas_call | solution.py:128
  83.7 4.4 %feed_forward.5 = (f32[128,768]{1,0:T(8,128)S(1)}, bf16[128,768]{1,0:T(8,128)(2,1)S(1)}, bf16[128,768]{1,0:T(8,128)(2,1)}, bf16[128,768]{1,0:T(8,128)(2,1)}) custom-call(s32[4,2]{1,0:T(4,128)S(1)} %copy.84.refs_0_, f32[2,8,768]{2,1,0:T(8,128)S(1)} %small_table.1.refs_1_, f32[2,8,768]{2,1,0:T(8,128)S(1)} %collective-permute-done.2.refs_2_, ...), custom_call_target="tpu_custom_call" | custom-call | flops 1207959552 | bytes 4227072 | tf_op jit(solution)/shard_map/feed_forward/pallas_call | solution.py:128
  90.9 2.0 collective-permute-done.29.refs_6_
  98.9 2.5 collective-permute-done.32.refs_6_
  103.1 3.7 queue_units.1.refs_5_
  106.9 3.0 collective-permute-done.35.refs_7_.refs_9_
  109.9 4.9 %attn_forward.6 = (f32[128,768]{1,0:T(8,128)S(1)}, bf16[128,768]{1,0:T(8,128)(2,1)S(1)}, bf16[128,768]{1,0:T(8,128)(2,1)S(1)}, bf16[128,768]{1,0:T(8,128)(2,1)S(...) custom-call(s32[4,2]{1,0:T(4,128)S(1)} %copy.88.refs_0_, ...), custom_call_target="tpu_custom_call" | custom-call | flops 704643072 | bytes 4623360 | tf_op jit(solution)/shard_map/attn_forward/pallas_call | solution.py:128
  118.8 7.4 %collective-permute-done.36.refs_3_ = f32[1,768]{1,0:T(1,128)S(1)} collective-permute-done((f32[1,768]{1,0:T(1,128)S(1)}, f32[1,768]{1,0:T(1,128)S(1)}, u32[]{:S(2)}, u32[]{:S(2)}) %collective-permute-start.36) | collective-permute-done | bytes 3104 | tf_op jit(solution)/shard_map/nb/ppermute | solution.py:204
  126.2 4.5 %attn_forward.7 = (f32[128,768]{1,0:T(8,128)S(1)}, bf16[128,768]{1,0:T(8,128)(2,1)S(1)}) custom-call(s32[4,2]{1,0:T(4,128)S(1)} %copy.89.refs_0_, f32[2,8,768]{2,1,0:T(8,128)S(1)} %small_table.1.refs_1_, f32[2,8,768]{2,1,0:T(8,128)S(1)} %collective-permute-done.2.refs_2_, f32[1,768]{1,0:T(1,128)S(1)} %collective-permute-done.36.refs_3_, ...), custom_call_target="tpu_custom_call" | custom-call | flops 704643072 | bytes 3443712 | tf_op jit(solution)/shard_map/attn_forward/pallas_call | solution.py:128
  134.0 2.1 collective-permute-start.44
  138.3 4.7 %collective-permute-start.47 = (bf16[128,768]{1,0:T(8,128)(2,1)S(1)}, bf16[128,768]{1,0:T(8,128)(2,1)S(1)}, u32[]{:S(2)}, u32[]{:S(2)}) collective-permute-start(bf16[128,768]{1,0:T(8,128)(2,1)S(1)} %norm_middle.7.refs_3_.refs_7_), channel_id=1, source_target_pairs={{0,2},{1,3},{2,0},{3,1},{16,17},{17,16},{18,19},{19,18},{4,6},{5,7... | collective-permute-start | bytes 589832 | tf_op jit(solution)/shard_map/ag2/ppermute | solution.py:204
  143.9 5.4 %collective-permute-start.48 = (bf16[128,768]{1,0:T(8,128)(2,1)S(1)}, bf16[128,768]{1,0:T(8,128)(2,1)S(1)}, u32[]{:S(2)}, u32[]{:S(2)}) collective-permute-start(bf16[128,768]{1,0:T(8,128)(2,1)S(1)} %norm_middle.7.refs_3_.refs_7_), channel_id=1, source_target_pairs={{0,3},{1,2},{2,1},{3,0},{16,19},{17,18},{18,17},{19,16},{4,7},{5,6... | collective-permute-start | bytes 589832 | tf_op jit(solution)/shard_map/ag2/ppermute | solution.py:204
  149.4 5.3 %feed_forward.6 = (f32[128,768]{1,0:T(8,128)S(1)}, bf16[128,768]{1,0:T(8,128)(2,1)}, bf16[128,768]{1,0:T(8,128)(2,1)S(1)}, bf16[128,768]{1,0:T(8,128)(2,1)S(1)},...) custom-call(s32[4,2]{1,0:T(4,128)S(1)} %copy.92.refs_0_, f32[2,8,768]{2,1,0:T(8,128)S(1)} %small_table.1.refs_1_, ...), custom_call_target="tpu_custom_call" | custom-call | flops 1207959552 | bytes 5799936 | tf_op jit(solution)/shard_map/feed_forward/pallas_call | solution.py:128
  158.0 3.7 feed_forward.7
  163.3 3.2 collective-permute-done.49.refs_4_
  169.7 2.4 collective-permute-done.55.refs_6_
  176.2 4.0 %collective-permute-start.58 = (bf16[3,768]{1,0:T(4,128)(2,1)S(1)}, bf16[3,768]{1,0:T(4,128)(2,1)S(1)}, u32[]{:S(2)}, u32[]{:S(2)}) collective-permute-start(bf16[3,768]{1,0:T(4,128)(2,1)S(1)} %unit_packet.1.refs_1_), channel_id=1, source_target_pairs={{0,8},{4,12},{8,0},{12,4},{1,9},{5,13},{9,1},{13,5},{2,10},{6,14},... | collective-permute-start | bytes 13832 | tf_op jit(solution)/shard_map/loss/ppermute | solution.py:197
  181.5 3.0 collective-permute-done.59.refs_4_
  184.5 2.8 queue_scores.1
  187.4 2.4 collective-permute-done.60.refs_9_
  190.0 2.4 collective-permute-done.61.refs_5_
  206.4 6.3 %collective-permute-done.68.refs_4_.refs_5_ = bf16[128,768]{1,0:T(8,128)(2,1)S(1)} collective-permute-done((bf16[128,768]{1,0:T(8,128)(2,1)S(1)}, bf16[128,768]{1,0:T(8,128)(2,1)S(1)}, u32[]{:S(2)}, u32[]{:S(2)}) %collective-permute-start.68) | collective-permute-done | bytes 196640 | tf_op jit(solution)/shard_map/ag3/ppermute | solution.py:204
  212.6 4.9 %feed_backward.2 = (bf16[128,768]{1,0:T(8,128)(2,1)S(1)}, bf16[128,768]{1,0:T(8,128)(2,1)S(1)}, bf16[128,768]{1,0:T(8,128)(2,1)S(1)}, f32[1,768]{1,0:T(1,128)S(1...) custom-call(s32[4,2]{1,0:T(4,128)S(1)} %copy.100.refs_0_, ...), custom_call_target="tpu_custom_call" | custom-call | flops 1207959552 | bytes 5704704 | tf_op jit(solution)/shard_map/feed_backward/pallas_call | solution.py:128
  217.7 2.0 collective-permute-start.71
  222.4 5.7 %feed_weights.2 = (bf16[4,208,768]{2,1,0:T(8,128)(2,1)S(1)}, bf16[4,208,768]{2,1,0:T(8,128)(2,1)}) custom-call(s32[4,2]{1,0:T(4,128)S(1)} %copy.101.refs_0_, f32[1,768]{1,0:T(1,128)S(1)} %get-tuple-element.244.refs_1_, bf16[128,768]{1,0:T(8,128)(2,1)} %copy-done.12, bf16[128,768]{1,0:T(8,128)(2,1)} %copy-done.33, bf16[128,768]{1,0:T(8,128)(2,1)} %copy-done.34, ...), custom_call_target="tpu_custom_call" | custom-call | flops 1207959552 | bytes 5704704 | tf_op jit(solution)/shard_map/feed_weights/pallas_call | solution.py:128
  229.8 2.2 middle_backward.2
  235.3 3.1 add_cores.4
  239.9 4.6 %collective-permute-done.76.refs_4_.refs_5_ = bf16[128,768]{1,0:T(8,128)(2,1)S(1)} collective-permute-done((bf16[128,768]{1,0:T(8,128)(2,1)S(1)}, bf16[128,768]{1,0:T(8,128)(2,1)S(1)}, u32[]{:S(2)}, u32[]{:S(2)}) %collective-permute-start.76) | collective-permute-done | bytes 196640 | tf_op jit(solution)/shard_map/ag4/ppermute | solution.py:204
  244.9 6.5 %attn_backward.2 = (bf16[128,768]{1,0:T(8,128)(2,1)S(1)}, bf16[128,768]{1,0:T(8,128)(2,1)S(1)}, bf16[128,768]{1,0:T(8,128)(2,1)S(1)}, f32[2,768]{1,0:T(2,128)S(1...) custom-call(s32[4,2]{1,0:T(4,128)S(1)} %copy.104.refs_0_, ...), custom_call_target="tpu_custom_call" | custom-call | flops 805306368 | bytes 5117952 | tf_op jit(solution)/shard_map/attn_backward/pallas_call | solution.py:128
  255.0 4.8 %attn_weights.2 = (bf16[4,112,768]{2,1,0:T(8,128)(2,1)S(1)}, bf16[4,112,768]{2,1,0:T(8,128)(2,1)}) custom-call(s32[4,2]{1,0:T(4,128)S(1)} %copy.105.refs_0_, f32[2,768]{1,0:T(2,128)S(1)} %get-tuple-element.265.refs_1_, bf16[128,768]{1,0:T(8,128)(2,1)} %copy-done.6, bf16[128,768]{1,0:T(8,128)(2,1)} %copy-done.14, bf16[128,768]{1,0:T(8,128)(2,1)} %copy-done.15, ...), custom_call_target="tpu_custom_call" | custom-call | flops 603979776 | bytes 3741696 | tf_op jit(solution)/shard_map/attn_weights/pallas_call | solution.py:128
  259.9 3.8 %collective-permute-done.80.refs_6_ = bf16[128,768]{1,0:T(8,128)(2,1)S(1)} collective-permute-done((bf16[128,768]{1,0:T(8,128)(2,1)S(1)}, bf16[128,768]{1,0:T(8,128)(2,1)S(1)}, u32[]{:S(2)}, u32[]{:S(2)}) %collective-permute-start.80) | collective-permute-done | bytes 196640 | tf_op jit(solution)/shard_map/rs4/ppermute | solution.py:204
  263.7 2.2 last_backward.3
  269.3 2.6 add_cores.5
  273.9 4.6 %collective-permute-done.84.refs_4_.refs_5_ = bf16[128,768]{1,0:T(8,128)(2,1)S(1)} collective-permute-done((bf16[128,768]{1,0:T(8,128)(2,1)S(1)}, bf16[128,768]{1,0:T(8,128)(2,1)S(1)}, u32[]{:S(2)}, u32[]{:S(2)}) %collective-permute-start.84) | collective-permute-done | bytes 196640 | tf_op jit(solution)/shard_map/ag3/ppermute | solution.py:204
  278.6 4.9 %feed_backward.3 = (bf16[128,768]{1,0:T(8,128)(2,1)S(1)}, bf16[128,768]{1,0:T(8,128)(2,1)S(1)}, bf16[128,768]{1,0:T(8,128)(2,1)S(1)}, f32[1,768]{1,0:T(1,128)S(1...) custom-call(s32[4,2]{1,0:T(4,128)S(1)} %copy.108.refs_0_, ...), custom_call_target="tpu_custom_call" | custom-call | flops 1207959552 | bytes 5704704 | tf_op jit(solution)/shard_map/feed_backward/pallas_call | solution.py:128
  287.7 5.8 %feed_weights.3 = (bf16[4,208,768]{2,1,0:T(8,128)(2,1)S(1)}, bf16[4,208,768]{2,1,0:T(8,128)(2,1)}) custom-call(s32[4,2]{1,0:T(4,128)S(1)} %copy.109.refs_0_, f32[1,768]{1,0:T(1,128)S(1)} %get-tuple-element.282.refs_1_, bf16[128,768]{1,0:T(8,128)(2,1)} %copy-done.17, bf16[128,768]{1,0:T(8,128)(2,1)} %copy-done.30, bf16[128,768]{1,0:T(8,128)(2,1)} %copy-done.31, ...), custom_call_target="tpu_custom_call" | custom-call | flops 1207959552 | bytes 5704704 | tf_op jit(solution)/shard_map/feed_weights/pallas_call | solution.py:128
  293.6 2.3 collective-permute-done.88.refs_8_
  295.9 2.2 middle_backward.3
  301.3 3.1 add_cores.6
  309.3 2.2 collective-permute-done.91.refs_3_.refs_4_.refs_5_
  311.5 3.4 collective-permute-done.92.refs_4_.refs_5_.refs_6_
  314.9 6.7 %attn_backward.3 = (bf16[128,768]{1,0:T(8,128)(2,1)S(1)}, bf16[128,768]{1,0:T(8,128)(2,1)S(1)}, bf16[128,768]{1,0:T(8,128)(2,1)S(1)}, f32[2,768]{1,0:T(2,128)S(1...) custom-call(s32[4,2]{1,0:T(4,128)S(1)} %copy.112.refs_0_, bf16[144,768]{1,0:T(8,128)(2,1)S(1)} %get-tuple-element.296.refs_1_.refs_2_, ...), custom_call_target="tpu_custom_call" | custom-call | flops 805306368 | bytes 5216256 | tf_op jit(solution)/shard_map/attn_backward/pallas_call | solution.py:128
  321.7 4.7 %attn_weights.3 = (bf16[4,112,768]{2,1,0:T(8,128)(2,1)S(1)}, bf16[4,112,768]{2,1,0:T(8,128)(2,1)}) custom-call(s32[4,2]{1,0:T(4,128)S(1)} %copy.113.refs_0_, f32[2,768]{1,0:T(2,128)S(1)} %get-tuple-element.304.refs_1_, bf16[144,768]{1,0:T(8,128)(2,1)} %copy-done.4, bf16[144,768]{1,0:T(8,128)(2,1)} %copy-done.1, bf16[144,768]{1,0:T(8,128)(2,1)} %copy-done.2, ...), custom_call_target="tpu_custom_call" | custom-call | flops 603979776 | bytes 3840000 | tf_op jit(solution)/shard_map/attn_weights/pallas_call | solution.py:128
  326.5 5.2 %collective-permute-start.94 = (bf16[4,112,768]{2,1,0:T(8,128)(2,1)S(1)}, bf16[4,112,768]{2,1,0:T(8,128)(2,1)S(1)}, u32[]{:S(2)}, u32[]{:S(2)}) collective-permute-start(bf16[4,112,768]{2,1,0:T(8,128)(2,1)S(1)} %get-tuple-element.311), channel_id=1, source_target_pairs={{0,16},{16,0},{1,17},{17,1},{2,18},{18,2},{3,19},{19,3},{4,20},{20... | collective-permute-start | bytes 2064392 | tf_op jit(solution)/shard_map/lg/ppermute | solution.py:197
  331.7 3.1 collective-permute-done.93
  334.9 2.8 add_cores.7
  342.9 2.2 collective-permute-done.97
  345.1 5.0 %collective-permute-done.98 = bf16[128,768]{1,0:T(8,128)(2,1)S(1)} collective-permute-done((bf16[128,768]{1,0:T(8,128)(2,1)S(1)}, bf16[128,768]{1,0:T(8,128)(2,1)S(1)}, u32[]{:S(2)}, u32[]{:S(2)}) %collective-permute-start.98) | collective-permute-done | bytes 196640 | tf_op jit(solution)/shard_map/rs4/ppermute | solution.py:204
  357.8 3.0 place_feed.1
  361.7 3.0 collective-permute-start.103
  367.7 2.8 place_attn.1
  (394 shorter events, 129.3 us)
Async XLA Ops:
  7.2 119.0 %all-gather.2.cloned.1.call-start = ((), (), s32[]{:S(2)}) async-start(), calls=%async_computation.4 | async-start | bytes 1474560 | tf_op jit(solution)/shard_map/nb/all_gather | solution.py:1137
  7.2 20.4 %collective-permute-start = (bf16[576,768]{1,0:T(8,128)(2,1)}, bf16[576,768]{1,0:T(8,128)(2,1)S(1)}, u32[]{:S(2)}, u32[]{:S(2)}) collective-permute-start(bf16[576,768]{1,0:T(8,128)(2,1)} %bitcast.80), channel_id=1, source_target_pairs={{0,16},{16,0},{1,17},{17,1},{2,18},{18,2},{3,19},{19,3},{4,20},{20... | collective-permute-start | bytes 2654216 | tf_op jit(solution)/shard_map/w/ppermute | solution.py:197
  7.3 18.1 %collective-permute-start.1 = (bf16[192,768]{1,0:T(8,128)(2,1)}, bf16[192,768]{1,0:T(8,128)(2,1)}, u32[]{:S(2)}, u32[]{:S(2)}) collective-permute-start(bf16[192,768]{1,0:T(8,128)(2,1)} %bitcast.89), channel_id=1, source_target_pairs={{0,16},{16,0},{1,17},{17,1},{2,18},{18,2},{3,19},{19,3},{4,20},{20... | collective-permute-start | bytes 884744 | tf_op jit(solution)/shard_map/w/ppermute | solution.py:197
  7.8 22.3 %collective-permute-start.6 = (bf16[576,768]{1,0:T(8,128)(2,1)}, bf16[576,768]{1,0:T(8,128)(2,1)}, u32[]{:S(2)}, u32[]{:S(2)}) collective-permute-start(bf16[576,768]{1,0:T(8,128)(2,1)} %bitcast.75), channel_id=1, source_target_pairs={{0,16},{16,0},{1,17},{17,1},{2,18},{18,2},{3,19},{19,3},{4,20},{20... | collective-permute-start | bytes 2654216 | tf_op jit(solution)/shard_map/w/ppermute | solution.py:197
  16.4 8.5 %collective-permute-start.5 = (bf16[2,64,768]{2,1,0:T(8,128)(2,1)S(1)}, bf16[2,64,768]{2,1,0:T(8,128)(2,1)S(1)}, u32[]{:S(2)}, u32[]{:S(2)}) collective-permute-start(bf16[2,64,768]{2,1,0:T(8,128)(2,1)S(1)} %pad_maximum_fusion.1.refs_4_.refs_7_.refs_6_), channel_id=1, source_target_pairs={{0,3},{1,2},{2,1},{3,0},{16,19},{17,18},{18,17},{19,16},{4,7},{5,6... | collective-permute-start | bytes 589832 | tf_op jit(solution)/shard_map/ag0/ppermute | solution.py:204
  20.0 10.1 %collective-permute-start.7 = (bf16[192,768]{1,0:T(8,128)(2,1)S(1)}, bf16[192,768]{1,0:T(8,128)(2,1)S(1)}, u32[]{:S(2)}, u32[]{:S(2)}) collective-permute-start(bf16[192,768]{1,0:T(8,128)(2,1)S(1)} %bitcast.88), channel_id=1, source_target_pairs={{0,16},{16,0},{1,17},{17,1},{2,18},{18,2},{3,19},{19,3},{4,20},{20... | collective-permute-start | bytes 884744 | tf_op jit(solution)/shard_map/w/ppermute | solution.py:197
  24.9 13.3 %collective-permute-start.10 = (bf16[2,64,768]{2,1,0:T(8,128)(2,1)S(1)}, bf16[2,64,768]{2,1,0:T(8,128)(2,1)S(1)}, u32[]{:S(2)}, u32[]{:S(2)}) collective-permute-start(bf16[2,64,768]{2,1,0:T(8,128)(2,1)S(1)} %pad_maximum_fusion.refs_4_.refs_7_), channel_id=1, source_target_pairs={{0,3},{1,2},{2,1},{3,0},{16,19},{17,18},{18,17},{19,16},{4,7},{5,6... | collective-permute-start | bytes 589832 | tf_op jit(solution)/shard_map/ag0/ppermute | solution.py:204
  25.5 13.7 %collective-permute-start.8 = (bf16[2,64,768]{2,1,0:T(8,128)(2,1)S(1)}, bf16[2,64,768]{2,1,0:T(8,128)(2,1)S(1)}, u32[]{:S(2)}, u32[]{:S(2)}) collective-permute-start(bf16[2,64,768]{2,1,0:T(8,128)(2,1)S(1)} %pad_maximum_fusion.refs_4_.refs_7_), channel_id=1, source_target_pairs={{0,1},{1,0},{2,3},{3,2},{16,18},{17,19},{18,16},{19,17},{4,5},{5,4... | collective-permute-start | bytes 589832 | tf_op jit(solution)/shard_map/ag0/ppermute | solution.py:204
  27.6 13.4 %collective-permute-start.9 = (bf16[2,64,768]{2,1,0:T(8,128)(2,1)S(1)}, bf16[2,64,768]{2,1,0:T(8,128)(2,1)S(1)}, u32[]{:S(2)}, u32[]{:S(2)}) collective-permute-start(bf16[2,64,768]{2,1,0:T(8,128)(2,1)S(1)} %pad_maximum_fusion.refs_4_.refs_7_), channel_id=1, source_target_pairs={{0,2},{1,3},{2,0},{3,1},{16,17},{17,16},{18,19},{19,18},{4,6},{5,7... | collective-permute-start | bytes 589832 | tf_op jit(solution)/shard_map/ag0/ppermute | solution.py:204
  36.4 9.2 %collective-permute-start.11 = (bf16[128,768]{1,0:T(8,128)(2,1)}, bf16[128,768]{1,0:T(8,128)(2,1)S(1)}, u32[]{:S(2)}, u32[]{:S(2)}) collective-permute-start(bf16[128,768]{1,0:T(8,128)(2,1)} %get-tuple-element.177), channel_id=1, source_target_pairs={{0,1},{1,0},{2,3},{3,2},{16,18},{17,19},{18,16},{19,17},{4,5},{5,4... | collective-permute-start | bytes 589832 | tf_op jit(solution)/shard_map/rs1/ppermute | solution.py:204
  37.9 9.1 %collective-permute-start.12 = (bf16[128,768]{1,0:T(8,128)(2,1)S(1)}, bf16[128,768]{1,0:T(8,128)(2,1)S(1)}, u32[]{:S(2)}, u32[]{:S(2)}) collective-permute-start(bf16[128,768]{1,0:T(8,128)(2,1)S(1)} %get-tuple-element.178), channel_id=1, source_target_pairs={{0,2},{1,3},{2,0},{3,1},{16,17},{17,16},{18,19},{19,18},{4,6},{5,7... | collective-permute-start | bytes 589832 | tf_op jit(solution)/shard_map/rs1/ppermute | solution.py:204
  38.2 9.2 %collective-permute-start.13 = (bf16[128,768]{1,0:T(8,128)(2,1)S(1)}, bf16[128,768]{1,0:T(8,128)(2,1)S(1)}, u32[]{:S(2)}, u32[]{:S(2)}) collective-permute-start(bf16[128,768]{1,0:T(8,128)(2,1)S(1)} %get-tuple-element.179), channel_id=1, source_target_pairs={{0,3},{1,2},{2,1},{3,0},{16,19},{17,18},{18,17},{19,16},{4,7},{5,6... | collective-permute-start | bytes 589832 | tf_op jit(solution)/shard_map/rs1/ppermute | solution.py:204
  39.2 23.5 %collective-permute-start.20 = (bf16[768,768]{1,0:T(8,128)(2,1)}, bf16[768,768]{1,0:T(8,128)(2,1)}, u32[]{:S(2)}, u32[]{:S(2)}) collective-permute-start(bf16[768,768]{1,0:T(8,128)(2,1)} %bitcast.26.refs_7_.refs_6_), channel_id=1, source_target_pairs={{0,16},{16,0},{1,17},{17,1},{2,18},{18,2},{3,19},{19,3},{4,20},{20... | collective-permute-start | bytes 3538952 | tf_op jit(solution)/shard_map/w/ppermute | solution.py:197
  41.1 22.5 %collective-permute-start.21 = (bf16[768,768]{1,0:T(8,128)(2,1)}, bf16[768,768]{1,0:T(8,128)(2,1)}, u32[]{:S(2)}, u32[]{:S(2)}) collective-permute-start(bf16[768,768]{1,0:T(8,128)(2,1)} %bitcast.27.refs_8_.refs_7_), channel_id=1, source_target_pairs={{0,16},{16,0},{1,17},{17,1},{2,18},{18,2},{3,19},{19,3},{4,20},{20... | collective-permute-start | bytes 3538952 | tf_op jit(solution)/shard_map/w/ppermute | solution.py:197
  47.4 10.0 %collective-permute-start.16 = (bf16[128,768]{1,0:T(8,128)(2,1)S(1)}, bf16[128,768]{1,0:T(8,128)(2,1)S(1)}, u32[]{:S(2)}, u32[]{:S(2)}) collective-permute-start(bf16[128,768]{1,0:T(8,128)(2,1)S(1)} %get-tuple-element.184), channel_id=1, source_target_pairs={{0,3},{1,2},{2,1},{3,0},{16,19},{17,18},{18,17},{19,16},{4,7},{5,6... | collective-permute-start | bytes 589832 | tf_op jit(solution)/shard_map/rs1/ppermute | solution.py:204
  51.2 10.5 %collective-permute-start.38 = (bf16[192,768]{1,0:T(8,128)(2,1)}, bf16[192,768]{1,0:T(8,128)(2,1)}, u32[]{:S(2)}, u32[]{:S(2)}) collective-permute-start(bf16[192,768]{1,0:T(8,128)(2,1)} %select_select_fusion), channel_id=1, source_target_pairs={{0,2},{1,3},{2,0},{3,1},{16,17},{17,16},{18,19},{19,18},{4,6},{5,7... | collective-permute-start | bytes 884744 | tf_op jit(solution)/shard_map/nb/ppermute | solution.py:204
  53.3 27.8 %collective-permute-start.25 = (bf16[768,768]{1,0:T(8,128)(2,1)}, bf16[768,768]{1,0:T(8,128)(2,1)}, u32[]{:S(2)}, u32[]{:S(2)}) collective-permute-start(bf16[768,768]{1,0:T(8,128)(2,1)} %bitcast.28.refs_7_), channel_id=1, source_target_pairs={{0,16},{16,0},{1,17},{17,1},{2,18},{18,2},{3,19},{19,3},{4,20},{20... | collective-permute-start | bytes 3538952 | tf_op jit(solution)/shard_map/w/ppermute | solution.py:197
  57.5 24.2 %collective-permute-start.26 = (bf16[768,768]{1,0:T(8,128)(2,1)}, bf16[768,768]{1,0:T(8,128)(2,1)}, u32[]{:S(2)}, u32[]{:S(2)}) collective-permute-start(bf16[768,768]{1,0:T(8,128)(2,1)} %bitcast.29.refs_8_), channel_id=1, source_target_pairs={{0,16},{16,0},{1,17},{17,1},{2,18},{18,2},{3,19},{19,3},{4,20},{20... | collective-permute-start | bytes 3538952 | tf_op jit(solution)/shard_map/w/ppermute | solution.py:197
  61.7 225.9 %reduce-scatter.5.cloned.1.call-start = ((), (), s32[]{:S(2)}) async-start(), calls=%async_computation.5 | async-start | bytes 1597440 | tf_op jit(solution)/shard_map/rg/reduce_scatter | solution.py:1230
  63.6 11.1 %collective-permute-start.19 = (bf16[128,768]{1,0:T(8,128)(2,1)S(1)}, bf16[128,768]{1,0:T(8,128)(2,1)S(1)}, u32[]{:S(2)}, u32[]{:S(2)}) collective-permute-start(bf16[128,768]{1,0:T(8,128)(2,1)S(1)} %get-tuple-element.180.refs_3_.refs_7_.refs_6_), channel_id=1, source_target_pairs={{0,3},{1,2},{2,1},{3,0},{16,19},{17,18},{18,17},{19,16},{4,7},{5,6... | collective-permute-start | bytes 589832 | tf_op jit(solution)/shard_map/ag2/ppermute | solution.py:204
  67.3 15.5 %collective-permute-start.22 = (bf16[128,768]{1,0:T(8,128)(2,1)S(1)}, bf16[128,768]{1,0:T(8,128)(2,1)S(1)}, u32[]{:S(2)}, u32[]{:S(2)}) collective-permute-start(bf16[128,768]{1,0:T(8,128)(2,1)S(1)} %norm_middle.5.refs_3_.refs_7_), channel_id=1, source_target_pairs={{0,1},{1,0},{2,3},{3,2},{16,18},{17,19},{18,16},{19,17},{4,5},{5,4... | collective-permute-start | bytes 589832 | tf_op jit(solution)/shard_map/ag2/ppermute | solution.py:204
  69.4 14.2 %collective-permute-start.23 = (bf16[128,768]{1,0:T(8,128)(2,1)S(1)}, bf16[128,768]{1,0:T(8,128)(2,1)S(1)}, u32[]{:S(2)}, u32[]{:S(2)}) collective-permute-start(bf16[128,768]{1,0:T(8,128)(2,1)S(1)} %norm_middle.5.refs_3_.refs_7_), channel_id=1, source_target_pairs={{0,2},{1,3},{2,0},{3,1},{16,17},{17,16},{18,19},{19,18},{4,6},{5,7... | collective-permute-start | bytes 589832 | tf_op jit(solution)/shard_map/ag2/ppermute | solution.py:204
  74.7 8.9 %collective-permute-start.24 = (bf16[128,768]{1,0:T(8,128)(2,1)S(1)}, bf16[128,768]{1,0:T(8,128)(2,1)S(1)}, u32[]{:S(2)}, u32[]{:S(2)}) collective-permute-start(bf16[128,768]{1,0:T(8,128)(2,1)S(1)} %norm_middle.5.refs_3_.refs_7_), channel_id=1, source_target_pairs={{0,3},{1,2},{2,1},{3,0},{16,19},{17,18},{18,17},{19,16},{4,7},{5,6... | collective-permute-start | bytes 589832 | tf_op jit(solution)/shard_map/ag2/ppermute | solution.py:204
  81.0 9.0 %collective-permute-start.27 = (bf16[128,768]{1,0:T(8,128)(2,1)}, bf16[128,768]{1,0:T(8,128)(2,1)S(1)}, u32[]{:S(2)}, u32[]{:S(2)}) collective-permute-start(bf16[128,768]{1,0:T(8,128)(2,1)} %get-tuple-element.190), channel_id=1, source_target_pairs={{0,1},{1,0},{2,3},{3,2},{16,18},{17,19},{18,16},{19,17},{4,5},{5,4... | collective-permute-start | bytes 589832 | tf_op jit(solution)/shard_map/rs2/ppermute | solution.py:204
  81.7 9.2 %collective-permute-start.28 = (bf16[128,768]{1,0:T(8,128)(2,1)}, bf16[128,768]{1,0:T(8,128)(2,1)S(1)}, u32[]{:S(2)}, u32[]{:S(2)}) collective-permute-start(bf16[128,768]{1,0:T(8,128)(2,1)} %get-tuple-element.191), channel_id=1, source_target_pairs={{0,2},{1,3},{2,0},{3,1},{16,17},{17,16},{18,19},{19,18},{4,6},{5,7... | collective-permute-start | bytes 589832 | tf_op jit(solution)/shard_map/rs2/ppermute | solution.py:204
  82.9 10.1 %collective-permute-start.29 = (bf16[128,768]{1,0:T(8,128)(2,1)S(1)}, bf16[128,768]{1,0:T(8,128)(2,1)S(1)}, u32[]{:S(2)}, u32[]{:S(2)}) collective-permute-start(bf16[128,768]{1,0:T(8,128)(2,1)S(1)} %get-tuple-element.192), channel_id=1, source_target_pairs={{0,3},{1,2},{2,1},{3,0},{16,19},{17,18},{18,17},{19,16},{4,7},{5,6... | collective-permute-start | bytes 589832 | tf_op jit(solution)/shard_map/rs2/ppermute | solution.py:204
  88.1 8.9 %collective-permute-start.30 = (bf16[128,768]{1,0:T(8,128)(2,1)S(1)}, bf16[128,768]{1,0:T(8,128)(2,1)S(1)}, u32[]{:S(2)}, u32[]{:S(2)}) collective-permute-start(bf16[128,768]{1,0:T(8,128)(2,1)S(1)} %get-tuple-element.195), channel_id=1, source_target_pairs={{0,1},{1,0},{2,3},{3,2},{16,18},{17,19},{18,16},{19,17},{4,5},{5,4... | collective-permute-start | bytes 589832 | tf_op jit(solution)/shard_map/rs2/ppermute | solution.py:204
  88.9 10.0 %collective-permute-start.31 = (bf16[128,768]{1,0:T(8,128)(2,1)}, bf16[128,768]{1,0:T(8,128)(2,1)S(1)}, u32[]{:S(2)}, u32[]{:S(2)}) collective-permute-start(bf16[128,768]{1,0:T(8,128)(2,1)} %get-tuple-element.196), channel_id=1, source_target_pairs={{0,2},{1,3},{2,0},{3,1},{16,17},{17,16},{18,19},{19,18},{4,6},{5,7... | collective-permute-start | bytes 589832 | tf_op jit(solution)/shard_map/rs2/ppermute | solution.py:204
  90.0 11.4 %collective-permute-start.32 = (bf16[128,768]{1,0:T(8,128)(2,1)}, bf16[128,768]{1,0:T(8,128)(2,1)S(1)}, u32[]{:S(2)}, u32[]{:S(2)}) collective-permute-start(bf16[128,768]{1,0:T(8,128)(2,1)} %get-tuple-element.197), channel_id=1, source_target_pairs={{0,3},{1,2},{2,1},{3,0},{16,19},{17,18},{18,17},{19,16},{4,7},{5,6... | collective-permute-start | bytes 589832 | tf_op jit(solution)/shard_map/rs2/ppermute | solution.py:204
  94.5 12.3 %collective-permute-start.33 = (bf16[128,768]{1,0:T(8,128)(2,1)S(1)}, bf16[128,768]{1,0:T(8,128)(2,1)S(1)}, u32[]{:S(2)}, u32[]{:S(2)}) collective-permute-start(bf16[128,768]{1,0:T(8,128)(2,1)S(1)} %get-tuple-element.193.refs_4_.refs_7_.refs_6_), channel_id=1, source_target_pairs={{0,1},{1,0},{2,3},{3,2},{16,18},{17,19},{18,16},{19,17},{4,5},{5,4... | collective-permute-start | bytes 589832 | tf_op jit(solution)/shard_map/ag1/ppermute | solution.py:204
  95.2 11.7 %collective-permute-start.34 = (bf16[128,768]{1,0:T(8,128)(2,1)S(1)}, bf16[128,768]{1,0:T(8,128)(2,1)S(1)}, u32[]{:S(2)}, u32[]{:S(2)}) collective-permute-start(bf16[128,768]{1,0:T(8,128)(2,1)S(1)} %get-tuple-element.193.refs_4_.refs_7_.refs_6_), channel_id=1, source_target_pairs={{0,2},{1,3},{2,0},{3,1},{16,17},{17,16},{18,19},{19,18},{4,6},{5,7... | collective-permute-start | bytes 589832 | tf_op jit(solution)/shard_map/ag1/ppermute | solution.py:204
  97.1 12.8 %collective-permute-start.35 = (bf16[128,768]{1,0:T(8,128)(2,1)S(1)}, bf16[128,768]{1,0:T(8,128)(2,1)S(1)}, u32[]{:S(2)}, u32[]{:S(2)}) collective-permute-start(bf16[128,768]{1,0:T(8,128)(2,1)S(1)} %get-tuple-element.193.refs_4_.refs_7_.refs_6_), channel_id=1, source_target_pairs={{0,3},{1,2},{2,1},{3,0},{16,19},{17,18},{18,17},{19,16},{4,7},{5,6... | collective-permute-start | bytes 589832 | tf_op jit(solution)/shard_map/ag1/ppermute | solution.py:204
  102.3 23.9 %collective-permute-start.37 = (bf16[128,768]{1,0:T(8,128)(2,1)S(1)}, bf16[128,768]{1,0:T(8,128)(2,1)S(1)}, u32[]{:S(2)}, u32[]{:S(2)}) collective-permute-start(bf16[128,768]{1,0:T(8,128)(2,1)S(1)} %norm_last.5.refs_4_.refs_5_), channel_id=1, source_target_pairs={{0,1},{1,0},{2,3},{3,2},{16,18},{17,19},{18,16},{19,17},{4,5},{5,4... | collective-permute-start | bytes 589832 | tf_op jit(solution)/shard_map/ag1/ppermute | solution.py:204
  114.9 16.2 %collective-permute-start.39 = (bf16[128,768]{1,0:T(8,128)(2,1)S(1)}, bf16[128,768]{1,0:T(8,128)(2,1)S(1)}, u32[]{:S(2)}, u32[]{:S(2)}) collective-permute-start(bf16[128,768]{1,0:T(8,128)(2,1)S(1)} %get-tuple-element.207), channel_id=1, source_target_pairs={{0,1},{1,0},{2,3},{3,2},{16,18},{17,19},{18,16},{19,17},{4,5},{5,4... | collective-permute-start | bytes 589832 | tf_op jit(solution)/shard_map/rs1/ppermute | solution.py:204
  115.5 15.5 %collective-permute-start.40 = (bf16[128,768]{1,0:T(8,128)(2,1)S(1)}, bf16[128,768]{1,0:T(8,128)(2,1)S(1)}, u32[]{:S(2)}, u32[]{:S(2)}) collective-permute-start(bf16[128,768]{1,0:T(8,128)(2,1)S(1)} %get-tuple-element.208), channel_id=1, source_target_pairs={{0,2},{1,3},{2,0},{3,1},{16,17},{17,16},{18,19},{19,18},{4,6},{5,7... | collective-permute-start | bytes 589832 | tf_op jit(solution)/shard_map/rs1/ppermute | solution.py:204
  117.4 13.7 %collective-permute-start.41 = (bf16[128,768]{1,0:T(8,128)(2,1)S(1)}, bf16[128,768]{1,0:T(8,128)(2,1)S(1)}, u32[]{:S(2)}, u32[]{:S(2)}) collective-permute-start(bf16[128,768]{1,0:T(8,128)(2,1)S(1)} %get-tuple-element.209), channel_id=1, source_target_pairs={{0,3},{1,2},{2,1},{3,0},{16,19},{17,18},{18,17},{19,16},{4,7},{5,6... | collective-permute-start | bytes 589832 | tf_op jit(solution)/shard_map/rs1/ppermute | solution.py:204
  117.6 8.6 %collective-permute-start.36 = (f32[1,768]{1,0:T(1,128)S(1)}, f32[1,768]{1,0:T(1,128)S(1)}, u32[]{:S(2)}, u32[]{:S(2)}) collective-permute-start(f32[1,768]{1,0:T(1,128)S(1)} %fusion.3), channel_id=1, source_target_pairs={{0,2},{1,3},{2,0},{3,1},{16,17},{17,16},{18,19},{19,18},{4,6},{5,7... | collective-permute-start | bytes 9224 | tf_op jit(solution)/shard_map/nb/ppermute | solution.py:204
  132.6 11.2 %collective-permute-start.43 = (bf16[128,768]{1,0:T(8,128)(2,1)S(1)}, bf16[128,768]{1,0:T(8,128)(2,1)S(1)}, u32[]{:S(2)}, u32[]{:S(2)}) collective-permute-start(bf16[128,768]{1,0:T(8,128)(2,1)S(1)} %get-tuple-element.210.refs_3_.refs_7_.refs_6_), channel_id=1, source_target_pairs={{0,1},{1,0},{2,3},{3,2},{16,18},{17,19},{18,16},{19,17},{4,5},{5,4... | collective-permute-start | bytes 589832 | tf_op jit(solution)/shard_map/ag2/ppermute | solution.py:204
  134.0 15.4 %collective-permute-start.44 = (bf16[128,768]{1,0:T(8,128)(2,1)S(1)}, bf16[128,768]{1,0:T(8,128)(2,1)S(1)}, u32[]{:S(2)}, u32[]{:S(2)}) collective-permute-start(bf16[128,768]{1,0:T(8,128)(2,1)S(1)} %get-tuple-element.210.refs_3_.refs_7_.refs_6_), channel_id=1, source_target_pairs={{0,2},{1,3},{2,0},{3,1},{16,17},{17,16},{18,19},{19,18},{4,6},{5,7... | collective-permute-start | bytes 589832 | tf_op jit(solution)/shard_map/ag2/ppermute | solution.py:204
  136.1 13.3 %collective-permute-start.45 = (bf16[128,768]{1,0:T(8,128)(2,1)S(1)}, bf16[128,768]{1,0:T(8,128)(2,1)S(1)}, u32[]{:S(2)}, u32[]{:S(2)}) collective-permute-start(bf16[128,768]{1,0:T(8,128)(2,1)S(1)} %get-tuple-element.210.refs_3_.refs_7_.refs_6_), channel_id=1, source_target_pairs={{0,3},{1,2},{2,1},{3,0},{16,19},{17,18},{18,17},{19,16},{4,7},{5,6... | collective-permute-start | bytes 589832 | tf_op jit(solution)/shard_map/ag2/ppermute | solution.py:204
  137.1 19.7 %collective-permute-start.46 = (bf16[128,768]{1,0:T(8,128)(2,1)S(1)}, bf16[128,768]{1,0:T(8,128)(2,1)S(1)}, u32[]{:S(2)}, u32[]{:S(2)}) collective-permute-start(bf16[128,768]{1,0:T(8,128)(2,1)S(1)} %norm_middle.7.refs_3_.refs_7_), channel_id=1, source_target_pairs={{0,1},{1,0},{2,3},{3,2},{16,18},{17,19},{18,16},{19,17},{4,5},{5,4... | collective-permute-start | bytes 589832 | tf_op jit(solution)/shard_map/ag2/ppermute | solution.py:204
  138.3 19.8 %collective-permute-start.47 = (bf16[128,768]{1,0:T(8,128)(2,1)S(1)}, bf16[128,768]{1,0:T(8,128)(2,1)S(1)}, u32[]{:S(2)}, u32[]{:S(2)}) collective-permute-start(bf16[128,768]{1,0:T(8,128)(2,1)S(1)} %norm_middle.7.refs_3_.refs_7_), channel_id=1, source_target_pairs={{0,2},{1,3},{2,0},{3,1},{16,17},{17,16},{18,19},{19,18},{4,6},{5,7... | collective-permute-start | bytes 589832 | tf_op jit(solution)/shard_map/ag2/ppermute | solution.py:204
  143.9 14.2 %collective-permute-start.48 = (bf16[128,768]{1,0:T(8,128)(2,1)S(1)}, bf16[128,768]{1,0:T(8,128)(2,1)S(1)}, u32[]{:S(2)}, u32[]{:S(2)}) collective-permute-start(bf16[128,768]{1,0:T(8,128)(2,1)S(1)} %norm_middle.7.refs_3_.refs_7_), channel_id=1, source_target_pairs={{0,3},{1,2},{2,1},{3,0},{16,19},{17,18},{18,17},{19,16},{4,7},{5,6... | collective-permute-start | bytes 589832 | tf_op jit(solution)/shard_map/ag2/ppermute | solution.py:204
  154.8 11.8 %collective-permute-start.49 = (bf16[128,768]{1,0:T(8,128)(2,1)}, bf16[128,768]{1,0:T(8,128)(2,1)S(1)}, u32[]{:S(2)}, u32[]{:S(2)}) collective-permute-start(bf16[128,768]{1,0:T(8,128)(2,1)} %get-tuple-element.218), channel_id=1, source_target_pairs={{0,1},{1,0},{2,3},{3,2},{16,18},{17,19},{18,16},{19,17},{4,5},{5,4... | collective-permute-start | bytes 589832 | tf_op jit(solution)/shard_map/rs2/ppermute | solution.py:204
  156.8 9.8 %collective-permute-start.50 = (bf16[128,768]{1,0:T(8,128)(2,1)S(1)}, bf16[128,768]{1,0:T(8,128)(2,1)S(1)}, u32[]{:S(2)}, u32[]{:S(2)}) collective-permute-start(bf16[128,768]{1,0:T(8,128)(2,1)S(1)} %get-tuple-element.219), channel_id=1, source_target_pairs={{0,2},{1,3},{2,0},{3,1},{16,17},{17,16},{18,19},{19,18},{4,6},{5,7... | collective-permute-start | bytes 589832 | tf_op jit(solution)/shard_map/rs2/ppermute | solution.py:204
  156.8 9.8 %collective-permute-start.51 = (bf16[128,768]{1,0:T(8,128)(2,1)S(1)}, bf16[128,768]{1,0:T(8,128)(2,1)S(1)}, u32[]{:S(2)}, u32[]{:S(2)}) collective-permute-start(bf16[128,768]{1,0:T(8,128)(2,1)S(1)} %get-tuple-element.220), channel_id=1, source_target_pairs={{0,3},{1,2},{2,1},{3,0},{16,19},{17,18},{18,17},{19,16},{4,7},{5,6... | collective-permute-start | bytes 589832 | tf_op jit(solution)/shard_map/rs2/ppermute | solution.py:204
  202.5 10.1 %collective-permute-start.68 = (bf16[128,768]{1,0:T(8,128)(2,1)S(1)}, bf16[128,768]{1,0:T(8,128)(2,1)S(1)}, u32[]{:S(2)}, u32[]{:S(2)}) collective-permute-start(bf16[128,768]{1,0:T(8,128)(2,1)S(1)} %get-tuple-element.241.refs_1_.refs_2_.refs_4_), channel_id=1, source_target_pairs={{0,3},{1,2},{2,1},{3,0},{16,19},{17,18},{18,17},{19,16},{4,7},{5,6... | collective-permute-start | bytes 589832 | tf_op jit(solution)/shard_map/ag3/ppermute | solution.py:204
  217.6 10.6 %collective-permute-start.70 = (bf16[128,768]{1,0:T(8,128)(2,1)S(1)}, bf16[128,768]{1,0:T(8,128)(2,1)S(1)}, u32[]{:S(2)}, u32[]{:S(2)}) collective-permute-start(bf16[128,768]{1,0:T(8,128)(2,1)S(1)} %get-tuple-element.252), channel_id=1, source_target_pairs={{0,1},{1,0},{2,3},{3,2},{16,18},{17,19},{18,16},{19,17},{4,5},{5,4... | collective-permute-start | bytes 589832 | tf_op jit(solution)/shard_map/rs3/ppermute | solution.py:204
  217.7 10.5 %collective-permute-start.71 = (bf16[128,768]{1,0:T(8,128)(2,1)S(1)}, bf16[128,768]{1,0:T(8,128)(2,1)S(1)}, u32[]{:S(2)}, u32[]{:S(2)}) collective-permute-start(bf16[128,768]{1,0:T(8,128)(2,1)S(1)} %get-tuple-element.253), channel_id=1, source_target_pairs={{0,2},{1,3},{2,0},{3,1},{16,17},{17,16},{18,19},{19,18},{4,6},{5,7... | collective-permute-start | bytes 589832 | tf_op jit(solution)/shard_map/rs3/ppermute | solution.py:204
  219.7 10.1 %collective-permute-start.72 = (bf16[128,768]{1,0:T(8,128)(2,1)S(1)}, bf16[128,768]{1,0:T(8,128)(2,1)S(1)}, u32[]{:S(2)}, u32[]{:S(2)}) collective-permute-start(bf16[128,768]{1,0:T(8,128)(2,1)S(1)} %get-tuple-element.254), channel_id=1, source_target_pairs={{0,3},{1,2},{2,1},{3,0},{16,19},{17,18},{18,17},{19,16},{4,7},{5,6... | collective-permute-start | bytes 589832 | tf_op jit(solution)/shard_map/rs3/ppermute | solution.py:204
  234.7 9.8 %collective-permute-start.76 = (bf16[128,768]{1,0:T(8,128)(2,1)S(1)}, bf16[128,768]{1,0:T(8,128)(2,1)S(1)}, u32[]{:S(2)}, u32[]{:S(2)}) collective-permute-start(bf16[128,768]{1,0:T(8,128)(2,1)S(1)} %get-tuple-element.257.refs_1_.refs_2_.refs_3_), channel_id=1, source_target_pairs={{0,3},{1,2},{2,1},{3,0},{16,19},{17,18},{18,17},{19,16},{4,7},{5,6... | collective-permute-start | bytes 589832 | tf_op jit(solution)/shard_map/ag4/ppermute | solution.py:204
  244.5 61.8 %reduce-scatter.7.cloned.1.call-start = ((), (), s32[]{:S(2)}) async-start(), calls=%async_computation.6 | async-start | bytes 860160 | tf_op jit(solution)/shard_map/rg/reduce_scatter | solution.py:1230
  253.7 10.0 %collective-permute-start.80 = (bf16[128,768]{1,0:T(8,128)(2,1)S(1)}, bf16[128,768]{1,0:T(8,128)(2,1)S(1)}, u32[]{:S(2)}, u32[]{:S(2)}) collective-permute-start(bf16[128,768]{1,0:T(8,128)(2,1)S(1)} %get-tuple-element.273), channel_id=1, source_target_pairs={{0,3},{1,2},{2,1},{3,0},{16,19},{17,18},{18,17},{19,16},{4,7},{5,6... | collective-permute-start | bytes 589832 | tf_op jit(solution)/shard_map/rs4/ppermute | solution.py:204
  268.8 9.8 %collective-permute-start.84 = (bf16[128,768]{1,0:T(8,128)(2,1)S(1)}, bf16[128,768]{1,0:T(8,128)(2,1)S(1)}, u32[]{:S(2)}, u32[]{:S(2)}) collective-permute-start(bf16[128,768]{1,0:T(8,128)(2,1)S(1)} %get-tuple-element.276.refs_1_.refs_2_.refs_5_), channel_id=1, source_target_pairs={{0,3},{1,2},{2,1},{3,0},{16,19},{17,18},{18,17},{19,16},{4,7},{5,6... | collective-permute-start | bytes 589832 | tf_op jit(solution)/shard_map/ag3/ppermute | solution.py:204
  283.5 10.0 %collective-permute-start.86 = (bf16[128,768]{1,0:T(8,128)(2,1)S(1)}, bf16[128,768]{1,0:T(8,128)(2,1)S(1)}, u32[]{:S(2)}, u32[]{:S(2)}) collective-permute-start(bf16[128,768]{1,0:T(8,128)(2,1)S(1)} %get-tuple-element.291), channel_id=1, source_target_pairs={{0,1},{1,0},{2,3},{3,2},{16,18},{17,19},{18,16},{19,17},{4,5},{5,4... | collective-permute-start | bytes 589832 | tf_op jit(solution)/shard_map/rs3/ppermute | solution.py:204
  284.3 9.3 %collective-permute-start.87 = (bf16[128,768]{1,0:T(8,128)(2,1)S(1)}, bf16[128,768]{1,0:T(8,128)(2,1)S(1)}, u32[]{:S(2)}, u32[]{:S(2)}) collective-permute-start(bf16[128,768]{1,0:T(8,128)(2,1)S(1)} %get-tuple-element.292), channel_id=1, source_target_pairs={{0,2},{1,3},{2,0},{3,1},{16,17},{17,16},{18,19},{19,18},{4,6},{5,7... | collective-permute-start | bytes 589832 | tf_op jit(solution)/shard_map/rs3/ppermute | solution.py:204
  285.7 10.2 %collective-permute-start.88 = (bf16[128,768]{1,0:T(8,128)(2,1)S(1)}, bf16[128,768]{1,0:T(8,128)(2,1)S(1)}, u32[]{:S(2)}, u32[]{:S(2)}) collective-permute-start(bf16[128,768]{1,0:T(8,128)(2,1)S(1)} %get-tuple-element.293), channel_id=1, source_target_pairs={{0,3},{1,2},{2,1},{3,0},{16,19},{17,18},{18,17},{19,16},{4,7},{5,6... | collective-permute-start | bytes 589832 | tf_op jit(solution)/shard_map/rs3/ppermute | solution.py:204
  287.6 65.1 %reduce-scatter.9.cloned.1.call-start = ((), (), s32[]{:S(2)}) async-start(), calls=%async_computation.7 | async-start | bytes 1597440 | tf_op jit(solution)/shard_map/rg/reduce_scatter | solution.py:1230
  306.4 55.3 %reduce-scatter.11.cloned.1.call-start = ((), (), s32[]{:S(2)}) async-start(), calls=%async_computation.8 | async-start | bytes 860160 | tf_op jit(solution)/shard_map/lg/reduce_scatter | solution.py:1325
  339.7 10.3 %collective-permute-start.98 = (bf16[128,768]{1,0:T(8,128)(2,1)S(1)}, bf16[128,768]{1,0:T(8,128)(2,1)S(1)}, u32[]{:S(2)}, u32[]{:S(2)}) collective-permute-start(bf16[128,768]{1,0:T(8,128)(2,1)S(1)} %get-tuple-element.317), channel_id=1, source_target_pairs={{0,3},{1,2},{2,1},{3,0},{16,19},{17,18},{18,17},{19,16},{4,7},{5,6... | collective-permute-start | bytes 589832 | tf_op jit(solution)/shard_map/rs4/ppermute | solution.py:204
  340.5 15.8 %collective-permute-start.102 = (bf16[208,768]{1,0:T(8,128)(2,1)S(1)}, bf16[208,768]{1,0:T(8,128)(2,1)S(1)}, u32[]{:S(2)}, u32[]{:S(2)}) collective-permute-start(bf16[208,768]{1,0:T(8,128)(2,1)S(1)} %bitcast.97), channel_id=1, source_target_pairs={{0,16},{16,0},{1,17},{17,1},{2,18},{18,2},{3,19},{19,3},{4,20},{20... | collective-permute-start | bytes 958472 | tf_op jit(solution)/shard_map/fg/ppermute | solution.py:197
  342.2 9.2 %collective-permute-start.95 = (f32[1,128]{1,0:T(1,128)S(1)}, f32[1,128]{1,0:T(1,128)S(1)}, u32[]{:S(2)}, u32[]{:S(2)}) collective-permute-start(f32[1,128]{1,0:T(1,128)S(1)} %add.91), channel_id=1, source_target_pairs={{0,8},{4,12},{8,0},{12,4},{1,9},{5,13},{9,1},{13,5},{2,10},{6,14},... | collective-permute-start | bytes 1544 | tf_op jit(solution)/shard_map/lg/sc/ppermute | solution.py:197
  354.2 10.5 %collective-permute-start.100 = (bf16[2,64,384]{2,1,0:T(8,128)(2,1)S(1)}, bf16[2,64,384]{2,1,0:T(8,128)(2,1)S(1)}, u32[]{:S(2)}, u32[]{:S(2)}) collective-permute-start(bf16[2,64,384]{2,1,0:T(8,128)(2,1)S(1)} %get-tuple-element.360), channel_id=1, source_target_pairs={{0,16},{16,0},{1,17},{17,1},{2,18},{18,2},{3,19},{19,3},{4,20},{20... | collective-permute-start | bytes 294920 | tf_op jit(solution)/shard_map/dx/ppermute | solution.py:197
  356.3 10.0 %collective-permute-start.104 = (bf16[112,768]{1,0:T(8,128)(2,1)S(1)}, bf16[112,768]{1,0:T(8,128)(2,1)S(1)}, u32[]{:S(2)}, u32[]{:S(2)}) collective-permute-start(bf16[112,768]{1,0:T(8,128)(2,1)S(1)} %bitcast.101), channel_id=1, source_target_pairs={{0,16},{16,0},{1,17},{17,1},{2,18},{18,2},{3,19},{19,3},{4,20},{20... | collective-permute-start | bytes 516104 | tf_op jit(solution)/shard_map/tg/ppermute | solution.py:197
  (106 other events, 876.7 us)
Sparse Core Ops, SparseCore 0:
  61.8 29.8 all-gather.1
  244.6 29.6 reduce-scatter.4
  287.7 18.5 reduce-scatter.6
  308.5 31.7 reduce-scatter.8
  342.5 19.1 reduce-scatter.10

commit v4 on v3

--- a/solution.py
+++ b/solution.py
@@ -1243,7 +1243,7 @@
         with jax.named_scope("ag3"):
             grads = gather(low, True)
         add_waiting()
-        reduce_summed(grads[1:])
+        reduce_summed(grads[1])
         *parts, d_inner, exp_row = feed_backward(
             order.tie(counts), grads, kept.slope, feed_w, layer
         )
@@ -1263,6 +1263,9 @@
         if few:
             share_grads(("feed", layer), *feed_got)
             scalar_steps(exp_row, 1)
+            if layer == 0:
+                add_waiting()
+                reduce_summed(pieces[1:])
         low, norm_rows = middle_backward(
             order.tie(counts),
             kept.mixed,
@@ -1280,7 +1283,7 @@
         with jax.named_scope("ag4"):
             grads = gather(low, True)
         add_waiting()
-        reduce_summed(grads[1] if layer == 0 else grads[1:])
+        reduce_summed(grads[1:])
         *parts, d_project, in_rows = attn_backward(
             order.tie(counts),
             grads,

time: 386 us -> 383 us (level)
  transfers between devices with their start and end apart: 110 -> 110, of which waited for: 44 -> 44; matrix products, arithmetic and copies ran while one was open for 3% -> 3% of each run, Pallas kernels for 29% -> 30%
where the time goes in v4:
time: 383 us; the launch traced here: 377 us
  Pallas kernels  128 us (33%)
  starting transfers between devices  116 us (30%)
  waiting for transfers between devices  99.8 us (26%)
  between operations  16 us (4%)
  local copies, waits for them, and re-layouts  14.2 us (4%)
    pallas_call x39, Pallas kernels, kernel_call(): pl.pallas_call(whole, out_shape=[jax.ShapeDtypeStruct(s, d) for s, d in o...  128 us
    ppermute x74, waiting for transfers between devices, hop(): return lax.ppermute(value, (SECTION, HEADS), route)  86.8 us
    ppermute x74, starting transfers between devices, hop(): return lax.ppermute(value, (SECTION, HEADS), route)  81.8 us
    ppermute x31, starting transfers between devices, swap(): return lax.ppermute(value, axis, [(i, i ^ distance) for i in range(count)])  33.5 us
    ppermute x31, waiting for transfers between devices, swap(): return lax.ppermute(value, axis, [(i, i ^ distance) for i in range(count)])  12.8 us
  transfers between devices with their start and end apart: 110, of which 44 were waited for; matrix products, arithmetic and copies ran while one was open for 3% of the time, Pallas kernels for 30%

profile of v4, /device:TPU:1, one launch (start us, length us, event | category | flops | bytes accessed | tf_op | source)
XLA Modules:
  0.0 376.7 jit_solution(17647587085093000578)
XLA Ops:
  7.9 2.2 constant_dynamic-slice_fusion.4
  10.3 2.7 collective-permute-start.3
  16.4 2.3 collective-permute-start.5
  20.0 4.5 %collective-permute-start.7 = (bf16[192,768]{1,0:T(8,128)(2,1)S(1)}, bf16[192,768]{1,0:T(8,128)(2,1)S(1)}, u32[]{:S(2)}, u32[]{:S(2)}) collective-permute-start(bf16[192,768]{1,0:T(8,128)(2,1)S(1)} %bitcast.88), channel_id=1, source_target_pairs={{0,16},{16,0},{1,17},{17,1},{2,18},{18,2},{3,19},{19,3},{4,20},{20... | collective-permute-start | bytes 884744 | tf_op jit(solution)/shard_map/w/ppermute | solution.py:197
  25.5 2.2 collective-permute-start.8
  27.9 2.0 select_select_fusion
  30.8 5.6 %attn_forward.4 = (f32[128,768]{1,0:T(8,128)S(1)}, bf16[128,768]{1,0:T(8,128)(2,1)}, bf16[128,768]{1,0:T(8,128)(2,1)S(1)}, bf16[128,768]{1,0:T(8,128)(2,1)S(1)},...) custom-call(s32[4,2]{1,0:T(4,128)S(1)} %copy.79.refs_0_, ...), custom_call_target="tpu_custom_call" | custom-call | flops 704643072 | bytes 4623360 | tf_op jit(solution)/shard_map/attn_forward/pallas_call | solution.py:128
  41.2 4.4 %attn_forward.5 = (f32[128,768]{1,0:T(8,128)S(1)}, bf16[128,768]{1,0:T(8,128)(2,1)S(1)}, bf16[128,768]{1,0:T(8,128)(2,1)S(1)}, bf16[128,768]{1,0:T(8,128)(2,1)S(1)}) custom-call(s32[4,2]{1,0:T(4,128)S(1)} %copy.80.refs_0_, f32[2,8,768]{2,1,0:T(8,128)S(1)} %small_table.1.refs_1_, f32[2,8,768]{2,1,0:T(8,128)S(1)} %collective-permute-done.2.refs_2_, ...), custom_call_target="tpu_custom_call" | custom-call | flops 704643072 | bytes 3050496 | tf_op jit(solution)/shard_map/attn_forward/pallas_call | solution.py:128
  49.2 2.0 collective-permute-done.14.refs_4_
  53.3 2.1 collective-permute-start.25
  55.4 2.1 collective-permute-done.16.refs_6_
  64.9 2.4 collective-permute-done.17.refs_4_.refs_7_
  70.4 4.4 %collective-permute-done.19.refs_6_.refs_9_ = bf16[128,768]{1,0:T(8,128)(2,1)S(1)} collective-permute-done((bf16[128,768]{1,0:T(8,128)(2,1)S(1)}, bf16[128,768]{1,0:T(8,128)(2,1)S(1)}, u32[]{:S(2)}, u32[]{:S(2)}) %collective-permute-start.19) | collective-permute-done | bytes 196640 | tf_op jit(solution)/shard_map/ag2/ppermute | solution.py:204
  75.6 5.3 %feed_forward.4 = (f32[128,768]{1,0:T(8,128)S(1)}, bf16[128,768]{1,0:T(8,128)(2,1)}, bf16[128,768]{1,0:T(8,128)(2,1)}, bf16[128,768]{1,0:T(8,128)(2,1)S(1)}, bf1...) custom-call(s32[4,2]{1,0:T(4,128)S(1)} %copy.83.refs_0_, f32[2,8,768]{2,1,0:T(8,128)S(1)} %small_table.1.refs_1_, ...), custom_call_target="tpu_custom_call" | custom-call | flops 1207959552 | bytes 5799936 | tf_op jit(solution)/shard_map/feed_forward/pallas_call | solution.py:128
  83.7 4.4 %feed_forward.5 = (f32[128,768]{1,0:T(8,128)S(1)}, bf16[128,768]{1,0:T(8,128)(2,1)S(1)}, bf16[128,768]{1,0:T(8,128)(2,1)}, bf16[128,768]{1,0:T(8,128)(2,1)}) custom-call(s32[4,2]{1,0:T(4,128)S(1)} %copy.84.refs_0_, f32[2,8,768]{2,1,0:T(8,128)S(1)} %small_table.1.refs_1_, f32[2,8,768]{2,1,0:T(8,128)S(1)} %collective-permute-done.2.refs_2_, ...), custom_call_target="tpu_custom_call" | custom-call | flops 1207959552 | bytes 4227072 | tf_op jit(solution)/shard_map/feed_forward/pallas_call | solution.py:128
  90.9 2.0 collective-permute-done.29.refs_6_
  98.9 2.5 collective-permute-done.32.refs_6_
  103.1 3.7 queue_units.1.refs_5_
  106.9 3.0 collective-permute-done.35.refs_7_.refs_9_
  109.9 4.9 %attn_forward.6 = (f32[128,768]{1,0:T(8,128)S(1)}, bf16[128,768]{1,0:T(8,128)(2,1)S(1)}, bf16[128,768]{1,0:T(8,128)(2,1)S(1)}, bf16[128,768]{1,0:T(8,128)(2,1)S(...) custom-call(s32[4,2]{1,0:T(4,128)S(1)} %copy.88.refs_0_, ...), custom_call_target="tpu_custom_call" | custom-call | flops 704643072 | bytes 4623360 | tf_op jit(solution)/shard_map/attn_forward/pallas_call | solution.py:128
  118.8 7.4 %collective-permute-done.36.refs_3_ = f32[1,768]{1,0:T(1,128)S(1)} collective-permute-done((f32[1,768]{1,0:T(1,128)S(1)}, f32[1,768]{1,0:T(1,128)S(1)}, u32[]{:S(2)}, u32[]{:S(2)}) %collective-permute-start.36) | collective-permute-done | bytes 3104 | tf_op jit(solution)/shard_map/nb/ppermute | solution.py:204
  126.2 4.5 %attn_forward.7 = (f32[128,768]{1,0:T(8,128)S(1)}, bf16[128,768]{1,0:T(8,128)(2,1)S(1)}) custom-call(s32[4,2]{1,0:T(4,128)S(1)} %copy.89.refs_0_, f32[2,8,768]{2,1,0:T(8,128)S(1)} %small_table.1.refs_1_, f32[2,8,768]{2,1,0:T(8,128)S(1)} %collective-permute-done.2.refs_2_, f32[1,768]{1,0:T(1,128)S(1)} %collective-permute-done.36.refs_3_, ...), custom_call_target="tpu_custom_call" | custom-call | flops 704643072 | bytes 3443712 | tf_op jit(solution)/shard_map/attn_forward/pallas_call | solution.py:128
  134.0 2.1 collective-permute-start.44
  138.3 4.7 %collective-permute-start.47 = (bf16[128,768]{1,0:T(8,128)(2,1)S(1)}, bf16[128,768]{1,0:T(8,128)(2,1)S(1)}, u32[]{:S(2)}, u32[]{:S(2)}) collective-permute-start(bf16[128,768]{1,0:T(8,128)(2,1)S(1)} %norm_middle.7.refs_3_.refs_7_), channel_id=1, source_target_pairs={{0,2},{1,3},{2,0},{3,1},{16,17},{17,16},{18,19},{19,18},{4,6},{5,7... | collective-permute-start | bytes 589832 | tf_op jit(solution)/shard_map/ag2/ppermute | solution.py:204
  143.9 5.4 %collective-permute-start.48 = (bf16[128,768]{1,0:T(8,128)(2,1)S(1)}, bf16[128,768]{1,0:T(8,128)(2,1)S(1)}, u32[]{:S(2)}, u32[]{:S(2)}) collective-permute-start(bf16[128,768]{1,0:T(8,128)(2,1)S(1)} %norm_middle.7.refs_3_.refs_7_), channel_id=1, source_target_pairs={{0,3},{1,2},{2,1},{3,0},{16,19},{17,18},{18,17},{19,16},{4,7},{5,6... | collective-permute-start | bytes 589832 | tf_op jit(solution)/shard_map/ag2/ppermute | solution.py:204
  149.4 5.3 %feed_forward.6 = (f32[128,768]{1,0:T(8,128)S(1)}, bf16[128,768]{1,0:T(8,128)(2,1)}, bf16[128,768]{1,0:T(8,128)(2,1)S(1)}, bf16[128,768]{1,0:T(8,128)(2,1)S(1)},...) custom-call(s32[4,2]{1,0:T(4,128)S(1)} %copy.92.refs_0_, f32[2,8,768]{2,1,0:T(8,128)S(1)} %small_table.1.refs_1_, ...), custom_call_target="tpu_custom_call" | custom-call | flops 1207959552 | bytes 5799936 | tf_op jit(solution)/shard_map/feed_forward/pallas_call | solution.py:128
  158.0 3.7 feed_forward.7
  163.3 3.2 collective-permute-done.49.refs_4_
  169.7 2.4 collective-permute-done.55.refs_6_
  176.2 4.0 %collective-permute-start.58 = (bf16[3,768]{1,0:T(4,128)(2,1)S(1)}, bf16[3,768]{1,0:T(4,128)(2,1)S(1)}, u32[]{:S(2)}, u32[]{:S(2)}) collective-permute-start(bf16[3,768]{1,0:T(4,128)(2,1)S(1)} %unit_packet.1.refs_1_), channel_id=1, source_target_pairs={{0,8},{4,12},{8,0},{12,4},{1,9},{5,13},{9,1},{13,5},{2,10},{6,14},... | collective-permute-start | bytes 13832 | tf_op jit(solution)/shard_map/loss/ppermute | solution.py:197
  181.5 3.0 collective-permute-done.59.refs_4_
  184.5 2.8 queue_scores.1
  187.4 2.4 collective-permute-done.60.refs_9_
  190.0 2.4 collective-permute-done.61.refs_5_
  206.4 6.3 %collective-permute-done.68.refs_4_.refs_5_ = bf16[128,768]{1,0:T(8,128)(2,1)S(1)} collective-permute-done((bf16[128,768]{1,0:T(8,128)(2,1)S(1)}, bf16[128,768]{1,0:T(8,128)(2,1)S(1)}, u32[]{:S(2)}, u32[]{:S(2)}) %collective-permute-start.68) | collective-permute-done | bytes 196640 | tf_op jit(solution)/shard_map/ag3/ppermute | solution.py:204
  212.6 4.9 %feed_backward.2 = (bf16[128,768]{1,0:T(8,128)(2,1)S(1)}, bf16[128,768]{1,0:T(8,128)(2,1)S(1)}, bf16[128,768]{1,0:T(8,128)(2,1)S(1)}, f32[1,768]{1,0:T(1,128)S(1...) custom-call(s32[4,2]{1,0:T(4,128)S(1)} %copy.100.refs_0_, ...), custom_call_target="tpu_custom_call" | custom-call | flops 1207959552 | bytes 5704704 | tf_op jit(solution)/shard_map/feed_backward/pallas_call | solution.py:128
  217.7 2.0 collective-permute-start.71
  222.4 5.7 %feed_weights.2 = (bf16[4,208,768]{2,1,0:T(8,128)(2,1)S(1)}, bf16[4,208,768]{2,1,0:T(8,128)(2,1)}) custom-call(s32[4,2]{1,0:T(4,128)S(1)} %copy.101.refs_0_, f32[1,768]{1,0:T(1,128)S(1)} %get-tuple-element.244.refs_1_, bf16[128,768]{1,0:T(8,128)(2,1)} %copy-done.12, bf16[128,768]{1,0:T(8,128)(2,1)} %copy-done.33, bf16[128,768]{1,0:T(8,128)(2,1)} %copy-done.34, ...), custom_call_target="tpu_custom_call" | custom-call | flops 1207959552 | bytes 5704704 | tf_op jit(solution)/shard_map/feed_weights/pallas_call | solution.py:128
  229.8 2.2 middle_backward.2
  235.3 3.1 add_cores.4
  239.9 4.6 %collective-permute-done.76.refs_4_.refs_5_ = bf16[128,768]{1,0:T(8,128)(2,1)S(1)} collective-permute-done((bf16[128,768]{1,0:T(8,128)(2,1)S(1)}, bf16[128,768]{1,0:T(8,128)(2,1)S(1)}, u32[]{:S(2)}, u32[]{:S(2)}) %collective-permute-start.76) | collective-permute-done | bytes 196640 | tf_op jit(solution)/shard_map/ag4/ppermute | solution.py:204
  244.9 6.5 %attn_backward.2 = (bf16[128,768]{1,0:T(8,128)(2,1)S(1)}, bf16[128,768]{1,0:T(8,128)(2,1)S(1)}, bf16[128,768]{1,0:T(8,128)(2,1)S(1)}, f32[2,768]{1,0:T(2,128)S(1...) custom-call(s32[4,2]{1,0:T(4,128)S(1)} %copy.104.refs_0_, ...), custom_call_target="tpu_custom_call" | custom-call | flops 805306368 | bytes 5117952 | tf_op jit(solution)/shard_map/attn_backward/pallas_call | solution.py:128
  255.0 4.8 %attn_weights.2 = (bf16[4,112,768]{2,1,0:T(8,128)(2,1)S(1)}, bf16[4,112,768]{2,1,0:T(8,128)(2,1)}) custom-call(s32[4,2]{1,0:T(4,128)S(1)} %copy.105.refs_0_, f32[2,768]{1,0:T(2,128)S(1)} %get-tuple-element.265.refs_1_, bf16[128,768]{1,0:T(8,128)(2,1)} %copy-done.6, bf16[128,768]{1,0:T(8,128)(2,1)} %copy-done.14, bf16[128,768]{1,0:T(8,128)(2,1)} %copy-done.15, ...), custom_call_target="tpu_custom_call" | custom-call | flops 603979776 | bytes 3741696 | tf_op jit(solution)/shard_map/attn_weights/pallas_call | solution.py:128
  259.9 3.8 %collective-permute-done.80.refs_6_ = bf16[128,768]{1,0:T(8,128)(2,1)S(1)} collective-permute-done((bf16[128,768]{1,0:T(8,128)(2,1)S(1)}, bf16[128,768]{1,0:T(8,128)(2,1)S(1)}, u32[]{:S(2)}, u32[]{:S(2)}) %collective-permute-start.80) | collective-permute-done | bytes 196640 | tf_op jit(solution)/shard_map/rs4/ppermute | solution.py:204
  263.7 2.2 last_backward.3
  269.3 2.6 add_cores.5
  273.9 4.6 %collective-permute-done.84.refs_4_.refs_5_ = bf16[128,768]{1,0:T(8,128)(2,1)S(1)} collective-permute-done((bf16[128,768]{1,0:T(8,128)(2,1)S(1)}, bf16[128,768]{1,0:T(8,128)(2,1)S(1)}, u32[]{:S(2)}, u32[]{:S(2)}) %collective-permute-start.84) | collective-permute-done | bytes 196640 | tf_op jit(solution)/shard_map/ag3/ppermute | solution.py:204
  278.6 5.7 %feed_backward.3 = (bf16[128,768]{1,0:T(8,128)(2,1)}, bf16[128,768]{1,0:T(8,128)(2,1)}, bf16[128,768]{1,0:T(8,128)(2,1)}, f32[1,768]{1,0:T(1,128)S(1)}, f32[128,...) custom-call(s32[4,2]{1,0:T(4,128)S(1)} %copy.108.refs_0_, bf16[128,768]{1,0:T(8,128)(2,1)S(1)} %get-tuple-element.276.refs_1_.refs_2_.refs_5_, ...), custom_call_target="tpu_custom_call" | custom-call | flops 1207959552 | bytes 5704704 | tf_op jit(solution)/shard_map/feed_backward/pallas_call | solution.py:128
  284.9 5.8 %feed_weights.3 = (bf16[4,208,768]{2,1,0:T(8,128)(2,1)S(1)}, bf16[4,208,768]{2,1,0:T(8,128)(2,1)}) custom-call(s32[4,2]{1,0:T(4,128)S(1)} %copy.109.refs_0_, f32[1,768]{1,0:T(1,128)S(1)} %get-tuple-element.282.refs_1_, bf16[128,768]{1,0:T(8,128)(2,1)} %copy-done.17, bf16[128,768]{1,0:T(8,128)(2,1)} %copy-done.30, bf16[128,768]{1,0:T(8,128)(2,1)} %copy-done.31, ...), custom_call_target="tpu_custom_call" | custom-call | flops 1207959552 | bytes 5704704 | tf_op jit(solution)/shard_map/feed_weights/pallas_call | solution.py:128
  293.8 3.1 add_cores.6
  298.6 4.9 %collective-permute-done.89.refs_8_ = bf16[128,768]{1,0:T(8,128)(2,1)S(1)} collective-permute-done((bf16[128,768]{1,0:T(8,128)(2,1)}, bf16[128,768]{1,0:T(8,128)(2,1)S(1)}, u32[]{:S(2)}, u32[]{:S(2)}) %collective-permute-start.89) | collective-permute-done | bytes 196640 | tf_op jit(solution)/shard_map/rs3/ppermute | solution.py:204
  304.0 2.2 middle_backward.3
  309.1 2.0 collective-permute-done.90.refs_2_.refs_3_.refs_4_
  312.6 4.3 %collective-permute-done.92.refs_4_.refs_5_.refs_6_ = bf16[144,768]{1,0:T(8,128)(2,1)S(1)} collective-permute-done((bf16[144,768]{1,0:T(8,128)(2,1)S(1)}, bf16[144,768]{1,0:T(8,128)(2,1)S(1)}, u32[]{:S(2)}, u32[]{:S(2)}) %collective-permute-start.92) | collective-permute-done | bytes 221216 | tf_op jit(solution)/shard_map/ag4/ppermute | solution.py:204
  316.9 6.5 %attn_backward.3 = (bf16[128,768]{1,0:T(8,128)(2,1)S(1)}, bf16[128,768]{1,0:T(8,128)(2,1)S(1)}, bf16[128,768]{1,0:T(8,128)(2,1)S(1)}, f32[2,768]{1,0:T(2,128)S(1...) custom-call(s32[4,2]{1,0:T(4,128)S(1)} %copy.112.refs_0_, bf16[144,768]{1,0:T(8,128)(2,1)S(1)} %get-tuple-element.299.refs_1_.refs_2_, ...), custom_call_target="tpu_custom_call" | custom-call | flops 805306368 | bytes 5216256 | tf_op jit(solution)/shard_map/attn_backward/pallas_call | solution.py:128
  323.6 4.7 %attn_weights.3 = (bf16[4,112,768]{2,1,0:T(8,128)(2,1)S(1)}, bf16[4,112,768]{2,1,0:T(8,128)(2,1)}) custom-call(s32[4,2]{1,0:T(4,128)S(1)} %copy.113.refs_0_, f32[2,768]{1,0:T(2,128)S(1)} %get-tuple-element.304.refs_1_, bf16[144,768]{1,0:T(8,128)(2,1)} %copy-done.4, bf16[144,768]{1,0:T(8,128)(2,1)} %copy-done.1, bf16[144,768]{1,0:T(8,128)(2,1)} %copy-done.2, ...), custom_call_target="tpu_custom_call" | custom-call | flops 603979776 | bytes 3840000 | tf_op jit(solution)/shard_map/attn_weights/pallas_call | solution.py:128
  328.4 3.5 collective-permute-start.94
  332.5 2.2 collective-permute-done.93
  334.8 2.8 add_cores.7
  343.6 2.6 collective-permute-done.97
  346.2 2.8 collective-permute-done.98
  353.4 2.2 collective-permute-start.100
  357.9 3.0 place_feed.1
  365.0 2.8 place_attn.1
  (394 shorter events, 127.6 us)
Async XLA Ops:
  7.2 119.0 %all-gather.2.cloned.1.call-start = ((), (), s32[]{:S(2)}) async-start(), calls=%async_computation.4 | async-start | bytes 1474560 | tf_op jit(solution)/shard_map/nb/all_gather | solution.py:1137
  7.2 20.4 %collective-permute-start = (bf16[576,768]{1,0:T(8,128)(2,1)}, bf16[576,768]{1,0:T(8,128)(2,1)S(1)}, u32[]{:S(2)}, u32[]{:S(2)}) collective-permute-start(bf16[576,768]{1,0:T(8,128)(2,1)} %bitcast.80), channel_id=1, source_target_pairs={{0,16},{16,0},{1,17},{17,1},{2,18},{18,2},{3,19},{19,3},{4,20},{20... | collective-permute-start | bytes 2654216 | tf_op jit(solution)/shard_map/w/ppermute | solution.py:197
  7.3 18.1 %collective-permute-start.1 = (bf16[192,768]{1,0:T(8,128)(2,1)}, bf16[192,768]{1,0:T(8,128)(2,1)}, u32[]{:S(2)}, u32[]{:S(2)}) collective-permute-start(bf16[192,768]{1,0:T(8,128)(2,1)} %bitcast.89), channel_id=1, source_target_pairs={{0,16},{16,0},{1,17},{17,1},{2,18},{18,2},{3,19},{19,3},{4,20},{20... | collective-permute-start | bytes 884744 | tf_op jit(solution)/shard_map/w/ppermute | solution.py:197
  7.8 22.3 %collective-permute-start.6 = (bf16[576,768]{1,0:T(8,128)(2,1)}, bf16[576,768]{1,0:T(8,128)(2,1)}, u32[]{:S(2)}, u32[]{:S(2)}) collective-permute-start(bf16[576,768]{1,0:T(8,128)(2,1)} %bitcast.75), channel_id=1, source_target_pairs={{0,16},{16,0},{1,17},{17,1},{2,18},{18,2},{3,19},{19,3},{4,20},{20... | collective-permute-start | bytes 2654216 | tf_op jit(solution)/shard_map/w/ppermute | solution.py:197
  16.4 8.5 %collective-permute-start.5 = (bf16[2,64,768]{2,1,0:T(8,128)(2,1)S(1)}, bf16[2,64,768]{2,1,0:T(8,128)(2,1)S(1)}, u32[]{:S(2)}, u32[]{:S(2)}) collective-permute-start(bf16[2,64,768]{2,1,0:T(8,128)(2,1)S(1)} %pad_maximum_fusion.1.refs_4_.refs_7_.refs_6_), channel_id=1, source_target_pairs={{0,3},{1,2},{2,1},{3,0},{16,19},{17,18},{18,17},{19,16},{4,7},{5,6... | collective-permute-start | bytes 589832 | tf_op jit(solution)/shard_map/ag0/ppermute | solution.py:204
  20.0 10.1 %collective-permute-start.7 = (bf16[192,768]{1,0:T(8,128)(2,1)S(1)}, bf16[192,768]{1,0:T(8,128)(2,1)S(1)}, u32[]{:S(2)}, u32[]{:S(2)}) collective-permute-start(bf16[192,768]{1,0:T(8,128)(2,1)S(1)} %bitcast.88), channel_id=1, source_target_pairs={{0,16},{16,0},{1,17},{17,1},{2,18},{18,2},{3,19},{19,3},{4,20},{20... | collective-permute-start | bytes 884744 | tf_op jit(solution)/shard_map/w/ppermute | solution.py:197
  24.9 13.3 %collective-permute-start.10 = (bf16[2,64,768]{2,1,0:T(8,128)(2,1)S(1)}, bf16[2,64,768]{2,1,0:T(8,128)(2,1)S(1)}, u32[]{:S(2)}, u32[]{:S(2)}) collective-permute-start(bf16[2,64,768]{2,1,0:T(8,128)(2,1)S(1)} %pad_maximum_fusion.refs_4_.refs_7_), channel_id=1, source_target_pairs={{0,3},{1,2},{2,1},{3,0},{16,19},{17,18},{18,17},{19,16},{4,7},{5,6... | collective-permute-start | bytes 589832 | tf_op jit(solution)/shard_map/ag0/ppermute | solution.py:204
  25.5 13.7 %collective-permute-start.8 = (bf16[2,64,768]{2,1,0:T(8,128)(2,1)S(1)}, bf16[2,64,768]{2,1,0:T(8,128)(2,1)S(1)}, u32[]{:S(2)}, u32[]{:S(2)}) collective-permute-start(bf16[2,64,768]{2,1,0:T(8,128)(2,1)S(1)} %pad_maximum_fusion.refs_4_.refs_7_), channel_id=1, source_target_pairs={{0,1},{1,0},{2,3},{3,2},{16,18},{17,19},{18,16},{19,17},{4,5},{5,4... | collective-permute-start | bytes 589832 | tf_op jit(solution)/shard_map/ag0/ppermute | solution.py:204
  27.6 13.4 %collective-permute-start.9 = (bf16[2,64,768]{2,1,0:T(8,128)(2,1)S(1)}, bf16[2,64,768]{2,1,0:T(8,128)(2,1)S(1)}, u32[]{:S(2)}, u32[]{:S(2)}) collective-permute-start(bf16[2,64,768]{2,1,0:T(8,128)(2,1)S(1)} %pad_maximum_fusion.refs_4_.refs_7_), channel_id=1, source_target_pairs={{0,2},{1,3},{2,0},{3,1},{16,17},{17,16},{18,19},{19,18},{4,6},{5,7... | collective-permute-start | bytes 589832 | tf_op jit(solution)/shard_map/ag0/ppermute | solution.py:204
  36.4 9.2 %collective-permute-start.11 = (bf16[128,768]{1,0:T(8,128)(2,1)}, bf16[128,768]{1,0:T(8,128)(2,1)S(1)}, u32[]{:S(2)}, u32[]{:S(2)}) collective-permute-start(bf16[128,768]{1,0:T(8,128)(2,1)} %get-tuple-element.177), channel_id=1, source_target_pairs={{0,1},{1,0},{2,3},{3,2},{16,18},{17,19},{18,16},{19,17},{4,5},{5,4... | collective-permute-start | bytes 589832 | tf_op jit(solution)/shard_map/rs1/ppermute | solution.py:204
  37.9 9.1 %collective-permute-start.12 = (bf16[128,768]{1,0:T(8,128)(2,1)S(1)}, bf16[128,768]{1,0:T(8,128)(2,1)S(1)}, u32[]{:S(2)}, u32[]{:S(2)}) collective-permute-start(bf16[128,768]{1,0:T(8,128)(2,1)S(1)} %get-tuple-element.178), channel_id=1, source_target_pairs={{0,2},{1,3},{2,0},{3,1},{16,17},{17,16},{18,19},{19,18},{4,6},{5,7... | collective-permute-start | bytes 589832 | tf_op jit(solution)/shard_map/rs1/ppermute | solution.py:204
  38.2 9.2 %collective-permute-start.13 = (bf16[128,768]{1,0:T(8,128)(2,1)S(1)}, bf16[128,768]{1,0:T(8,128)(2,1)S(1)}, u32[]{:S(2)}, u32[]{:S(2)}) collective-permute-start(bf16[128,768]{1,0:T(8,128)(2,1)S(1)} %get-tuple-element.179), channel_id=1, source_target_pairs={{0,3},{1,2},{2,1},{3,0},{16,19},{17,18},{18,17},{19,16},{4,7},{5,6... | collective-permute-start | bytes 589832 | tf_op jit(solution)/shard_map/rs1/ppermute | solution.py:204
  39.2 23.5 %collective-permute-start.20 = (bf16[768,768]{1,0:T(8,128)(2,1)}, bf16[768,768]{1,0:T(8,128)(2,1)}, u32[]{:S(2)}, u32[]{:S(2)}) collective-permute-start(bf16[768,768]{1,0:T(8,128)(2,1)} %bitcast.26.refs_7_.refs_6_), channel_id=1, source_target_pairs={{0,16},{16,0},{1,17},{17,1},{2,18},{18,2},{3,19},{19,3},{4,20},{20... | collective-permute-start | bytes 3538952 | tf_op jit(solution)/shard_map/w/ppermute | solution.py:197
  41.1 22.5 %collective-permute-start.21 = (bf16[768,768]{1,0:T(8,128)(2,1)}, bf16[768,768]{1,0:T(8,128)(2,1)}, u32[]{:S(2)}, u32[]{:S(2)}) collective-permute-start(bf16[768,768]{1,0:T(8,128)(2,1)} %bitcast.27.refs_8_.refs_7_), channel_id=1, source_target_pairs={{0,16},{16,0},{1,17},{17,1},{2,18},{18,2},{3,19},{19,3},{4,20},{20... | collective-permute-start | bytes 3538952 | tf_op jit(solution)/shard_map/w/ppermute | solution.py:197
  47.4 10.0 %collective-permute-start.16 = (bf16[128,768]{1,0:T(8,128)(2,1)S(1)}, bf16[128,768]{1,0:T(8,128)(2,1)S(1)}, u32[]{:S(2)}, u32[]{:S(2)}) collective-permute-start(bf16[128,768]{1,0:T(8,128)(2,1)S(1)} %get-tuple-element.184), channel_id=1, source_target_pairs={{0,3},{1,2},{2,1},{3,0},{16,19},{17,18},{18,17},{19,16},{4,7},{5,6... | collective-permute-start | bytes 589832 | tf_op jit(solution)/shard_map/rs1/ppermute | solution.py:204
  51.2 10.5 %collective-permute-start.38 = (bf16[192,768]{1,0:T(8,128)(2,1)}, bf16[192,768]{1,0:T(8,128)(2,1)}, u32[]{:S(2)}, u32[]{:S(2)}) collective-permute-start(bf16[192,768]{1,0:T(8,128)(2,1)} %select_select_fusion), channel_id=1, source_target_pairs={{0,2},{1,3},{2,0},{3,1},{16,17},{17,16},{18,19},{19,18},{4,6},{5,7... | collective-permute-start | bytes 884744 | tf_op jit(solution)/shard_map/nb/ppermute | solution.py:204
  53.3 27.8 %collective-permute-start.25 = (bf16[768,768]{1,0:T(8,128)(2,1)}, bf16[768,768]{1,0:T(8,128)(2,1)}, u32[]{:S(2)}, u32[]{:S(2)}) collective-permute-start(bf16[768,768]{1,0:T(8,128)(2,1)} %bitcast.28.refs_7_), channel_id=1, source_target_pairs={{0,16},{16,0},{1,17},{17,1},{2,18},{18,2},{3,19},{19,3},{4,20},{20... | collective-permute-start | bytes 3538952 | tf_op jit(solution)/shard_map/w/ppermute | solution.py:197
  57.5 24.2 %collective-permute-start.26 = (bf16[768,768]{1,0:T(8,128)(2,1)}, bf16[768,768]{1,0:T(8,128)(2,1)}, u32[]{:S(2)}, u32[]{:S(2)}) collective-permute-start(bf16[768,768]{1,0:T(8,128)(2,1)} %bitcast.29.refs_8_), channel_id=1, source_target_pairs={{0,16},{16,0},{1,17},{17,1},{2,18},{18,2},{3,19},{19,3},{4,20},{20... | collective-permute-start | bytes 3538952 | tf_op jit(solution)/shard_map/w/ppermute | solution.py:197
  61.7 223.2 %reduce-scatter.5.cloned.1.call-start = ((), (), s32[]{:S(2)}) async-start(), calls=%async_computation.5 | async-start | bytes 1597440 | tf_op jit(solution)/shard_map/rg/reduce_scatter | solution.py:1230
  63.6 11.1 %collective-permute-start.19 = (bf16[128,768]{1,0:T(8,128)(2,1)S(1)}, bf16[128,768]{1,0:T(8,128)(2,1)S(1)}, u32[]{:S(2)}, u32[]{:S(2)}) collective-permute-start(bf16[128,768]{1,0:T(8,128)(2,1)S(1)} %get-tuple-element.180.refs_3_.refs_7_.refs_6_), channel_id=1, source_target_pairs={{0,3},{1,2},{2,1},{3,0},{16,19},{17,18},{18,17},{19,16},{4,7},{5,6... | collective-permute-start | bytes 589832 | tf_op jit(solution)/shard_map/ag2/ppermute | solution.py:204
  67.3 15.5 %collective-permute-start.22 = (bf16[128,768]{1,0:T(8,128)(2,1)S(1)}, bf16[128,768]{1,0:T(8,128)(2,1)S(1)}, u32[]{:S(2)}, u32[]{:S(2)}) collective-permute-start(bf16[128,768]{1,0:T(8,128)(2,1)S(1)} %norm_middle.5.refs_3_.refs_7_), channel_id=1, source_target_pairs={{0,1},{1,0},{2,3},{3,2},{16,18},{17,19},{18,16},{19,17},{4,5},{5,4... | collective-permute-start | bytes 589832 | tf_op jit(solution)/shard_map/ag2/ppermute | solution.py:204
  69.4 14.2 %collective-permute-start.23 = (bf16[128,768]{1,0:T(8,128)(2,1)S(1)}, bf16[128,768]{1,0:T(8,128)(2,1)S(1)}, u32[]{:S(2)}, u32[]{:S(2)}) collective-permute-start(bf16[128,768]{1,0:T(8,128)(2,1)S(1)} %norm_middle.5.refs_3_.refs_7_), channel_id=1, source_target_pairs={{0,2},{1,3},{2,0},{3,1},{16,17},{17,16},{18,19},{19,18},{4,6},{5,7... | collective-permute-start | bytes 589832 | tf_op jit(solution)/shard_map/ag2/ppermute | solution.py:204
  74.7 8.9 %collective-permute-start.24 = (bf16[128,768]{1,0:T(8,128)(2,1)S(1)}, bf16[128,768]{1,0:T(8,128)(2,1)S(1)}, u32[]{:S(2)}, u32[]{:S(2)}) collective-permute-start(bf16[128,768]{1,0:T(8,128)(2,1)S(1)} %norm_middle.5.refs_3_.refs_7_), channel_id=1, source_target_pairs={{0,3},{1,2},{2,1},{3,0},{16,19},{17,18},{18,17},{19,16},{4,7},{5,6... | collective-permute-start | bytes 589832 | tf_op jit(solution)/shard_map/ag2/ppermute | solution.py:204
  81.0 9.0 %collective-permute-start.27 = (bf16[128,768]{1,0:T(8,128)(2,1)}, bf16[128,768]{1,0:T(8,128)(2,1)S(1)}, u32[]{:S(2)}, u32[]{:S(2)}) collective-permute-start(bf16[128,768]{1,0:T(8,128)(2,1)} %get-tuple-element.190), channel_id=1, source_target_pairs={{0,1},{1,0},{2,3},{3,2},{16,18},{17,19},{18,16},{19,17},{4,5},{5,4... | collective-permute-start | bytes 589832 | tf_op jit(solution)/shard_map/rs2/ppermute | solution.py:204
  81.7 9.2 %collective-permute-start.28 = (bf16[128,768]{1,0:T(8,128)(2,1)}, bf16[128,768]{1,0:T(8,128)(2,1)S(1)}, u32[]{:S(2)}, u32[]{:S(2)}) collective-permute-start(bf16[128,768]{1,0:T(8,128)(2,1)} %get-tuple-element.191), channel_id=1, source_target_pairs={{0,2},{1,3},{2,0},{3,1},{16,17},{17,16},{18,19},{19,18},{4,6},{5,7... | collective-permute-start | bytes 589832 | tf_op jit(solution)/shard_map/rs2/ppermute | solution.py:204
  82.9 10.1 %collective-permute-start.29 = (bf16[128,768]{1,0:T(8,128)(2,1)S(1)}, bf16[128,768]{1,0:T(8,128)(2,1)S(1)}, u32[]{:S(2)}, u32[]{:S(2)}) collective-permute-start(bf16[128,768]{1,0:T(8,128)(2,1)S(1)} %get-tuple-element.192), channel_id=1, source_target_pairs={{0,3},{1,2},{2,1},{3,0},{16,19},{17,18},{18,17},{19,16},{4,7},{5,6... | collective-permute-start | bytes 589832 | tf_op jit(solution)/shard_map/rs2/ppermute | solution.py:204
  88.1 8.9 %collective-permute-start.30 = (bf16[128,768]{1,0:T(8,128)(2,1)S(1)}, bf16[128,768]{1,0:T(8,128)(2,1)S(1)}, u32[]{:S(2)}, u32[]{:S(2)}) collective-permute-start(bf16[128,768]{1,0:T(8,128)(2,1)S(1)} %get-tuple-element.195), channel_id=1, source_target_pairs={{0,1},{1,0},{2,3},{3,2},{16,18},{17,19},{18,16},{19,17},{4,5},{5,4... | collective-permute-start | bytes 589832 | tf_op jit(solution)/shard_map/rs2/ppermute | solution.py:204
  88.9 10.0 %collective-permute-start.31 = (bf16[128,768]{1,0:T(8,128)(2,1)}, bf16[128,768]{1,0:T(8,128)(2,1)S(1)}, u32[]{:S(2)}, u32[]{:S(2)}) collective-permute-start(bf16[128,768]{1,0:T(8,128)(2,1)} %get-tuple-element.196), channel_id=1, source_target_pairs={{0,2},{1,3},{2,0},{3,1},{16,17},{17,16},{18,19},{19,18},{4,6},{5,7... | collective-permute-start | bytes 589832 | tf_op jit(solution)/shard_map/rs2/ppermute | solution.py:204
  90.0 11.4 %collective-permute-start.32 = (bf16[128,768]{1,0:T(8,128)(2,1)}, bf16[128,768]{1,0:T(8,128)(2,1)S(1)}, u32[]{:S(2)}, u32[]{:S(2)}) collective-permute-start(bf16[128,768]{1,0:T(8,128)(2,1)} %get-tuple-element.197), channel_id=1, source_target_pairs={{0,3},{1,2},{2,1},{3,0},{16,19},{17,18},{18,17},{19,16},{4,7},{5,6... | collective-permute-start | bytes 589832 | tf_op jit(solution)/shard_map/rs2/ppermute | solution.py:204
  94.5 12.3 %collective-permute-start.33 = (bf16[128,768]{1,0:T(8,128)(2,1)S(1)}, bf16[128,768]{1,0:T(8,128)(2,1)S(1)}, u32[]{:S(2)}, u32[]{:S(2)}) collective-permute-start(bf16[128,768]{1,0:T(8,128)(2,1)S(1)} %get-tuple-element.193.refs_4_.refs_7_.refs_6_), channel_id=1, source_target_pairs={{0,1},{1,0},{2,3},{3,2},{16,18},{17,19},{18,16},{19,17},{4,5},{5,4... | collective-permute-start | bytes 589832 | tf_op jit(solution)/shard_map/ag1/ppermute | solution.py:204
  95.2 11.7 %collective-permute-start.34 = (bf16[128,768]{1,0:T(8,128)(2,1)S(1)}, bf16[128,768]{1,0:T(8,128)(2,1)S(1)}, u32[]{:S(2)}, u32[]{:S(2)}) collective-permute-start(bf16[128,768]{1,0:T(8,128)(2,1)S(1)} %get-tuple-element.193.refs_4_.refs_7_.refs_6_), channel_id=1, source_target_pairs={{0,2},{1,3},{2,0},{3,1},{16,17},{17,16},{18,19},{19,18},{4,6},{5,7... | collective-permute-start | bytes 589832 | tf_op jit(solution)/shard_map/ag1/ppermute | solution.py:204
  97.1 12.8 %collective-permute-start.35 = (bf16[128,768]{1,0:T(8,128)(2,1)S(1)}, bf16[128,768]{1,0:T(8,128)(2,1)S(1)}, u32[]{:S(2)}, u32[]{:S(2)}) collective-permute-start(bf16[128,768]{1,0:T(8,128)(2,1)S(1)} %get-tuple-element.193.refs_4_.refs_7_.refs_6_), channel_id=1, source_target_pairs={{0,3},{1,2},{2,1},{3,0},{16,19},{17,18},{18,17},{19,16},{4,7},{5,6... | collective-permute-start | bytes 589832 | tf_op jit(solution)/shard_map/ag1/ppermute | solution.py:204
  102.3 23.9 %collective-permute-start.37 = (bf16[128,768]{1,0:T(8,128)(2,1)S(1)}, bf16[128,768]{1,0:T(8,128)(2,1)S(1)}, u32[]{:S(2)}, u32[]{:S(2)}) collective-permute-start(bf16[128,768]{1,0:T(8,128)(2,1)S(1)} %norm_last.5.refs_4_.refs_5_), channel_id=1, source_target_pairs={{0,1},{1,0},{2,3},{3,2},{16,18},{17,19},{18,16},{19,17},{4,5},{5,4... | collective-permute-start | bytes 589832 | tf_op jit(solution)/shard_map/ag1/ppermute | solution.py:204
  114.9 16.2 %collective-permute-start.39 = (bf16[128,768]{1,0:T(8,128)(2,1)S(1)}, bf16[128,768]{1,0:T(8,128)(2,1)S(1)}, u32[]{:S(2)}, u32[]{:S(2)}) collective-permute-start(bf16[128,768]{1,0:T(8,128)(2,1)S(1)} %get-tuple-element.207), channel_id=1, source_target_pairs={{0,1},{1,0},{2,3},{3,2},{16,18},{17,19},{18,16},{19,17},{4,5},{5,4... | collective-permute-start | bytes 589832 | tf_op jit(solution)/shard_map/rs1/ppermute | solution.py:204
  115.5 15.5 %collective-permute-start.40 = (bf16[128,768]{1,0:T(8,128)(2,1)S(1)}, bf16[128,768]{1,0:T(8,128)(2,1)S(1)}, u32[]{:S(2)}, u32[]{:S(2)}) collective-permute-start(bf16[128,768]{1,0:T(8,128)(2,1)S(1)} %get-tuple-element.208), channel_id=1, source_target_pairs={{0,2},{1,3},{2,0},{3,1},{16,17},{17,16},{18,19},{19,18},{4,6},{5,7... | collective-permute-start | bytes 589832 | tf_op jit(solution)/shard_map/rs1/ppermute | solution.py:204
  117.4 13.7 %collective-permute-start.41 = (bf16[128,768]{1,0:T(8,128)(2,1)S(1)}, bf16[128,768]{1,0:T(8,128)(2,1)S(1)}, u32[]{:S(2)}, u32[]{:S(2)}) collective-permute-start(bf16[128,768]{1,0:T(8,128)(2,1)S(1)} %get-tuple-element.209), channel_id=1, source_target_pairs={{0,3},{1,2},{2,1},{3,0},{16,19},{17,18},{18,17},{19,16},{4,7},{5,6... | collective-permute-start | bytes 589832 | tf_op jit(solution)/shard_map/rs1/ppermute | solution.py:204
  117.6 8.6 %collective-permute-start.36 = (f32[1,768]{1,0:T(1,128)S(1)}, f32[1,768]{1,0:T(1,128)S(1)}, u32[]{:S(2)}, u32[]{:S(2)}) collective-permute-start(f32[1,768]{1,0:T(1,128)S(1)} %fusion.3), channel_id=1, source_target_pairs={{0,2},{1,3},{2,0},{3,1},{16,17},{17,16},{18,19},{19,18},{4,6},{5,7... | collective-permute-start | bytes 9224 | tf_op jit(solution)/shard_map/nb/ppermute | solution.py:204
  132.6 11.2 %collective-permute-start.43 = (bf16[128,768]{1,0:T(8,128)(2,1)S(1)}, bf16[128,768]{1,0:T(8,128)(2,1)S(1)}, u32[]{:S(2)}, u32[]{:S(2)}) collective-permute-start(bf16[128,768]{1,0:T(8,128)(2,1)S(1)} %get-tuple-element.210.refs_3_.refs_7_.refs_6_), channel_id=1, source_target_pairs={{0,1},{1,0},{2,3},{3,2},{16,18},{17,19},{18,16},{19,17},{4,5},{5,4... | collective-permute-start | bytes 589832 | tf_op jit(solution)/shard_map/ag2/ppermute | solution.py:204
  134.0 15.4 %collective-permute-start.44 = (bf16[128,768]{1,0:T(8,128)(2,1)S(1)}, bf16[128,768]{1,0:T(8,128)(2,1)S(1)}, u32[]{:S(2)}, u32[]{:S(2)}) collective-permute-start(bf16[128,768]{1,0:T(8,128)(2,1)S(1)} %get-tuple-element.210.refs_3_.refs_7_.refs_6_), channel_id=1, source_target_pairs={{0,2},{1,3},{2,0},{3,1},{16,17},{17,16},{18,19},{19,18},{4,6},{5,7... | collective-permute-start | bytes 589832 | tf_op jit(solution)/shard_map/ag2/ppermute | solution.py:204
  136.1 13.3 %collective-permute-start.45 = (bf16[128,768]{1,0:T(8,128)(2,1)S(1)}, bf16[128,768]{1,0:T(8,128)(2,1)S(1)}, u32[]{:S(2)}, u32[]{:S(2)}) collective-permute-start(bf16[128,768]{1,0:T(8,128)(2,1)S(1)} %get-tuple-element.210.refs_3_.refs_7_.refs_6_), channel_id=1, source_target_pairs={{0,3},{1,2},{2,1},{3,0},{16,19},{17,18},{18,17},{19,16},{4,7},{5,6... | collective-permute-start | bytes 589832 | tf_op jit(solution)/shard_map/ag2/ppermute | solution.py:204
  137.1 19.7 %collective-permute-start.46 = (bf16[128,768]{1,0:T(8,128)(2,1)S(1)}, bf16[128,768]{1,0:T(8,128)(2,1)S(1)}, u32[]{:S(2)}, u32[]{:S(2)}) collective-permute-start(bf16[128,768]{1,0:T(8,128)(2,1)S(1)} %norm_middle.7.refs_3_.refs_7_), channel_id=1, source_target_pairs={{0,1},{1,0},{2,3},{3,2},{16,18},{17,19},{18,16},{19,17},{4,5},{5,4... | collective-permute-start | bytes 589832 | tf_op jit(solution)/shard_map/ag2/ppermute | solution.py:204
  138.3 19.8 %collective-permute-start.47 = (bf16[128,768]{1,0:T(8,128)(2,1)S(1)}, bf16[128,768]{1,0:T(8,128)(2,1)S(1)}, u32[]{:S(2)}, u32[]{:S(2)}) collective-permute-start(bf16[128,768]{1,0:T(8,128)(2,1)S(1)} %norm_middle.7.refs_3_.refs_7_), channel_id=1, source_target_pairs={{0,2},{1,3},{2,0},{3,1},{16,17},{17,16},{18,19},{19,18},{4,6},{5,7... | collective-permute-start | bytes 589832 | tf_op jit(solution)/shard_map/ag2/ppermute | solution.py:204
  143.9 14.2 %collective-permute-start.48 = (bf16[128,768]{1,0:T(8,128)(2,1)S(1)}, bf16[128,768]{1,0:T(8,128)(2,1)S(1)}, u32[]{:S(2)}, u32[]{:S(2)}) collective-permute-start(bf16[128,768]{1,0:T(8,128)(2,1)S(1)} %norm_middle.7.refs_3_.refs_7_), channel_id=1, source_target_pairs={{0,3},{1,2},{2,1},{3,0},{16,19},{17,18},{18,17},{19,16},{4,7},{5,6... | collective-permute-start | bytes 589832 | tf_op jit(solution)/shard_map/ag2/ppermute | solution.py:204
  154.8 11.8 %collective-permute-start.49 = (bf16[128,768]{1,0:T(8,128)(2,1)}, bf16[128,768]{1,0:T(8,128)(2,1)S(1)}, u32[]{:S(2)}, u32[]{:S(2)}) collective-permute-start(bf16[128,768]{1,0:T(8,128)(2,1)} %get-tuple-element.218), channel_id=1, source_target_pairs={{0,1},{1,0},{2,3},{3,2},{16,18},{17,19},{18,16},{19,17},{4,5},{5,4... | collective-permute-start | bytes 589832 | tf_op jit(solution)/shard_map/rs2/ppermute | solution.py:204
  156.8 9.8 %collective-permute-start.50 = (bf16[128,768]{1,0:T(8,128)(2,1)S(1)}, bf16[128,768]{1,0:T(8,128)(2,1)S(1)}, u32[]{:S(2)}, u32[]{:S(2)}) collective-permute-start(bf16[128,768]{1,0:T(8,128)(2,1)S(1)} %get-tuple-element.219), channel_id=1, source_target_pairs={{0,2},{1,3},{2,0},{3,1},{16,17},{17,16},{18,19},{19,18},{4,6},{5,7... | collective-permute-start | bytes 589832 | tf_op jit(solution)/shard_map/rs2/ppermute | solution.py:204
  156.8 9.8 %collective-permute-start.51 = (bf16[128,768]{1,0:T(8,128)(2,1)S(1)}, bf16[128,768]{1,0:T(8,128)(2,1)S(1)}, u32[]{:S(2)}, u32[]{:S(2)}) collective-permute-start(bf16[128,768]{1,0:T(8,128)(2,1)S(1)} %get-tuple-element.220), channel_id=1, source_target_pairs={{0,3},{1,2},{2,1},{3,0},{16,19},{17,18},{18,17},{19,16},{4,7},{5,6... | collective-permute-start | bytes 589832 | tf_op jit(solution)/shard_map/rs2/ppermute | solution.py:204
  161.7 7.9 %collective-permute-start.53 = (bf16[128,768]{1,0:T(8,128)(2,1)S(1)}, bf16[128,768]{1,0:T(8,128)(2,1)S(1)}, u32[]{:S(2)}, u32[]{:S(2)}) collective-permute-start(bf16[128,768]{1,0:T(8,128)(2,1)S(1)} %get-tuple-element.223), channel_id=1, source_target_pairs={{0,1},{1,0},{2,3},{3,2},{16,18},{17,19},{18,16},{19,17},{4,5},{5,4... | collective-permute-start | bytes 589832 | tf_op jit(solution)/shard_map/rs2/ppermute | solution.py:204
  202.5 10.1 %collective-permute-start.68 = (bf16[128,768]{1,0:T(8,128)(2,1)S(1)}, bf16[128,768]{1,0:T(8,128)(2,1)S(1)}, u32[]{:S(2)}, u32[]{:S(2)}) collective-permute-start(bf16[128,768]{1,0:T(8,128)(2,1)S(1)} %get-tuple-element.241.refs_1_.refs_2_.refs_4_), channel_id=1, source_target_pairs={{0,3},{1,2},{2,1},{3,0},{16,19},{17,18},{18,17},{19,16},{4,7},{5,6... | collective-permute-start | bytes 589832 | tf_op jit(solution)/shard_map/ag3/ppermute | solution.py:204
  217.6 10.6 %collective-permute-start.70 = (bf16[128,768]{1,0:T(8,128)(2,1)S(1)}, bf16[128,768]{1,0:T(8,128)(2,1)S(1)}, u32[]{:S(2)}, u32[]{:S(2)}) collective-permute-start(bf16[128,768]{1,0:T(8,128)(2,1)S(1)} %get-tuple-element.252), channel_id=1, source_target_pairs={{0,1},{1,0},{2,3},{3,2},{16,18},{17,19},{18,16},{19,17},{4,5},{5,4... | collective-permute-start | bytes 589832 | tf_op jit(solution)/shard_map/rs3/ppermute | solution.py:204
  217.7 10.5 %collective-permute-start.71 = (bf16[128,768]{1,0:T(8,128)(2,1)S(1)}, bf16[128,768]{1,0:T(8,128)(2,1)S(1)}, u32[]{:S(2)}, u32[]{:S(2)}) collective-permute-start(bf16[128,768]{1,0:T(8,128)(2,1)S(1)} %get-tuple-element.253), channel_id=1, source_target_pairs={{0,2},{1,3},{2,0},{3,1},{16,17},{17,16},{18,19},{19,18},{4,6},{5,7... | collective-permute-start | bytes 589832 | tf_op jit(solution)/shard_map/rs3/ppermute | solution.py:204
  219.7 10.1 %collective-permute-start.72 = (bf16[128,768]{1,0:T(8,128)(2,1)S(1)}, bf16[128,768]{1,0:T(8,128)(2,1)S(1)}, u32[]{:S(2)}, u32[]{:S(2)}) collective-permute-start(bf16[128,768]{1,0:T(8,128)(2,1)S(1)} %get-tuple-element.254), channel_id=1, source_target_pairs={{0,3},{1,2},{2,1},{3,0},{16,19},{17,18},{18,17},{19,16},{4,7},{5,6... | collective-permute-start | bytes 589832 | tf_op jit(solution)/shard_map/rs3/ppermute | solution.py:204
  234.7 9.8 %collective-permute-start.76 = (bf16[128,768]{1,0:T(8,128)(2,1)S(1)}, bf16[128,768]{1,0:T(8,128)(2,1)S(1)}, u32[]{:S(2)}, u32[]{:S(2)}) collective-permute-start(bf16[128,768]{1,0:T(8,128)(2,1)S(1)} %get-tuple-element.257.refs_1_.refs_2_.refs_3_), channel_id=1, source_target_pairs={{0,3},{1,2},{2,1},{3,0},{16,19},{17,18},{18,17},{19,16},{4,7},{5,6... | collective-permute-start | bytes 589832 | tf_op jit(solution)/shard_map/ag4/ppermute | solution.py:204
  244.5 59.1 %reduce-scatter.7.cloned.1.call-start = ((), (), s32[]{:S(2)}) async-start(), calls=%async_computation.6 | async-start | bytes 860160 | tf_op jit(solution)/shard_map/rg/reduce_scatter | solution.py:1230
  251.5 8.4 %collective-permute-start.78 = (bf16[128,768]{1,0:T(8,128)(2,1)S(1)}, bf16[128,768]{1,0:T(8,128)(2,1)S(1)}, u32[]{:S(2)}, u32[]{:S(2)}) collective-permute-start(bf16[128,768]{1,0:T(8,128)(2,1)S(1)} %get-tuple-element.271), channel_id=1, source_target_pairs={{0,1},{1,0},{2,3},{3,2},{16,18},{17,19},{18,16},{19,17},{4,5},{5,4... | collective-permute-start | bytes 589832 | tf_op jit(solution)/shard_map/rs4/ppermute | solution.py:204
  253.7 10.0 %collective-permute-start.80 = (bf16[128,768]{1,0:T(8,128)(2,1)S(1)}, bf16[128,768]{1,0:T(8,128)(2,1)S(1)}, u32[]{:S(2)}, u32[]{:S(2)}) collective-permute-start(bf16[128,768]{1,0:T(8,128)(2,1)S(1)} %get-tuple-element.273), channel_id=1, source_target_pairs={{0,3},{1,2},{2,1},{3,0},{16,19},{17,18},{18,17},{19,16},{4,7},{5,6... | collective-permute-start | bytes 589832 | tf_op jit(solution)/shard_map/rs4/ppermute | solution.py:204
  268.8 9.8 %collective-permute-start.84 = (bf16[128,768]{1,0:T(8,128)(2,1)S(1)}, bf16[128,768]{1,0:T(8,128)(2,1)S(1)}, u32[]{:S(2)}, u32[]{:S(2)}) collective-permute-start(bf16[128,768]{1,0:T(8,128)(2,1)S(1)} %get-tuple-element.276.refs_1_.refs_2_.refs_5_), channel_id=1, source_target_pairs={{0,3},{1,2},{2,1},{3,0},{16,19},{17,18},{18,17},{19,16},{4,7},{5,6... | collective-permute-start | bytes 589832 | tf_op jit(solution)/shard_map/ag3/ppermute | solution.py:204
  284.9 66.7 %reduce-scatter.9.cloned.1.call-start = ((), (), s32[]{:S(2)}) async-start(), calls=%async_computation.7 | async-start | bytes 1597440 | tf_op jit(solution)/shard_map/rg/reduce_scatter | solution.py:1230
  293.0 10.5 %collective-permute-start.89 = (bf16[128,768]{1,0:T(8,128)(2,1)}, bf16[128,768]{1,0:T(8,128)(2,1)S(1)}, u32[]{:S(2)}, u32[]{:S(2)}) collective-permute-start(bf16[128,768]{1,0:T(8,128)(2,1)} %get-tuple-element.296), channel_id=1, source_target_pairs={{0,3},{1,2},{2,1},{3,0},{16,19},{17,18},{18,17},{19,16},{4,7},{5,6... | collective-permute-start | bytes 589832 | tf_op jit(solution)/shard_map/rs3/ppermute | solution.py:204
  303.6 57.3 %reduce-scatter.11.cloned.1.call-start = ((), (), s32[]{:S(2)}) async-start(), calls=%async_computation.8 | async-start | bytes 860160 | tf_op jit(solution)/shard_map/lg/reduce_scatter | solution.py:1328
  309.0 8.0 %collective-permute-start.92 = (bf16[144,768]{1,0:T(8,128)(2,1)S(1)}, bf16[144,768]{1,0:T(8,128)(2,1)S(1)}, u32[]{:S(2)}, u32[]{:S(2)}) collective-permute-start(bf16[144,768]{1,0:T(8,128)(2,1)S(1)} %get-tuple-element.299.refs_1_.refs_2_), channel_id=1, source_target_pairs={{0,3},{1,2},{2,1},{3,0},{16,19},{17,18},{18,17},{19,16},{4,7},{5,6... | collective-permute-start | bytes 663560 | tf_op jit(solution)/shard_map/ag4/ppermute | solution.py:204
  340.3 8.7 %collective-permute-start.98 = (bf16[128,768]{1,0:T(8,128)(2,1)S(1)}, bf16[128,768]{1,0:T(8,128)(2,1)S(1)}, u32[]{:S(2)}, u32[]{:S(2)}) collective-permute-start(bf16[128,768]{1,0:T(8,128)(2,1)S(1)} %get-tuple-element.317), channel_id=1, source_target_pairs={{0,3},{1,2},{2,1},{3,0},{16,19},{17,18},{18,17},{19,16},{4,7},{5,6... | collective-permute-start | bytes 589832 | tf_op jit(solution)/shard_map/rs4/ppermute | solution.py:204
  340.6 15.8 %collective-permute-start.102 = (bf16[208,768]{1,0:T(8,128)(2,1)S(1)}, bf16[208,768]{1,0:T(8,128)(2,1)S(1)}, u32[]{:S(2)}, u32[]{:S(2)}) collective-permute-start(bf16[208,768]{1,0:T(8,128)(2,1)S(1)} %bitcast.97), channel_id=1, source_target_pairs={{0,16},{16,0},{1,17},{17,1},{2,18},{18,2},{3,19},{19,3},{4,20},{20... | collective-permute-start | bytes 958472 | tf_op jit(solution)/shard_map/fg/ppermute | solution.py:197
  342.2 8.1 %collective-permute-start.95 = (f32[1,128]{1,0:T(1,128)S(1)}, f32[1,128]{1,0:T(1,128)S(1)}, u32[]{:S(2)}, u32[]{:S(2)}) collective-permute-start(f32[1,128]{1,0:T(1,128)S(1)} %add.91), channel_id=1, source_target_pairs={{0,8},{4,12},{8,0},{12,4},{1,9},{5,13},{9,1},{13,5},{2,10},{6,14},... | collective-permute-start | bytes 1544 | tf_op jit(solution)/shard_map/lg/sc/ppermute | solution.py:197
  353.4 8.6 %collective-permute-start.100 = (bf16[2,64,384]{2,1,0:T(8,128)(2,1)S(1)}, bf16[2,64,384]{2,1,0:T(8,128)(2,1)S(1)}, u32[]{:S(2)}, u32[]{:S(2)}) collective-permute-start(bf16[2,64,384]{2,1,0:T(8,128)(2,1)S(1)} %get-tuple-element.360), channel_id=1, source_target_pairs={{0,16},{16,0},{1,17},{17,1},{2,18},{18,2},{3,19},{19,3},{4,20},{20... | collective-permute-start | bytes 294920 | tf_op jit(solution)/shard_map/dx/ppermute | solution.py:197
  (106 other events, 868.6 us)
Sparse Core Ops, SparseCore 0:
  61.8 29.8 all-gather.1
  244.6 29.6 reduce-scatter.4
  285.0 18.5 reduce-scatter.6
  305.8 31.7 reduce-scatter.8
  339.8 19.1 reduce-scatter.10

commit v5 on v4

--- a/solution.py
+++ b/solution.py
@@ -500,7 +500,7 @@
 
 
 def scattered(part, *others):
-    total = part[...]
+    total = part[...].astype(F32)
     for value in others:
         total = total + value[: part.shape[0], :].astype(F32)
     return total
@@ -607,7 +607,7 @@
         bias_r[...] = total
         put_rows(targets, outs)
 
-    part, *outs = parts_shapes(rows, width, count)
+    part, *outs = [((rows, width), LOW)] * count
     outs, stores = outs + [((1, units), F32)], [part, ((2, full, units), LOW)]
     flops = 8 * full * width * units
     got = kernel_call(
@@ -668,7 +668,7 @@
             outs.append(dot_nn(d_project, w_r[side, :triple, :]))
         put_rows(targets, outs)
 
-    part = ((rows, width), F32)
+    part = ((rows, width), LOW)
     outs = [((rows, width), LOW)] * (count - 1)
     outs, stores = outs + [((2, width), F32)], [part, ((2, full, triple), LOW)]
     flops = 4 * full * (4 * local * width + 4 * local * full)
@@ -928,9 +928,8 @@
         key_r[...] = jnp.concatenate([p[1:2] for p in packets] + [p[2:3] for p in packets], axis=0)
 
     outs = [((1, width + 128), F32)] * count + [((2 * count, width), LOW)]
-    return kernel_call(
-        body, outs, [counts], lanes, 4 * count * queue.size, "queue_scores", [queue]
-    )
+    near = lanes + [queue]
+    return kernel_call(body, outs, [counts], near, 4 * count * queue.size, "queue_scores")
 
 
 def loss_end(counts, live, sums, keys, pulls, squares):

time: 383 us -> 383 us (level)
  waiting for transfers between devices: 99.8 us -> 92.4 us
  starting transfers between devices: 116 us -> 123 us
    ppermute x74, waiting for transfers between devices: 86.8 us -> 79.4 us  [hop(): return lax.ppermute(value, (SECTION, HEADS), route)]
    ppermute x74, starting transfers between devices: 81.8 us -> 86.6 us  [hop(): return lax.ppermute(value, (SECTION, HEADS), route)]
where the time goes in v5:
time: 383 us; the launch traced here: 375 us
  Pallas kernels  128 us (33%)
  starting transfers between devices  123 us (32%)
  waiting for transfers between devices  92.4 us (24%)
  between operations  16 us (4%)
  local copies, waits for them, and re-layouts  14.2 us (4%)
    pallas_call x39, Pallas kernels, kernel_call(): pl.pallas_call(whole, out_shape=[jax.ShapeDtypeStruct(s, d) for s, d in o...  128 us
    ppermute x74, starting transfers between devices, hop(): return lax.ppermute(value, (SECTION, HEADS), route)  86.6 us
    ppermute x74, waiting for transfers between devices, hop(): return lax.ppermute(value, (SECTION, HEADS), route)  79.4 us
    ppermute x31, starting transfers between devices, swap(): return lax.ppermute(value, axis, [(i, i ^ distance) for i in range(count)])  35.1 us
    ppermute x31, waiting for transfers between devices, swap(): return lax.ppermute(value, axis, [(i, i ^ distance) for i in range(count)])  12.7 us
  transfers between devices with their start and end apart: 110, of which 44 were waited for; matrix products, arithmetic and copies ran while one was open for 3% of the time, Pallas kernels for 30%

profile of v5, /device:TPU:1, one launch (start us, length us, event | category | flops | bytes accessed | tf_op | source)
XLA Modules:
  0.0 375.4 jit_solution(15224590916754935187)
XLA Ops:
  7.9 2.2 constant_dynamic-slice_fusion.4
  10.3 2.7 collective-permute-start.3
  16.4 2.3 collective-permute-start.5
  20.0 4.5 %collective-permute-start.7 = (bf16[192,768]{1,0:T(8,128)(2,1)S(1)}, bf16[192,768]{1,0:T(8,128)(2,1)S(1)}, u32[]{:S(2)}, u32[]{:S(2)}) collective-permute-start(bf16[192,768]{1,0:T(8,128)(2,1)S(1)} %bitcast.88), channel_id=1, source_target_pairs={{0,16},{16,0},{1,17},{17,1},{2,18},{18,2},{3,19},{19,3},{4,20},{20... | collective-permute-start | bytes 884744 | tf_op jit(solution)/shard_map/w/ppermute | solution.py:197
  25.5 2.2 collective-permute-start.8
  27.9 2.0 select_select_fusion
  30.8 5.9 %attn_forward.4 = (f32[128,768]{1,0:T(8,128)S(1)}, bf16[128,768]{1,0:T(8,128)(2,1)}, bf16[128,768]{1,0:T(8,128)(2,1)}, bf16[128,768]{1,0:T(8,128)(2,1)}, bf16[2,...) custom-call(s32[4,2]{1,0:T(4,128)S(1)} %copy.79.refs_0_, ...), custom_call_target="tpu_custom_call" | custom-call | flops 704643072 | bytes 4623360 | tf_op jit(solution)/shard_map/attn_forward/pallas_call | solution.py:128
  39.4 1.9 collective-permute-start.20
  41.5 4.4 %attn_forward.5 = (f32[128,768]{1,0:T(8,128)S(1)}, bf16[128,768]{1,0:T(8,128)(2,1)S(1)}, bf16[128,768]{1,0:T(8,128)(2,1)S(1)}, bf16[128,768]{1,0:T(8,128)(2,1)S(1)}) custom-call(s32[4,2]{1,0:T(4,128)S(1)} %copy.80.refs_0_, f32[2,8,768]{2,1,0:T(8,128)S(1)} %small_table.1.refs_1_, f32[2,8,768]{2,1,0:T(8,128)S(1)} %collective-permute-done.2.refs_2_, ...), custom_call_target="tpu_custom_call" | custom-call | flops 704643072 | bytes 3050496 | tf_op jit(solution)/shard_map/attn_forward/pallas_call | solution.py:128
  49.9 2.0 collective-permute-done.14.refs_4_
  53.7 1.9 collective-permute-start.25
  55.6 2.1 collective-permute-done.16.refs_6_
  65.2 2.4 collective-permute-done.17.refs_4_.refs_7_
  70.6 4.4 %collective-permute-done.19.refs_6_.refs_9_ = bf16[128,768]{1,0:T(8,128)(2,1)S(1)} collective-permute-done((bf16[128,768]{1,0:T(8,128)(2,1)S(1)}, bf16[128,768]{1,0:T(8,128)(2,1)S(1)}, u32[]{:S(2)}, u32[]{:S(2)}) %collective-permute-start.19) | collective-permute-done | bytes 196640 | tf_op jit(solution)/shard_map/ag2/ppermute | solution.py:204
  75.9 5.2 %feed_forward.4 = (f32[128,768]{1,0:T(8,128)S(1)}, bf16[128,768]{1,0:T(8,128)(2,1)}, bf16[128,768]{1,0:T(8,128)(2,1)}, bf16[128,768]{1,0:T(8,128)(2,1)S(1)}, bf1...) custom-call(s32[4,2]{1,0:T(4,128)S(1)} %copy.83.refs_0_, f32[2,8,768]{2,1,0:T(8,128)S(1)} %small_table.1.refs_1_, ...), custom_call_target="tpu_custom_call" | custom-call | flops 1207959552 | bytes 5799936 | tf_op jit(solution)/shard_map/feed_forward/pallas_call | solution.py:128
  83.9 4.4 %feed_forward.5 = (f32[128,768]{1,0:T(8,128)S(1)}, bf16[128,768]{1,0:T(8,128)(2,1)}, bf16[128,768]{1,0:T(8,128)(2,1)}, bf16[128,768]{1,0:T(8,128)(2,1)S(1)}) custom-call(s32[4,2]{1,0:T(4,128)S(1)} %copy.84.refs_0_, f32[2,8,768]{2,1,0:T(8,128)S(1)} %small_table.1.refs_1_, f32[2,8,768]{2,1,0:T(8,128)S(1)} %collective-permute-done.2.refs_2_, ...), custom_call_target="tpu_custom_call" | custom-call | flops 1207959552 | bytes 4227072 | tf_op jit(solution)/shard_map/feed_forward/pallas_call | solution.py:128
  91.1 2.1 collective-permute-done.29.refs_6_
  99.2 2.4 collective-permute-done.32.refs_6_
  103.3 3.6 queue_units.1.refs_5_
  107.0 3.1 collective-permute-done.35.refs_7_.refs_9_
  110.1 4.9 %attn_forward.6 = (f32[128,768]{1,0:T(8,128)S(1)}, bf16[128,768]{1,0:T(8,128)(2,1)S(1)}, bf16[128,768]{1,0:T(8,128)(2,1)S(1)}, bf16[128,768]{1,0:T(8,128)(2,1)S(...) custom-call(s32[4,2]{1,0:T(4,128)S(1)} %copy.88.refs_0_, ...), custom_call_target="tpu_custom_call" | custom-call | flops 704643072 | bytes 4623360 | tf_op jit(solution)/shard_map/attn_forward/pallas_call | solution.py:128
  119.3 7.3 %collective-permute-done.36.refs_3_ = f32[1,768]{1,0:T(1,128)S(1)} collective-permute-done((f32[1,768]{1,0:T(1,128)S(1)}, f32[1,768]{1,0:T(1,128)S(1)}, u32[]{:S(2)}, u32[]{:S(2)}) %collective-permute-start.36) | collective-permute-done | bytes 3104 | tf_op jit(solution)/shard_map/nb/ppermute | solution.py:204
  126.6 4.5 %attn_forward.7 = (f32[128,768]{1,0:T(8,128)S(1)}, bf16[128,768]{1,0:T(8,128)(2,1)S(1)}) custom-call(s32[4,2]{1,0:T(4,128)S(1)} %copy.89.refs_0_, f32[2,8,768]{2,1,0:T(8,128)S(1)} %small_table.1.refs_1_, f32[2,8,768]{2,1,0:T(8,128)S(1)} %collective-permute-done.2.refs_2_, f32[1,768]{1,0:T(1,128)S(1)} %collective-permute-done.36.refs_3_, ...), custom_call_target="tpu_custom_call" | custom-call | flops 704643072 | bytes 3443712 | tf_op jit(solution)/shard_map/attn_forward/pallas_call | solution.py:128
  134.3 2.2 collective-permute-start.44
  138.7 4.7 %collective-permute-start.47 = (bf16[128,768]{1,0:T(8,128)(2,1)S(1)}, bf16[128,768]{1,0:T(8,128)(2,1)S(1)}, u32[]{:S(2)}, u32[]{:S(2)}) collective-permute-start(bf16[128,768]{1,0:T(8,128)(2,1)S(1)} %norm_middle.7.refs_3_.refs_7_), channel_id=1, source_target_pairs={{0,2},{1,3},{2,0},{3,1},{16,17},{17,16},{18,19},{19,18},{4,6},{5,7... | collective-permute-start | bytes 589832 | tf_op jit(solution)/shard_map/ag2/ppermute | solution.py:204
  143.8 6.1 %collective-permute-start.48 = (bf16[128,768]{1,0:T(8,128)(2,1)S(1)}, bf16[128,768]{1,0:T(8,128)(2,1)S(1)}, u32[]{:S(2)}, u32[]{:S(2)}) collective-permute-start(bf16[128,768]{1,0:T(8,128)(2,1)S(1)} %norm_middle.7.refs_3_.refs_7_), channel_id=1, source_target_pairs={{0,3},{1,2},{2,1},{3,0},{16,19},{17,18},{18,17},{19,16},{4,7},{5,6... | collective-permute-start | bytes 589832 | tf_op jit(solution)/shard_map/ag2/ppermute | solution.py:204
  150.0 5.4 %feed_forward.6 = (f32[128,768]{1,0:T(8,128)S(1)}, bf16[128,768]{1,0:T(8,128)(2,1)S(1)}, bf16[128,768]{1,0:T(8,128)(2,1)}, bf16[128,768]{1,0:T(8,128)(2,1)}, bf1...) custom-call(s32[4,2]{1,0:T(4,128)S(1)} %copy.92.refs_0_, f32[2,8,768]{2,1,0:T(8,128)S(1)} %small_table.1.refs_1_, ...), custom_call_target="tpu_custom_call" | custom-call | flops 1207959552 | bytes 5799936 | tf_op jit(solution)/shard_map/feed_forward/pallas_call | solution.py:128
  155.5 1.9 collective-permute-start.49
  158.7 4.4 %feed_forward.7 = (f32[128,768]{1,0:T(8,128)S(1)}, bf16[128,768]{1,0:T(8,128)(2,1)}, bf16[128,768]{1,0:T(8,128)(2,1)}, bf16[128,768]{1,0:T(8,128)(2,1)}) custom-call(s32[4,2]{1,0:T(4,128)S(1)} %copy.93.refs_0_, f32[2,8,768]{2,1,0:T(8,128)S(1)} %small_table.1.refs_1_, f32[2,8,768]{2,1,0:T(8,128)S(1)} %collective-permute-done.2.refs_2_, ...), custom_call_target="tpu_custom_call" | custom-call | flops 1207959552 | bytes 4227072 | tf_op jit(solution)/shard_map/feed_forward/pallas_call | solution.py:128
  178.2 1.9 collective-permute-start.58
  181.6 2.8 collective-permute-done.59.refs_4_
  186.0 2.4 collective-permute-done.60.refs_9_
  197.4 1.9 last_backward.2
  202.2 2.0 collective-permute-done.66.refs_2_.refs_3_
  206.1 4.8 %collective-permute-done.68.refs_4_.refs_5_ = bf16[128,768]{1,0:T(8,128)(2,1)S(1)} collective-permute-done((bf16[128,768]{1,0:T(8,128)(2,1)S(1)}, bf16[128,768]{1,0:T(8,128)(2,1)S(1)}, u32[]{:S(2)}, u32[]{:S(2)}) %collective-permute-start.68) | collective-permute-done | bytes 196640 | tf_op jit(solution)/shard_map/ag3/ppermute | solution.py:204
  210.9 4.8 %feed_backward.2 = (bf16[128,768]{1,0:T(8,128)(2,1)S(1)}, bf16[128,768]{1,0:T(8,128)(2,1)S(1)}, bf16[128,768]{1,0:T(8,128)(2,1)S(1)}, f32[1,768]{1,0:T(1,128)S(1...) custom-call(s32[4,2]{1,0:T(4,128)S(1)} %copy.100.refs_0_, ...), custom_call_target="tpu_custom_call" | custom-call | flops 1207959552 | bytes 5508096 | tf_op jit(solution)/shard_map/feed_backward/pallas_call | solution.py:128
  221.0 5.7 %feed_weights.2 = (bf16[4,208,768]{2,1,0:T(8,128)(2,1)S(1)}, bf16[4,208,768]{2,1,0:T(8,128)(2,1)}) custom-call(s32[4,2]{1,0:T(4,128)S(1)} %copy.101.refs_0_, f32[1,768]{1,0:T(1,128)S(1)} %get-tuple-element.244.refs_1_, bf16[128,768]{1,0:T(8,128)(2,1)} %copy-done.18, bf16[128,768]{1,0:T(8,128)(2,1)} %copy-done.34, bf16[128,768]{1,0:T(8,128)(2,1)} %copy-done.35, ...), custom_call_target="tpu_custom_call" | custom-call | flops 1207959552 | bytes 5704704 | tf_op jit(solution)/shard_map/feed_weights/pallas_call | solution.py:128
  229.0 2.2 middle_backward.2
  234.4 3.1 add_cores.4
  238.8 4.4 %collective-permute-done.76.refs_4_.refs_5_ = bf16[128,768]{1,0:T(8,128)(2,1)S(1)} collective-permute-done((bf16[128,768]{1,0:T(8,128)(2,1)S(1)}, bf16[128,768]{1,0:T(8,128)(2,1)S(1)}, u32[]{:S(2)}, u32[]{:S(2)}) %collective-permute-start.76) | collective-permute-done | bytes 196640 | tf_op jit(solution)/shard_map/ag4/ppermute | solution.py:204
  243.5 6.5 %attn_backward.2 = (bf16[128,768]{1,0:T(8,128)(2,1)S(1)}, bf16[128,768]{1,0:T(8,128)(2,1)S(1)}, bf16[128,768]{1,0:T(8,128)(2,1)S(1)}, f32[2,768]{1,0:T(2,128)S(1...) custom-call(s32[4,2]{1,0:T(4,128)S(1)} %copy.104.refs_0_, ...), custom_call_target="tpu_custom_call" | custom-call | flops 805306368 | bytes 4921344 | tf_op jit(solution)/shard_map/attn_backward/pallas_call | solution.py:128
  253.9 4.8 %attn_weights.2 = (bf16[4,112,768]{2,1,0:T(8,128)(2,1)S(1)}, bf16[4,112,768]{2,1,0:T(8,128)(2,1)}) custom-call(s32[4,2]{1,0:T(4,128)S(1)} %copy.105.refs_0_, f32[2,768]{1,0:T(2,128)S(1)} %get-tuple-element.265.refs_1_, bf16[128,768]{1,0:T(8,128)(2,1)} %copy-done.7, bf16[128,768]{1,0:T(8,128)(2,1)} %copy-done.13, bf16[128,768]{1,0:T(8,128)(2,1)} %copy-done.14, ...), custom_call_target="tpu_custom_call" | custom-call | flops 603979776 | bytes 3741696 | tf_op jit(solution)/shard_map/attn_weights/pallas_call | solution.py:128
  258.8 3.2 collective-permute-done.80.refs_6_
  262.0 2.2 last_backward.3
  267.9 2.6 add_cores.5
  272.5 4.7 %collective-permute-done.84.refs_4_.refs_5_ = bf16[128,768]{1,0:T(8,128)(2,1)S(1)} collective-permute-done((bf16[128,768]{1,0:T(8,128)(2,1)S(1)}, bf16[128,768]{1,0:T(8,128)(2,1)S(1)}, u32[]{:S(2)}, u32[]{:S(2)}) %collective-permute-start.84) | collective-permute-done | bytes 196640 | tf_op jit(solution)/shard_map/ag3/ppermute | solution.py:204
  277.2 5.7 %feed_backward.3 = (bf16[128,768]{1,0:T(8,128)(2,1)}, bf16[128,768]{1,0:T(8,128)(2,1)}, bf16[128,768]{1,0:T(8,128)(2,1)}, f32[1,768]{1,0:T(1,128)S(1)}, bf16[128...) custom-call(s32[4,2]{1,0:T(4,128)S(1)} %copy.108.refs_0_, ...), custom_call_target="tpu_custom_call" | custom-call | flops 1207959552 | bytes 5508096 | tf_op jit(solution)/shard_map/feed_backward/pallas_call | solution.py:128
  283.6 5.8 %feed_weights.3 = (bf16[4,208,768]{2,1,0:T(8,128)(2,1)S(1)}, bf16[4,208,768]{2,1,0:T(8,128)(2,1)}) custom-call(s32[4,2]{1,0:T(4,128)S(1)} %copy.109.refs_0_, f32[1,768]{1,0:T(1,128)S(1)} %get-tuple-element.282.refs_1_, bf16[128,768]{1,0:T(8,128)(2,1)} %copy-done.16, bf16[128,768]{1,0:T(8,128)(2,1)} %copy-done.31, bf16[128,768]{1,0:T(8,128)(2,1)} %copy-done.32, ...), custom_call_target="tpu_custom_call" | custom-call | flops 1207959552 | bytes 5704704 | tf_op jit(solution)/shard_map/feed_weights/pallas_call | solution.py:128
  292.4 3.1 add_cores.6
  297.3 4.8 %collective-permute-done.89.refs_8_ = bf16[128,768]{1,0:T(8,128)(2,1)S(1)} collective-permute-done((bf16[128,768]{1,0:T(8,128)(2,1)}, bf16[128,768]{1,0:T(8,128)(2,1)S(1)}, u32[]{:S(2)}, u32[]{:S(2)}) %collective-permute-start.89) | collective-permute-done | bytes 196640 | tf_op jit(solution)/shard_map/rs3/ppermute | solution.py:204
  302.7 2.2 middle_backward.3
  307.7 2.0 collective-permute-done.90.refs_2_.refs_3_.refs_4_
  311.2 3.7 collective-permute-done.92.refs_4_.refs_5_.refs_6_
  315.0 6.5 %attn_backward.3 = (bf16[128,768]{1,0:T(8,128)(2,1)S(1)}, bf16[128,768]{1,0:T(8,128)(2,1)S(1)}, bf16[128,768]{1,0:T(8,128)(2,1)S(1)}, f32[2,768]{1,0:T(2,128)S(1...) custom-call(s32[4,2]{1,0:T(4,128)S(1)} %copy.112.refs_0_, ...), custom_call_target="tpu_custom_call" | custom-call | flops 805306368 | bytes 5019648 | tf_op jit(solution)/shard_map/attn_backward/pallas_call | solution.py:128
  321.6 4.8 %attn_weights.3 = (bf16[4,112,768]{2,1,0:T(8,128)(2,1)S(1)}, bf16[4,112,768]{2,1,0:T(8,128)(2,1)}) custom-call(s32[4,2]{1,0:T(4,128)S(1)} %copy.113.refs_0_, f32[2,768]{1,0:T(2,128)S(1)} %get-tuple-element.304.refs_1_, bf16[144,768]{1,0:T(8,128)(2,1)} %copy-done.5, bf16[144,768]{1,0:T(8,128)(2,1)} %copy-done.2, bf16[144,768]{1,0:T(8,128)(2,1)} %copy-done.3, ...), custom_call_target="tpu_custom_call" | custom-call | flops 603979776 | bytes 3840000 | tf_op jit(solution)/shard_map/attn_weights/pallas_call | solution.py:128
  326.3 4.1 %collective-permute-start.94 = (bf16[4,112,768]{2,1,0:T(8,128)(2,1)S(1)}, bf16[4,112,768]{2,1,0:T(8,128)(2,1)S(1)}, u32[]{:S(2)}, u32[]{:S(2)}) collective-permute-start(bf16[4,112,768]{2,1,0:T(8,128)(2,1)S(1)} %get-tuple-element.311), channel_id=1, source_target_pairs={{0,16},{16,0},{1,17},{17,1},{2,18},{18,2},{3,19},{19,3},{4,20},{20... | collective-permute-start | bytes 2064392 | tf_op jit(solution)/shard_map/lg/ppermute | solution.py:197
  331.0 2.3 collective-permute-done.93
  333.4 2.8 add_cores.7
  342.3 2.6 collective-permute-done.97
  344.9 2.8 collective-permute-done.98
  349.9 1.9 collective-permute-start.101
  351.9 2.3 collective-permute-start.100
  356.6 3.0 place_feed.1
  363.7 2.8 place_attn.1
  (388 shorter events, 132.8 us)
Async XLA Ops:
  7.2 119.4 %all-gather.2.cloned.1.call-start = ((), (), s32[]{:S(2)}) async-start(), calls=%async_computation.4 | async-start | bytes 1474560 | tf_op jit(solution)/shard_map/nb/all_gather | solution.py:1136
  7.2 20.4 %collective-permute-start = (bf16[576,768]{1,0:T(8,128)(2,1)}, bf16[576,768]{1,0:T(8,128)(2,1)S(1)}, u32[]{:S(2)}, u32[]{:S(2)}) collective-permute-start(bf16[576,768]{1,0:T(8,128)(2,1)} %bitcast.80), channel_id=1, source_target_pairs={{0,16},{16,0},{1,17},{17,1},{2,18},{18,2},{3,19},{19,3},{4,20},{20... | collective-permute-start | bytes 2654216 | tf_op jit(solution)/shard_map/w/ppermute | solution.py:197
  7.3 18.1 %collective-permute-start.1 = (bf16[192,768]{1,0:T(8,128)(2,1)}, bf16[192,768]{1,0:T(8,128)(2,1)}, u32[]{:S(2)}, u32[]{:S(2)}) collective-permute-start(bf16[192,768]{1,0:T(8,128)(2,1)} %bitcast.89), channel_id=1, source_target_pairs={{0,16},{16,0},{1,17},{17,1},{2,18},{18,2},{3,19},{19,3},{4,20},{20... | collective-permute-start | bytes 884744 | tf_op jit(solution)/shard_map/w/ppermute | solution.py:197
  7.8 22.3 %collective-permute-start.6 = (bf16[576,768]{1,0:T(8,128)(2,1)}, bf16[576,768]{1,0:T(8,128)(2,1)}, u32[]{:S(2)}, u32[]{:S(2)}) collective-permute-start(bf16[576,768]{1,0:T(8,128)(2,1)} %bitcast.75), channel_id=1, source_target_pairs={{0,16},{16,0},{1,17},{17,1},{2,18},{18,2},{3,19},{19,3},{4,20},{20... | collective-permute-start | bytes 2654216 | tf_op jit(solution)/shard_map/w/ppermute | solution.py:197
  16.4 8.5 %collective-permute-start.5 = (bf16[2,64,768]{2,1,0:T(8,128)(2,1)S(1)}, bf16[2,64,768]{2,1,0:T(8,128)(2,1)S(1)}, u32[]{:S(2)}, u32[]{:S(2)}) collective-permute-start(bf16[2,64,768]{2,1,0:T(8,128)(2,1)S(1)} %pad_maximum_fusion.1.refs_4_.refs_7_.refs_6_), channel_id=1, source_target_pairs={{0,3},{1,2},{2,1},{3,0},{16,19},{17,18},{18,17},{19,16},{4,7},{5,6... | collective-permute-start | bytes 589832 | tf_op jit(solution)/shard_map/ag0/ppermute | solution.py:204
  20.0 10.1 %collective-permute-start.7 = (bf16[192,768]{1,0:T(8,128)(2,1)S(1)}, bf16[192,768]{1,0:T(8,128)(2,1)S(1)}, u32[]{:S(2)}, u32[]{:S(2)}) collective-permute-start(bf16[192,768]{1,0:T(8,128)(2,1)S(1)} %bitcast.88), channel_id=1, source_target_pairs={{0,16},{16,0},{1,17},{17,1},{2,18},{18,2},{3,19},{19,3},{4,20},{20... | collective-permute-start | bytes 884744 | tf_op jit(solution)/shard_map/w/ppermute | solution.py:197
  24.9 13.6 %collective-permute-start.10 = (bf16[2,64,768]{2,1,0:T(8,128)(2,1)S(1)}, bf16[2,64,768]{2,1,0:T(8,128)(2,1)S(1)}, u32[]{:S(2)}, u32[]{:S(2)}) collective-permute-start(bf16[2,64,768]{2,1,0:T(8,128)(2,1)S(1)} %pad_maximum_fusion.refs_4_.refs_7_), channel_id=1, source_target_pairs={{0,3},{1,2},{2,1},{3,0},{16,19},{17,18},{18,17},{19,16},{4,7},{5,6... | collective-permute-start | bytes 589832 | tf_op jit(solution)/shard_map/ag0/ppermute | solution.py:204
  25.5 14.0 %collective-permute-start.8 = (bf16[2,64,768]{2,1,0:T(8,128)(2,1)S(1)}, bf16[2,64,768]{2,1,0:T(8,128)(2,1)S(1)}, u32[]{:S(2)}, u32[]{:S(2)}) collective-permute-start(bf16[2,64,768]{2,1,0:T(8,128)(2,1)S(1)} %pad_maximum_fusion.refs_4_.refs_7_), channel_id=1, source_target_pairs={{0,1},{1,0},{2,3},{3,2},{16,18},{17,19},{18,16},{19,17},{4,5},{5,4... | collective-permute-start | bytes 589832 | tf_op jit(solution)/shard_map/ag0/ppermute | solution.py:204
  27.6 13.7 %collective-permute-start.9 = (bf16[2,64,768]{2,1,0:T(8,128)(2,1)S(1)}, bf16[2,64,768]{2,1,0:T(8,128)(2,1)S(1)}, u32[]{:S(2)}, u32[]{:S(2)}) collective-permute-start(bf16[2,64,768]{2,1,0:T(8,128)(2,1)S(1)} %pad_maximum_fusion.refs_4_.refs_7_), channel_id=1, source_target_pairs={{0,2},{1,3},{2,0},{3,1},{16,17},{17,16},{18,19},{19,18},{4,6},{5,7... | collective-permute-start | bytes 589832 | tf_op jit(solution)/shard_map/ag0/ppermute | solution.py:204
  36.7 9.2 %collective-permute-start.11 = (bf16[128,768]{1,0:T(8,128)(2,1)}, bf16[128,768]{1,0:T(8,128)(2,1)S(1)}, u32[]{:S(2)}, u32[]{:S(2)}) collective-permute-start(bf16[128,768]{1,0:T(8,128)(2,1)} %get-tuple-element.177), channel_id=1, source_target_pairs={{0,1},{1,0},{2,3},{3,2},{16,18},{17,19},{18,16},{19,17},{4,5},{5,4... | collective-permute-start | bytes 589832 | tf_op jit(solution)/shard_map/rs1/ppermute | solution.py:204
  38.1 9.1 %collective-permute-start.12 = (bf16[128,768]{1,0:T(8,128)(2,1)}, bf16[128,768]{1,0:T(8,128)(2,1)S(1)}, u32[]{:S(2)}, u32[]{:S(2)}) collective-permute-start(bf16[128,768]{1,0:T(8,128)(2,1)} %get-tuple-element.178), channel_id=1, source_target_pairs={{0,2},{1,3},{2,0},{3,1},{16,17},{17,16},{18,19},{19,18},{4,6},{5,7... | collective-permute-start | bytes 589832 | tf_op jit(solution)/shard_map/rs1/ppermute | solution.py:204
  38.5 9.5 %collective-permute-start.13 = (bf16[128,768]{1,0:T(8,128)(2,1)}, bf16[128,768]{1,0:T(8,128)(2,1)S(1)}, u32[]{:S(2)}, u32[]{:S(2)}) collective-permute-start(bf16[128,768]{1,0:T(8,128)(2,1)} %get-tuple-element.179), channel_id=1, source_target_pairs={{0,3},{1,2},{2,1},{3,0},{16,19},{17,18},{18,17},{19,16},{4,7},{5,6... | collective-permute-start | bytes 589832 | tf_op jit(solution)/shard_map/rs1/ppermute | solution.py:204
  39.4 23.7 %collective-permute-start.20 = (bf16[768,768]{1,0:T(8,128)(2,1)}, bf16[768,768]{1,0:T(8,128)(2,1)}, u32[]{:S(2)}, u32[]{:S(2)}) collective-permute-start(bf16[768,768]{1,0:T(8,128)(2,1)} %bitcast.26.refs_7_.refs_6_), channel_id=1, source_target_pairs={{0,16},{16,0},{1,17},{17,1},{2,18},{18,2},{3,19},{19,3},{4,20},{20... | collective-permute-start | bytes 3538952 | tf_op jit(solution)/shard_map/w/ppermute | solution.py:197
  41.3 22.5 %collective-permute-start.21 = (bf16[768,768]{1,0:T(8,128)(2,1)}, bf16[768,768]{1,0:T(8,128)(2,1)}, u32[]{:S(2)}, u32[]{:S(2)}) collective-permute-start(bf16[768,768]{1,0:T(8,128)(2,1)} %bitcast.27.refs_8_.refs_7_), channel_id=1, source_target_pairs={{0,16},{16,0},{1,17},{17,1},{2,18},{18,2},{3,19},{19,3},{4,20},{20... | collective-permute-start | bytes 3538952 | tf_op jit(solution)/shard_map/w/ppermute | solution.py:197
  48.0 9.7 %collective-permute-start.16 = (bf16[128,768]{1,0:T(8,128)(2,1)S(1)}, bf16[128,768]{1,0:T(8,128)(2,1)S(1)}, u32[]{:S(2)}, u32[]{:S(2)}) collective-permute-start(bf16[128,768]{1,0:T(8,128)(2,1)S(1)} %get-tuple-element.184), channel_id=1, source_target_pairs={{0,3},{1,2},{2,1},{3,0},{16,19},{17,18},{18,17},{19,16},{4,7},{5,6... | collective-permute-start | bytes 589832 | tf_op jit(solution)/shard_map/rs1/ppermute | solution.py:204
  51.9 10.1 %collective-permute-start.38 = (bf16[192,768]{1,0:T(8,128)(2,1)}, bf16[192,768]{1,0:T(8,128)(2,1)}, u32[]{:S(2)}, u32[]{:S(2)}) collective-permute-start(bf16[192,768]{1,0:T(8,128)(2,1)} %select_select_fusion), channel_id=1, source_target_pairs={{0,2},{1,3},{2,0},{3,1},{16,17},{17,16},{18,19},{19,18},{4,6},{5,7... | collective-permute-start | bytes 884744 | tf_op jit(solution)/shard_map/nb/ppermute | solution.py:204
  53.7 27.6 %collective-permute-start.25 = (bf16[768,768]{1,0:T(8,128)(2,1)}, bf16[768,768]{1,0:T(8,128)(2,1)}, u32[]{:S(2)}, u32[]{:S(2)}) collective-permute-start(bf16[768,768]{1,0:T(8,128)(2,1)} %bitcast.28.refs_7_), channel_id=1, source_target_pairs={{0,16},{16,0},{1,17},{17,1},{2,18},{18,2},{3,19},{19,3},{4,20},{20... | collective-permute-start | bytes 3538952 | tf_op jit(solution)/shard_map/w/ppermute | solution.py:197
  57.7 24.2 %collective-permute-start.26 = (bf16[768,768]{1,0:T(8,128)(2,1)}, bf16[768,768]{1,0:T(8,128)(2,1)}, u32[]{:S(2)}, u32[]{:S(2)}) collective-permute-start(bf16[768,768]{1,0:T(8,128)(2,1)} %bitcast.29.refs_8_), channel_id=1, source_target_pairs={{0,16},{16,0},{1,17},{17,1},{2,18},{18,2},{3,19},{19,3},{4,20},{20... | collective-permute-start | bytes 3538952 | tf_op jit(solution)/shard_map/w/ppermute | solution.py:197
  61.9 221.5 %reduce-scatter.5.cloned.1.call-start = ((), (), s32[]{:S(2)}) async-start(), calls=%async_computation.5 | async-start | bytes 1597440 | tf_op jit(solution)/shard_map/rg/reduce_scatter | solution.py:1229
  63.9 11.1 %collective-permute-start.19 = (bf16[128,768]{1,0:T(8,128)(2,1)S(1)}, bf16[128,768]{1,0:T(8,128)(2,1)S(1)}, u32[]{:S(2)}, u32[]{:S(2)}) collective-permute-start(bf16[128,768]{1,0:T(8,128)(2,1)S(1)} %get-tuple-element.180.refs_3_.refs_7_.refs_6_), channel_id=1, source_target_pairs={{0,3},{1,2},{2,1},{3,0},{16,19},{17,18},{18,17},{19,16},{4,7},{5,6... | collective-permute-start | bytes 589832 | tf_op jit(solution)/shard_map/ag2/ppermute | solution.py:204
  67.6 15.5 %collective-permute-start.22 = (bf16[128,768]{1,0:T(8,128)(2,1)S(1)}, bf16[128,768]{1,0:T(8,128)(2,1)S(1)}, u32[]{:S(2)}, u32[]{:S(2)}) collective-permute-start(bf16[128,768]{1,0:T(8,128)(2,1)S(1)} %norm_middle.5.refs_3_.refs_7_), channel_id=1, source_target_pairs={{0,1},{1,0},{2,3},{3,2},{16,18},{17,19},{18,16},{19,17},{4,5},{5,4... | collective-permute-start | bytes 589832 | tf_op jit(solution)/shard_map/ag2/ppermute | solution.py:204
  69.9 14.1 %collective-permute-start.23 = (bf16[128,768]{1,0:T(8,128)(2,1)S(1)}, bf16[128,768]{1,0:T(8,128)(2,1)S(1)}, u32[]{:S(2)}, u32[]{:S(2)}) collective-permute-start(bf16[128,768]{1,0:T(8,128)(2,1)S(1)} %norm_middle.5.refs_3_.refs_7_), channel_id=1, source_target_pairs={{0,2},{1,3},{2,0},{3,1},{16,17},{17,16},{18,19},{19,18},{4,6},{5,7... | collective-permute-start | bytes 589832 | tf_op jit(solution)/shard_map/ag2/ppermute | solution.py:204
  75.0 8.9 %collective-permute-start.24 = (bf16[128,768]{1,0:T(8,128)(2,1)S(1)}, bf16[128,768]{1,0:T(8,128)(2,1)S(1)}, u32[]{:S(2)}, u32[]{:S(2)}) collective-permute-start(bf16[128,768]{1,0:T(8,128)(2,1)S(1)} %norm_middle.5.refs_3_.refs_7_), channel_id=1, source_target_pairs={{0,3},{1,2},{2,1},{3,0},{16,19},{17,18},{18,17},{19,16},{4,7},{5,6... | collective-permute-start | bytes 589832 | tf_op jit(solution)/shard_map/ag2/ppermute | solution.py:204
  81.3 9.0 %collective-permute-start.27 = (bf16[128,768]{1,0:T(8,128)(2,1)}, bf16[128,768]{1,0:T(8,128)(2,1)S(1)}, u32[]{:S(2)}, u32[]{:S(2)}) collective-permute-start(bf16[128,768]{1,0:T(8,128)(2,1)} %get-tuple-element.190), channel_id=1, source_target_pairs={{0,1},{1,0},{2,3},{3,2},{16,18},{17,19},{18,16},{19,17},{4,5},{5,4... | collective-permute-start | bytes 589832 | tf_op jit(solution)/shard_map/rs2/ppermute | solution.py:204
  81.9 9.2 %collective-permute-start.28 = (bf16[128,768]{1,0:T(8,128)(2,1)}, bf16[128,768]{1,0:T(8,128)(2,1)S(1)}, u32[]{:S(2)}, u32[]{:S(2)}) collective-permute-start(bf16[128,768]{1,0:T(8,128)(2,1)} %get-tuple-element.191), channel_id=1, source_target_pairs={{0,2},{1,3},{2,0},{3,1},{16,17},{17,16},{18,19},{19,18},{4,6},{5,7... | collective-permute-start | bytes 589832 | tf_op jit(solution)/shard_map/rs2/ppermute | solution.py:204
  83.1 10.1 %collective-permute-start.29 = (bf16[128,768]{1,0:T(8,128)(2,1)S(1)}, bf16[128,768]{1,0:T(8,128)(2,1)S(1)}, u32[]{:S(2)}, u32[]{:S(2)}) collective-permute-start(bf16[128,768]{1,0:T(8,128)(2,1)S(1)} %get-tuple-element.192), channel_id=1, source_target_pairs={{0,3},{1,2},{2,1},{3,0},{16,19},{17,18},{18,17},{19,16},{4,7},{5,6... | collective-permute-start | bytes 589832 | tf_op jit(solution)/shard_map/rs2/ppermute | solution.py:204
  88.3 9.1 %collective-permute-start.30 = (bf16[128,768]{1,0:T(8,128)(2,1)}, bf16[128,768]{1,0:T(8,128)(2,1)S(1)}, u32[]{:S(2)}, u32[]{:S(2)}) collective-permute-start(bf16[128,768]{1,0:T(8,128)(2,1)} %get-tuple-element.195), channel_id=1, source_target_pairs={{0,1},{1,0},{2,3},{3,2},{16,18},{17,19},{18,16},{19,17},{4,5},{5,4... | collective-permute-start | bytes 589832 | tf_op jit(solution)/shard_map/rs2/ppermute | solution.py:204
  89.0 10.2 %collective-permute-start.31 = (bf16[128,768]{1,0:T(8,128)(2,1)}, bf16[128,768]{1,0:T(8,128)(2,1)S(1)}, u32[]{:S(2)}, u32[]{:S(2)}) collective-permute-start(bf16[128,768]{1,0:T(8,128)(2,1)} %get-tuple-element.196), channel_id=1, source_target_pairs={{0,2},{1,3},{2,0},{3,1},{16,17},{17,16},{18,19},{19,18},{4,6},{5,7... | collective-permute-start | bytes 589832 | tf_op jit(solution)/shard_map/rs2/ppermute | solution.py:204
  90.2 11.4 %collective-permute-start.32 = (bf16[128,768]{1,0:T(8,128)(2,1)S(1)}, bf16[128,768]{1,0:T(8,128)(2,1)S(1)}, u32[]{:S(2)}, u32[]{:S(2)}) collective-permute-start(bf16[128,768]{1,0:T(8,128)(2,1)S(1)} %get-tuple-element.197), channel_id=1, source_target_pairs={{0,3},{1,2},{2,1},{3,0},{16,19},{17,18},{18,17},{19,16},{4,7},{5,6... | collective-permute-start | bytes 589832 | tf_op jit(solution)/shard_map/rs2/ppermute | solution.py:204
  94.7 12.3 %collective-permute-start.33 = (bf16[128,768]{1,0:T(8,128)(2,1)S(1)}, bf16[128,768]{1,0:T(8,128)(2,1)S(1)}, u32[]{:S(2)}, u32[]{:S(2)}) collective-permute-start(bf16[128,768]{1,0:T(8,128)(2,1)S(1)} %get-tuple-element.193.refs_4_.refs_7_.refs_6_), channel_id=1, source_target_pairs={{0,1},{1,0},{2,3},{3,2},{16,18},{17,19},{18,16},{19,17},{4,5},{5,4... | collective-permute-start | bytes 589832 | tf_op jit(solution)/shard_map/ag1/ppermute | solution.py:204
  95.4 11.6 %collective-permute-start.34 = (bf16[128,768]{1,0:T(8,128)(2,1)S(1)}, bf16[128,768]{1,0:T(8,128)(2,1)S(1)}, u32[]{:S(2)}, u32[]{:S(2)}) collective-permute-start(bf16[128,768]{1,0:T(8,128)(2,1)S(1)} %get-tuple-element.193.refs_4_.refs_7_.refs_6_), channel_id=1, source_target_pairs={{0,2},{1,3},{2,0},{3,1},{16,17},{17,16},{18,19},{19,18},{4,6},{5,7... | collective-permute-start | bytes 589832 | tf_op jit(solution)/shard_map/ag1/ppermute | solution.py:204
  97.3 12.8 %collective-permute-start.35 = (bf16[128,768]{1,0:T(8,128)(2,1)S(1)}, bf16[128,768]{1,0:T(8,128)(2,1)S(1)}, u32[]{:S(2)}, u32[]{:S(2)}) collective-permute-start(bf16[128,768]{1,0:T(8,128)(2,1)S(1)} %get-tuple-element.193.refs_4_.refs_7_.refs_6_), channel_id=1, source_target_pairs={{0,3},{1,2},{2,1},{3,0},{16,19},{17,18},{18,17},{19,16},{4,7},{5,6... | collective-permute-start | bytes 589832 | tf_op jit(solution)/shard_map/ag1/ppermute | solution.py:204
  102.5 24.0 %collective-permute-start.37 = (bf16[128,768]{1,0:T(8,128)(2,1)S(1)}, bf16[128,768]{1,0:T(8,128)(2,1)S(1)}, u32[]{:S(2)}, u32[]{:S(2)}) collective-permute-start(bf16[128,768]{1,0:T(8,128)(2,1)S(1)} %norm_last.5.refs_4_.refs_5_), channel_id=1, source_target_pairs={{0,1},{1,0},{2,3},{3,2},{16,18},{17,19},{18,16},{19,17},{4,5},{5,4... | collective-permute-start | bytes 589832 | tf_op jit(solution)/shard_map/ag1/ppermute | solution.py:204
  115.1 16.2 %collective-permute-start.39 = (bf16[128,768]{1,0:T(8,128)(2,1)S(1)}, bf16[128,768]{1,0:T(8,128)(2,1)S(1)}, u32[]{:S(2)}, u32[]{:S(2)}) collective-permute-start(bf16[128,768]{1,0:T(8,128)(2,1)S(1)} %get-tuple-element.207), channel_id=1, source_target_pairs={{0,1},{1,0},{2,3},{3,2},{16,18},{17,19},{18,16},{19,17},{4,5},{5,4... | collective-permute-start | bytes 589832 | tf_op jit(solution)/shard_map/rs1/ppermute | solution.py:204
  115.7 15.6 %collective-permute-start.40 = (bf16[128,768]{1,0:T(8,128)(2,1)S(1)}, bf16[128,768]{1,0:T(8,128)(2,1)S(1)}, u32[]{:S(2)}, u32[]{:S(2)}) collective-permute-start(bf16[128,768]{1,0:T(8,128)(2,1)S(1)} %get-tuple-element.208), channel_id=1, source_target_pairs={{0,2},{1,3},{2,0},{3,1},{16,17},{17,16},{18,19},{19,18},{4,6},{5,7... | collective-permute-start | bytes 589832 | tf_op jit(solution)/shard_map/rs1/ppermute | solution.py:204
  117.6 13.6 %collective-permute-start.41 = (bf16[128,768]{1,0:T(8,128)(2,1)S(1)}, bf16[128,768]{1,0:T(8,128)(2,1)S(1)}, u32[]{:S(2)}, u32[]{:S(2)}) collective-permute-start(bf16[128,768]{1,0:T(8,128)(2,1)S(1)} %get-tuple-element.209), channel_id=1, source_target_pairs={{0,3},{1,2},{2,1},{3,0},{16,19},{17,18},{18,17},{19,16},{4,7},{5,6... | collective-permute-start | bytes 589832 | tf_op jit(solution)/shard_map/rs1/ppermute | solution.py:204
  117.8 8.7 %collective-permute-start.36 = (f32[1,768]{1,0:T(1,128)S(1)}, f32[1,768]{1,0:T(1,128)S(1)}, u32[]{:S(2)}, u32[]{:S(2)}) collective-permute-start(f32[1,768]{1,0:T(1,128)S(1)} %fusion.3), channel_id=1, source_target_pairs={{0,2},{1,3},{2,0},{3,1},{16,17},{17,16},{18,19},{19,18},{4,6},{5,7... | collective-permute-start | bytes 9224 | tf_op jit(solution)/shard_map/nb/ppermute | solution.py:204
  132.9 10.9 %collective-permute-start.43 = (bf16[128,768]{1,0:T(8,128)(2,1)S(1)}, bf16[128,768]{1,0:T(8,128)(2,1)S(1)}, u32[]{:S(2)}, u32[]{:S(2)}) collective-permute-start(bf16[128,768]{1,0:T(8,128)(2,1)S(1)} %get-tuple-element.210.refs_3_.refs_7_.refs_6_), channel_id=1, source_target_pairs={{0,1},{1,0},{2,3},{3,2},{16,18},{17,19},{18,16},{19,17},{4,5},{5,4... | collective-permute-start | bytes 589832 | tf_op jit(solution)/shard_map/ag2/ppermute | solution.py:204
  134.3 15.7 %collective-permute-start.44 = (bf16[128,768]{1,0:T(8,128)(2,1)S(1)}, bf16[128,768]{1,0:T(8,128)(2,1)S(1)}, u32[]{:S(2)}, u32[]{:S(2)}) collective-permute-start(bf16[128,768]{1,0:T(8,128)(2,1)S(1)} %get-tuple-element.210.refs_3_.refs_7_.refs_6_), channel_id=1, source_target_pairs={{0,2},{1,3},{2,0},{3,1},{16,17},{17,16},{18,19},{19,18},{4,6},{5,7... | collective-permute-start | bytes 589832 | tf_op jit(solution)/shard_map/ag2/ppermute | solution.py:204
  136.5 13.5 %collective-permute-start.45 = (bf16[128,768]{1,0:T(8,128)(2,1)S(1)}, bf16[128,768]{1,0:T(8,128)(2,1)S(1)}, u32[]{:S(2)}, u32[]{:S(2)}) collective-permute-start(bf16[128,768]{1,0:T(8,128)(2,1)S(1)} %get-tuple-element.210.refs_3_.refs_7_.refs_6_), channel_id=1, source_target_pairs={{0,3},{1,2},{2,1},{3,0},{16,19},{17,18},{18,17},{19,16},{4,7},{5,6... | collective-permute-start | bytes 589832 | tf_op jit(solution)/shard_map/ag2/ppermute | solution.py:204
  137.5 20.0 %collective-permute-start.46 = (bf16[128,768]{1,0:T(8,128)(2,1)S(1)}, bf16[128,768]{1,0:T(8,128)(2,1)S(1)}, u32[]{:S(2)}, u32[]{:S(2)}) collective-permute-start(bf16[128,768]{1,0:T(8,128)(2,1)S(1)} %norm_middle.7.refs_3_.refs_7_), channel_id=1, source_target_pairs={{0,1},{1,0},{2,3},{3,2},{16,18},{17,19},{18,16},{19,17},{4,5},{5,4... | collective-permute-start | bytes 589832 | tf_op jit(solution)/shard_map/ag2/ppermute | solution.py:204
  138.7 20.0 %collective-permute-start.47 = (bf16[128,768]{1,0:T(8,128)(2,1)S(1)}, bf16[128,768]{1,0:T(8,128)(2,1)S(1)}, u32[]{:S(2)}, u32[]{:S(2)}) collective-permute-start(bf16[128,768]{1,0:T(8,128)(2,1)S(1)} %norm_middle.7.refs_3_.refs_7_), channel_id=1, source_target_pairs={{0,2},{1,3},{2,0},{3,1},{16,17},{17,16},{18,19},{19,18},{4,6},{5,7... | collective-permute-start | bytes 589832 | tf_op jit(solution)/shard_map/ag2/ppermute | solution.py:204
  143.8 14.9 %collective-permute-start.48 = (bf16[128,768]{1,0:T(8,128)(2,1)S(1)}, bf16[128,768]{1,0:T(8,128)(2,1)S(1)}, u32[]{:S(2)}, u32[]{:S(2)}) collective-permute-start(bf16[128,768]{1,0:T(8,128)(2,1)S(1)} %norm_middle.7.refs_3_.refs_7_), channel_id=1, source_target_pairs={{0,3},{1,2},{2,1},{3,0},{16,19},{17,18},{18,17},{19,16},{4,7},{5,6... | collective-permute-start | bytes 589832 | tf_op jit(solution)/shard_map/ag2/ppermute | solution.py:204
  155.5 9.3 %collective-permute-start.49 = (bf16[128,768]{1,0:T(8,128)(2,1)S(1)}, bf16[128,768]{1,0:T(8,128)(2,1)S(1)}, u32[]{:S(2)}, u32[]{:S(2)}) collective-permute-start(bf16[128,768]{1,0:T(8,128)(2,1)S(1)} %get-tuple-element.218), channel_id=1, source_target_pairs={{0,1},{1,0},{2,3},{3,2},{16,18},{17,19},{18,16},{19,17},{4,5},{5,4... | collective-permute-start | bytes 589832 | tf_op jit(solution)/shard_map/rs2/ppermute | solution.py:204
  157.5 8.5 %collective-permute-start.50 = (bf16[128,768]{1,0:T(8,128)(2,1)}, bf16[128,768]{1,0:T(8,128)(2,1)S(1)}, u32[]{:S(2)}, u32[]{:S(2)}) collective-permute-start(bf16[128,768]{1,0:T(8,128)(2,1)} %get-tuple-element.219), channel_id=1, source_target_pairs={{0,2},{1,3},{2,0},{3,1},{16,17},{17,16},{18,19},{19,18},{4,6},{5,7... | collective-permute-start | bytes 589832 | tf_op jit(solution)/shard_map/rs2/ppermute | solution.py:204
  157.5 9.8 %collective-permute-start.51 = (bf16[128,768]{1,0:T(8,128)(2,1)}, bf16[128,768]{1,0:T(8,128)(2,1)S(1)}, u32[]{:S(2)}, u32[]{:S(2)}) collective-permute-start(bf16[128,768]{1,0:T(8,128)(2,1)} %get-tuple-element.220), channel_id=1, source_target_pairs={{0,3},{1,2},{2,1},{3,0},{16,19},{17,18},{18,17},{19,16},{4,7},{5,6... | collective-permute-start | bytes 589832 | tf_op jit(solution)/shard_map/rs2/ppermute | solution.py:204
  163.1 7.7 %collective-permute-start.53 = (bf16[128,768]{1,0:T(8,128)(2,1)}, bf16[128,768]{1,0:T(8,128)(2,1)}, u32[]{:S(2)}, u32[]{:S(2)}) collective-permute-start(bf16[128,768]{1,0:T(8,128)(2,1)} %get-tuple-element.223), channel_id=1, source_target_pairs={{0,1},{1,0},{2,3},{3,2},{16,18},{17,19},{18,16},{19,17},{4,5},{5,4... | collective-permute-start | bytes 589832 | tf_op jit(solution)/shard_map/rs2/ppermute | solution.py:204
  201.0 9.8 %collective-permute-start.68 = (bf16[128,768]{1,0:T(8,128)(2,1)S(1)}, bf16[128,768]{1,0:T(8,128)(2,1)S(1)}, u32[]{:S(2)}, u32[]{:S(2)}) collective-permute-start(bf16[128,768]{1,0:T(8,128)(2,1)S(1)} %get-tuple-element.241.refs_1_.refs_2_.refs_4_), channel_id=1, source_target_pairs={{0,3},{1,2},{2,1},{3,0},{16,19},{17,18},{18,17},{19,16},{4,7},{5,6... | collective-permute-start | bytes 589832 | tf_op jit(solution)/shard_map/ag3/ppermute | solution.py:204
  215.7 11.5 %collective-permute-start.70 = (bf16[128,768]{1,0:T(8,128)(2,1)S(1)}, bf16[128,768]{1,0:T(8,128)(2,1)S(1)}, u32[]{:S(2)}, u32[]{:S(2)}) collective-permute-start(bf16[128,768]{1,0:T(8,128)(2,1)S(1)} %get-tuple-element.252), channel_id=1, source_target_pairs={{0,1},{1,0},{2,3},{3,2},{16,18},{17,19},{18,16},{19,17},{4,5},{5,4... | collective-permute-start | bytes 589832 | tf_op jit(solution)/shard_map/rs3/ppermute | solution.py:204
  216.4 10.8 %collective-permute-start.71 = (bf16[128,768]{1,0:T(8,128)(2,1)S(1)}, bf16[128,768]{1,0:T(8,128)(2,1)S(1)}, u32[]{:S(2)}, u32[]{:S(2)}) collective-permute-start(bf16[128,768]{1,0:T(8,128)(2,1)S(1)} %get-tuple-element.253), channel_id=1, source_target_pairs={{0,2},{1,3},{2,0},{3,1},{16,17},{17,16},{18,19},{19,18},{4,6},{5,7... | collective-permute-start | bytes 589832 | tf_op jit(solution)/shard_map/rs3/ppermute | solution.py:204
  218.3 10.7 %collective-permute-start.72 = (bf16[128,768]{1,0:T(8,128)(2,1)S(1)}, bf16[128,768]{1,0:T(8,128)(2,1)S(1)}, u32[]{:S(2)}, u32[]{:S(2)}) collective-permute-start(bf16[128,768]{1,0:T(8,128)(2,1)S(1)} %get-tuple-element.254), channel_id=1, source_target_pairs={{0,3},{1,2},{2,1},{3,0},{16,19},{17,18},{18,17},{19,16},{4,7},{5,6... | collective-permute-start | bytes 589832 | tf_op jit(solution)/shard_map/rs3/ppermute | solution.py:204
  233.3 9.8 %collective-permute-start.76 = (bf16[128,768]{1,0:T(8,128)(2,1)S(1)}, bf16[128,768]{1,0:T(8,128)(2,1)S(1)}, u32[]{:S(2)}, u32[]{:S(2)}) collective-permute-start(bf16[128,768]{1,0:T(8,128)(2,1)S(1)} %get-tuple-element.257.refs_1_.refs_2_.refs_3_), channel_id=1, source_target_pairs={{0,3},{1,2},{2,1},{3,0},{16,19},{17,18},{18,17},{19,16},{4,7},{5,6... | collective-permute-start | bytes 589832 | tf_op jit(solution)/shard_map/ag4/ppermute | solution.py:204
  243.2 59.1 %reduce-scatter.7.cloned.1.call-start = ((), (), s32[]{:S(2)}) async-start(), calls=%async_computation.6 | async-start | bytes 860160 | tf_op jit(solution)/shard_map/rg/reduce_scatter | solution.py:1229
  250.0 8.7 %collective-permute-start.78 = (bf16[128,768]{1,0:T(8,128)(2,1)S(1)}, bf16[128,768]{1,0:T(8,128)(2,1)S(1)}, u32[]{:S(2)}, u32[]{:S(2)}) collective-permute-start(bf16[128,768]{1,0:T(8,128)(2,1)S(1)} %get-tuple-element.271), channel_id=1, source_target_pairs={{0,1},{1,0},{2,3},{3,2},{16,18},{17,19},{18,16},{19,17},{4,5},{5,4... | collective-permute-start | bytes 589832 | tf_op jit(solution)/shard_map/rs4/ppermute | solution.py:204
  251.1 7.6 %collective-permute-start.79 = (bf16[128,768]{1,0:T(8,128)(2,1)S(1)}, bf16[128,768]{1,0:T(8,128)(2,1)S(1)}, u32[]{:S(2)}, u32[]{:S(2)}) collective-permute-start(bf16[128,768]{1,0:T(8,128)(2,1)S(1)} %get-tuple-element.272), channel_id=1, source_target_pairs={{0,2},{1,3},{2,0},{3,1},{16,17},{17,16},{18,19},{19,18},{4,6},{5,7... | collective-permute-start | bytes 589832 | tf_op jit(solution)/shard_map/rs4/ppermute | solution.py:204
  252.0 10.0 %collective-permute-start.80 = (bf16[128,768]{1,0:T(8,128)(2,1)S(1)}, bf16[128,768]{1,0:T(8,128)(2,1)S(1)}, u32[]{:S(2)}, u32[]{:S(2)}) collective-permute-start(bf16[128,768]{1,0:T(8,128)(2,1)S(1)} %get-tuple-element.273), channel_id=1, source_target_pairs={{0,3},{1,2},{2,1},{3,0},{16,19},{17,18},{18,17},{19,16},{4,7},{5,6... | collective-permute-start | bytes 589832 | tf_op jit(solution)/shard_map/rs4/ppermute | solution.py:204
  267.0 10.2 %collective-permute-start.84 = (bf16[128,768]{1,0:T(8,128)(2,1)S(1)}, bf16[128,768]{1,0:T(8,128)(2,1)S(1)}, u32[]{:S(2)}, u32[]{:S(2)}) collective-permute-start(bf16[128,768]{1,0:T(8,128)(2,1)S(1)} %get-tuple-element.276.refs_1_.refs_2_.refs_5_), channel_id=1, source_target_pairs={{0,3},{1,2},{2,1},{3,0},{16,19},{17,18},{18,17},{19,16},{4,7},{5,6... | collective-permute-start | bytes 589832 | tf_op jit(solution)/shard_map/ag3/ppermute | solution.py:204
  283.5 66.4 %reduce-scatter.9.cloned.1.call-start = ((), (), s32[]{:S(2)}) async-start(), calls=%async_computation.7 | async-start | bytes 1597440 | tf_op jit(solution)/shard_map/rg/reduce_scatter | solution.py:1229
  291.4 10.7 %collective-permute-start.89 = (bf16[128,768]{1,0:T(8,128)(2,1)}, bf16[128,768]{1,0:T(8,128)(2,1)S(1)}, u32[]{:S(2)}, u32[]{:S(2)}) collective-permute-start(bf16[128,768]{1,0:T(8,128)(2,1)} %get-tuple-element.296), channel_id=1, source_target_pairs={{0,3},{1,2},{2,1},{3,0},{16,19},{17,18},{18,17},{19,16},{4,7},{5,6... | collective-permute-start | bytes 589832 | tf_op jit(solution)/shard_map/rs3/ppermute | solution.py:204
  302.3 57.2 %reduce-scatter.11.cloned.1.call-start = ((), (), s32[]{:S(2)}) async-start(), calls=%async_computation.8 | async-start | bytes 860160 | tf_op jit(solution)/shard_map/lg/reduce_scatter | solution.py:1327
  338.7 8.9 %collective-permute-start.98 = (bf16[128,768]{1,0:T(8,128)(2,1)S(1)}, bf16[128,768]{1,0:T(8,128)(2,1)S(1)}, u32[]{:S(2)}, u32[]{:S(2)}) collective-permute-start(bf16[128,768]{1,0:T(8,128)(2,1)S(1)} %get-tuple-element.317), channel_id=1, source_target_pairs={{0,3},{1,2},{2,1},{3,0},{16,19},{17,18},{18,17},{19,16},{4,7},{5,6... | collective-permute-start | bytes 589832 | tf_op jit(solution)/shard_map/rs4/ppermute | solution.py:204
  339.2 15.8 %collective-permute-start.102 = (bf16[208,768]{1,0:T(8,128)(2,1)S(1)}, bf16[208,768]{1,0:T(8,128)(2,1)S(1)}, u32[]{:S(2)}, u32[]{:S(2)}) collective-permute-start(bf16[208,768]{1,0:T(8,128)(2,1)S(1)} %bitcast.97), channel_id=1, source_target_pairs={{0,16},{16,0},{1,17},{17,1},{2,18},{18,2},{3,19},{19,3},{4,20},{20... | collective-permute-start | bytes 958472 | tf_op jit(solution)/shard_map/fg/ppermute | solution.py:197
  340.8 7.9 %collective-permute-start.95 = (f32[1,128]{1,0:T(1,128)S(1)}, f32[1,128]{1,0:T(1,128)S(1)}, u32[]{:S(2)}, u32[]{:S(2)}) collective-permute-start(f32[1,128]{1,0:T(1,128)S(1)} %add.91), channel_id=1, source_target_pairs={{0,8},{4,12},{8,0},{12,4},{1,9},{5,13},{9,1},{13,5},{2,10},{6,14},... | collective-permute-start | bytes 1544 | tf_op jit(solution)/shard_map/lg/sc/ppermute | solution.py:197
  351.9 8.8 %collective-permute-start.100 = (bf16[2,64,384]{2,1,0:T(8,128)(2,1)S(1)}, bf16[2,64,384]{2,1,0:T(8,128)(2,1)S(1)}, u32[]{:S(2)}, u32[]{:S(2)}) collective-permute-start(bf16[2,64,384]{2,1,0:T(8,128)(2,1)S(1)} %get-tuple-element.360), channel_id=1, source_target_pairs={{0,16},{16,0},{1,17},{17,1},{2,18},{18,2},{3,19},{19,3},{4,20},{20... | collective-permute-start | bytes 294920 | tf_op jit(solution)/shard_map/dx/ppermute | solution.py:197
  (103 other events, 854.5 us)
Sparse Core Ops, SparseCore 0:
  62.1 29.8 all-gather.1
  243.3 29.6 reduce-scatter.4
  283.6 18.6 reduce-scatter.6
  304.5 31.7 reduce-scatter.8
  338.5 19.1 reduce-scatter.10
